TPU v7x, 32 devices: a whole 2x2x4 slice. The times are simulated.
32 devices in a mesh: wide: 16 (over z, y, core), narrow: 2 (over x).
Axes of the slice: x: 2, y: 2, z: 4, core: 2. Of those that a mesh axis runs over, the one named last changes fastest.
Arguments:
- tokens: bfloat16 [32, 1024, 1024], P('wide', 'narrow'), may hold values from -6 to 6
- doc_ids: int32 [32, 1024], P('wide'), may hold values from 0 to 3, as said below
- w_qkv: bfloat16 [1024, 3072], replicated, may hold values from -0.1875 to 0.1875
- w_out: bfloat16 [1024, 1024], replicated, may hold values from -0.1875 to 0.1875
- w_up: bfloat16 [1024, 4096], replicated, may hold values from -0.1875 to 0.1875
- w_down: bfloat16 [4096, 1024], replicated, may hold values from -0.09375 to 0.09375
- norm_gains: float32 [4, 1024], replicated, may hold values from 0.5 to 1.5
- norm_biases: float32 [4, 1024], replicated, may hold values from -2 to 2
- cotangent: bfloat16 [32, 1024, 1024], P('wide', 'narrow'), may hold values from -6 to 6
Outputs:
- layer_out: bfloat16 [32, 1024, 1024], P('wide', 'narrow')
- grad_tokens: bfloat16 [32, 1024, 1024], P('wide', 'narrow')
- grad_qkv: float32 [1024, 3072], P('narrow')
- grad_out_proj: float32 [1024, 1024], P('narrow')
- grad_up: float32 [1024, 4096], P('narrow')
- grad_down: float32 [4096, 1024], P('narrow')
- grad_gains: float32 [4, 1024], P(None, 'narrow')
- grad_biases: float32 [4, 1024], P(None, 'narrow')
Inputs may be any that keep to these rules, and one draw needn't show every extreme that they name: `doc_ids`: each pack holds either one document of all 1024 positions (number 0 throughout) or four documents of 256 positions numbered 0 to 3 in order; exactly half of the packs are of each kind.
All inputs are finite; a program needn't handle non-finite values.
Results may differ from a plain program's by a relative error of at most 0.015.
Values may be sent and summed in bfloat16 or wider, within the bound.
No kernel may reach another device: no remote copies, remote signals or barrier semaphores. Data moves between devices by JAX's collectives and lax.ppermute only.
A program may use at most 384 MiB of HBM per device.

v0:
```python
from functools import partial
import math

import jax
import jax.numpy as jnp
from jax import lax
from jax.sharding import PartitionSpec as P

HEADS = 16
HEAD_DIM = 64


EPS = 1e-05


def layer_norm(values, gain_row, bias_row):
    centre = values - jnp.mean(values, axis=-1, keepdims=True)
    spread = jnp.mean(centre * centre, axis=-1, keepdims=True)
    return centre * lax.rsqrt(spread + EPS) * gain_row + bias_row


def mirrored_positions(pack_len, groups):
    places = jnp.arange(pack_len, dtype=jnp.int32)
    block_len = pack_len // (2 * groups)
    owner_dev = places // (2 * block_len)
    within = places % (2 * block_len)
    return jnp.where(
        within < block_len,
        owner_dev * block_len + within,
        (2 * groups - 1 - owner_dev) * block_len + within - block_len,
    )


def rotary_tables(places, head_size):
    halves = head_size // 2
    frequency = jnp.exp(
        -math.log(10000.0) * jnp.arange(halves, dtype=jnp.float32) * 2.0 / head_size
    )
    angles = places.astype(jnp.float32)[:, None] * frequency[None, :]
    cosine = jnp.cos(angles)
    sine_table = jnp.sin(angles)
    return (jnp.concatenate([cosine, cosine], -1), jnp.concatenate([sine_table, sine_table], -1))


def rotate_half(values):
    first_half, second_half = jnp.split(values, 2, axis=-1)
    return jnp.concatenate([-second_half, first_half], axis=-1)


def rotary(values, cosine, sine_table):
    return values * cosine[:, None, :] + rotate_half(values) * sine_table[:, None, :]


def rotary_back(grad_rows, cosine, sine_table):
    return grad_rows * cosine[:, None, :] - rotate_half(grad_rows * sine_table[:, None, :])


def product(formula, left, right):
    return jnp.einsum(formula, left, right, preferred_element_type=jnp.float32)


def masked_scores(query_part, key_part, allowed, scale):
    scores = product("qhd,khd->hqk", query_part, key_part) * scale
    return jnp.where(allowed[None], scores, -1e30)


def local(tokens, doc_ids, w_qkv, w_out, w_up, w_down, norm_gains, norm_biases, cotangent):
    narrow_size = lax.axis_size("narrow")
    tok_rows = tokens.shape[1]
    model_width = tokens.shape[2]
    ff_width = w_up.shape[1]
    head_count = HEADS
    head_size = HEAD_DIM
    per_group = min(4, head_count)
    scale = 1.0 / math.sqrt(head_size)
    pack_len = tok_rows * narrow_size
    places = mirrored_positions(pack_len, narrow_size)
    first_row = lax.axis_index("narrow") * tok_rows
    own_places = lax.dynamic_slice_in_dim(places, first_row, tok_rows)
    cosine, sine_table = rotary_tables(own_places, head_size)
    causal = own_places[:, None] >= places[None, :]
    gelu_tanh = partial(jax.nn.gelu, approximate=True)

    def micro_step(totals, item_parts):
        inputs, doc_row, upstream = item_parts
        documents = jnp.take(doc_row, places)
        own_docs = lax.dynamic_slice_in_dim(documents, first_row, tok_rows)
        allowed = causal & (own_docs[:, None] == documents[None, :])
        residual = inputs.astype(jnp.float32)
        normed, norm_back0 = jax.vjp(layer_norm, residual, norm_gains[0], norm_biases[0])
        normed_low = normed.astype(jnp.bfloat16)
        mixed = jnp.dot(normed_low, w_qkv, preferred_element_type=jnp.float32)
        query_raw = mixed[:, :model_width].reshape(tok_rows, head_count, head_size)
        key_raw = mixed[:, model_width : 2 * model_width].reshape(tok_rows, head_count, head_size)
        queries = rotary(query_raw, cosine, sine_table).astype(jnp.bfloat16)
        key_rows = rotary(key_raw, cosine, sine_table).astype(jnp.bfloat16)
        values = mixed[:, 2 * model_width :].astype(jnp.bfloat16)
        key_flat, value_flat = (
            lax.all_gather(key_rows.reshape(tok_rows, model_width), "narrow", axis=0, tiled=True),
            lax.all_gather(values, "narrow", axis=0, tiled=True),
        )
        all_keys = key_flat.reshape(pack_len, head_count, head_size)
        all_values = value_flat.reshape(pack_len, head_count, head_size)
        head_outs = []
        log_sums = []
        for first_head in range(0, head_count, per_group):
            head_part = slice(first_head, first_head + per_group)
            scores = masked_scores(queries[:, head_part], all_keys[:, head_part], allowed, scale)
            row_peak = jnp.max(scores, axis=-1, keepdims=True)
            row_total = jnp.sum(jnp.exp(scores - row_peak), axis=-1, keepdims=True)
            log_total = row_peak + jnp.log(row_total)
            weights = jnp.exp(scores - log_total).astype(jnp.bfloat16)
            head_outs.append(product("hqk,khd->qhd", weights, all_values[:, head_part]))
            log_sums.append(log_total)
        attended_low = (
            jnp.concatenate(head_outs, axis=1).reshape(tok_rows, model_width).astype(jnp.bfloat16)
        )
        branch = jnp.dot(attended_low, w_out, preferred_element_type=jnp.float32)
        post_attn, norm_back1 = jax.vjp(layer_norm, branch, norm_gains[1], norm_biases[1])
        middle = residual + post_attn
        normed2, norm_back2 = jax.vjp(layer_norm, middle, norm_gains[2], norm_biases[2])
        normed2_low = normed2.astype(jnp.bfloat16)
        hidden = jnp.dot(normed2_low, w_up, preferred_element_type=jnp.float32)
        active, gelu_back = jax.vjp(gelu_tanh, hidden)
        active_low = active.astype(jnp.bfloat16)
        branch2 = jnp.dot(active_low, w_down, preferred_element_type=jnp.float32)
        post_ffn, norm_back3 = jax.vjp(layer_norm, branch2, norm_gains[3], norm_biases[3])
        outputs = (middle + post_ffn).astype(jnp.bfloat16)
        grad_output = upstream.astype(jnp.float32)
        grad_branch2, gain_three, bias_three = norm_back3(grad_output)
        grad_branch2_low = grad_branch2.astype(jnp.bfloat16)
        down_term = product("tf,td->fd", active_low, grad_branch2_low)
        grad_active = product("td,fd->tf", grad_branch2_low, w_down)
        grad_hidden_low = gelu_back(grad_active)[0].astype(jnp.bfloat16)
        up_term = product("tm,tf->mf", normed2_low, grad_hidden_low)
        grad_normed2 = product("tf,mf->tm", grad_hidden_low, w_up)
        grad_part2, gain_two, bias_two = norm_back2(grad_normed2)
        grad_middle = grad_output + grad_part2
        grad_branch, gain_one, bias_one = norm_back1(grad_middle)
        grad_branch_low = grad_branch.astype(jnp.bfloat16)
        out_term = product("tm,tn->mn", attended_low, grad_branch_low)
        grad_attended = product("tn,mn->tm", grad_branch_low, w_out).astype(jnp.bfloat16)
        grad_heads = grad_attended.reshape(tok_rows, head_count, head_size)
        query_grads = []
        inner_sums = []
        score_grads = []
        weight_lows = []
        for group_number, first_head in enumerate(range(0, head_count, per_group)):
            head_part = slice(first_head, first_head + per_group)
            scores = masked_scores(queries[:, head_part], all_keys[:, head_part], allowed, scale)
            weights = jnp.exp(scores - log_sums[group_number])
            grad_weights = product(
                "qhd,khd->hqk", grad_heads[:, head_part], all_values[:, head_part]
            )
            inner = jnp.sum(weights * grad_weights, axis=-1, keepdims=True)
            grad_scores = (weights * (grad_weights - inner)).astype(jnp.bfloat16)
            query_grads.append(product("hqk,khd->qhd", grad_scores, all_keys[:, head_part]) * scale)
            inner_sums.append(inner)
            score_grads.append(grad_scores)
            weight_lows.append(weights.astype(jnp.bfloat16))
        grad_queries = jnp.concatenate(query_grads, axis=1)
        key_grads = []
        value_grads = []
        for group_number, first_head in enumerate(range(0, head_count, per_group)):
            head_part = slice(first_head, first_head + per_group)
            key_grads.append(
                product("hqk,qhd->khd", score_grads[group_number], queries[:, head_part]) * scale
            )
            value_grads.append(
                product("hqk,qhd->khd", weight_lows[group_number], grad_heads[:, head_part])
            )
        key_total = jnp.concatenate(key_grads, axis=1).reshape(pack_len, model_width)
        value_total = jnp.concatenate(value_grads, axis=1).reshape(pack_len, model_width)
        grad_keys, grad_values = (
            lax.psum_scatter(
                key_total.astype(jnp.bfloat16), "narrow", scatter_dimension=0, tiled=True
            ).astype(jnp.float32),
            lax.psum_scatter(
                value_total.astype(jnp.bfloat16), "narrow", scatter_dimension=0, tiled=True
            ).astype(jnp.float32),
        )
        grad_query_raw = rotary_back(grad_queries, cosine, sine_table).reshape(
            tok_rows, model_width
        )
        grad_key_raw = rotary_back(
            grad_keys.reshape(tok_rows, head_count, head_size), cosine, sine_table
        ).reshape(tok_rows, model_width)
        grad_mixed = jnp.concatenate([grad_query_raw, grad_key_raw, grad_values], axis=1).astype(
            jnp.bfloat16
        )
        qkv_term = product("tm,tn->mn", normed_low, grad_mixed)
        grad_normed = product("tn,mn->tm", grad_mixed, w_qkv)
        grad_part0, gain_zero, bias_zero = norm_back0(grad_normed)
        grad_inputs = (grad_middle + grad_part0).astype(jnp.bfloat16)
        norm_term = jnp.stack(
            [gain_zero, gain_one, gain_two, gain_three, bias_zero, bias_one, bias_two, bias_three]
        )
        updated = (
            totals[0] + qkv_term,
            totals[1] + out_term,
            totals[2] + up_term,
            totals[3] + down_term,
            totals[4] + norm_term,
        )
        return (updated, (outputs, grad_inputs))

    start_totals = (
        jnp.zeros((model_width, 3 * model_width), jnp.float32),
        jnp.zeros((model_width, model_width), jnp.float32),
        jnp.zeros((model_width, ff_width), jnp.float32),
        jnp.zeros((ff_width, model_width), jnp.float32),
        jnp.zeros((8, model_width), jnp.float32),
    )
    totals, stacked = lax.scan(micro_step, start_totals, (tokens, doc_ids, cotangent))
    layer_out, grad_tokens = stacked
    local_terms = (totals[0], totals[1], totals[2], totals[3], jnp.transpose(totals[4]))
    narrowed = (
        lax.psum_scatter(
            local_terms[0].astype(jnp.bfloat16), "narrow", scatter_dimension=0, tiled=True
        ).astype(jnp.float32),
        lax.psum_scatter(
            local_terms[1].astype(jnp.bfloat16), "narrow", scatter_dimension=0, tiled=True
        ).astype(jnp.float32),
        lax.psum_scatter(
            local_terms[2].astype(jnp.bfloat16), "narrow", scatter_dimension=0, tiled=True
        ).astype(jnp.float32),
        lax.psum_scatter(
            local_terms[3].astype(jnp.bfloat16), "narrow", scatter_dimension=0, tiled=True
        ).astype(jnp.float32),
        lax.psum_scatter(
            local_terms[4].astype(jnp.bfloat16), "narrow", scatter_dimension=0, tiled=True
        ).astype(jnp.float32),
    )
    summed = lax.psum((narrowed[0], narrowed[1], narrowed[2], narrowed[3], narrowed[4]), "wide")
    norm_part = jnp.transpose(summed[4])
    return (
        layer_out,
        grad_tokens,
        summed[0],
        summed[1],
        summed[2],
        summed[3],
        norm_part[:4],
        norm_part[4:],
    )


def solution(mesh):
    return jax.shard_map(
        local,
        mesh=mesh,
        in_specs=(
            P("wide", "narrow", None),
            P("wide", None),
            P(),
            P(),
            P(),
            P(),
            P(),
            P(),
            P("wide", "narrow", None),
        ),
        out_specs=(
            P("wide", "narrow", None),
            P("wide", "narrow", None),
            P("narrow", None),
            P("narrow", None),
            P("narrow", None),
            P("narrow", None),
            P(None, "narrow"),
            P(None, "narrow"),
        ),
        check_vma=False,
    )
```

profile of v0, /device:TPU:0, one launch (start us, length us, event | category | flops | bytes accessed | tf_op | source)
XLA Modules:
  0.0 1606.1 jit_solution(11097686850534382987)
XLA Ops:
  11.0 736.8 %while.26 = (s32[]{:T(128)}, f32[1024,3072]{1,0:T(8,128)}, f32[1024,1024]{1,0:T(8,128)}, f32[1024,4096]{1,0:T(8,128)}, f32[4096,1024]{1,0:T(8,128)}, /*index=5*/...) while((s32[]{:T(128)}, f32[1024,3072]{1,0:T(8,128)}, ...), condition=%wide.region_39.40_spmd.clone.clone, body=%wide.region_0.39_spmd.clone.clone.sunk | while | flops 45539713024 | bytes 1463145216 | solution.py:214
  56.8 21.1 %all-gather.5.cloned.1.call-done = bf16[1024,1024]{1,0:T(8,128)(2,1)} async-done(((bf16[512,1024]{1,0:T(8,128)(2,1)}), bf16[1024,1024]{1,0:T(8,128)(2,1)}) %all-gather.5.cloned.1.call-update) | async-done | bytes 2097168 | tf_op jit(solution)/shard_map/while/body/eval_jaxpr/all_gather | solution.py:99
  94.9 11.9 exponential_reduce_fusion.6
  106.8 9.3 exponential_reduce_fusion.7
  140.1 11.4 fusion.371
  151.5 8.7 fusion.372
  162.8 13.2 fusion.376
  176.0 9.8 multiply_reduce_fusion.20
  226.8 21.2 %multiply_reduce_fusion.22 = (f32[4,512]{1,0:T(4,128)S(1)}, f32[4,512]{1,0:T(4,128)S(1)}, f32[4,512]{1,0:T(4,128)S(1)}, f32[4,512]{1,0:T(4,128)S(1)}, f32[4,512,1024]{2,1,0:T(8,128)}) fusion(f32[4,512,1024]{2,1,0:T(8,128)} %get-tuple-element.760, f32[4,512]{1,0:T(4,128)S(1)} %log_add_fusion.11, pred[512,1024]{1,0:T(8,128)(4,1)S(1)} %compare_and_fusion.2, ...), kind=kOutput, calls=%fused_computation.22.clone.1 | convolution fusion | flops 310370304 | bytes 69271552 | tf_op jit(solution)/shard_map/while/body/eval_jaxpr/qhd,khd->hqk/dot_general | solution.py:59
  248.0 26.9 %multiply_convert_fusion.10 = (bf16[4,512,1024]{2,1,0:T(8,128)(2,1)}, bf16[4,512,1024]{2,1,0:T(8,128)(2,1)}, bf16[4,512,1024]{2,1,0:T(8,128)(2,1)}, bf16[4,512,1024]{2,1,0:T(8,128)(2,1)}) fusion(f32[4,512,1024]{2,1,0:T(8,128)} %get-tuple-element.792, f32[4,512,1024]{2,1,0:T(8,128)} %get-tuple-element.760, f32[4,512]{1,0:T(4,128)S(1)} %get-tuple-element.793, ...), kind=kLoop, calls=%fused_computation.21.clone.1 | loop fusion | flops 50331648 | bytes 84475904 | tf_op jit(solution)/shard_map/while/body/eval_jaxpr/convert_element_type | solution.py:156
  313.4 12.9 select_add_fusion.13
  333.4 20.6 %reduce-scatter.18.cloned.1.call-done = bf16[512,1024]{0,1:T(8,128)(2,1)} async-done(((bf16[1024,1024]{0,1:T(8,128)(2,1)}), bf16[512,1024]{0,1:T(8,128)(2,1)}) %reduce-scatter.18.cloned.1.call-update) | async-done | bytes 1048592 | tf_op jit(solution)/shard_map/while/body/eval_jaxpr/reduce_scatter | solution.py:178
  367.7 9.9 select_add_fusion.10
  423.9 18.2 %all-gather.5.cloned.1.call-done = bf16[1024,1024]{1,0:T(8,128)(2,1)} async-done(((bf16[512,1024]{1,0:T(8,128)(2,1)}), bf16[1024,1024]{1,0:T(8,128)(2,1)}) %all-gather.5.cloned.1.call-update) | async-done | bytes 2097168 | tf_op jit(solution)/shard_map/while/body/eval_jaxpr/all_gather | solution.py:99
  459.0 11.9 exponential_reduce_fusion.6
  471.0 9.3 exponential_reduce_fusion.7
  504.2 11.4 fusion.371
  526.6 13.2 fusion.376
  539.9 10.0 multiply_reduce_fusion.20
  590.9 21.2 %multiply_reduce_fusion.22 = (f32[4,512]{1,0:T(4,128)S(1)}, f32[4,512]{1,0:T(4,128)S(1)}, f32[4,512]{1,0:T(4,128)S(1)}, f32[4,512]{1,0:T(4,128)S(1)}, f32[4,512,1024]{2,1,0:T(8,128)}) fusion(f32[4,512,1024]{2,1,0:T(8,128)} %get-tuple-element.760, f32[4,512]{1,0:T(4,128)S(1)} %log_add_fusion.11, pred[512,1024]{1,0:T(8,128)(4,1)S(1)} %compare_and_fusion.2, ...), kind=kOutput, calls=%fused_computation.22.clone.1 | convolution fusion | flops 310370304 | bytes 69271552 | tf_op jit(solution)/shard_map/while/body/eval_jaxpr/qhd,khd->hqk/dot_general | solution.py:59
  612.1 26.9 %multiply_convert_fusion.10 = (bf16[4,512,1024]{2,1,0:T(8,128)(2,1)}, bf16[4,512,1024]{2,1,0:T(8,128)(2,1)}, bf16[4,512,1024]{2,1,0:T(8,128)(2,1)}, bf16[4,512,1024]{2,1,0:T(8,128)(2,1)}) fusion(f32[4,512,1024]{2,1,0:T(8,128)} %get-tuple-element.792, f32[4,512,1024]{2,1,0:T(8,128)} %get-tuple-element.760, f32[4,512]{1,0:T(4,128)S(1)} %get-tuple-element.793, ...), kind=kLoop, calls=%fused_computation.21.clone.1 | loop fusion | flops 50331648 | bytes 84475904 | tf_op jit(solution)/shard_map/while/body/eval_jaxpr/convert_element_type | solution.py:156
  668.9 11.9 select_add_fusion.12
  680.8 15.9 select_add_fusion.13
  703.9 14.3 reduce-scatter.18.cloned.1.call-done
  731.9 12.7 select_add_fusion.10
  761.6 9.0 convert_element_type.217
  770.7 9.1 convert_element_type.219
  780.5 14.5 reduce-scatter.10.cloned.1.call-done
  795.0 79.8 %reduce-scatter.8.cloned.1.call-done = bf16[512,3072]{1,0:T(8,128)(2,1)} async-done(((bf16[1024,3072]{1,0:T(8,128)(2,1)}), bf16[512,3072]{1,0:T(8,128)(2,1)}) %reduce-scatter.8.cloned.1.call-update) | async-done | bytes 3145744 | tf_op jit(solution)/shard_map/reduce_scatter | solution.py:218
  874.8 102.2 %reduce-scatter.12.cloned.1.call-done = bf16[512,4096]{1,0:T(8,128)(2,1)} async-done(((bf16[1024,4096]{1,0:T(8,128)(2,1)}), bf16[512,4096]{1,0:T(8,128)(2,1)}) %reduce-scatter.12.cloned.1.call-update) | async-done | bytes 4194320 | tf_op jit(solution)/shard_map/reduce_scatter | solution.py:224
  977.0 102.2 %reduce-scatter.14.cloned.1.call-done = bf16[2048,1024]{1,0:T(8,128)(2,1)} async-done(((bf16[4096,1024]{1,0:T(8,128)(2,1)}), bf16[2048,1024]{1,0:T(8,128)(2,1)}) %reduce-scatter.14.cloned.1.call-update) | async-done | bytes 4194320 | tf_op jit(solution)/shard_map/reduce_scatter | solution.py:227
  1079.2 518.5 %all-reduce.2 = (f32[512,3072]{1,0:T(8,128)}, f32[512,1024]{1,0:T(8,128)}, f32[512,4096]{1,0:T(8,128)}, f32[2048,1024]{1,0:T(8,128)}, f32[8,512]{1,0:T(8,128)S(1)}) all-reduce(bf16[512,3072]{1,0:T(8,128)(2,1)} %reduce-scatter.8.cloned.1.call-done, ...), channel_id=1, replica_groups=mesh['wide'=16,'narrow'=2] {'wide'}, use_global_device_ids=true, to_apply=%region_41.42 | all-reduce | flops 6295552 | bytes 37781504 | tf_op jit(solution)/shard_map/psum | solution.py:234
  (586 shorter events, 395.5 us)
Async XLA Ops:
  11.0 66.9 %all-gather.5.cloned.1.call-start = ((), (), s32[]{:S(2)}) async-start(), calls=%async_computation.13 | async-start | bytes 3145728 | tf_op jit(solution)/shard_map/while/body/eval_jaxpr/all_gather | solution.py:99
  12.6 14.0 copy-start.55
  20.9 119.2 %copy-start.53 = (f32[1,1024]{1,0:T(1,128)}, f32[1,1024]{1,0:T(1,128)S(1)}, u32[]{:S(2)}) copy-start(f32[1,1024]{1,0:T(1,128)S(1)} %get-tuple-element.777) | copy-start | bytes 12292 | tf_op jit(solution)/shard_map/while
  41.9 74.3 %all-gather.3.cloned.1.call-start = ((), (), s32[]{:S(2)}) async-start(), calls=%async_computation.12 | async-start | bytes 3145728 | tf_op jit(solution)/shard_map/while/body/eval_jaxpr/all_gather | solution.py:100
  44.9 281.5 %reduce-scatter.20.cloned.1.call-start = ((), (), s32[]{:S(2)}) async-start(), calls=%async_computation.15 | async-start | bytes 3145728 | tf_op jit(solution)/shard_map/while/body/eval_jaxpr/reduce_scatter | solution.py:175
  55.6 26.3 %copy-start.42 = (bf16[512,16,64]{0,2,1:T(8,128)(2,1)S(1)}, bf16[512,16,64]{0,2,1:T(8,128)(2,1)}, u32[]{:S(2)}) copy-start(bf16[512,16,64]{0,2,1:T(8,128)(2,1)} %fusion.358) | copy-start | bytes 3145732 | tf_op jit(solution)/shard_map/while
  84.4 22.5 %copy-start = (f32[4,512,1024]{2,1,0:T(8,128)}, f32[4,512,1024]{2,1,0:T(8,128)S(1)}, u32[]{:S(2)}) copy-start(f32[4,512,1024]{2,1,0:T(8,128)S(1)} %fusion.362) | copy-start | bytes 25165828 | tf_op jit(solution)/shard_map/while
  139.7 46.1 %copy-start.1 = (f32[512,1024]{1,0:T(8,128)}, f32[512,1024]{1,0:T(8,128)S(1)}, u32[]{:S(2)}) copy-start(f32[512,1024]{1,0:T(8,128)S(1)} %get-tuple-element.774) | copy-start | bytes 6291460 | tf_op jit(solution)/shard_map/while
  287.3 66.7 %reduce-scatter.18.cloned.1.call-start = ((), (), s32[]{:S(2)}) async-start(), calls=%async_computation.14 | async-start | bytes 3145728 | tf_op jit(solution)/shard_map/while/body/eval_jaxpr/reduce_scatter | solution.py:178
  330.2 23.8 %copy-start.8 = (bf16[2,512,1024]{2,1,0:T(8,128)(2,1)S(1)}, bf16[2,512,1024]{2,1,0:T(8,128)(2,1)}, u32[]{:S(2)}) copy-start(bf16[2,512,1024]{2,1,0:T(8,128)(2,1)} %get-tuple-element.877) | copy-start | bytes 6291460 | tf_op jit(solution)/shard_map/while
  330.2 23.8 %copy-start.50 = (f32[1,1024]{1,0:T(1,128)S(1)}, f32[1,1024]{1,0:T(1,128)}, u32[]{:S(2)}) copy-start(f32[1,1024]{1,0:T(1,128)} %copy-done.49) | copy-start | bytes 12292 | tf_op jit(solution)/shard_map/while
  330.2 23.8 %copy-start.56 = (f32[512]{0:T(512)S(1)}, f32[512]{0:T(512)}, u32[]{:S(2)}) copy-start(f32[512]{0:T(512)} %copy-done.55) | copy-start | bytes 6148 | tf_op jit(solution)/shard_map/while
  362.9 14.7 copy-start.60
  377.8 64.2 %all-gather.5.cloned.1.call-start = ((), (), s32[]{:S(2)}) async-start(), calls=%async_computation.13 | async-start | bytes 3145728 | tf_op jit(solution)/shard_map/while/body/eval_jaxpr/all_gather | solution.py:99
  387.8 116.4 %copy-start.53 = (f32[1,1024]{1,0:T(1,128)}, f32[1,1024]{1,0:T(1,128)S(1)}, u32[]{:S(2)}) copy-start(f32[1,1024]{1,0:T(1,128)S(1)} %get-tuple-element.777) | copy-start | bytes 12292 | tf_op jit(solution)/shard_map/while
  408.8 71.6 %all-gather.3.cloned.1.call-start = ((), (), s32[]{:S(2)}) async-start(), calls=%async_computation.12 | async-start | bytes 3145728 | tf_op jit(solution)/shard_map/while/body/eval_jaxpr/all_gather | solution.py:100
  411.8 285.0 %reduce-scatter.20.cloned.1.call-start = ((), (), s32[]{:S(2)}) async-start(), calls=%async_computation.15 | async-start | bytes 3145728 | tf_op jit(solution)/shard_map/while/body/eval_jaxpr/reduce_scatter | solution.py:175
  422.6 23.4 %copy-start.42 = (bf16[512,16,64]{0,2,1:T(8,128)(2,1)S(1)}, bf16[512,16,64]{0,2,1:T(8,128)(2,1)}, u32[]{:S(2)}) copy-start(bf16[512,16,64]{0,2,1:T(8,128)(2,1)} %fusion.358) | copy-start | bytes 3145732 | tf_op jit(solution)/shard_map/while
  448.5 22.5 %copy-start = (f32[4,512,1024]{2,1,0:T(8,128)}, f32[4,512,1024]{2,1,0:T(8,128)S(1)}, u32[]{:S(2)}) copy-start(f32[4,512,1024]{2,1,0:T(8,128)S(1)} %fusion.362) | copy-start | bytes 25165828 | tf_op jit(solution)/shard_map/while
  503.8 46.1 %copy-start.1 = (f32[512,1024]{1,0:T(8,128)}, f32[512,1024]{1,0:T(8,128)S(1)}, u32[]{:S(2)}) copy-start(f32[512,1024]{1,0:T(8,128)S(1)} %get-tuple-element.774) | copy-start | bytes 6291460 | tf_op jit(solution)/shard_map/while
  651.4 66.8 %reduce-scatter.18.cloned.1.call-start = ((), (), s32[]{:S(2)}) async-start(), calls=%async_computation.14 | async-start | bytes 3145728 | tf_op jit(solution)/shard_map/while/body/eval_jaxpr/reduce_scatter | solution.py:178
  680.8 16.0 copy-start.44
  680.8 16.0 copy-start.45
  700.6 17.6 %copy-start.8 = (bf16[2,512,1024]{2,1,0:T(8,128)(2,1)S(1)}, bf16[2,512,1024]{2,1,0:T(8,128)(2,1)}, u32[]{:S(2)}) copy-start(bf16[2,512,1024]{2,1,0:T(8,128)(2,1)} %get-tuple-element.877) | copy-start | bytes 6291460 | tf_op jit(solution)/shard_map/while
  700.6 17.6 %copy-start.50 = (f32[1,1024]{1,0:T(1,128)S(1)}, f32[1,1024]{1,0:T(1,128)}, u32[]{:S(2)}) copy-start(f32[1,1024]{1,0:T(1,128)} %copy-done.49) | copy-start | bytes 12292 | tf_op jit(solution)/shard_map/while
  700.6 17.6 %copy-start.56 = (f32[512]{0:T(512)S(1)}, f32[512]{0:T(512)}, u32[]{:S(2)}) copy-start(f32[512]{0:T(512)} %copy-done.55) | copy-start | bytes 6148 | tf_op jit(solution)/shard_map/while
  727.1 17.5 %copy-start.60 = (f32[8,1024]{1,0:T(8,128)}, f32[8,1024]{1,0:T(8,128)S(1)}, u32[]{:S(2)}) copy-start(f32[8,1024]{1,0:T(8,128)S(1)} %select_add_fusion.14) | copy-start | bytes 98308 | tf_op jit(solution)/shard_map/while
  747.8 31.9 %reduce-scatter.16.cloned.1.call-start = ((), (), s32[]{:S(2)}) async-start(), calls=%async_computation.11 | async-start | bytes 24576 | tf_op jit(solution)/shard_map/reduce_scatter | solution.py:230
  749.3 45.7 %reduce-scatter.10.cloned.1.call-start = ((), (), s32[]{:S(2)}) async-start(), calls=%async_computation.8 | async-start | bytes 3145728 | tf_op jit(solution)/shard_map/reduce_scatter | solution.py:221
  753.2 121.6 %reduce-scatter.8.cloned.1.call-start = ((), (), s32[]{:S(2)}) async-start(), calls=%async_computation.7 | async-start | bytes 9437184 | tf_op jit(solution)/shard_map/reduce_scatter | solution.py:218
  761.5 215.5 %reduce-scatter.12.cloned.1.call-start = ((), (), s32[]{:S(2)}) async-start(), calls=%async_computation.9 | async-start | bytes 12582912 | tf_op jit(solution)/shard_map/reduce_scatter | solution.py:224
  770.6 308.6 %reduce-scatter.14.cloned.1.call-start = ((), (), s32[]{:S(2)}) async-start(), calls=%async_computation.10 | async-start | bytes 12582912 | tf_op jit(solution)/shard_map/reduce_scatter | solution.py:227
  (147 other events, 800.3 us)
Sparse Core Ops, SparseCore 0:
  42.1 35.8 all-gather.4
  79.5 33.0 all-gather.2
  287.4 31.8 reduce-scatter.19
  322.0 31.8 reduce-scatter.17
  408.9 33.0 all-gather.4
  443.5 33.0 all-gather.2
  651.5 31.8 reduce-scatter.19
  686.2 31.8 reduce-scatter.17
Sparse Core Ops, SparseCore 1:
  750.5 9.9 reduce-scatter.15
  763.1 31.8 reduce-scatter.9
  797.7 77.0 reduce-scatter.7
  877.7 99.2 reduce-scatter.11
  979.9 99.2 reduce-scatter.13
where the time goes:
time: 1620 us; the launch traced here: 1610 us
  blocking collectives  519 us (32%)
  matrix products  408 us (25%)
  waiting for transfers between devices  373 us (23%)
  other arithmetic  188 us (12%)
  local copies, waits for them, and re-layouts  95.1 us (6%)
    psum x1, blocking collectives, local(): lax.psum((narrowed[0], narrowed[1], narrowed[2], narrowed[3], narrowed[4]...  519 us
    dot_general x64, matrix products, product(): return jnp.einsum(formula, left, right, preferred_element_type=jnp.float32)  354 us
    reduce_scatter x1, waiting for transfers between devices, local(): lax.psum_scatter(local_terms[3].astype(jnp.bfloat16), 'narrow', scatter_d...  102 us
    reduce_scatter x1, waiting for transfers between devices, local(): lax.psum_scatter(local_terms[2].astype(jnp.bfloat16), 'narrow', scatter_d...  102 us
    reduce_scatter x1, waiting for transfers between devices, local(): lax.psum_scatter(local_terms[0].astype(jnp.bfloat16), 'narrow', scatter_d...  79.8 us
    convert_element_type x2, other arithmetic, micro_step(): grad_scores = (weights * (grad_weights - inner)).astype(jnp.bfloat16)  53.7 us
    all_gather x2, waiting for transfers between devices, micro_step(): lax.all_gather(key_rows.reshape(tok_rows, model_width), 'narrow', axis=0,...  39.2 us
    reduce_scatter x2, waiting for transfers between devices, micro_step(): lax.psum_scatter(value_total.astype(jnp.bfloat16), 'narrow', scatter_dime...  34.9 us
  transfers between devices with their start and end apart: 13, of which 8 were waited for; matrix products, arithmetic and copies ran while one was open for 14% of the time, Pallas kernels for 0%

commit v1 on v0

v1 whole, which is shorter than its diff:
```python
import functools
import math

import jax
import jax.numpy as jnp
from jax import lax
from jax.experimental import pallas as pl
from jax.experimental.pallas import tpu as pltpu
from jax.sharding import PartitionSpec as P

HEAD_DIM = 64
EPS = 1e-05
F32 = jnp.float32
BF16 = jnp.bfloat16
TILE = 256
GROUP = 256
VMEM_LIMIT = 60 * 1024 * 1024
NN = (((1,), (0,)), ((), ()))
NT = (((1,), (1,)), ((), ()))
TN = (((0,), (0,)), ((), ()))


def dot(left, right, dims=NN):
    return lax.dot_general(left, right, dims, preferred_element_type=F32)


def params(**extra):
    return pltpu.CompilerParams(vmem_limit_bytes=VMEM_LIMIT, **extra)


def whole(shape):
    return pl.BlockSpec(shape, lambda *_: (0,) * len(shape), pipeline_mode=pl.Buffered(1))


def norm_parts(rows):
    centre = rows - jnp.mean(rows, axis=-1, keepdims=True)
    rstd = lax.rsqrt(jnp.mean(centre * centre, axis=-1, keepdims=True) + EPS)
    return centre * rstd, rstd


def norm_back(unit, rstd, gain, grad):
    scaled = grad * gain
    first = jnp.mean(scaled, axis=-1, keepdims=True)
    second = jnp.mean(scaled * unit, axis=-1, keepdims=True)
    return rstd * (scaled - first - unit * second)


def token_sum(rows):
    return jnp.sum(rows, axis=0, keepdims=True)


def project_kernel(tok, w, gains, biases, cosine, sine, *refs):
    normed_out, mixed_out = refs[-2:]
    unit, _ = norm_parts(tok[...].astype(F32))
    normed = (unit * gains[0:1, :] + biases[0:1, :]).astype(BF16)
    normed_out[...] = normed
    width = tok.shape[1]
    lanes = lax.broadcasted_iota(jnp.int32, (TILE, 128), 1)
    first_half = lanes % HEAD_DIM < HEAD_DIM // 2
    scale = 1.0 / math.sqrt(HEAD_DIM)
    cos = cosine[...]
    sin = sine[...]
    for start in range(0, 3 * width, 256):
        part = dot(normed, w[:, start : start + 256])
        if start >= 2 * width:
            mixed_out[:, start : start + 256] = part.astype(BF16)
            continue
        for sub in range(0, 256, 128):
            u = part[:, sub : sub + 128]
            turned = jnp.where(first_half, pltpu.roll(u, 96, 1), pltpu.roll(u, 32, 1))
            out = u * cos + turned * sin
            out = out.astype(BF16)
            if start < width:
                out = out * jnp.asarray(scale, BF16)
            mixed_out[:, start + sub : start + sub + 128] = out


def project(tok, w_qkv, gains, biases, cosine, sine, first_block, earlier, pack_len):
    rows, width = tok.shape
    wide = w_qkv.shape[1]
    out_shape = (
        jax.ShapeDtypeStruct((pack_len, width), BF16),
        jax.ShapeDtypeStruct((pack_len, wide), BF16),
    )
    in_specs = [
        pl.BlockSpec((TILE, width), lambda i: (i, 0)),
        whole((width, wide)),
        whole(gains.shape),
        whole(biases.shape),
        pl.BlockSpec((TILE, 128), lambda i: (i + first_block, 0)),
        pl.BlockSpec((TILE, 128), lambda i: (i + first_block, 0)),
    ]
    args = [tok, w_qkv, gains, biases, cosine, sine]
    aliases = {}
    if earlier is not None:
        in_specs += [pl.BlockSpec(memory_space=pl.ANY)] * 2
        aliases = {6: 0, 7: 1}
        args += list(earlier)
    return pl.pallas_call(
        project_kernel,
        grid=(rows // TILE,),
        in_specs=in_specs,
        out_specs=(
            pl.BlockSpec((TILE, width), lambda i: (i + first_block, 0)),
            pl.BlockSpec((TILE, wide), lambda i: (i + first_block, 0)),
        ),
        out_shape=out_shape,
        input_output_aliases=aliases,
        compiler_params=params(),
        name="project",
    )(*args)


def diagonal_mask(scores):
    size = scores.shape[1]
    first = scores.shape[0] - size
    keys = lax.broadcasted_iota(jnp.int32, (size, size), 0)
    asks = lax.broadcasted_iota(jnp.int32, (size, size), 1)
    tail = jnp.where(keys <= asks, scores[first:], -1e30)
    if first == 0:
        return tail
    return jnp.concatenate([scores[:first], tail], axis=0)


def attend_kernel(info, q, k, v, out, stats, key_heads, q_t, v_t, out_t):
    heads = GROUP // HEAD_DIM
    blocks = q.shape[0] // TILE
    for i in range(blocks):
        rows = slice(i * TILE, (i + 1) * TILE)
        at = pl.multiple_of(info[i] * TILE, TILE)
        q_t[:, pl.ds(at, TILE)] = q[rows, :].T
        v_t[:, pl.ds(at, TILE)] = v[rows, :].T
        for h in range(heads):
            key_heads[h, pl.ds(at, TILE), :] = k[rows, h * HEAD_DIM : (h + 1) * HEAD_DIM]

    def one_head(h, first_key):
        head_rows = pl.ds(pl.multiple_of(h * HEAD_DIM, HEAD_DIM), HEAD_DIM)
        for block in range(blocks):
            cols = slice(block * TILE, (block + 1) * TILE)
            keys = slice(first_key(block), (block + 1) * TILE)
            scores = diagonal_mask(dot(key_heads[h, keys, :], q_t[head_rows, cols]))
            peak = jnp.max(scores, axis=0, keepdims=True)
            weights = jnp.exp(scores - peak)
            total = jnp.sum(weights, axis=0, keepdims=True)
            mixed = dot(v_t[head_rows, keys], weights.astype(BF16))
            out_t[head_rows, cols] = mixed * (1.0 / total)
            stats[0, pl.ds(h, 1), cols] = peak + jnp.log(total)

    many = info[blocks] != 0

    @pl.when(jnp.logical_not(many))
    def _():
        @pl.loop(0, heads)
        def _(h):
            one_head(h, lambda block: 0)

    @pl.when(many)
    def _():
        @pl.loop(0, heads)
        def _(h):
            one_head(h, lambda block: block * TILE)

    for i in range(blocks):
        at = pl.multiple_of(info[i] * TILE, TILE)
        out[i * TILE : (i + 1) * TILE, :] = out_t[:, pl.ds(at, TILE)].T.astype(BF16)


def attend(info, mixed):
    rows, wide = mixed.shape
    width = wide // 3
    groups = width // GROUP
    heads = GROUP // HEAD_DIM
    return pl.pallas_call(
        attend_kernel,
        grid_spec=pltpu.PrefetchScalarGridSpec(
            num_scalar_prefetch=1,
            grid=(groups,),
            in_specs=[
                pl.BlockSpec((rows, GROUP), lambda g, s: (0, g)),
                pl.BlockSpec((rows, GROUP), lambda g, s: (0, g + groups)),
                pl.BlockSpec((rows, GROUP), lambda g, s: (0, g + 2 * groups)),
            ],
            out_specs=(
                pl.BlockSpec((rows, GROUP), lambda g, s: (0, g)),
                pl.BlockSpec((1, heads, rows), lambda g, s: (g, 0, 0)),
            ),
            scratch_shapes=[
                pltpu.VMEM((heads, rows, HEAD_DIM), BF16),
                pltpu.VMEM((GROUP, rows), BF16),
                pltpu.VMEM((GROUP, rows), BF16),
                pltpu.VMEM((GROUP, rows), F32),
            ],
        ),
        out_shape=(
            jax.ShapeDtypeStruct((rows, width), BF16),
            jax.ShapeDtypeStruct((groups, heads, rows), F32),
        ),
        compiler_params=params(),
        name="attend",
    )(info, mixed, mixed, mixed)


def feed_kernel(tok, cot, att, w_out, w_up, w_down, gains, biases,
                layer_out, branch_out, normed2_out, active_out, back2_out, hidden_back_out, sums,
                slope):
    chunk = 1024
    residual = tok[...].astype(F32)
    branch = dot(att[...], w_out[...])
    branch_out[...] = branch
    unit1, _ = norm_parts(branch)
    middle = residual + unit1 * gains[1:2, :] + biases[1:2, :]
    unit2, _ = norm_parts(middle)
    normed2 = (unit2 * gains[2:3, :] + biases[2:3, :]).astype(BF16)
    normed2_out[...] = normed2
    ff = w_up.shape[1]
    root = math.sqrt(2.0 / math.pi)
    branch2 = jnp.zeros_like(branch)
    for start in range(0, ff, chunk):
        cols = slice(start, start + chunk)
        z = dot(normed2, w_up[:, cols])
        square = z * z
        bend = jnp.tanh(z * (root + (root * 0.044715) * square))
        half = 0.5 + 0.5 * bend
        active = (z * half).astype(BF16)
        active_out[:, cols] = active
        inner = (0.5 * root) + (1.5 * root * 0.044715) * square
        slope[:, cols] = half + z * (1.0 - bend * bend) * inner
        branch2 = branch2 + dot(active, w_down[cols, :])
    unit3, rstd3 = norm_parts(branch2)
    layer_out[...] = (middle + unit3 * gains[3:4, :] + biases[3:4, :]).astype(BF16)
    upstream = cot[...].astype(F32)
    back2 = norm_back(unit3, rstd3, gains[3:4, :], upstream).astype(BF16)
    back2_out[...] = back2

    @pl.when(pl.program_id(0) == 0)
    def _():
        sums[...] = jnp.zeros_like(sums)

    sums[0:1, :] += token_sum(upstream * unit3)
    sums[1:2, :] += token_sum(upstream)
    for start in range(0, ff, chunk):
        cols = slice(start, start + chunk)
        grad_active = dot(back2, w_down[cols, :], NT)
        hidden_back_out[:, cols] = (grad_active * slope[:, cols]).astype(BF16)


def feed(tok, cot, att, w_out, w_up, w_down, gains, biases):
    rows, width = tok.shape
    ff = w_up.shape[1]
    row_block = lambda size: pl.BlockSpec((TILE, size), lambda i: (i, 0))
    return pl.pallas_call(
        feed_kernel,
        grid=(rows // TILE,),
        in_specs=[
            row_block(width), row_block(width), row_block(width),
            whole(w_out.shape), whole(w_up.shape), whole(w_down.shape),
            whole(gains.shape), whole(biases.shape),
        ],
        out_specs=(
            row_block(width), row_block(width), row_block(width), row_block(ff),
            row_block(width), row_block(ff), pl.BlockSpec((8, width), lambda i: (0, 0)),
        ),
        out_shape=(
            jax.ShapeDtypeStruct((rows, width), BF16),
            jax.ShapeDtypeStruct((rows, width), F32),
            jax.ShapeDtypeStruct((rows, width), BF16),
            jax.ShapeDtypeStruct((rows, ff), BF16),
            jax.ShapeDtypeStruct((rows, width), BF16),
            jax.ShapeDtypeStruct((rows, ff), BF16),
            jax.ShapeDtypeStruct((8, width), F32),
        ),
        scratch_shapes=[pltpu.VMEM((TILE, ff), F32)],
        compiler_params=params(),
        name="feed",
    )(tok, cot, att, w_out, w_up, w_down, gains, biases)


def return_kernel(tok, cot, branch, hidden_back, w_out, w_up, gains, biases,
                  middle_back_out, branch_back_out, att_back_out, sums):
    unit1, rstd1 = norm_parts(branch[...])
    middle = tok[...].astype(F32) + unit1 * gains[1:2, :] + biases[1:2, :]
    unit2, rstd2 = norm_parts(middle)
    grad2 = dot(hidden_back[...], w_up[...], NT)
    middle_back = cot[...].astype(F32) + norm_back(unit2, rstd2, gains[2:3, :], grad2)
    middle_back_out[...] = middle_back
    branch_back = norm_back(unit1, rstd1, gains[1:2, :], middle_back).astype(BF16)
    branch_back_out[...] = branch_back
    att_back_out[...] = dot(branch_back, w_out[...], NT).astype(BF16)

    @pl.when(pl.program_id(0) == 0)
    def _():
        sums[...] = jnp.zeros_like(sums)

    sums[0:1, :] += token_sum(middle_back * unit1)
    sums[1:2, :] += token_sum(middle_back)
    sums[2:3, :] += token_sum(grad2 * unit2)
    sums[3:4, :] += token_sum(grad2)


def return_pass(tok, cot, branch, hidden_back, w_out, w_up, gains, biases):
    rows, width = tok.shape
    ff = w_up.shape[1]
    row_block = lambda size: pl.BlockSpec((TILE, size), lambda i: (i, 0))
    return pl.pallas_call(
        return_kernel,
        grid=(rows // TILE,),
        in_specs=[
            row_block(width), row_block(width), row_block(width), row_block(ff),
            whole(w_out.shape), whole(w_up.shape), whole(gains.shape), whole(biases.shape),
        ],
        out_specs=(
            row_block(width), row_block(width), row_block(width),
            pl.BlockSpec((8, width), lambda i: (0, 0)),
        ),
        out_shape=(
            jax.ShapeDtypeStruct((rows, width), F32),
            jax.ShapeDtypeStruct((rows, width), BF16),
            jax.ShapeDtypeStruct((rows, width), BF16),
            jax.ShapeDtypeStruct((8, width), F32),
        ),
        compiler_params=params(),
        name="return_pass",
    )(tok, cot, branch, hidden_back, w_out, w_up, gains, biases)


def attend_back_kernel(info, q, k, v, att, grad, stats, cos_t, sin_t, q_back, k_back, v_back,
                       q_heads, k_heads, v_heads, g_heads, q_t, k_t, g_t, inner, q_acc, k_acc, v_acc):
    heads = GROUP // HEAD_DIM
    half = HEAD_DIM // 2
    blocks = q.shape[0] // TILE
    rows_all = blocks * TILE
    for i in range(blocks):
        rows = slice(i * TILE, (i + 1) * TILE)
        at = pl.multiple_of(info[i] * TILE, TILE)
        spot = pl.ds(at, TILE)
        q_t[:, spot] = q[rows, :].T
        k_t[:, spot] = k[rows, :].T
        grad_t = grad[rows, :].T
        g_t[:, spot] = grad_t
        product = att[rows, :].T.astype(F32) * grad_t.astype(F32)
        for h in range(heads):
            lanes = slice(h * HEAD_DIM, (h + 1) * HEAD_DIM)
            q_heads[h, spot, :] = q[rows, lanes]
            k_heads[h, spot, :] = k[rows, lanes]
            v_heads[h, spot, :] = v[rows, lanes]
            g_heads[h, spot, :] = grad[rows, lanes]
            inner[pl.ds(h, 1), spot] = jnp.sum(product[lanes, :], axis=0, keepdims=True)

    def one_head(h, last_ask):
        head_rows = pl.ds(pl.multiple_of(h * HEAD_DIM, HEAD_DIM), HEAD_DIM)
        for block in range(blocks):
            keys = slice(block * TILE, (block + 1) * TILE)
            cols = slice(block * TILE, last_ask(block))
            scores = dot(k_heads[h, keys, :], q_t[head_rows, cols])
            low = scores[:, :TILE]
            keys_at = lax.broadcasted_iota(jnp.int32, (TILE, TILE), 0)
            asks_at = lax.broadcasted_iota(jnp.int32, (TILE, TILE), 1)
            low = jnp.where(keys_at <= asks_at, low, -1e30)
            if scores.shape[1] > TILE:
                scores = jnp.concatenate([low, scores[:, TILE:]], axis=1)
            else:
                scores = low
            weights = jnp.exp(scores - stats[0, pl.ds(h, 1), cols])
            weight_back = dot(v_heads[h, keys, :], g_t[head_rows, cols])
            score_back = (weights * (weight_back - inner[pl.ds(h, 1), cols])).astype(BF16)
            v_acc[h, keys, :] = dot(weights.astype(BF16), g_heads[h, cols, :])
            k_acc[h, keys, :] = dot(score_back, q_heads[h, cols, :])
            change = dot(k_t[head_rows, keys], score_back)
            if block == 0:
                q_acc[head_rows, cols] = change
            elif last_ask(0) < rows_all:
                q_acc[head_rows, cols] = change
            else:
                q_acc[head_rows, cols] += change

    many = info[blocks] != 0

    @pl.when(jnp.logical_not(many))
    def _():
        @pl.loop(0, heads)
        def _(h):
            one_head(h, lambda block: rows_all)

    @pl.when(many)
    def _():
        @pl.loop(0, heads)
        def _(h):
            one_head(h, lambda block: (block + 1) * TILE)

    scale = 1.0 / math.sqrt(HEAD_DIM)
    for i in range(blocks):
        rows = slice(i * TILE, (i + 1) * TILE)
        spot = pl.ds(pl.multiple_of(info[i] * TILE, TILE), TILE)
        cos = cos_t[:, rows]
        sin = sin_t[:, rows]

        def turn_back(parts, factor):
            turned = []
            for part in parts:
                first, second = part[:half], part[half:]
                turned.append(first * cos + second * sin)
                turned.append(second * cos - first * sin)
            return (jnp.concatenate(turned, axis=0) * factor).T.astype(BF16)

        q_back[rows, :] = turn_back(
            [q_acc[h * HEAD_DIM : (h + 1) * HEAD_DIM, spot] for h in range(heads)], scale
        )
        k_back[rows, :] = turn_back([k_acc[h, spot, :].T for h in range(heads)], 1.0)
        v_back[rows, :] = jnp.concatenate(
            [v_acc[h, spot, :] for h in range(heads)], axis=1
        ).astype(BF16)


def attend_back(info, mixed, att, grad, stats, cos_t, sin_t):
    rows, wide = mixed.shape
    width = wide // 3
    groups = width // GROUP
    heads = GROUP // HEAD_DIM
    spec = lambda shift: pl.BlockSpec((rows, GROUP), lambda g, s: (0, g + shift * groups))
    out = jax.ShapeDtypeStruct((rows, width), BF16)
    per_head = pltpu.VMEM((heads, rows, HEAD_DIM), BF16)
    turned = pltpu.VMEM((GROUP, rows), BF16)
    return pl.pallas_call(
        attend_back_kernel,
        grid_spec=pltpu.PrefetchScalarGridSpec(
            num_scalar_prefetch=1,
            grid=(groups,),
            in_specs=[
                spec(0), spec(1), spec(2), spec(0), spec(0),
                pl.BlockSpec((1, heads, rows), lambda g, s: (g, 0, 0)),
                pl.BlockSpec((HEAD_DIM // 2, rows), lambda g, s: (0, 0)),
                pl.BlockSpec((HEAD_DIM // 2, rows), lambda g, s: (0, 0)),
            ],
            out_specs=(spec(0), spec(0), spec(0)),
            scratch_shapes=[
                per_head, per_head, per_head, per_head,
                turned, turned, turned,
                pltpu.VMEM((8, rows), F32),
                pltpu.VMEM((GROUP, rows), F32),
                pltpu.VMEM((heads, rows, HEAD_DIM), F32),
                pltpu.VMEM((heads, rows, HEAD_DIM), F32),
            ],
        ),
        out_shape=(out, out, out),
        compiler_params=params(),
        name="attend_back",
    )(info, mixed, mixed, mixed, att, grad, stats, cos_t, sin_t)


def finish_kernel(tok, middle_back, q_back, k_back, v_back, w_qkv, gains, grad_out, sums):
    width = tok.shape[1]
    unit, rstd = norm_parts(tok[...].astype(F32))
    grad = (
        dot(q_back[...], w_qkv[:, :width], NT)
        + dot(k_back[...], w_qkv[:, width : 2 * width], NT)
        + dot(v_back[...], w_qkv[:, 2 * width :], NT)
    )
    back = middle_back[...] + norm_back(unit, rstd, gains[0:1, :], grad)
    grad_out[...] = back.astype(BF16)

    @pl.when(pl.program_id(0) == 0)
    def _():
        sums[...] = jnp.zeros_like(sums)

    sums[0:1, :] += token_sum(grad * unit)
    sums[1:2, :] += token_sum(grad)


def finish(tok, middle_back, q_back, k_back, v_back, w_qkv, gains):
    rows, width = tok.shape
    row_block = pl.BlockSpec((TILE, width), lambda i: (i, 0))
    return pl.pallas_call(
        finish_kernel,
        grid=(rows // TILE,),
        in_specs=[row_block] * 5 + [whole(w_qkv.shape), whole(gains.shape)],
        out_specs=(row_block, pl.BlockSpec((8, width), lambda i: (0, 0))),
        out_shape=(
            jax.ShapeDtypeStruct((rows, width), BF16),
            jax.ShapeDtypeStruct((8, width), F32),
        ),
        compiler_params=params(),
        name="finish",
    )(tok, middle_back, q_back, k_back, v_back, w_qkv, gains)


def weight_grad_kernel(picks, left, right, *refs):
    out = refs[-1]
    total = dot(left[...], right[...], TN)
    if len(refs) == 2:
        total = total + refs[0][...].astype(F32)
    out[...] = total.astype(BF16)


def weight_grad(picks, left, right, col_at, cols, addend=None, add_at=0):
    tokens = left.shape[0]
    count = picks.shape[0]
    in_specs = [
        pl.BlockSpec((tokens, TILE), lambda i, s: (0, s[i])),
        pl.BlockSpec((tokens, cols), lambda i, s: (0, col_at), pipeline_mode=pl.Buffered(1)),
    ]
    args = [picks, left, right]
    if addend is not None:
        in_specs.append(pl.BlockSpec((TILE, cols), lambda i, s: (i + add_at, 0)))
        args.append(addend)
    return pl.pallas_call(
        weight_grad_kernel,
        grid_spec=pltpu.PrefetchScalarGridSpec(
            num_scalar_prefetch=1,
            grid=(count,),
            in_specs=in_specs,
            out_specs=pl.BlockSpec((TILE, cols), lambda i, s: (i, 0)),
        ),
        out_shape=jax.ShapeDtypeStruct((count * TILE, cols), BF16),
        compiler_params=params(),
        name="weight_grad",
    )(*args)


def swap_wide(rows, bit):
    size = lax.axis_size("wide")
    return lax.ppermute(rows, "wide", [(i, i ^ bit) for i in range(size)])


def swap_narrow(rows):
    return lax.ppermute(rows, "narrow", [(0, 1), (1, 0)])


def add_up(parts, dtype=BF16):
    total = parts[0].astype(F32)
    for part in parts[1:]:
        total = total + part.astype(F32)
    return total.astype(dtype)


def half_of(parts, which):
    size = parts[0].shape[0] // 2
    return [lax.dynamic_slice_in_dim(part, which * size, size, 0) for part in parts]


def in_order(mine, theirs, which):
    return jnp.concatenate(
        [jnp.where(which == 0, mine, theirs), jnp.where(which == 0, theirs, mine)], axis=0
    )


def reduced_grad(left, right, col_at, cols, row_at, rows):
    n = lax.axis_index("narrow")
    w = lax.axis_index("wide")
    core = w % 2
    half_rows = left.shape[1] // 2
    per_core = rows // 2 // TILE
    block = jnp.arange(per_core, dtype=jnp.int32)

    def picks(x, c):
        return ((x * half_rows + row_at + c * (rows // 2)) // TILE + block).astype(jnp.int32)

    far = weight_grad(
        jnp.concatenate([picks(1 - n, 1 - core), picks(n, 1 - core)]), left, right, col_at, cols
    )
    from_core = swap_wide(far, 1)
    give = weight_grad(picks(1 - n, core), left, right, col_at, cols, from_core, 0)
    from_x = swap_narrow(give)
    parts = [weight_grad(picks(n, core), left, right, col_at, cols, from_core, per_core), from_x]
    bits = []
    bit = 2
    while bit < lax.axis_size("wide"):
        bits.append(bit)
        bit *= 2
    for bit in bits:
        mine = (w // bit) % 2
        got = swap_wide(add_up(half_of(parts, 1 - mine)), bit)
        parts = half_of(parts, mine) + [got]
    piece = add_up(parts)
    for bit in reversed(bits):
        piece = in_order(piece, swap_wide(piece, bit), (w // bit) % 2)
    return in_order(piece.astype(F32), swap_wide(piece, 1).astype(F32), core)


def local(tokens, doc_ids, w_qkv, w_out, w_up, w_down, norm_gains, norm_biases, cotangent):
    narrow_size = lax.axis_size("narrow")
    packs, tok_rows, width = tokens.shape
    assert narrow_size == 2 and packs == 2 and tok_rows == 2 * TILE
    pack_len = tok_rows * narrow_size
    ff = w_up.shape[1]
    n = lax.axis_index("narrow")
    pick = lambda array, index: lax.dynamic_index_in_dim(array, index, 0, keepdims=False)

    own_tok = pick(tokens, n)
    far_tok = swap_narrow(pick(tokens, 1 - n))
    own_cot = pick(cotangent, n)
    far_cot = swap_narrow(pick(cotangent, 1 - n))
    doc_row = pick(doc_ids, n)
    many = (doc_row[pack_len - 1] != 0).astype(jnp.int32)
    own_blocks = jnp.stack([n, 3 - n])
    far_blocks = jnp.stack([1 - n, 2 + n])
    block_at = jnp.concatenate([own_blocks, far_blocks]).astype(jnp.int32)
    info = jnp.concatenate([block_at, many[None]])

    halves = HEAD_DIM // 2
    frequency = jnp.exp(
        -math.log(10000.0) * jnp.arange(halves, dtype=F32) * 2.0 / HEAD_DIM
    )
    places = (block_at[:, None] * TILE + jnp.arange(TILE, dtype=jnp.int32)[None, :]).reshape(-1)
    angles_t = frequency[:, None] * places.astype(F32)[None, :]
    cos_t = jnp.cos(angles_t)
    sin_t = jnp.sin(angles_t)
    cos = cos_t.T
    sin = sin_t.T
    cosine = jnp.concatenate([cos] * 4, axis=1)
    sine = jnp.concatenate([-sin, sin, -sin, sin], axis=1)

    early = project(own_tok, w_qkv, norm_gains, norm_biases, cosine, sine, 0, None, pack_len)
    normed, mixed = project(
        far_tok, w_qkv, norm_gains, norm_biases, cosine, sine, 2, early, pack_len
    )
    tok = jnp.concatenate([own_tok, far_tok], axis=0)
    cot = jnp.concatenate([own_cot, far_cot], axis=0)
    att, stats = attend(info, mixed)
    out, branch, normed2, active, back2, hidden_back, sums3 = feed(
        tok, cot, att, w_out, w_up, w_down, norm_gains, norm_biases
    )
    far_out = swap_narrow(out[tok_rows:])
    grad_down = jnp.concatenate(
        [reduced_grad(active, back2, 0, width, at, ff // 4) for at in range(0, ff // 2, ff // 4)], axis=0
    )
    grad_up = jnp.concatenate(
        [reduced_grad(normed2, hidden_back, at, ff // 2, 0, width // 2) for at in range(2)], axis=1
    )
    middle_back, branch_back, att_back, sums12 = return_pass(
        tok, cot, branch, hidden_back, w_out, w_up, norm_gains, norm_biases
    )
    grad_out_proj = reduced_grad(att, branch_back, 0, width, 0, width // 2)
    q_back, k_back, v_back = attend_back(info, mixed, att, att_back, stats, cos_t, sin_t)
    grad_qkv = jnp.concatenate(
        [reduced_grad(normed, part, 0, width, 0, width // 2) for part in (q_back, k_back, v_back)],
        axis=1,
    )
    grad_tok, sums0 = finish(tok, middle_back, q_back, k_back, v_back, w_qkv, norm_gains)
    far_grad = swap_narrow(grad_tok[tok_rows:])

    norm_term = jnp.concatenate(
        [sums0[0:1], sums12[0:1], sums12[2:3], sums3[0:1],
         sums0[1:2], sums12[1:2], sums12[3:4], sums3[1:2]], axis=0
    )
    norm_term = norm_term + swap_narrow(norm_term)
    bit = 1
    while bit < lax.axis_size("wide"):
        norm_term = norm_term + swap_wide(norm_term, bit)
        bit *= 2
    norm_term = lax.dynamic_slice_in_dim(norm_term, n * (width // 2), width // 2, 1)

    def in_packs(own, far):
        return jnp.stack([jnp.where(n == 0, own, far), jnp.where(n == 0, far, own)])

    return (
        in_packs(out[:tok_rows], far_out),
        in_packs(grad_tok[:tok_rows], far_grad),
        grad_qkv,
        grad_out_proj,
        grad_up,
        grad_down,
        norm_term[:4],
        norm_term[4:],
    )


def solution(mesh):
    rows = P("wide", "narrow", None)
    return jax.shard_map(
        local,
        mesh=mesh,
        in_specs=(rows, P("wide", None), P(), P(), P(), P(), P(), P(), rows),
        out_specs=(
            rows, rows,
            P("narrow", None), P("narrow", None), P("narrow", None), P("narrow", None),
            P(None, "narrow"), P(None, "narrow"),
        ),
        check_vma=False,
    )
```

time: 1620 us -> 680 us (0.42)
  blocking collectives: 519 us -> 0 us
  matrix products: 408 us -> 0 us
  Pallas kernels: 0 us -> 275 us
  waiting for transfers between devices: 373 us -> 219 us
  other arithmetic: 188 us -> 74.5 us
  starting transfers between devices: 1.15 us -> 83.8 us
  local copies, waits for them, and re-layouts: 95.1 us -> 14.3 us
    psum x1 -> x0, blocking collectives: 519 us -> none  [local(): lax.psum((narrowed[0], narrowed[1], narrowed[2], narrowed[3], narrowed[4]...]
    dot_general x72 -> x0, matrix products: 408 us -> none  [the longest x64 354 us: product(): return jnp.einsum(formula, left, right, preferred_element_type=jnp.float32)]
    reduce_scatter x9 -> x0, waiting for transfers between devices: 334 us -> none  [the longest x1 102 us: local(): lax.psum_scatter(local_terms[3].astype(jnp.bfloat16), 'narrow', scatter_d...]
    pallas_call x0 -> x31, Pallas kernels: none -> 275 us  [the longest x24 113 us: weight_grad(): pl.pallas_call(weight_grad_kernel, grid_spec=pltpu.PrefetchScalarGridSpec...]
    ppermute x0 -> x81, waiting for transfers between devices: none -> 219 us  [the longest x68 155 us: swap_wide(): return lax.ppermute(rows, 'wide', [(i, i ^ bit) for i in range(size)])]
    ppermute x0 -> x81, starting transfers between devices: none -> 83.8 us  [the longest x68 45.5 us: swap_wide(): return lax.ppermute(rows, 'wide', [(i, i ^ bit) for i in range(size)])]
    convert_element_type x12 -> x32, other arithmetic: 104 us -> 23.2 us  [add_up(): return total.astype(dtype)]
    reduce_sum x28 -> x0, other arithmetic: 42.8 us -> none  [the longest x2 18.6 us: micro_step(): row_total = jnp.sum(jnp.exp(scores - row_peak), axis=-1, keepdims=True)]
  transfers between devices with their start and end apart: 13 -> 81, of which waited for: 8 -> 46; matrix products, arithmetic and copies ran while one was open for 14% -> 10% of each run, Pallas kernels for 0% -> 23%
where the time goes in v1:
time: 680 us; the launch traced here: 669 us
  Pallas kernels  275 us (40%)
  waiting for transfers between devices  219 us (32%)
  starting transfers between devices  83.8 us (12%)
  other arithmetic  74.5 us (11%)
  local copies, waits for them, and re-layouts  14.3 us (2%)
    ppermute x68, waiting for transfers between devices, swap_wide(): return lax.ppermute(rows, 'wide', [(i, i ^ bit) for i in range(size)])  155 us
    pallas_call x24, Pallas kernels, weight_grad(): pl.pallas_call(weight_grad_kernel, grid_spec=pltpu.PrefetchScalarGridSpec...  113 us
    ppermute x13, waiting for transfers between devices, swap_narrow(): return lax.ppermute(rows, 'narrow', [(0, 1), (1, 0)])  64.8 us
    pallas_call x1, Pallas kernels, feed(): pl.pallas_call(feed_kernel, grid=(rows // TILE,), in_specs=[row_block(wid...  48.6 us
    ppermute x68, starting transfers between devices, swap_wide(): return lax.ppermute(rows, 'wide', [(i, i ^ bit) for i in range(size)])  45.5 us
    ppermute x13, starting transfers between devices, swap_narrow(): return lax.ppermute(rows, 'narrow', [(0, 1), (1, 0)])  38.3 us
    pallas_call x1, Pallas kernels, attend_back(): pl.pallas_call(attend_back_kernel, grid_spec=pltpu.PrefetchScalarGridSpec...  32.9 us
    pallas_call x1, Pallas kernels, attend(): pl.pallas_call(attend_kernel, grid_spec=pltpu.PrefetchScalarGridSpec(num_...  24.6 us
  transfers between devices with their start and end apart: 81, of which 46 were waited for; matrix products, arithmetic and copies ran while one was open for 10% of the time, Pallas kernels for 23%

profile of v1, /device:TPU:0, one launch (start us, length us, event | category | flops | bytes accessed | tf_op | source)
XLA Modules:
  0.0 669.2 jit_solution(8366706895037634842)
XLA Ops:
  14.0 8.5 %project.2 = (bf16[1024,1024]{1,0:T(8,128)(2,1)}, bf16[1024,3072]{1,0:T(8,128)(2,1)}) custom-call(bf16[512,1024]{1,0:T(8,128)(2,1)} %get-tuple-element.66.tok, bf16[1024,3072]{1,0:T(8,128)(2,1)} %w_qkv.1, f32[4,1024]{1,0:T(4,128)} %gains.9, f32[4,1024]{1,0:T(4,128)} %biases.7, f32[1024,128]{1,0:T(8,128)} %get-tuple-element.141.cosine, ...), custom_call_target="tpu_custom_call" | custom-call | tf_op jit(solution)/shard_map/project/pallas_call | solution.py:99
  23.8 6.7 %collective-permute-done.tok = bf16[512,1024]{1,0:T(8,128)(2,1)S(1)} collective-permute-done((bf16[512,1024]{1,0:T(8,128)(2,1)S(1)}, bf16[512,1024]{1,0:T(8,128)(2,1)S(1)}, u32[]{:S(2)}, u32[]{:S(2)}) %collective-permute-start) | collective-permute-done | bytes 1048608 | tf_op jit(solution)/shard_map/ppermute | solution.py:525
  31.4 8.5 %project.3 = (bf16[1024,1024]{1,0:T(8,128)(2,1)}, bf16[1024,3072]{1,0:T(8,128)(2,1)}) custom-call(bf16[512,1024]{1,0:T(8,128)(2,1)} %copy-done.2, bf16[1024,3072]{1,0:T(8,128)(2,1)} %w_qkv.1, f32[4,1024]{1,0:T(4,128)} %gains.9, f32[4,1024]{1,0:T(4,128)} %biases.7, ...), custom_call_target="tpu_custom_call", output_to_operand_aliasing={{0}: (6, {}), {1}: (7, {})} | custom-call | tf_op jit(solution)/shard_map/project/pallas_call | solution.py:99
  39.9 24.6 %attend.1 = (bf16[1024,1024]{1,0:T(8,128)(2,1)}, f32[4,4,1024]{2,1,0:T(4,128)}) custom-call(s32[5]{0:T(128)} %concatenate.141.info, bf16[1024,3072]{1,0:T(8,128)(2,1)} %get-tuple-element.32.q.k.v, bf16[1024,3072]{1,0:T(8,128)(2,1)} %get-tuple-element.32.q.k.v, bf16[1024,3072]{1,0:T(8,128)(2,1)} %get-tuple-element.32.q.k.v), custom_call_target="tpu_custom_call" | custom-call | tf_op jit(solution)/shard_map/attend/pallas_call | solution.py:173
  68.7 48.6 %feed.1 = (bf16[1024,1024]{1,0:T(8,128)(2,1)}, f32[1024,1024]{1,0:T(8,128)}, bf16[1024,1024]{1,0:T(8,128)(2,1)}, bf16[1024,4096]{1,0:T(8,128)(2,1)}, bf16[1024,1...) custom-call(bf16[1024,1024]{1,0:T(8,128)(2,1)} %pad_maximum_fusion.1.tok, ...), custom_call_target="tpu_custom_call" | custom-call | tf_op jit(solution)/shard_map/feed/pallas_call | solution.py:251
  117.3 24.4 %return_pass.1 = (f32[1024,1024]{1,0:T(8,128)}, bf16[1024,1024]{1,0:T(8,128)(2,1)}, bf16[1024,1024]{1,0:T(8,128)(2,1)}, f32[8,1024]{1,0:T(8,128)}) custom-call(bf16[1024,1024]{1,0:T(8,128)(2,1)} %pad_maximum_fusion.1.tok, bf16[1024,1024]{1,0:T(8,128)(2,1)} %pad_maximum_fusion.2.cot, f32[1024,1024]{1,0:T(8,128)} %get-tuple-element.35.branch, ...), custom_call_target="tpu_custom_call" | custom-call | tf_op jit(solution)/shard_map/return_pass/pallas_call | solution.py:304
  141.7 32.9 %attend_back.1 = (bf16[1024,1024]{1,0:T(8,128)(2,1)}, bf16[1024,1024]{1,0:T(8,128)(2,1)}, bf16[1024,1024]{1,0:T(8,128)(2,1)}) custom-call(s32[5]{0:T(128)} %concatenate.141.info, bf16[1024,3072]{1,0:T(8,128)(2,1)} %get-tuple-element.32.q.k.v, bf16[1024,3072]{1,0:T(8,128)(2,1)} %get-tuple-element.32.q.k.v, bf16[1024,3072]{1,0:T(8,128)(2,1)} %get-tuple-element.32.q.k.v, ...), custom_call_target="tpu_custom_call" | custom-call | tf_op jit(solution)/shard_map/attend_back/pallas_call | solution.py:423
  174.6 14.5 %finish.1 = (bf16[1024,1024]{1,0:T(8,128)(2,1)}, f32[8,1024]{1,0:T(8,128)}) custom-call(bf16[1024,1024]{1,0:T(8,128)(2,1)} %pad_maximum_fusion.1.tok, f32[1024,1024]{1,0:T(8,128)} %get-tuple-element.37.middle_back, bf16[1024,1024]{1,0:T(8,128)(2,1)} %get-tuple-element.40.q_back.right, bf16[1024,1024]{1,0:T(8,128)(2,1)} %get-tuple-element.41.k_back.right, ...), custom_call_target="tpu_custom_call" | custom-call | tf_op jit(solution)/shard_map/finish/pallas_call | solution.py:472
  190.9 25.0 %collective-permute-start.76 = (f32[8,1024]{1,0:T(8,128)S(1)}, f32[8,1024]{1,0:T(8,128)S(1)}, u32[]{:S(2)}, u32[]{:S(2)}) collective-permute-start(f32[8,1024]{1,0:T(8,128)S(1)} %concatenate.181), channel_id=1, source_target_pairs={{0,1},{1,0},{2,3},{3,2},{4,5},{5,4},{6,7},{7,6},{8,9},{9,8},{10,11... | collective-permute-start | bytes 98312 | tf_op jit(solution)/shard_map/ppermute | solution.py:525
  221.1 5.0 weight_grad.33
  254.5 6.6 weight_grad.36
  261.2 6.6 weight_grad.39
  267.8 6.8 %weight_grad.42 = bf16[1024,1024]{1,0:T(8,128)(2,1)} custom-call(s32[4]{0:T(128)} %get-tuple-element.139.picks, bf16[1024,4096]{1,0:T(8,128)(2,1)} %get-tuple-element.47.left, bf16[1024,1024]{1,0:T(8,128)(2,1)} %get-tuple-element.48.right), custom_call_target="tpu_custom_call" | custom-call | tf_op jit(solution)/shard_map/weight_grad/pallas_call | solution.py:505
  274.6 6.8 %weight_grad.45 = bf16[1024,1024]{1,0:T(8,128)(2,1)} custom-call(s32[4]{0:T(128)} %get-tuple-element.140.picks, bf16[1024,4096]{1,0:T(8,128)(2,1)} %get-tuple-element.47.left, bf16[1024,1024]{1,0:T(8,128)(2,1)} %get-tuple-element.48.right), custom_call_target="tpu_custom_call" | custom-call | tf_op jit(solution)/shard_map/weight_grad/pallas_call | solution.py:505
  322.3 10.1 %collective-permute-done.5 = bf16[256,1024]{1,0:T(8,128)(2,1)S(1)} collective-permute-done((bf16[256,1024]{1,0:T(8,128)(2,1)}, bf16[256,1024]{1,0:T(8,128)(2,1)S(1)}, u32[]{:S(2)}, u32[]{:S(2)}) %collective-permute-start.5) | collective-permute-done | bytes 524320 | tf_op jit(solution)/shard_map/ppermute | solution.py:525
  332.9 10.7 %collective-permute-done.14 = bf16[256,1024]{1,0:T(8,128)(2,1)S(1)} collective-permute-done((bf16[256,1024]{1,0:T(8,128)(2,1)}, bf16[256,1024]{1,0:T(8,128)(2,1)S(1)}, u32[]{:S(2)}, u32[]{:S(2)}) %collective-permute-start.14) | collective-permute-done | bytes 524320 | tf_op jit(solution)/shard_map/ppermute | solution.py:525
  344.2 9.9 %collective-permute-done.23 = bf16[256,1024]{1,0:T(8,128)(2,1)S(1)} collective-permute-done((bf16[256,1024]{1,0:T(8,128)(2,1)}, bf16[256,1024]{1,0:T(8,128)(2,1)S(1)}, u32[]{:S(2)}, u32[]{:S(2)}) %collective-permute-start.23) | collective-permute-done | bytes 524320 | tf_op jit(solution)/shard_map/ppermute | solution.py:525
  358.2 5.0 collective-permute-done.15
  396.1 5.7 collective-permute-done.8
  401.9 5.8 collective-permute-done.17
  407.8 5.1 collective-permute-done.26
  439.0 5.0 weight_grad.43
  491.9 8.9 %maximum_maximum_fusion.1 = f32[512,3072]{1,0:T(8,128)} fusion(f32[256,1024]{1,0:T(8,128)S(1)} %get-tuple-element.83, f32[256,1024]{1,0:T(8,128)S(1)} %get-tuple-element.82, f32[256,1024]{1,0:T(8,128)S(1)} %get-tuple-element.81, f32[256,1024]{1,0:T(8,128)S(1)} %get-tuple-element.80, f32[256,1024]{1,0:T(8,128)S(1)} %get-tuple-element.79, ...), kind=kLoop, calls=%fused_computation.2 | loop fusion | flops 7864320 | bytes 12582912 | tf_op jit(solution)/shard_map/concatenate | solution.py:634
  506.0 12.4 %collective-permute-done.41 = bf16[256,2048]{1,0:T(8,128)(2,1)} collective-permute-done((bf16[256,2048]{1,0:T(8,128)(2,1)}, bf16[256,2048]{1,0:T(8,128)(2,1)}, u32[]{:S(2)}, u32[]{:S(2)}) %collective-permute-start.41) | collective-permute-done | bytes 1048608 | tf_op jit(solution)/shard_map/ppermute | solution.py:525
  519.6 10.0 %collective-permute-done.50 = bf16[256,2048]{1,0:T(8,128)(2,1)} collective-permute-done((bf16[256,2048]{1,0:T(8,128)(2,1)}, bf16[256,2048]{1,0:T(8,128)(2,1)}, u32[]{:S(2)}, u32[]{:S(2)}) %collective-permute-start.50) | collective-permute-done | bytes 1048608 | tf_op jit(solution)/shard_map/ppermute | solution.py:525
  541.0 9.3 %collective-permute-done.51 = bf16[128,2048]{1,0:T(8,128)(2,1)S(1)} collective-permute-done((bf16[128,2048]{1,0:T(8,128)(2,1)S(1)}, bf16[128,2048]{1,0:T(8,128)(2,1)S(1)}, u32[]{:S(2)}, u32[]{:S(2)}) %collective-permute-start.51) | collective-permute-done | bytes 524320 | tf_op jit(solution)/shard_map/ppermute | solution.py:521
  564.0 8.2 %collective-permute-done.62 = bf16[64,1024]{1,0:T(8,128)(2,1)S(1)} collective-permute-done((bf16[64,1024]{1,0:T(8,128)(2,1)S(1)}, bf16[64,1024]{1,0:T(8,128)(2,1)S(1)}, u32[]{:S(2)}, u32[]{:S(2)}) %collective-permute-start.62) | collective-permute-done | bytes 131104 | tf_op jit(solution)/shard_map/ppermute | solution.py:521
  601.3 5.1 collective-permute-done.64
  623.8 8.8 %collective-permute-done.74 = bf16[256,1024]{1,0:T(8,128)(2,1)S(1)} collective-permute-done((bf16[256,1024]{1,0:T(8,128)(2,1)S(1)}, bf16[256,1024]{1,0:T(8,128)(2,1)S(1)}, u32[]{:S(2)}, u32[]{:S(2)}) %collective-permute-start.74) | collective-permute-done | bytes 524320 | tf_op jit(solution)/shard_map/ppermute | solution.py:521
  633.0 10.8 %collective-permute-done.47 = bf16[128,2048]{1,0:T(8,128)(2,1)S(1)} collective-permute-done((bf16[128,2048]{1,0:T(8,128)(2,1)S(1)}, bf16[128,2048]{1,0:T(8,128)(2,1)S(1)}, u32[]{:S(2)}, u32[]{:S(2)}) %collective-permute-start.47) | collective-permute-done | bytes 524320 | tf_op jit(solution)/shard_map/ppermute | solution.py:521
  644.3 7.3 %collective-permute-done.56 = bf16[128,2048]{1,0:T(8,128)(2,1)S(1)} collective-permute-done((bf16[128,2048]{1,0:T(8,128)(2,1)S(1)}, bf16[128,2048]{1,0:T(8,128)(2,1)S(1)}, u32[]{:S(2)}, u32[]{:S(2)}) %collective-permute-start.56) | collective-permute-done | bytes 524320 | tf_op jit(solution)/shard_map/ppermute | solution.py:521
  661.9 7.1 %maximum_maximum_fusion = f32[512,4096]{1,0:T(8,128)} fusion(f32[256,2048]{1,0:T(8,128)} %get-tuple-element.63, f32[256,2048]{1,0:T(8,128)} %get-tuple-element.62, f32[256,2048]{1,0:T(8,128)} %get-tuple-element.61, f32[256,2048]{1,0:T(8,128)S(1)} %get-tuple-element.60), kind=kLoop, calls=%fused_computation | loop fusion | flops 6291456 | bytes 16777216 | tf_op jit(solution)/shard_map/concatenate | solution.py:626
  (336 shorter events, 296.1 us)
Async XLA Ops:
  3.5 27.0 %collective-permute-start = (bf16[512,1024]{1,0:T(8,128)(2,1)S(1)}, bf16[512,1024]{1,0:T(8,128)(2,1)S(1)}, u32[]{:S(2)}, u32[]{:S(2)}) collective-permute-start(bf16[512,1024]{1,0:T(8,128)(2,1)S(1)} %get-tuple-element.67), channel_id=1, source_target_pairs={{0,1},{1,0},{2,3},{3,2},{4,5},{5,4},{6,7},{7,6},{8,9},{9,8},{10,11... | collective-permute-start | bytes 3145736 | tf_op jit(solution)/shard_map/ppermute | solution.py:525
  7.6 58.4 %collective-permute-start.1 = (bf16[512,1024]{1,0:T(8,128)(2,1)}, bf16[512,1024]{1,0:T(8,128)(2,1)}, u32[]{:S(2)}, u32[]{:S(2)}) collective-permute-start(bf16[512,1024]{1,0:T(8,128)(2,1)} %get-tuple-element.65), channel_id=1, source_target_pairs={{0,1},{1,0},{2,3},{3,2},{4,5},{5,4},{6,7},{7,6},{8,9},{9,8},{10,11... | collective-permute-start | bytes 3145736 | tf_op jit(solution)/shard_map/ppermute | solution.py:525
  190.9 26.9 %collective-permute-start.76 = (f32[8,1024]{1,0:T(8,128)S(1)}, f32[8,1024]{1,0:T(8,128)S(1)}, u32[]{:S(2)}, u32[]{:S(2)}) collective-permute-start(f32[8,1024]{1,0:T(8,128)S(1)} %concatenate.181), channel_id=1, source_target_pairs={{0,1},{1,0},{2,3},{3,2},{4,5},{5,4},{6,7},{7,6},{8,9},{9,8},{10,11... | collective-permute-start | bytes 98312 | tf_op jit(solution)/shard_map/ppermute | solution.py:525
  226.1 57.5 %collective-permute-start.31 = (bf16[512,1024]{1,0:T(8,128)(2,1)}, bf16[512,1024]{1,0:T(8,128)(2,1)S(1)}, u32[]{:S(2)}, u32[]{:S(2)}) collective-permute-start(bf16[512,1024]{1,0:T(8,128)(2,1)} %weight_grad.33), channel_id=1, source_target_pairs={{0,2},{2,0},{4,6},{6,4},{8,10},{10,8},{12,14},{14,12},{16,18},{18,... | collective-permute-start | bytes 3145736 | tf_op jit(solution)/shard_map/ppermute | solution.py:521
  235.6 52.4 %collective-permute-start.4 = (bf16[512,1024]{1,0:T(8,128)(2,1)}, bf16[512,1024]{1,0:T(8,128)(2,1)S(1)}, u32[]{:S(2)}, u32[]{:S(2)}) collective-permute-start(bf16[512,1024]{1,0:T(8,128)(2,1)} %weight_grad.24), channel_id=1, source_target_pairs={{0,2},{2,0},{4,6},{6,4},{8,10},{10,8},{12,14},{14,12},{16,18},{18,... | collective-permute-start | bytes 3145736 | tf_op jit(solution)/shard_map/ppermute | solution.py:521
  236.2 56.3 %collective-permute-start.13 = (bf16[512,1024]{1,0:T(8,128)(2,1)}, bf16[512,1024]{1,0:T(8,128)(2,1)S(1)}, u32[]{:S(2)}, u32[]{:S(2)}) collective-permute-start(bf16[512,1024]{1,0:T(8,128)(2,1)} %weight_grad.27), channel_id=1, source_target_pairs={{0,2},{2,0},{4,6},{6,4},{8,10},{10,8},{12,14},{14,12},{16,18},{18,... | collective-permute-start | bytes 3145736 | tf_op jit(solution)/shard_map/ppermute | solution.py:521
  248.1 59.5 %collective-permute-start.22 = (bf16[512,1024]{1,0:T(8,128)(2,1)}, bf16[512,1024]{1,0:T(8,128)(2,1)}, u32[]{:S(2)}, u32[]{:S(2)}) collective-permute-start(bf16[512,1024]{1,0:T(8,128)(2,1)} %weight_grad.30), channel_id=1, source_target_pairs={{0,2},{2,0},{4,6},{6,4},{8,10},{10,8},{12,14},{14,12},{16,18},{18,... | collective-permute-start | bytes 3145736 | tf_op jit(solution)/shard_map/ppermute | solution.py:521
  250.3 65.2 %collective-permute-start.3 = (bf16[512,1024]{1,0:T(8,128)(2,1)}, bf16[512,1024]{1,0:T(8,128)(2,1)}, u32[]{:S(2)}, u32[]{:S(2)}) collective-permute-start(bf16[512,1024]{1,0:T(8,128)(2,1)} %slice.50), channel_id=1, source_target_pairs={{0,1},{1,0},{2,3},{3,2},{4,5},{5,4},{6,7},{7,6},{8,9},{9,8},{10,11... | collective-permute-start | bytes 3145736 | tf_op jit(solution)/shard_map/ppermute | solution.py:525
  283.7 71.0 %collective-permute-start.2 = (bf16[512,1024]{1,0:T(8,128)(2,1)}, bf16[512,1024]{1,0:T(8,128)(2,1)}, u32[]{:S(2)}, u32[]{:S(2)}) collective-permute-start(bf16[512,1024]{1,0:T(8,128)(2,1)} %slice.48), channel_id=1, source_target_pairs={{0,1},{1,0},{2,3},{3,2},{4,5},{5,4},{6,7},{7,6},{8,9},{9,8},{10,11... | collective-permute-start | bytes 3145736 | tf_op jit(solution)/shard_map/ppermute | solution.py:525
  288.1 33.2 %collective-permute-start.32 = (bf16[256,1024]{1,0:T(8,128)(2,1)}, bf16[256,1024]{1,0:T(8,128)(2,1)}, u32[]{:S(2)}, u32[]{:S(2)}) collective-permute-start(bf16[256,1024]{1,0:T(8,128)(2,1)} %weight_grad.35), channel_id=1, source_target_pairs={{0,1},{1,0},{2,3},{3,2},{4,5},{5,4},{6,7},{7,6},{8,9},{9,8},{10,11... | collective-permute-start | bytes 1572872 | tf_op jit(solution)/shard_map/ppermute | solution.py:525
  292.5 39.9 %collective-permute-start.5 = (bf16[256,1024]{1,0:T(8,128)(2,1)}, bf16[256,1024]{1,0:T(8,128)(2,1)S(1)}, u32[]{:S(2)}, u32[]{:S(2)}) collective-permute-start(bf16[256,1024]{1,0:T(8,128)(2,1)} %weight_grad.26), channel_id=1, source_target_pairs={{0,1},{1,0},{2,3},{3,2},{4,5},{5,4},{6,7},{7,6},{8,9},{9,8},{10,11... | collective-permute-start | bytes 1572872 | tf_op jit(solution)/shard_map/ppermute | solution.py:525
  307.6 36.0 %collective-permute-start.14 = (bf16[256,1024]{1,0:T(8,128)(2,1)}, bf16[256,1024]{1,0:T(8,128)(2,1)S(1)}, u32[]{:S(2)}, u32[]{:S(2)}) collective-permute-start(bf16[256,1024]{1,0:T(8,128)(2,1)} %weight_grad.29), channel_id=1, source_target_pairs={{0,1},{1,0},{2,3},{3,2},{4,5},{5,4},{6,7},{7,6},{8,9},{9,8},{10,11... | collective-permute-start | bytes 1572872 | tf_op jit(solution)/shard_map/ppermute | solution.py:525
  315.6 38.5 %collective-permute-start.23 = (bf16[256,1024]{1,0:T(8,128)(2,1)}, bf16[256,1024]{1,0:T(8,128)(2,1)S(1)}, u32[]{:S(2)}, u32[]{:S(2)}) collective-permute-start(bf16[256,1024]{1,0:T(8,128)(2,1)} %weight_grad.32), channel_id=1, source_target_pairs={{0,1},{1,0},{2,3},{3,2},{4,5},{5,4},{6,7},{7,6},{8,9},{9,8},{10,11... | collective-permute-start | bytes 1572872 | tf_op jit(solution)/shard_map/ppermute | solution.py:525
  321.2 114.5 %collective-permute-start.58 = (bf16[1024,1024]{1,0:T(8,128)(2,1)}, bf16[1024,1024]{1,0:T(8,128)(2,1)S(1)}, u32[]{:S(2)}, u32[]{:S(2)}) collective-permute-start(bf16[1024,1024]{1,0:T(8,128)(2,1)} %weight_grad.42), channel_id=1, source_target_pairs={{0,2},{2,0},{4,6},{6,4},{8,10},{10,8},{12,14},{14,12},{16,18},{18,... | collective-permute-start | bytes 6291464 | tf_op jit(solution)/shard_map/ppermute | solution.py:521
  332.4 25.3 %collective-permute-start.33 = (bf16[128,1024]{1,0:T(8,128)(2,1)S(1)}, bf16[128,1024]{1,0:T(8,128)(2,1)S(1)}, u32[]{:S(2)}, u32[]{:S(2)}) collective-permute-start(bf16[128,1024]{1,0:T(8,128)(2,1)S(1)} %add_convert_fusion.8), channel_id=1, source_target_pairs={{0,4},{2,6},{4,0},{6,2},{8,12},{10,14},{12,8},{14,10},{16,20},{18,... | collective-permute-start | bytes 786440 | tf_op jit(solution)/shard_map/ppermute | solution.py:521
  357.7 91.3 %collective-permute-start.67 = (bf16[1024,1024]{1,0:T(8,128)(2,1)}, bf16[1024,1024]{1,0:T(8,128)(2,1)}, u32[]{:S(2)}, u32[]{:S(2)}) collective-permute-start(bf16[1024,1024]{1,0:T(8,128)(2,1)} %weight_grad.45), channel_id=1, source_target_pairs={{0,2},{2,0},{4,6},{6,4},{8,10},{10,8},{12,14},{14,12},{16,18},{18,... | collective-permute-start | bytes 6291464 | tf_op jit(solution)/shard_map/ppermute | solution.py:521
  357.8 55.2 %collective-permute-start.40 = (bf16[512,2048]{1,0:T(8,128)(2,1)S(1)}, bf16[512,2048]{1,0:T(8,128)(2,1)}, u32[]{:S(2)}, u32[]{:S(2)}) collective-permute-start(bf16[512,2048]{1,0:T(8,128)(2,1)S(1)} %copy-done.13), channel_id=1, source_target_pairs={{0,2},{2,0},{4,6},{6,4},{8,10},{10,8},{12,14},{14,12},{16,18},{18,... | collective-permute-start | bytes 6291464 | tf_op jit(solution)/shard_map/ppermute | solution.py:521
  363.3 62.6 %collective-permute-start.49 = (bf16[512,2048]{1,0:T(8,128)(2,1)}, bf16[512,2048]{1,0:T(8,128)(2,1)}, u32[]{:S(2)}, u32[]{:S(2)}) collective-permute-start(bf16[512,2048]{1,0:T(8,128)(2,1)} %weight_grad.39), channel_id=1, source_target_pairs={{0,2},{2,0},{4,6},{6,4},{8,10},{10,8},{12,14},{14,12},{16,18},{18,... | collective-permute-start | bytes 6291464 | tf_op jit(solution)/shard_map/ppermute | solution.py:521
  412.9 45.9 %collective-permute-start.36 = (bf16[32,1024]{1,0:T(8,128)(2,1)S(1)}, bf16[32,1024]{1,0:T(8,128)(2,1)S(1)}, u32[]{:S(2)}, u32[]{:S(2)}) collective-permute-start(bf16[32,1024]{1,0:T(8,128)(2,1)S(1)} %add_convert_fusion.24), channel_id=1, source_target_pairs={{0,16},{2,18},{4,20},{6,22},{8,24},{10,26},{12,28},{14,30},{16,0},... | collective-permute-start | bytes 196616 | tf_op jit(solution)/shard_map/ppermute | solution.py:521
  413.0 47.9 %collective-permute-start.9 = (bf16[32,1024]{1,0:T(8,128)(2,1)S(1)}, bf16[32,1024]{1,0:T(8,128)(2,1)S(1)}, u32[]{:S(2)}, u32[]{:S(2)}) collective-permute-start(bf16[32,1024]{1,0:T(8,128)(2,1)S(1)} %add_convert_fusion.30), channel_id=1, source_target_pairs={{0,16},{2,18},{4,20},{6,22},{8,24},{10,26},{12,28},{14,30},{16,0},... | collective-permute-start | bytes 196616 | tf_op jit(solution)/shard_map/ppermute | solution.py:521
  425.8 35.2 %collective-permute-start.18 = (bf16[32,1024]{1,0:T(8,128)(2,1)S(1)}, bf16[32,1024]{1,0:T(8,128)(2,1)S(1)}, u32[]{:S(2)}, u32[]{:S(2)}) collective-permute-start(bf16[32,1024]{1,0:T(8,128)(2,1)S(1)} %add_convert_fusion.28), channel_id=1, source_target_pairs={{0,16},{2,18},{4,20},{6,22},{8,24},{10,26},{12,28},{14,30},{16,0},... | collective-permute-start | bytes 196616 | tf_op jit(solution)/shard_map/ppermute | solution.py:521
  435.7 25.4 %collective-permute-start.27 = (bf16[32,1024]{1,0:T(8,128)(2,1)S(1)}, bf16[32,1024]{1,0:T(8,128)(2,1)S(1)}, u32[]{:S(2)}, u32[]{:S(2)}) collective-permute-start(bf16[32,1024]{1,0:T(8,128)(2,1)S(1)} %add_convert_fusion.26), channel_id=1, source_target_pairs={{0,16},{2,18},{4,20},{6,22},{8,24},{10,26},{12,28},{14,30},{16,0},... | collective-permute-start | bytes 196616 | tf_op jit(solution)/shard_map/ppermute | solution.py:521
  448.9 51.9 %collective-permute-start.59 = (bf16[512,1024]{1,0:T(8,128)(2,1)}, bf16[512,1024]{1,0:T(8,128)(2,1)}, u32[]{:S(2)}, u32[]{:S(2)}) collective-permute-start(bf16[512,1024]{1,0:T(8,128)(2,1)} %weight_grad.44), channel_id=1, source_target_pairs={{0,1},{1,0},{2,3},{3,2},{4,5},{5,4},{6,7},{7,6},{8,9},{9,8},{10,11... | collective-permute-start | bytes 3145736 | tf_op jit(solution)/shard_map/ppermute | solution.py:525
  458.8 44.1 %collective-permute-start.68 = (bf16[512,1024]{1,0:T(8,128)(2,1)}, bf16[512,1024]{1,0:T(8,128)(2,1)}, u32[]{:S(2)}, u32[]{:S(2)}) collective-permute-start(bf16[512,1024]{1,0:T(8,128)(2,1)} %weight_grad.47), channel_id=1, source_target_pairs={{0,1},{1,0},{2,3},{3,2},{4,5},{5,4},{6,7},{7,6},{8,9},{9,8},{10,11... | collective-permute-start | bytes 3145736 | tf_op jit(solution)/shard_map/ppermute | solution.py:525
  460.9 57.5 %collective-permute-start.41 = (bf16[256,2048]{1,0:T(8,128)(2,1)}, bf16[256,2048]{1,0:T(8,128)(2,1)}, u32[]{:S(2)}, u32[]{:S(2)}) collective-permute-start(bf16[256,2048]{1,0:T(8,128)(2,1)} %weight_grad.38), channel_id=1, source_target_pairs={{0,1},{1,0},{2,3},{3,2},{4,5},{5,4},{6,7},{7,6},{8,9},{9,8},{10,11... | collective-permute-start | bytes 3145736 | tf_op jit(solution)/shard_map/ppermute | solution.py:525
  489.3 40.3 %collective-permute-start.50 = (bf16[256,2048]{1,0:T(8,128)(2,1)}, bf16[256,2048]{1,0:T(8,128)(2,1)}, u32[]{:S(2)}, u32[]{:S(2)}) collective-permute-start(bf16[256,2048]{1,0:T(8,128)(2,1)} %weight_grad.41), channel_id=1, source_target_pairs={{0,1},{1,0},{2,3},{3,2},{4,5},{5,4},{6,7},{7,6},{8,9},{9,8},{10,11... | collective-permute-start | bytes 3145736 | tf_op jit(solution)/shard_map/ppermute | solution.py:525
  502.4 29.9 %collective-permute-start.60 = (bf16[256,1024]{1,0:T(8,128)(2,1)S(1)}, bf16[256,1024]{1,0:T(8,128)(2,1)S(1)}, u32[]{:S(2)}, u32[]{:S(2)}) collective-permute-start(bf16[256,1024]{1,0:T(8,128)(2,1)S(1)} %add_convert_fusion.1), channel_id=1, source_target_pairs={{0,4},{2,6},{4,0},{6,2},{8,12},{10,14},{12,8},{14,10},{16,20},{18,... | collective-permute-start | bytes 1572872 | tf_op jit(solution)/shard_map/ppermute | solution.py:521
  504.4 29.6 %collective-permute-start.69 = (bf16[256,1024]{1,0:T(8,128)(2,1)S(1)}, bf16[256,1024]{1,0:T(8,128)(2,1)S(1)}, u32[]{:S(2)}, u32[]{:S(2)}) collective-permute-start(bf16[256,1024]{1,0:T(8,128)(2,1)S(1)} %add_convert_fusion), channel_id=1, source_target_pairs={{0,4},{2,6},{4,0},{6,2},{8,12},{10,14},{12,8},{14,10},{16,20},{18,... | collective-permute-start | bytes 1572872 | tf_op jit(solution)/shard_map/ppermute | solution.py:521
  557.7 23.0 %collective-permute-start.44 = (bf16[32,2048]{1,0:T(8,128)(2,1)S(1)}, bf16[32,2048]{1,0:T(8,128)(2,1)S(1)}, u32[]{:S(2)}, u32[]{:S(2)}) collective-permute-start(bf16[32,2048]{1,0:T(8,128)(2,1)S(1)} %add_convert_fusion.19), channel_id=1, source_target_pairs={{0,16},{2,18},{4,20},{6,22},{8,24},{10,26},{12,28},{14,30},{16,0},... | collective-permute-start | bytes 393224 | tf_op jit(solution)/shard_map/ppermute | solution.py:521
  617.7 26.1 %collective-permute-start.47 = (bf16[128,2048]{1,0:T(8,128)(2,1)S(1)}, bf16[128,2048]{1,0:T(8,128)(2,1)S(1)}, u32[]{:S(2)}, u32[]{:S(2)}) collective-permute-start(bf16[128,2048]{1,0:T(8,128)(2,1)S(1)} %pad_maximum_fusion.16), channel_id=1, source_target_pairs={{0,4},{2,6},{4,0},{6,2},{8,12},{10,14},{12,8},{14,10},{16,20},{18,... | collective-permute-start | bytes 1572872 | tf_op jit(solution)/shard_map/ppermute | solution.py:521
  621.5 30.2 %collective-permute-start.56 = (bf16[128,2048]{1,0:T(8,128)(2,1)S(1)}, bf16[128,2048]{1,0:T(8,128)(2,1)S(1)}, u32[]{:S(2)}, u32[]{:S(2)}) collective-permute-start(bf16[128,2048]{1,0:T(8,128)(2,1)S(1)} %pad_maximum_fusion.17), channel_id=1, source_target_pairs={{0,4},{2,6},{4,0},{6,2},{8,12},{10,14},{12,8},{14,10},{16,20},{18,... | collective-permute-start | bytes 1572872 | tf_op jit(solution)/shard_map/ppermute | solution.py:521
  623.8 28.3 %collective-permute-start.66 = (bf16[512,1024]{1,0:T(8,128)(2,1)S(1)}, bf16[512,1024]{1,0:T(8,128)(2,1)S(1)}, u32[]{:S(2)}, u32[]{:S(2)}) collective-permute-start(bf16[512,1024]{1,0:T(8,128)(2,1)S(1)} %pad_maximum_fusion.8), channel_id=1, source_target_pairs={{0,2},{2,0},{4,6},{6,4},{8,10},{10,8},{12,14},{14,12},{16,18},{18,... | collective-permute-start | bytes 3145736 | tf_op jit(solution)/shard_map/ppermute | solution.py:521
  (71 other events, 879.7 us)

commit v2 on v1

v2 whole, which is shorter than its diff:
```python
import functools
import math

import jax
import jax.numpy as jnp
from jax import lax
from jax.experimental import pallas as pl
from jax.experimental.pallas import tpu as pltpu
from jax.sharding import PartitionSpec as P

HEAD_DIM = 64
EPS = 1e-05
F32 = jnp.float32
BF16 = jnp.bfloat16
TILE = 256
GROUP = 256
VMEM_LIMIT = 60 * 1024 * 1024
BYTES_PER_US = 900000
NN = (((1,), (0,)), ((), ()))
NT = (((1,), (1,)), ((), ()))
TN = (((0,), (0,)), ((), ()))


def dot(left, right, dims=NN):
    return lax.dot_general(left, right, dims, preferred_element_type=F32)


def call(kernel, grid, prefetch, inputs, outputs, deps, name, us, scratch=(), aliases=None):
    given = len(prefetch) + len(inputs)

    def body(*refs):
        kernel(*refs[:given], *refs[given + len(deps) :])

    in_specs = [spec for _, spec in inputs] + [pl.BlockSpec(memory_space=pl.ANY)] * len(deps)
    return pl.pallas_call(
        body,
        grid_spec=pltpu.PrefetchScalarGridSpec(
            num_scalar_prefetch=len(prefetch),
            grid=grid,
            in_specs=in_specs,
            out_specs=tuple(spec for _, spec in outputs),
            scratch_shapes=list(scratch),
        ),
        out_shape=tuple(shape for shape, _ in outputs),
        input_output_aliases=aliases or {},
        compiler_params=pltpu.CompilerParams(vmem_limit_bytes=VMEM_LIMIT),
        cost_estimate=pl.CostEstimate(
            flops=0, transcendentals=0, bytes_accessed=int(us * BYTES_PER_US)
        ),
        name=name,
    )(*prefetch, *[array for array, _ in inputs], *deps)


def shape(dims, dtype):
    return jax.ShapeDtypeStruct(dims, dtype)


def whole(dims):
    return pl.BlockSpec(dims, lambda *_: (0,) * len(dims), pipeline_mode=pl.Buffered(1))


def row_block(size):
    return pl.BlockSpec((TILE, size), lambda i, *_: (i, 0))


def own_rows(size):
    return pl.BlockSpec((1, TILE, size), lambda i, place, *_: (place[0], jnp.minimum(i, 1), 0))


def near_rows(size):
    return pl.BlockSpec((TILE, size), lambda i, *_: (jnp.minimum(i, 1), 0))


def far_rows(size):
    return pl.BlockSpec((TILE, size), lambda i, *_: (jnp.maximum(i - 2, 0), 0))


def pick_rows(own, far):
    return jnp.where(pl.program_id(0) < 2, own[0].astype(F32), far[...].astype(F32))


def put_rows(near, far, rows):
    @pl.when(pl.program_id(0) < 2)
    def _():
        near[...] = rows

    @pl.when(pl.program_id(0) >= 2)
    def _():
        far[...] = rows


def tie(array, *deps):
    return lax.optimization_barrier((array,) + deps)[0]


def norm_parts(rows):
    centre = rows - jnp.mean(rows, axis=-1, keepdims=True)
    rstd = lax.rsqrt(jnp.mean(centre * centre, axis=-1, keepdims=True) + EPS)
    return centre * rstd, rstd


def norm_back(unit, rstd, gain, grad):
    scaled = grad * gain
    first = jnp.mean(scaled, axis=-1, keepdims=True)
    second = jnp.mean(scaled * unit, axis=-1, keepdims=True)
    return rstd * (scaled - first - unit * second)


def token_sum(rows):
    return jnp.sum(rows, axis=0, keepdims=True)


def project_kernel(place, tok, w, gains, biases, cosine, sine, normed_out, mixed_out):
    rows = tok[0] if len(tok.shape) == 3 else tok[...]
    unit, _ = norm_parts(rows.astype(F32))
    normed = (unit * gains[0:1, :] + biases[0:1, :]).astype(BF16)
    normed_out[...] = normed
    width = normed.shape[1]
    lanes = lax.broadcasted_iota(jnp.int32, (TILE, 128), 1)
    first_half = lanes % HEAD_DIM < HEAD_DIM // 2
    scale = 1.0 / math.sqrt(HEAD_DIM)
    cos = cosine[...]
    sin = sine[...]
    for start in range(0, 3 * width, 256):
        part = dot(normed, w[:, start : start + 256])
        if start >= 2 * width:
            mixed_out[:, start : start + 256] = part.astype(BF16)
            continue
        for sub in range(0, 256, 128):
            u = part[:, sub : sub + 128]
            turned = jnp.where(first_half, pltpu.roll(u, 96, 1), pltpu.roll(u, 32, 1))
            out = u * cos + turned * sin
            out = out.astype(BF16)
            if start < width:
                out = out * jnp.asarray(scale, BF16)
            mixed_out[:, start + sub : start + sub + 128] = out


def project(place, tok, w_qkv, gains, biases, cosine, sine, first_block, earlier, pack_len):
    width, wide = w_qkv.shape
    steps = tok.shape[-2] // TILE
    at = lambda size: pl.BlockSpec((TILE, size), lambda i, *_: (i + first_block, 0))
    own = tok.ndim == 3
    return call(
        project_kernel,
        (steps,),
        [place],
        [
            (tok, own_rows(width) if own else row_block(width)),
            (w_qkv, whole(w_qkv.shape)),
            (gains, whole(gains.shape)),
            (biases, whole(biases.shape)),
            (cosine, at(128)),
            (sine, at(128)),
        ],
        [
            (shape((pack_len, width), BF16), at(width)),
            (shape((pack_len, wide), BF16), at(wide)),
        ],
        list(earlier),
        "project",
        8,
        aliases={7: 0, 8: 1} if earlier else None,
    )


def diagonal_mask(scores):
    size = scores.shape[1]
    first = scores.shape[0] - size
    keys = lax.broadcasted_iota(jnp.int32, (size, size), 0)
    asks = lax.broadcasted_iota(jnp.int32, (size, size), 1)
    tail = jnp.where(keys <= asks, scores[first:], -1e30)
    if first == 0:
        return tail
    return jnp.concatenate([scores[:first], tail], axis=0)


def attend_kernel(info, q, k, v, out, stats, key_heads, q_t, v_t, out_t):
    heads = GROUP // HEAD_DIM
    blocks = q.shape[0] // TILE
    for i in range(blocks):
        rows = slice(i * TILE, (i + 1) * TILE)
        at = pl.multiple_of(info[i] * TILE, TILE)
        q_t[:, pl.ds(at, TILE)] = q[rows, :].T
        v_t[:, pl.ds(at, TILE)] = v[rows, :].T
        for h in range(heads):
            key_heads[h, pl.ds(at, TILE), :] = k[rows, h * HEAD_DIM : (h + 1) * HEAD_DIM]

    def one_head(h, first_key):
        head_rows = pl.ds(pl.multiple_of(h * HEAD_DIM, HEAD_DIM), HEAD_DIM)
        for block in range(blocks):
            cols = slice(block * TILE, (block + 1) * TILE)
            keys = slice(first_key(block), (block + 1) * TILE)
            scores = diagonal_mask(dot(key_heads[h, keys, :], q_t[head_rows, cols]))
            peak = jnp.max(scores, axis=0, keepdims=True)
            weights = jnp.exp(scores - peak)
            total = jnp.sum(weights, axis=0, keepdims=True)
            mixed = dot(v_t[head_rows, keys], weights.astype(BF16))
            out_t[head_rows, cols] = mixed * (1.0 / total)
            stats[0, pl.ds(h, 1), cols] = peak + jnp.log(total)

    many = info[blocks] != 0

    @pl.when(jnp.logical_not(many))
    def _():
        @pl.loop(0, heads)
        def _(h):
            one_head(h, lambda block: 0)

    @pl.when(many)
    def _():
        @pl.loop(0, heads)
        def _(h):
            one_head(h, lambda block: block * TILE)

    for i in range(blocks):
        at = pl.multiple_of(info[i] * TILE, TILE)
        out[i * TILE : (i + 1) * TILE, :] = out_t[:, pl.ds(at, TILE)].T.astype(BF16)


def attend(info, mixed):
    rows, wide = mixed.shape
    width = wide // 3
    groups = width // GROUP
    heads = GROUP // HEAD_DIM
    part = lambda shift: pl.BlockSpec((rows, GROUP), lambda g, s: (0, g + shift * groups))
    return call(
        attend_kernel,
        (groups,),
        [info],
        [(mixed, part(0)), (mixed, part(1)), (mixed, part(2))],
        [
            (shape((rows, width), BF16), part(0)),
            (
                shape((groups, heads, rows), F32),
                pl.BlockSpec((1, heads, rows), lambda g, s: (g, 0, 0)),
            ),
        ],
        [],
        "attend",
        36,
        scratch=[
            pltpu.VMEM((heads, rows, HEAD_DIM), BF16),
            pltpu.VMEM((GROUP, rows), BF16),
            pltpu.VMEM((GROUP, rows), BF16),
            pltpu.VMEM((GROUP, rows), F32),
        ],
    )


def feed_kernel(place, own_tok, far_tok, own_cot, far_cot, att, w_out, w_up, w_down, gains, biases,
                near_out, far_out, branch_out, normed2_out, active_out, back2_out, hidden_back_out, sums,
                slope):
    chunk = 1024
    residual = pick_rows(own_tok, far_tok)
    branch = dot(att[...], w_out[...])
    branch_out[...] = branch
    unit1, _ = norm_parts(branch)
    middle = residual + unit1 * gains[1:2, :] + biases[1:2, :]
    unit2, _ = norm_parts(middle)
    normed2 = (unit2 * gains[2:3, :] + biases[2:3, :]).astype(BF16)
    normed2_out[...] = normed2
    ff = w_up.shape[1]
    root = math.sqrt(2.0 / math.pi)
    branch2 = jnp.zeros_like(branch)
    for start in range(0, ff, chunk):
        cols = slice(start, start + chunk)
        z = dot(normed2, w_up[:, cols])
        square = z * z
        bend = jnp.tanh(z * (root + (root * 0.044715) * square))
        half = 0.5 + 0.5 * bend
        active = (z * half).astype(BF16)
        active_out[:, cols] = active
        inner = (0.5 * root) + (1.5 * root * 0.044715) * square
        slope[:, cols] = half + z * (1.0 - bend * bend) * inner
        branch2 = branch2 + dot(active, w_down[cols, :])
    unit3, rstd3 = norm_parts(branch2)
    put_rows(near_out, far_out, (middle + unit3 * gains[3:4, :] + biases[3:4, :]).astype(BF16))
    upstream = pick_rows(own_cot, far_cot)
    back2 = norm_back(unit3, rstd3, gains[3:4, :], upstream).astype(BF16)
    back2_out[...] = back2

    @pl.when(pl.program_id(0) == 0)
    def _():
        sums[...] = jnp.zeros_like(sums)

    sums[0:1, :] += token_sum(upstream * unit3)
    sums[1:2, :] += token_sum(upstream)
    for start in range(0, ff, chunk):
        cols = slice(start, start + chunk)
        grad_active = dot(back2, w_down[cols, :], NT)
        hidden_back_out[:, cols] = (grad_active * slope[:, cols]).astype(BF16)


def feed(place, tokens, far_tok, cotangent, far_cot, att, w_out, w_up, w_down, gains, biases):
    rows, width = att.shape
    ff = w_up.shape[1]
    return call(
        feed_kernel,
        (rows // TILE,),
        [place],
        [
            (tokens, own_rows(width)), (far_tok, far_rows(width)),
            (cotangent, own_rows(width)), (far_cot, far_rows(width)),
            (att, row_block(width)),
            (w_out, whole(w_out.shape)), (w_up, whole(w_up.shape)), (w_down, whole(w_down.shape)),
            (gains, whole(gains.shape)), (biases, whole(biases.shape)),
        ],
        [
            (shape((rows // 2, width), BF16), near_rows(width)),
            (shape((rows // 2, width), BF16), far_rows(width)),
            (shape((rows, width), F32), row_block(width)),
            (shape((rows, width), BF16), row_block(width)),
            (shape((rows, ff), BF16), row_block(ff)),
            (shape((rows, width), BF16), row_block(width)),
            (shape((rows, ff), BF16), row_block(ff)),
            (shape((8, width), F32), whole((8, width))),
        ],
        [],
        "feed",
        49,
        scratch=[pltpu.VMEM((TILE, ff), F32)],
    )


def return_kernel(place, own_tok, far_tok, own_cot, far_cot, branch, hidden_back, w_out, w_up, gains, biases,
                  middle_back_out, branch_back_out, att_back_out, sums):
    unit1, rstd1 = norm_parts(branch[...])
    middle = pick_rows(own_tok, far_tok) + unit1 * gains[1:2, :] + biases[1:2, :]
    unit2, rstd2 = norm_parts(middle)
    grad2 = dot(hidden_back[...], w_up[...], NT)
    middle_back = pick_rows(own_cot, far_cot) + norm_back(unit2, rstd2, gains[2:3, :], grad2)
    middle_back_out[...] = middle_back
    branch_back = norm_back(unit1, rstd1, gains[1:2, :], middle_back).astype(BF16)
    branch_back_out[...] = branch_back
    att_back_out[...] = dot(branch_back, w_out[...], NT).astype(BF16)

    @pl.when(pl.program_id(0) == 0)
    def _():
        sums[...] = jnp.zeros_like(sums)

    sums[0:1, :] += token_sum(middle_back * unit1)
    sums[1:2, :] += token_sum(middle_back)
    sums[2:3, :] += token_sum(grad2 * unit2)
    sums[3:4, :] += token_sum(grad2)


def return_pass(place, tokens, far_tok, cotangent, far_cot, branch, hidden_back, w_out, w_up,
                gains, biases, deps):
    rows, width = branch.shape
    ff = w_up.shape[1]
    return call(
        return_kernel,
        (rows // TILE,),
        [place],
        [
            (tokens, own_rows(width)), (far_tok, far_rows(width)),
            (cotangent, own_rows(width)), (far_cot, far_rows(width)),
            (branch, row_block(width)), (hidden_back, row_block(ff)),
            (w_out, whole(w_out.shape)), (w_up, whole(w_up.shape)),
            (gains, whole(gains.shape)), (biases, whole(biases.shape)),
        ],
        [
            (shape((rows, width), F32), row_block(width)),
            (shape((rows, width), BF16), row_block(width)),
            (shape((rows, width), BF16), row_block(width)),
            (shape((8, width), F32), whole((8, width))),
        ],
        deps,
        "return_pass",
        24,
    )


def attend_back_kernel(info, q, k, v, att, grad, stats, cos_t, sin_t, back,
                       q_heads, k_heads, v_heads, g_heads, q_t, k_t, g_t, inner, q_acc, k_acc, v_acc):
    heads = GROUP // HEAD_DIM
    half = HEAD_DIM // 2
    blocks = q.shape[0] // TILE
    rows_all = blocks * TILE
    for i in range(blocks):
        rows = slice(i * TILE, (i + 1) * TILE)
        at = pl.multiple_of(info[i] * TILE, TILE)
        spot = pl.ds(at, TILE)
        q_t[:, spot] = q[rows, :].T
        k_t[:, spot] = k[rows, :].T
        grad_t = grad[rows, :].T
        g_t[:, spot] = grad_t
        product = att[rows, :].T.astype(F32) * grad_t.astype(F32)
        for h in range(heads):
            lanes = slice(h * HEAD_DIM, (h + 1) * HEAD_DIM)
            q_heads[h, spot, :] = q[rows, lanes]
            k_heads[h, spot, :] = k[rows, lanes]
            v_heads[h, spot, :] = v[rows, lanes]
            g_heads[h, spot, :] = grad[rows, lanes]
            inner[pl.ds(h, 1), spot] = jnp.sum(product[lanes, :], axis=0, keepdims=True)

    def one_head(h, last_ask):
        head_rows = pl.ds(pl.multiple_of(h * HEAD_DIM, HEAD_DIM), HEAD_DIM)
        for block in range(blocks):
            keys = slice(block * TILE, (block + 1) * TILE)
            cols = slice(block * TILE, last_ask(block))
            scores = dot(k_heads[h, keys, :], q_t[head_rows, cols])
            low = scores[:, :TILE]
            keys_at = lax.broadcasted_iota(jnp.int32, (TILE, TILE), 0)
            asks_at = lax.broadcasted_iota(jnp.int32, (TILE, TILE), 1)
            low = jnp.where(keys_at <= asks_at, low, -1e30)
            if scores.shape[1] > TILE:
                scores = jnp.concatenate([low, scores[:, TILE:]], axis=1)
            else:
                scores = low
            weights = jnp.exp(scores - stats[0, pl.ds(h, 1), cols])
            weight_back = dot(v_heads[h, keys, :], g_t[head_rows, cols])
            score_back = (weights * (weight_back - inner[pl.ds(h, 1), cols])).astype(BF16)
            v_acc[h, keys, :] = dot(weights.astype(BF16), g_heads[h, cols, :])
            k_acc[h, keys, :] = dot(score_back, q_heads[h, cols, :])
            change = dot(k_t[head_rows, keys], score_back)
            if block == 0:
                q_acc[head_rows, cols] = change
            elif last_ask(0) < rows_all:
                q_acc[head_rows, cols] = change
            else:
                q_acc[head_rows, cols] += change

    many = info[blocks] != 0

    @pl.when(jnp.logical_not(many))
    def _():
        @pl.loop(0, heads)
        def _(h):
            one_head(h, lambda block: rows_all)

    @pl.when(many)
    def _():
        @pl.loop(0, heads)
        def _(h):
            one_head(h, lambda block: (block + 1) * TILE)

    scale = 1.0 / math.sqrt(HEAD_DIM)
    for i in range(blocks):
        rows = slice(i * TILE, (i + 1) * TILE)
        spot = pl.ds(pl.multiple_of(info[i] * TILE, TILE), TILE)
        cos = cos_t[:, rows]
        sin = sin_t[:, rows]

        def turn_back(parts, factor):
            turned = []
            for part in parts:
                first, second = part[:half], part[half:]
                turned.append(first * cos + second * sin)
                turned.append(second * cos - first * sin)
            return (jnp.concatenate(turned, axis=0) * factor).T.astype(BF16)

        back[0, rows, :] = turn_back(
            [q_acc[h * HEAD_DIM : (h + 1) * HEAD_DIM, spot] for h in range(heads)], scale
        )
        back[1, rows, :] = turn_back([k_acc[h, spot, :].T for h in range(heads)], 1.0)
        back[2, rows, :] = jnp.concatenate(
            [v_acc[h, spot, :] for h in range(heads)], axis=1
        ).astype(BF16)


def attend_back(info, mixed, att, grad, stats, cos_t, sin_t, half, deps):
    rows, wide = mixed.shape
    width = wide // 3
    groups = width // GROUP
    heads = GROUP // HEAD_DIM
    first = half * (groups // 2)
    spec = lambda shift: pl.BlockSpec((rows, GROUP), lambda g, s: (0, g + first + shift * groups))
    per_head = pltpu.VMEM((heads, rows, HEAD_DIM), BF16)
    turned = pltpu.VMEM((GROUP, rows), BF16)
    angles = pl.BlockSpec((HEAD_DIM // 2, rows), lambda g, s: (0, 0))
    return call(
        attend_back_kernel,
        (groups // 2,),
        [info],
        [
            (mixed, spec(0)), (mixed, spec(1)), (mixed, spec(2)), (att, spec(0)), (grad, spec(0)),
            (stats, pl.BlockSpec((1, heads, rows), lambda g, s: (g + first, 0, 0))),
            (cos_t, angles), (sin_t, angles),
        ],
        [
            (
                shape((3, rows, width // 2), BF16),
                pl.BlockSpec((3, rows, GROUP), lambda g, s: (0, 0, g)),
            ),
        ],
        deps,
        "attend_back",
        22,
        scratch=[
            per_head, per_head, per_head, per_head,
            turned, turned, turned,
            pltpu.VMEM((8, rows), F32),
            pltpu.VMEM((GROUP, rows), F32),
            pltpu.VMEM((heads, rows, HEAD_DIM), F32),
            pltpu.VMEM((heads, rows, HEAD_DIM), F32),
        ],
    )[0]


def finish_kernel(place, own_tok, far_tok, middle_back, left_back, right_back, w_qkv, gains,
                  near_out, far_out, sums):
    half = left_back.shape[2]
    unit, rstd = norm_parts(pick_rows(own_tok, far_tok))
    grad = None
    for part in range(3):
        for side, back in enumerate((left_back, right_back)):
            start = (2 * part + side) * half
            term = dot(back[part], w_qkv[:, start : start + half], NT)
            grad = term if grad is None else grad + term
    back = middle_back[...] + norm_back(unit, rstd, gains[0:1, :], grad)
    put_rows(near_out, far_out, back.astype(BF16))

    @pl.when(pl.program_id(0) == 0)
    def _():
        sums[...] = jnp.zeros_like(sums)

    sums[0:1, :] += token_sum(grad * unit)
    sums[1:2, :] += token_sum(grad)


def finish(place, tokens, far_tok, middle_back, left_back, right_back, w_qkv, gains, deps):
    rows, width = middle_back.shape
    parts = pl.BlockSpec((3, TILE, width // 2), lambda i, *_: (0, i, 0))
    return call(
        finish_kernel,
        (rows // TILE,),
        [place],
        [
            (tokens, own_rows(width)), (far_tok, far_rows(width)),
            (middle_back, row_block(width)), (left_back, parts), (right_back, parts),
            (w_qkv, whole(w_qkv.shape)), (gains, whole(gains.shape)),
        ],
        [
            (shape((rows // 2, width), BF16), near_rows(width)),
            (shape((rows // 2, width), BF16), far_rows(width)),
            (shape((8, width), F32), whole((8, width))),
        ],
        deps,
        "finish",
        15,
    )


def in_packs_kernel(place, own, got, out):
    @pl.when(pl.program_id(0) < 2)
    def _():
        out[0] = own[...]

    @pl.when(pl.program_id(0) >= 2)
    def _():
        out[0] = got[...]


def in_packs(place, own, got, deps):
    rows, width = own.shape

    def at(i, place):
        mine = i < 2
        return (jnp.where(mine, place[0], 1 - place[0]), jnp.where(mine, i, i - 2), 0)

    return call(
        in_packs_kernel,
        (2 * rows // TILE,),
        [place],
        [(own, near_rows(width)), (got, far_rows(width))],
        [(shape((2, rows, width), BF16), pl.BlockSpec((1, TILE, width), at))],
        deps,
        "in_packs",
        3,
    )[0]


def weight_grad_kernel(addend_count, place, left, right, *refs):
    addends = refs[:addend_count]
    outs = refs[addend_count:]
    step = pl.program_id(0)
    share = pl.num_programs(0) // len(outs)
    rights = [right[...]] if len(right.shape) == 2 else [right[p] for p in range(right.shape[0])]
    start = 0
    for piece in rights:
        cols = slice(start, start + piece.shape[1])
        start = cols.stop
        total = dot(left[...], piece, TN)
        for addend in addends:
            total = total + addend[:, cols].astype(F32)
        total = total.astype(BF16)
        if len(outs) == 1:
            outs[0][:, cols] = total
            continue
        for number, out in enumerate(outs):

            @pl.when(step // share == number)
            def _(out=out, cols=cols, total=total):
                out[:, cols] = total


def swap_wide(rows, bit):
    size = lax.axis_size("wide")
    return lax.ppermute(rows, "wide", [(i, i ^ bit) for i in range(size)])


def swap_narrow(rows):
    return lax.ppermute(rows, "narrow", [(0, 1), (1, 0)])


def pair_sum(mine, theirs):
    return (mine.astype(F32) + theirs.astype(F32)).astype(BF16)


def choose(which, bit):
    return jnp.where(which == 1, bit, 1 - bit)


class Reduction:
    def __init__(self, place, left, right, count, cols, row_of, right_of, us):
        self.place, self.left, self.right = place, left, right
        self.count, self.cols, self.us = count, cols, us
        self.row_of, self.right_of = row_of, right_of
        self.state = [None] * count

    def blocks(self, steps, block_of, addends, outs, deps):
        tokens = self.left.shape[0]
        row = lambda i, place: (0, self.row_of(*block_of(i, place)))
        if self.right.ndim == 2:
            right = pl.BlockSpec(
                (tokens, self.cols), lambda i, place: (0, self.right_of(*block_of(i, place)))
            )
        else:
            right = pl.BlockSpec(
                (3, tokens, self.cols // 3),
                lambda i, place: (0, 0, self.right_of(*block_of(i, place))),
            )
        share = steps // outs
        out = shape((share * TILE, self.cols), BF16)
        out_at = lambda number: pl.BlockSpec(
            (TILE, self.cols), lambda i, place: (jnp.clip(i - number * share, 0, share - 1), 0)
        )
        add_at = lambda at: pl.BlockSpec((TILE, self.cols), lambda i, place: (at(i), 0))
        return call(
            functools.partial(weight_grad_kernel, len(addends)),
            (steps,),
            [self.place],
            [(self.left, pl.BlockSpec((tokens, TILE), row)), (self.right, right)]
            + [(array, add_at(at)) for array, at in addends],
            [(out, out_at(number)) for number in range(outs)],
            deps,
            "weight_grad",
            1.5 + self.us * steps,
        )

    def far(self, deps):
        count = self.count

        def block_of(i, place):
            n, c, b = place[0], place[1], place[2]
            return choose(i // (2 * count), n), 1 - c, choose(i % 2, b), (i // 2) % count

        sent = self.blocks(4 * count, block_of, [], 1, deps)[0]
        self.from_core = swap_wide(sent, 1)
        return sent

    def give(self, deps):
        def block_of(i, place):
            n, c, b = place[0], place[1], place[2]
            return 1 - n, c, choose(i % 2, b), i // 2

        sent = self.blocks(
            2 * self.count, block_of, [(self.from_core, lambda i: i)], self.count, deps
        )
        for k, part in enumerate(sent):
            self.state[k] = swap_narrow(part)
        return sent[0]

    def keep(self, k, deps):
        count = self.count

        def block_of(i, place):
            n, c, b = place[0], place[1], place[2]
            return n, c, choose(i, b), k

        addends = [(self.from_core, lambda i: 2 * (count + k) + i), (self.state[k], lambda i: i)]
        sent, kept = self.blocks(2, block_of, addends, 2, deps)
        self.state[k] = (kept, swap_wide(sent, 2), 4)
        return sent

    def step(self, k, dep):
        mine, got, bit = self.state[k]
        total = pair_sum(mine, tie(got, dep))
        if bit < lax.axis_size("wide"):
            self.state[k] = (total, swap_wide(total, bit), 2 * bit)
        else:
            self.state[k] = [total, swap_wide(total, 2), swap_wide(total, 1)]
        return total

    def spread(self, k, dep):
        whole_y = tie(self.state[k][1], dep)
        self.state[k][1] = whole_y
        self.state[k].append(swap_wide(whole_y, 1))
        return whole_y

    def done_steps(self, k):
        return isinstance(self.state[k], list)


def gather_kernel(place, *refs):
    out = refs[-1]
    for number, piece in enumerate(refs[:-1]):

        @pl.when(pl.program_id(0) == number)
        def _(piece=piece):
            out[...] = piece[...].astype(F32)


def gather(place, pieces, dims, block_at, deps):
    flat = [piece for group in pieces for piece in group]
    rows, cols = flat[0].shape

    def at(i, place):
        c = jnp.where(i % 4 < 2, place[1], 1 - place[1])
        b = jnp.where(i % 2 == 0, place[2], 1 - place[2])
        return block_at(c, b, i // 4)

    return call(
        gather_kernel,
        (len(flat),),
        [place],
        [(piece, pl.BlockSpec((rows, cols), lambda i, *_: (0, 0))) for piece in flat],
        [(shape(dims, F32), pl.BlockSpec((rows, cols), at))],
        deps,
        "gather",
        1 + 0.7 * len(flat),
    )[0]


def gather_mixed_kernel(place, *refs):
    out = refs[-1]
    quarter = refs[0].shape[1] // 3
    for core in range(2):

        @pl.when((pl.program_id(0) == place[1]) == (core == 0))
        def _(core=core):
            for side in range(2):
                for other in range(2):
                    piece = refs[4 * side + 2 * core + other]
                    b = place[2] if other == 0 else 1 - place[2]
                    for part in range(3):
                        at = pl.multiple_of((4 * part + 2 * side + b) * quarter, quarter)
                        values = piece[:, part * quarter : (part + 1) * quarter]
                        out[:, pl.ds(at, quarter)] = values.astype(F32)


def gather_mixed(place, pieces, dims, deps):
    flat = [piece for group in pieces for piece in group]
    return call(
        gather_mixed_kernel,
        (2,),
        [place],
        [(piece, whole(piece.shape)) for piece in flat],
        [(shape(dims, F32), pl.BlockSpec((TILE, dims[1]), lambda i, *_: (i, 0)))],
        deps,
        "gather_mixed",
        5,
    )[0]


def local(tokens, doc_ids, w_qkv, w_out, w_up, w_down, norm_gains, norm_biases, cotangent):
    narrow_size = lax.axis_size("narrow")
    packs, tok_rows, width = tokens.shape
    assert narrow_size == 2 and packs == 2 and tok_rows == 2 * TILE
    pack_len = tok_rows * narrow_size
    ff = w_up.shape[1]
    n = lax.axis_index("narrow")
    w = lax.axis_index("wide")
    place = jnp.stack([n, w % 2, (w // 2) % 2]).astype(jnp.int32)
    pick = lambda array, index: lax.dynamic_index_in_dim(array, index, 0, keepdims=False)

    far_tok = swap_narrow(pick(tokens, 1 - n))
    doc_row = pick(doc_ids, n)
    many = (doc_row[pack_len - 1] != 0).astype(jnp.int32)
    block_at = jnp.stack([n, 3 - n, 1 - n, 2 + n]).astype(jnp.int32)
    info = jnp.concatenate([block_at, many[None]])

    halves = HEAD_DIM // 2
    frequency = jnp.exp(
        -math.log(10000.0) * jnp.arange(halves, dtype=F32) * 2.0 / HEAD_DIM
    )
    places = (block_at[:, None] * TILE + jnp.arange(TILE, dtype=jnp.int32)[None, :]).reshape(-1)
    angles_t = frequency[:, None] * places.astype(F32)[None, :]
    cos_t = jnp.cos(angles_t)
    sin_t = jnp.sin(angles_t)
    cos = cos_t.T
    sin = sin_t.T
    cosine = jnp.concatenate([cos] * 4, axis=1)
    sine = jnp.concatenate([-sin, sin, -sin, sin], axis=1)

    early = project(
        place, tokens, w_qkv, norm_gains, norm_biases, cosine, sine, 0, (), pack_len
    )
    far_cot = swap_narrow(tie(pick(cotangent, 1 - n), early[0]))
    normed, mixed = project(
        place, far_tok, w_qkv, norm_gains, norm_biases, cosine, sine, 2, early, pack_len
    )
    att, stats = attend(info, mixed)
    near_out, far_out, branch, normed2, active, back2, hidden_back, sums3 = feed(
        place, tokens, far_tok, cotangent, far_cot, att, w_out, w_up, w_down,
        norm_gains, norm_biases,
    )
    got_out = swap_narrow(far_out)

    reduce = functools.partial(Reduction, place)
    down = reduce(active, back2, 2, 1024, lambda x, c, b, k: 8 * x + 4 * c + 2 * b + k,
                  lambda x, c, b, k: 0, 0.8)
    up = reduce(normed2, hidden_back, 2, 1024, lambda x, c, b, k: 2 * x + c,
                lambda x, c, b, k: 2 * b + k, 0.8)
    last = down.far([])
    last = up.far([last])
    last = down.give([last])
    last = up.give([last])
    middle_back, branch_back, att_back, sums12 = return_pass(
        place, tokens, far_tok, cotangent, far_cot, branch, hidden_back, w_out, w_up,
        norm_gains, norm_biases, [last],
    )
    proj = reduce(att, branch_back, 1, 512, lambda x, c, b, k: 2 * x + c, lambda x, c, b, k: b, 0.5)
    a = proj.far([])
    b = down.keep(0, [a])
    left_back = attend_back(info, mixed, att, att_back, stats, cos_t, sin_t, 0, [b])
    qkv = [reduce(normed, left_back, 1, 768, lambda x, c, b, k: 2 * x + c, lambda x, c, b, k: b, 0.7)]
    a = qkv[0].far([])
    b = down.keep(1, [a])
    d = proj.give([b])
    e = down.step(0, d)
    right_back = attend_back(info, mixed, att, att_back, stats, cos_t, sin_t, 1, [d, e])
    qkv.append(
        reduce(normed, right_back, 1, 768, lambda x, c, b, k: 2 * x + c, lambda x, c, b, k: b, 0.7)
    )
    a = qkv[1].far([])
    b = qkv[0].give([a])
    d = up.keep(0, [b])
    e = down.step(1, d)
    f = down.step(0, e)
    near_grad, far_grad, sums0 = finish(
        place, tokens, far_tok, middle_back, left_back, right_back, w_qkv, norm_gains, [d, f]
    )
    a = qkv[1].give([near_grad])
    got_grad = swap_narrow(tie(far_grad, a))
    norm_term = jnp.concatenate(
        [sums0[0:1], sums12[0:1], sums12[2:3], sums3[0:1],
         sums0[1:2], sums12[1:2], sums12[3:4], sums3[1:2]], axis=0
    )
    norm_term = norm_term + swap_narrow(norm_term)
    a = up.keep(1, [a])
    out = in_packs(place, near_out, got_out, [a])
    last = proj.keep(0, [a])
    bit = 1
    chunks = [(down, 0), (down, 1), (up, 0), (up, 1), (proj, 0)]
    mixed_chunks = [(qkv[0], 0), (qkv[1], 0)]
    waiting = list(mixed_chunks)
    while chunks:
        later = []
        for red, k in chunks:
            if red.done_steps(k):
                last = red.spread(k, last)
            else:
                last = red.step(k, last)
                later.append((red, k))
        chunks = later
        if bit < lax.axis_size("wide"):
            norm_term = norm_term + swap_wide(norm_term, bit)
            bit *= 2
        if waiting:
            red, k = waiting.pop(0)
            last = red.keep(k, [last])
            chunks.append((red, k))
    while bit < lax.axis_size("wide"):
        norm_term = norm_term + swap_wide(norm_term, bit)
        bit *= 2
    grad_down = gather(
        place, down.state, (ff // 2, width), lambda c, b, k: (4 * c + 2 * b + k, 0), []
    )
    grad_up = gather(place, up.state, (width // 2, ff), lambda c, b, k: (c, 2 * b + k), [])
    grad_out_proj = gather(place, proj.state, (width // 2, width), lambda c, b, k: (c, b), [])
    grad_qkv = gather_mixed(
        place, [qkv[0].state[0], qkv[1].state[0]], (width // 2, 3 * width), []
    )
    grad_tok = in_packs(place, near_grad, got_grad, [])
    norm_term = lax.dynamic_slice_in_dim(norm_term, n * (width // 2), width // 2, 1)
    return (
        out,
        grad_tok,
        grad_qkv,
        grad_out_proj,
        grad_up,
        grad_down,
        norm_term[:4],
        norm_term[4:],
    )


def solution(mesh):
    rows = P("wide", "narrow", None)
    return jax.shard_map(
        local,
        mesh=mesh,
        in_specs=(rows, P("wide", None), P(), P(), P(), P(), P(), P(), rows),
        out_specs=(
            rows, rows,
            P("narrow", None), P("narrow", None), P("narrow", None), P("narrow", None),
            P(None, "narrow"), P(None, "narrow"),
        ),
        check_vma=False,
    )
```

time: 680 us -> 570 us (0.84)
  waiting for transfers between devices: 219 us -> 124 us
  other arithmetic: 74.5 us -> 25.4 us
  Pallas kernels: 275 us -> 316 us
    ppermute x13 -> x12, waiting for transfers between devices: 64.8 us -> 9.81 us  [swap_narrow(): return lax.ppermute(rows, 'narrow', [(0, 1), (1, 0)])]
    pallas_call x31, Pallas kernels: 275 us -> 316 us  [call(): pl.pallas_call(body, grid_spec=pltpu.PrefetchScalarGridSpec(num_scalar_pr...]
    ppermute x68 -> x51, waiting for transfers between devices: 155 us -> 114 us  [swap_wide(): return lax.ppermute(rows, 'wide', [(i, i ^ bit) for i in range(size)])]
    concatenate x32 -> x0, other arithmetic: 27.9 us -> none  [the longest x1 8.93 us: local(): jnp.concatenate([reduced_grad(normed, part, 0, width, 0, width // 2) for...]
    ppermute x13 -> x12, starting transfers between devices: 38.3 us -> 13.2 us  [swap_narrow(): return lax.ppermute(rows, 'narrow', [(0, 1), (1, 0)])]
    ppermute x68 -> x51, starting transfers between devices: 45.5 us -> 65.4 us  [swap_wide(): return lax.ppermute(rows, 'wide', [(i, i ^ bit) for i in range(size)])]
    select_n x32 -> x0, other arithmetic: 10.3 us -> none  [in_order(): jnp.where(which == 0, mine, theirs)]
    convert_element_type x32 -> x21, other arithmetic: 23.2 us -> 18.9 us  [pair_sum(): return (mine.astype(F32) + theirs.astype(F32)).astype(BF16)]
  transfers between devices with their start and end apart: 81 -> 63, of which waited for: 46 -> 22; matrix products, arithmetic and copies ran while one was open for 10% -> 5% of each run, Pallas kernels for 23% -> 44%
where the time goes in v2:
time: 570 us; the launch traced here: 561 us
  Pallas kernels  316 us (55%)
  waiting for transfers between devices  124 us (22%)
  starting transfers between devices  78.7 us (14%)
  other arithmetic  25.4 us (4%)
  local copies, waits for them, and re-layouts  14.4 us (3%)
    pallas_call x31, Pallas kernels, call(): pl.pallas_call(body, grid_spec=pltpu.PrefetchScalarGridSpec(num_scalar_pr...  316 us
    ppermute x51, waiting for transfers between devices, swap_wide(): return lax.ppermute(rows, 'wide', [(i, i ^ bit) for i in range(size)])  114 us
    ppermute x51, starting transfers between devices, swap_wide(): return lax.ppermute(rows, 'wide', [(i, i ^ bit) for i in range(size)])  65.4 us
    convert_element_type x21, other arithmetic, pair_sum(): return (mine.astype(F32) + theirs.astype(F32)).astype(BF16)  18.9 us
    ppermute x12, starting transfers between devices, swap_narrow(): return lax.ppermute(rows, 'narrow', [(0, 1), (1, 0)])  13.2 us
  transfers between devices with their start and end apart: 63, of which 22 were waited for; matrix products, arithmetic and copies ran while one was open for 5% of the time, Pallas kernels for 44%

profile of v2, /device:TPU:0, one launch (start us, length us, event | category | flops | bytes accessed | tf_op | source)
XLA Modules:
  0.0 560.6 jit_solution(6251248396938281343)
XLA Ops:
  11.6 9.3 %project.2 = (bf16[1024,1024]{1,0:T(8,128)(2,1)}, bf16[1024,3072]{1,0:T(8,128)(2,1)}) custom-call(s32[3]{0:T(128)} %pad_add_fusion.refs_0_, bf16[2,512,1024]{2,1,0:T(8,128)(2,1)} %refs_1_.7, bf16[1024,3072]{1,0:T(8,128)(2,1)} %refs_6_.3, f32[4,1024]{1,0:T(4,128)} %refs_7_.5, f32[4,1024]{1,0:T(4,128)} %refs_10_.3, f32[1024,128]{1,0:T(8,128)} %get-tuple-element.161.refs_5_, ...), custom_call_target="tpu_custom_call" | custom-call | bytes 7200000 | tf_op jit(solution)/shard_map/project/pallas_call | solution.py:35
  23.4 6.8 %collective-permute-done.refs_1_.refs_2_ = bf16[512,1024]{1,0:T(8,128)(2,1)S(1)} collective-permute-done((bf16[512,1024]{1,0:T(8,128)(2,1)}, bf16[512,1024]{1,0:T(8,128)(2,1)S(1)}, u32[]{:S(2)}, u32[]{:S(2)}) %collective-permute-start) | collective-permute-done | bytes 1048608 | tf_op jit(solution)/shard_map/ppermute | solution.py:605
  31.3 9.2 %project.3 = (bf16[1024,1024]{1,0:T(8,128)(2,1)}, bf16[1024,3072]{1,0:T(8,128)(2,1)}) custom-call(s32[3]{0:T(128)} %pad_add_fusion.refs_0_, bf16[512,1024]{1,0:T(8,128)(2,1)} %copy-done, bf16[1024,3072]{1,0:T(8,128)(2,1)} %refs_6_.3, f32[4,1024]{1,0:T(4,128)} %refs_7_.5, f32[4,1024]{1,0:T(4,128)} %refs_10_.3, ...), custom_call_target="tpu_custom_call", output_to_operand_aliasing={{0}: (7, {}), {1}: (8, {})} | custom-call | bytes 7200000 | tf_op jit(solution)/shard_map/project/pallas_call | solution.py:35
  40.4 24.4 %attend.1 = (bf16[1024,1024]{1,0:T(8,128)(2,1)}, f32[4,4,1024]{2,1,0:T(4,128)}) custom-call(s32[5]{0:T(128)} %concatenate.19.refs_0_, bf16[1024,3072]{1,0:T(8,128)(2,1)} %get-tuple-element.80.refs_1_.refs_2_.refs_3_, bf16[1024,3072]{1,0:T(8,128)(2,1)} %get-tuple-element.80.refs_1_.refs_2_.refs_3_, bf16[1024,3072]{1,0:T(8,128)(2,1)} %get-tuple-element.80.refs_1_.refs_2_.refs_3_), custom_call_target="tpu_custom_call" | custom-call | bytes 32400000 | tf_op jit(solution)/shard_map/attend/pallas_call | solution.py:35
  65.9 50.7 %feed.1 = (bf16[512,1024]{1,0:T(8,128)(2,1)}, bf16[512,1024]{1,0:T(8,128)(2,1)}, f32[1024,1024]{1,0:T(8,128)}, bf16[1024,1024]{1,0:T(8,128)(2,1)}, bf16[1024,409...) custom-call(s32[3]{0:T(128)} %pad_add_fusion.refs_0_, ...), custom_call_target="tpu_custom_call" | custom-call | bytes 44100000 | tf_op jit(solution)/shard_map/feed/pallas_call | solution.py:35
  116.6 10.9 %weight_grad.17.refs_3_ = bf16[2048,1024]{1,0:T(8,128)(2,1)} custom-call(s32[3]{0:T(128)} %pad_add_fusion.refs_0_, bf16[1024,4096]{1,0:T(8,128)(2,1)} %get-tuple-element.86.refs_1_, bf16[1024,1024]{1,0:T(8,128)(2,1)} %get-tuple-element.87.refs_2_), custom_call_target="tpu_custom_call" | custom-call | bytes 7110000 | tf_op jit(solution)/shard_map/weight_grad/pallas_call | solution.py:35
  127.5 10.1 %collective-permute-start.4 = (bf16[2048,1024]{1,0:T(8,128)(2,1)}, bf16[2048,1024]{1,0:T(8,128)(2,1)}, u32[]{:S(2)}, u32[]{:S(2)}) collective-permute-start(bf16[2048,1024]{1,0:T(8,128)(2,1)} %weight_grad.17.refs_3_), channel_id=1, source_target_pairs={{0,2},{2,0},{4,6},{6,4},{8,10},{10,8},{12,14},{14,12},{16,18},{18,... | collective-permute-start | bytes 12582920 | tf_op jit(solution)/shard_map/ppermute | solution.py:601
  137.6 13.0 %weight_grad.18.refs_4_ = bf16[2048,1024]{1,0:T(8,128)(2,1)} custom-call(s32[3]{0:T(128)} %pad_add_fusion.refs_0_, bf16[1024,1024]{1,0:T(8,128)(2,1)} %get-tuple-element.84.refs_1_, bf16[1024,4096]{1,0:T(8,128)(2,1)} %get-tuple-element.85.refs_2_.refs_6_, bf16[2048,1024]{1,0:T(8,128)(2,1)} %weight_grad.17.refs_3_), custom_call_target="tpu_custom_call" | custom-call | bytes 7110000 | tf_op jit(solution)/shard_map/weight_grad/pallas_call | solution.py:35
  150.6 7.5 %weight_grad.19 = (bf16[512,1024]{1,0:T(8,128)(2,1)}, bf16[512,1024]{1,0:T(8,128)(2,1)}) custom-call(s32[3]{0:T(128)} %pad_add_fusion.refs_0_, bf16[1024,4096]{1,0:T(8,128)(2,1)} %get-tuple-element.86.refs_1_, bf16[1024,1024]{1,0:T(8,128)(2,1)} %get-tuple-element.87.refs_2_, bf16[2048,1024]{1,0:T(8,128)(2,1)} %collective-permute-done.4.refs_3_, ...), custom_call_target="tpu_custom_call" | custom-call | bytes 4230000 | tf_op jit(solution)/shard_map/weight_grad/pallas_call | solution.py:35
  160.2 8.0 %weight_grad.20 = (bf16[512,1024]{1,0:T(8,128)(2,1)}, bf16[512,1024]{1,0:T(8,128)(2,1)}) custom-call(s32[3]{0:T(128)} %pad_add_fusion.refs_0_, bf16[1024,1024]{1,0:T(8,128)(2,1)} %get-tuple-element.84.refs_1_, bf16[1024,4096]{1,0:T(8,128)(2,1)} %get-tuple-element.85.refs_2_.refs_6_, bf16[2048,1024]{1,0:T(8,128)(2,1)} %collective-permute-done.3.refs_3_, ...), custom_call_target="tpu_custom_call" | custom-call | bytes 4230000 | tf_op jit(solution)/shard_map/weight_grad/pallas_call | solution.py:35
  168.1 25.5 %return_pass.1 = (f32[1024,1024]{1,0:T(8,128)}, bf16[1024,1024]{1,0:T(8,128)(2,1)}, bf16[1024,1024]{1,0:T(8,128)(2,1)}, f32[8,1024]{1,0:T(8,128)}) custom-call(s32[3]{0:T(128)} %pad_add_fusion.refs_0_, bf16[2,512,1024]{2,1,0:T(8,128)(2,1)} %refs_1_.7, bf16[512,1024]{1,0:T(8,128)(2,1)} %copy-done, bf16[2,512,1024]{2,1,0:T(8,128)(2,1)} %refs_3_.7, ...), custom_call_target="tpu_custom_call" | custom-call | bytes 21600000 | tf_op jit(solution)/shard_map/return_pass/pallas_call | solution.py:35
  193.6 5.8 %weight_grad.21.refs_5_ = bf16[1024,512]{1,0:T(8,128)(2,1)} custom-call(s32[3]{0:T(128)} %pad_add_fusion.refs_0_, bf16[1024,1024]{1,0:T(8,128)(2,1)} %get-tuple-element.81.refs_5_.refs_1_.refs_4_, bf16[1024,1024]{1,0:T(8,128)(2,1)} %get-tuple-element.95.refs_2_), custom_call_target="tpu_custom_call" | custom-call | bytes 3150000 | tf_op jit(solution)/shard_map/weight_grad/pallas_call | solution.py:35
  201.7 5.6 weight_grad.22
  207.3 18.6 %attend_back.2.refs_2_.refs_4_ = bf16[3,1024,512]{2,1,0:T(8,128)(2,1)} custom-call(s32[5]{0:T(128)} %concatenate.19.refs_0_, bf16[1024,3072]{1,0:T(8,128)(2,1)} %get-tuple-element.80.refs_1_.refs_2_.refs_3_, bf16[1024,3072]{1,0:T(8,128)(2,1)} %get-tuple-element.80.refs_1_.refs_2_.refs_3_, bf16[1024,3072]{1,0:T(8,128)(2,1)} %get-tuple-element.80.refs_1_.refs_2_.refs_3_, ...), custom_call_target="tpu_custom_call" | custom-call | bytes 19800000 | tf_op jit(solution)/shard_map/attend_back/pallas_call | solution.py:35
  225.9 6.9 %weight_grad.23.refs_5_ = bf16[1024,768]{1,0:T(8,128)(2,1)} custom-call(s32[3]{0:T(128)} %pad_add_fusion.refs_0_, bf16[1024,1024]{1,0:T(8,128)(2,1)} %get-tuple-element.90.refs_1_, bf16[3,1024,512]{2,1,0:T(8,128)(2,1)} %attend_back.2.refs_2_.refs_4_), custom_call_target="tpu_custom_call" | custom-call | bytes 3870000 | tf_op jit(solution)/shard_map/weight_grad/pallas_call | solution.py:35
  232.9 6.1 %collective-permute-start.12 = (bf16[1024,768]{1,0:T(8,128)(2,1)}, bf16[1024,768]{1,0:T(8,128)(2,1)S(1)}, u32[]{:S(2)}, u32[]{:S(2)}) collective-permute-start(bf16[1024,768]{1,0:T(8,128)(2,1)} %weight_grad.23.refs_5_), channel_id=1, source_target_pairs={{0,2},{2,0},{4,6},{6,4},{8,10},{10,8},{12,14},{14,12},{16,18},{18,... | collective-permute-start | bytes 4718600 | tf_op jit(solution)/shard_map/ppermute | solution.py:601
  240.5 6.0 %weight_grad.24 = (bf16[256,1024]{1,0:T(8,128)(2,1)}, bf16[256,1024]{1,0:T(8,128)(2,1)}) custom-call(s32[3]{0:T(128)} %pad_add_fusion.refs_0_, bf16[1024,4096]{1,0:T(8,128)(2,1)} %get-tuple-element.86.refs_1_, bf16[1024,1024]{1,0:T(8,128)(2,1)} %get-tuple-element.87.refs_2_, bf16[2048,1024]{1,0:T(8,128)(2,1)} %collective-permute-done.4.refs_3_, ...), custom_call_target="tpu_custom_call" | custom-call | bytes 2790000 | tf_op jit(solution)/shard_map/weight_grad/pallas_call | solution.py:35
  256.0 18.6 %attend_back.3.refs_2_.refs_5_ = bf16[3,1024,512]{2,1,0:T(8,128)(2,1)} custom-call(s32[5]{0:T(128)} %concatenate.19.refs_0_, bf16[1024,3072]{1,0:T(8,128)(2,1)} %get-tuple-element.80.refs_1_.refs_2_.refs_3_, bf16[1024,3072]{1,0:T(8,128)(2,1)} %get-tuple-element.80.refs_1_.refs_2_.refs_3_, bf16[1024,3072]{1,0:T(8,128)(2,1)} %get-tuple-element.80.refs_1_.refs_2_.refs_3_, ...), custom_call_target="tpu_custom_call" | custom-call | bytes 19800000 | tf_op jit(solution)/shard_map/attend_back/pallas_call | solution.py:35
  274.6 7.0 %weight_grad.26.refs_4_ = bf16[1024,768]{1,0:T(8,128)(2,1)} custom-call(s32[3]{0:T(128)} %pad_add_fusion.refs_0_, bf16[1024,1024]{1,0:T(8,128)(2,1)} %get-tuple-element.90.refs_1_, bf16[3,1024,512]{2,1,0:T(8,128)(2,1)} %attend_back.3.refs_2_.refs_5_), custom_call_target="tpu_custom_call" | custom-call | bytes 3870000 | tf_op jit(solution)/shard_map/weight_grad/pallas_call | solution.py:35
  299.3 5.5 weight_grad.28
  310.8 15.6 %finish.1 = (bf16[512,1024]{1,0:T(8,128)(2,1)}, bf16[512,1024]{1,0:T(8,128)(2,1)}, f32[8,1024]{1,0:T(8,128)}) custom-call(s32[3]{0:T(128)} %pad_add_fusion.refs_0_, bf16[2,512,1024]{2,1,0:T(8,128)(2,1)} %refs_1_.7, bf16[512,1024]{1,0:T(8,128)(2,1)} %copy-done, f32[1024,1024]{1,0:T(8,128)} %get-tuple-element.101.refs_3_, ...), custom_call_target="tpu_custom_call" | custom-call | bytes 13500000 | tf_op jit(solution)/shard_map/finish/pallas_call | solution.py:35
  368.7 6.2 %weight_grad.32 = (bf16[256,768]{1,0:T(8,128)(2,1)}, bf16[256,768]{1,0:T(8,128)(2,1)}) custom-call(s32[3]{0:T(128)} %pad_add_fusion.refs_0_, bf16[1024,1024]{1,0:T(8,128)(2,1)} %get-tuple-element.90.refs_1_, bf16[3,1024,512]{2,1,0:T(8,128)(2,1)} %attend_back.2.refs_2_.refs_4_, bf16[1024,768]{1,0:T(8,128)(2,1)} %copy-done.2, ...), custom_call_target="tpu_custom_call" | custom-call | bytes 2610000 | tf_op jit(solution)/shard_map/weight_grad/pallas_call | solution.py:35
  387.6 12.1 %collective-permute-done.25 = bf16[256,1024]{1,0:T(8,128)(2,1)S(1)} collective-permute-done((bf16[256,1024]{1,0:T(8,128)(2,1)}, bf16[256,1024]{1,0:T(8,128)(2,1)S(1)}, u32[]{:S(2)}, u32[]{:S(2)}) %collective-permute-start.25) | collective-permute-done | bytes 524320 | tf_op jit(solution)/shard_map/ppermute | solution.py:601
  405.8 6.1 %weight_grad.33 = (bf16[256,768]{1,0:T(8,128)(2,1)}, bf16[256,768]{1,0:T(8,128)(2,1)}) custom-call(s32[3]{0:T(128)} %pad_add_fusion.refs_0_, bf16[1024,1024]{1,0:T(8,128)(2,1)} %get-tuple-element.90.refs_1_, bf16[3,1024,512]{2,1,0:T(8,128)(2,1)} %attend_back.3.refs_2_.refs_5_, bf16[1024,768]{1,0:T(8,128)(2,1)} %copy-done.3, ...), custom_call_target="tpu_custom_call" | custom-call | bytes 2610000 | tf_op jit(solution)/shard_map/weight_grad/pallas_call | solution.py:35
  413.1 25.9 %collective-permute-done.32 = bf16[256,1024]{1,0:T(8,128)(2,1)} collective-permute-done((bf16[256,1024]{1,0:T(8,128)(2,1)S(1)}, bf16[256,1024]{1,0:T(8,128)(2,1)}, u32[]{:S(2)}, u32[]{:S(2)}) %collective-permute-start.32) | collective-permute-done | bytes 524320 | tf_op jit(solution)/shard_map/ppermute | solution.py:601
  441.5 8.8 %collective-permute-done.31 = bf16[256,1024]{1,0:T(8,128)(2,1)} collective-permute-done((bf16[256,1024]{1,0:T(8,128)(2,1)S(1)}, bf16[256,1024]{1,0:T(8,128)(2,1)}, u32[]{:S(2)}, u32[]{:S(2)}) %collective-permute-start.31) | collective-permute-done | bytes 524320 | tf_op jit(solution)/shard_map/ppermute | solution.py:601
  456.1 6.8 %collective-permute-done.29 = bf16[256,768]{1,0:T(8,128)(2,1)S(1)} collective-permute-done((bf16[256,768]{1,0:T(8,128)(2,1)S(1)}, bf16[256,768]{1,0:T(8,128)(2,1)S(1)}, u32[]{:S(2)}, u32[]{:S(2)}) %collective-permute-start.29) | collective-permute-done | bytes 393248 | tf_op jit(solution)/shard_map/ppermute | solution.py:601
  469.3 10.8 %collective-permute-done.37.refs_6_ = bf16[256,1024]{1,0:T(8,128)(2,1)} collective-permute-done((bf16[256,1024]{1,0:T(8,128)(2,1)S(1)}, bf16[256,1024]{1,0:T(8,128)(2,1)}, u32[]{:S(2)}, u32[]{:S(2)}) %collective-permute-start.37) | collective-permute-done | bytes 524320 | tf_op jit(solution)/shard_map/ppermute | solution.py:601
  490.6 17.9 %collective-permute-done.62 = f32[8,1024]{1,0:T(8,128)S(1)} collective-permute-done((f32[8,1024]{1,0:T(8,128)S(1)}, f32[8,1024]{1,0:T(8,128)S(1)}, u32[]{:S(2)}, u32[]{:S(2)}) %collective-permute-start.62) | collective-permute-done | bytes 32800 | tf_op jit(solution)/shard_map/ppermute | solution.py:601
  512.8 8.9 %collective-permute-done.45.refs_6_ = bf16[256,768]{1,0:T(8,128)(2,1)} collective-permute-done((bf16[256,768]{1,0:T(8,128)(2,1)S(1)}, bf16[256,768]{1,0:T(8,128)(2,1)}, u32[]{:S(2)}, u32[]{:S(2)}) %collective-permute-start.45) | collective-permute-done | bytes 393248 | tf_op jit(solution)/shard_map/ppermute | solution.py:601
  534.8 7.5 %gather.5 = f32[2048,1024]{1,0:T(8,128)} custom-call(s32[3]{0:T(128)} %pad_add_fusion.refs_0_, bf16[256,1024]{1,0:T(8,128)(2,1)} %copy-done.14, bf16[256,1024]{1,0:T(8,128)(2,1)} %collective-permute-done.28.refs_2_, bf16[256,1024]{1,0:T(8,128)(2,1)} %copy-done.25, bf16[256,1024]{1,0:T(8,128)(2,1)} %copy-done.29, bf16[256,1024]{1,0:T(8,128)(2,1)} %copy-done.15, ...), custom_call_target="tpu_custom_call" | custom-call | bytes 5940000 | tf_op jit(solution)/shard_map/gather/pallas_call | solution.py:35
  546.8 7.5 %gather.4 = f32[512,4096]{1,0:T(8,128)} custom-call(s32[3]{0:T(128)} %pad_add_fusion.refs_0_, bf16[256,1024]{1,0:T(8,128)(2,1)} %copy-done.16, bf16[256,1024]{1,0:T(8,128)(2,1)} %copy-done.24, bf16[256,1024]{1,0:T(8,128)(2,1)} %copy-done.27, bf16[256,1024]{1,0:T(8,128)(2,1)} %copy-done.32, bf16[256,1024]{1,0:T(8,128)(2,1)} %copy-done.17, ...), custom_call_target="tpu_custom_call" | custom-call | bytes 5940000 | tf_op jit(solution)/shard_map/gather/pallas_call | solution.py:35
  (266 shorter events, 169.1 us)
Async XLA Ops:
  3.1 27.2 %collective-permute-start = (bf16[512,1024]{1,0:T(8,128)(2,1)}, bf16[512,1024]{1,0:T(8,128)(2,1)S(1)}, u32[]{:S(2)}, u32[]{:S(2)}) collective-permute-start(bf16[512,1024]{1,0:T(8,128)(2,1)} %dynamic-slice_bitcast_fusion.1), channel_id=1, source_target_pairs={{0,1},{1,0},{2,3},{3,2},{4,5},{5,4},{6,7},{7,6},{8,9},{9,8},{10,11... | collective-permute-start | bytes 3145736 | tf_op jit(solution)/shard_map/ppermute | solution.py:605
  20.9 43.9 %collective-permute-start.1 = (bf16[512,1024]{1,0:T(8,128)(2,1)S(1)}, bf16[512,1024]{1,0:T(8,128)(2,1)S(1)}, u32[]{:S(2)}, u32[]{:S(2)}) collective-permute-start(bf16[512,1024]{1,0:T(8,128)(2,1)S(1)} %copy-done.22), channel_id=1, source_target_pairs={{0,1},{1,0},{2,3},{3,2},{4,5},{5,4},{6,7},{7,6},{8,9},{9,8},{10,11... | collective-permute-start | bytes 3145736 | tf_op jit(solution)/shard_map/ppermute | solution.py:605
  158.2 42.5 %collective-permute-start.8 = (bf16[512,1024]{1,0:T(8,128)(2,1)}, bf16[512,1024]{1,0:T(8,128)(2,1)S(1)}, u32[]{:S(2)}, u32[]{:S(2)}) collective-permute-start(bf16[512,1024]{1,0:T(8,128)(2,1)} %get-tuple-element.88.refs_4_), channel_id=1, source_target_pairs={{0,1},{1,0},{2,3},{3,2},{4,5},{5,4},{6,7},{7,6},{8,9},{9,8},{10,11... | collective-permute-start | bytes 3145736 | tf_op jit(solution)/shard_map/ppermute | solution.py:605
  159.6 80.9 %collective-permute-start.7 = (bf16[512,1024]{1,0:T(8,128)(2,1)}, bf16[512,1024]{1,0:T(8,128)(2,1)}, u32[]{:S(2)}, u32[]{:S(2)}) collective-permute-start(bf16[512,1024]{1,0:T(8,128)(2,1)} %get-tuple-element.96), channel_id=1, source_target_pairs={{0,1},{1,0},{2,3},{3,2},{4,5},{5,4},{6,7},{7,6},{8,9},{9,8},{10,11... | collective-permute-start | bytes 3145736 | tf_op jit(solution)/shard_map/ppermute | solution.py:605
  199.5 49.0 %collective-permute-start.6 = (bf16[1024,512]{1,0:T(8,128)(2,1)}, bf16[1024,512]{1,0:T(8,128)(2,1)S(1)}, u32[]{:S(2)}, u32[]{:S(2)}) collective-permute-start(bf16[1024,512]{1,0:T(8,128)(2,1)} %weight_grad.21.refs_5_), channel_id=1, source_target_pairs={{0,2},{2,0},{4,6},{6,4},{8,10},{10,8},{12,14},{14,12},{16,18},{18,... | collective-permute-start | bytes 3145736 | tf_op jit(solution)/shard_map/ppermute | solution.py:601
  232.9 59.0 %collective-permute-start.12 = (bf16[1024,768]{1,0:T(8,128)(2,1)}, bf16[1024,768]{1,0:T(8,128)(2,1)S(1)}, u32[]{:S(2)}, u32[]{:S(2)}) collective-permute-start(bf16[1024,768]{1,0:T(8,128)(2,1)} %weight_grad.23.refs_5_), channel_id=1, source_target_pairs={{0,2},{2,0},{4,6},{6,4},{8,10},{10,8},{12,14},{14,12},{16,18},{18,... | collective-permute-start | bytes 4718600 | tf_op jit(solution)/shard_map/ppermute | solution.py:601
  240.5 57.7 %collective-permute-start.11 = (bf16[512,1024]{1,0:T(8,128)(2,1)}, bf16[512,1024]{1,0:T(8,128)(2,1)}, u32[]{:S(2)}, u32[]{:S(2)}) collective-permute-start(bf16[512,1024]{1,0:T(8,128)(2,1)} %get-tuple-element.92.refs_11_), channel_id=1, source_target_pairs={{0,1},{1,0},{2,3},{3,2},{4,5},{5,4},{6,7},{7,6},{8,9},{9,8},{10,11... | collective-permute-start | bytes 3145736 | tf_op jit(solution)/shard_map/ppermute | solution.py:605
  246.5 58.3 %collective-permute-start.14 = (bf16[256,1024]{1,0:T(8,128)(2,1)}, bf16[256,1024]{1,0:T(8,128)(2,1)}, u32[]{:S(2)}, u32[]{:S(2)}) collective-permute-start(bf16[256,1024]{1,0:T(8,128)(2,1)} %get-tuple-element.98.refs_4_), channel_id=1, source_target_pairs={{0,4},{2,6},{4,0},{6,2},{8,12},{10,14},{12,8},{14,10},{16,20},{18,... | collective-permute-start | bytes 1572872 | tf_op jit(solution)/shard_map/ppermute | solution.py:601
  281.5 51.1 %collective-permute-start.10 = (bf16[1024,768]{1,0:T(8,128)(2,1)}, bf16[1024,768]{1,0:T(8,128)(2,1)S(1)}, u32[]{:S(2)}, u32[]{:S(2)}) collective-permute-start(bf16[1024,768]{1,0:T(8,128)(2,1)} %weight_grad.26.refs_4_), channel_id=1, source_target_pairs={{0,2},{2,0},{4,6},{6,4},{8,10},{10,8},{12,14},{14,12},{16,18},{18,... | collective-permute-start | bytes 4718600 | tf_op jit(solution)/shard_map/ppermute | solution.py:601
  291.8 46.8 %collective-permute-start.5 = (bf16[512,1024]{1,0:T(8,128)(2,1)}, bf16[512,1024]{1,0:T(8,128)(2,1)}, u32[]{:S(2)}, u32[]{:S(2)}) collective-permute-start(bf16[512,1024]{1,0:T(8,128)(2,1)} %get-tuple-element.89), channel_id=1, source_target_pairs={{0,1},{1,0},{2,3},{3,2},{4,5},{5,4},{6,7},{7,6},{8,9},{9,8},{10,11... | collective-permute-start | bytes 3145736 | tf_op jit(solution)/shard_map/ppermute | solution.py:605
  298.2 47.0 %collective-permute-start.17 = (bf16[512,512]{1,0:T(8,128)(2,1)}, bf16[512,512]{1,0:T(8,128)(2,1)}, u32[]{:S(2)}, u32[]{:S(2)}) collective-permute-start(bf16[512,512]{1,0:T(8,128)(2,1)} %weight_grad.25.refs_9_), channel_id=1, source_target_pairs={{0,1},{1,0},{2,3},{3,2},{4,5},{5,4},{6,7},{7,6},{8,9},{9,8},{10,11... | collective-permute-start | bytes 1572872 | tf_op jit(solution)/shard_map/ppermute | solution.py:605
  308.2 42.3 %collective-permute-start.22 = (bf16[256,1024]{1,0:T(8,128)(2,1)S(1)}, bf16[256,1024]{1,0:T(8,128)(2,1)}, u32[]{:S(2)}, u32[]{:S(2)}) collective-permute-start(bf16[256,1024]{1,0:T(8,128)(2,1)S(1)} %add_convert_fusion.9.refs_9_), channel_id=1, source_target_pairs={{0,16},{2,18},{4,20},{6,22},{8,24},{10,26},{12,28},{14,30},{16,0},... | collective-permute-start | bytes 1572872 | tf_op jit(solution)/shard_map/ppermute | solution.py:601
  338.7 28.3 %collective-permute-start.16 = (bf16[512,768]{1,0:T(8,128)(2,1)S(1)}, bf16[512,768]{1,0:T(8,128)(2,1)}, u32[]{:S(2)}, u32[]{:S(2)}) collective-permute-start(bf16[512,768]{1,0:T(8,128)(2,1)S(1)} %copy-done.10), channel_id=1, source_target_pairs={{0,1},{1,0},{2,3},{3,2},{4,5},{5,4},{6,7},{7,6},{8,9},{9,8},{10,11... | collective-permute-start | bytes 2359304 | tf_op jit(solution)/shard_map/ppermute | solution.py:605
  355.3 25.0 %collective-permute-start.27 = (bf16[256,1024]{1,0:T(8,128)(2,1)S(1)}, bf16[256,1024]{1,0:T(8,128)(2,1)}, u32[]{:S(2)}, u32[]{:S(2)}) collective-permute-start(bf16[256,1024]{1,0:T(8,128)(2,1)S(1)} %add_convert_fusion.7), channel_id=1, source_target_pairs={{0,16},{2,18},{4,20},{6,22},{8,24},{10,26},{12,28},{14,30},{16,0},... | collective-permute-start | bytes 1572872 | tf_op jit(solution)/shard_map/ppermute | solution.py:601
  360.4 25.0 %collective-permute-start.26 = (bf16[256,1024]{1,0:T(8,128)(2,1)S(1)}, bf16[256,1024]{1,0:T(8,128)(2,1)}, u32[]{:S(2)}, u32[]{:S(2)}) collective-permute-start(bf16[256,1024]{1,0:T(8,128)(2,1)S(1)} %add_convert_fusion.6), channel_id=1, source_target_pairs={{0,8},{2,10},{4,12},{6,14},{8,0},{10,2},{12,4},{14,6},{16,24},{18,... | collective-permute-start | bytes 1572872 | tf_op jit(solution)/shard_map/ppermute | solution.py:601
  365.9 39.0 %collective-permute-start.34 = (bf16[512,768]{1,0:T(8,128)(2,1)S(1)}, bf16[512,768]{1,0:T(8,128)(2,1)}, u32[]{:S(2)}, u32[]{:S(2)}) collective-permute-start(bf16[512,768]{1,0:T(8,128)(2,1)S(1)} %copy-done.11), channel_id=1, source_target_pairs={{0,1},{1,0},{2,3},{3,2},{4,5},{5,4},{6,7},{7,6},{8,9},{9,8},{10,11... | collective-permute-start | bytes 2359304 | tf_op jit(solution)/shard_map/ppermute | solution.py:605
  367.0 34.4 %collective-permute-start.24 = (bf16[256,512]{1,0:T(8,128)(2,1)S(1)}, bf16[256,512]{1,0:T(8,128)(2,1)S(1)}, u32[]{:S(2)}, u32[]{:S(2)}) collective-permute-start(bf16[256,512]{1,0:T(8,128)(2,1)S(1)} %add_convert_fusion.20.refs_5_), channel_id=1, source_target_pairs={{0,8},{2,10},{4,12},{6,14},{8,0},{10,2},{12,4},{14,6},{16,24},{18,... | collective-permute-start | bytes 786440 | tf_op jit(solution)/shard_map/ppermute | solution.py:601
  375.7 23.9 %collective-permute-start.25 = (bf16[256,1024]{1,0:T(8,128)(2,1)}, bf16[256,1024]{1,0:T(8,128)(2,1)S(1)}, u32[]{:S(2)}, u32[]{:S(2)}) collective-permute-start(bf16[256,1024]{1,0:T(8,128)(2,1)} %add_convert_fusion.5), channel_id=1, source_target_pairs={{0,8},{2,10},{4,12},{6,14},{8,0},{10,2},{12,4},{14,6},{16,24},{18,... | collective-permute-start | bytes 1572872 | tf_op jit(solution)/shard_map/ppermute | solution.py:601
  380.3 23.6 %collective-permute-start.23 = (bf16[256,768]{1,0:T(8,128)(2,1)}, bf16[256,768]{1,0:T(8,128)(2,1)S(1)}, u32[]{:S(2)}, u32[]{:S(2)}) collective-permute-start(bf16[256,768]{1,0:T(8,128)(2,1)} %get-tuple-element.120), channel_id=1, source_target_pairs={{0,4},{2,6},{4,0},{6,2},{8,12},{10,14},{12,8},{14,10},{16,20},{18,... | collective-permute-start | bytes 1179656 | tf_op jit(solution)/shard_map/ppermute | solution.py:601
  385.4 26.5 %collective-permute-start.33 = (bf16[256,1024]{1,0:T(8,128)(2,1)S(1)}, bf16[256,1024]{1,0:T(8,128)(2,1)}, u32[]{:S(2)}, u32[]{:S(2)}) collective-permute-start(bf16[256,1024]{1,0:T(8,128)(2,1)S(1)} %add_convert_fusion.4.refs_5_), channel_id=1, source_target_pairs={{0,4},{2,6},{4,0},{6,2},{8,12},{10,14},{12,8},{14,10},{16,20},{18,... | collective-permute-start | bytes 1572872 | tf_op jit(solution)/shard_map/ppermute | solution.py:601
  399.6 39.4 %collective-permute-start.32 = (bf16[256,1024]{1,0:T(8,128)(2,1)S(1)}, bf16[256,1024]{1,0:T(8,128)(2,1)}, u32[]{:S(2)}, u32[]{:S(2)}) collective-permute-start(bf16[256,1024]{1,0:T(8,128)(2,1)S(1)} %add_convert_fusion.3), channel_id=1, source_target_pairs={{0,16},{2,18},{4,20},{6,22},{8,24},{10,26},{12,28},{14,30},{16,0},... | collective-permute-start | bytes 1572872 | tf_op jit(solution)/shard_map/ppermute | solution.py:601
  401.5 48.7 %collective-permute-start.31 = (bf16[256,1024]{1,0:T(8,128)(2,1)S(1)}, bf16[256,1024]{1,0:T(8,128)(2,1)}, u32[]{:S(2)}, u32[]{:S(2)}) collective-permute-start(bf16[256,1024]{1,0:T(8,128)(2,1)S(1)} %add_convert_fusion.2), channel_id=1, source_target_pairs={{0,16},{2,18},{4,20},{6,22},{8,24},{10,26},{12,28},{14,30},{16,0},... | collective-permute-start | bytes 1572872 | tf_op jit(solution)/shard_map/ppermute | solution.py:601
  403.9 85.5 %collective-permute-start.2 = (bf16[512,1024]{1,0:T(8,128)(2,1)}, bf16[512,1024]{1,0:T(8,128)(2,1)}, u32[]{:S(2)}, u32[]{:S(2)}) collective-permute-start(bf16[512,1024]{1,0:T(8,128)(2,1)} %get-tuple-element.83), channel_id=1, source_target_pairs={{0,1},{1,0},{2,3},{3,2},{4,5},{5,4},{6,7},{7,6},{8,9},{9,8},{10,11... | collective-permute-start | bytes 3145736 | tf_op jit(solution)/shard_map/ppermute | solution.py:605
  404.9 60.3 %collective-permute-start.60 = (f32[8,1024]{1,0:T(8,128)S(1)}, f32[8,1024]{1,0:T(8,128)S(1)}, u32[]{:S(2)}, u32[]{:S(2)}) collective-permute-start(f32[8,1024]{1,0:T(8,128)S(1)} %add.148), channel_id=1, source_target_pairs={{0,4},{2,6},{4,0},{6,2},{8,12},{10,14},{12,8},{14,10},{16,20},{18,... | collective-permute-start | bytes 98312 | tf_op jit(solution)/shard_map/ppermute | solution.py:601
  411.9 42.6 %collective-permute-start.30 = (bf16[256,512]{1,0:T(8,128)(2,1)S(1)}, bf16[256,512]{1,0:T(8,128)(2,1)S(1)}, u32[]{:S(2)}, u32[]{:S(2)}) collective-permute-start(bf16[256,512]{1,0:T(8,128)(2,1)S(1)} %add_convert_fusion.19), channel_id=1, source_target_pairs={{0,16},{2,18},{4,20},{6,22},{8,24},{10,26},{12,28},{14,30},{16,0},... | collective-permute-start | bytes 786440 | tf_op jit(solution)/shard_map/ppermute | solution.py:601
  439.0 25.4 %collective-permute-start.39 = (bf16[256,768]{1,0:T(8,128)(2,1)}, bf16[256,768]{1,0:T(8,128)(2,1)S(1)}, u32[]{:S(2)}, u32[]{:S(2)}) collective-permute-start(bf16[256,768]{1,0:T(8,128)(2,1)} %get-tuple-element.127), channel_id=1, source_target_pairs={{0,4},{2,6},{4,0},{6,2},{8,12},{10,14},{12,8},{14,10},{16,20},{18,... | collective-permute-start | bytes 1179656 | tf_op jit(solution)/shard_map/ppermute | solution.py:601
  484.0 25.8 %collective-permute-start.15 = (bf16[512,1024]{1,0:T(8,128)(2,1)S(1)}, bf16[512,1024]{1,0:T(8,128)(2,1)S(1)}, u32[]{:S(2)}, u32[]{:S(2)}) collective-permute-start(bf16[512,1024]{1,0:T(8,128)(2,1)S(1)} %copy-done.48), channel_id=1, source_target_pairs={{0,1},{1,0},{2,3},{3,2},{4,5},{5,4},{6,7},{7,6},{8,9},{9,8},{10,11... | collective-permute-start | bytes 3145736 | tf_op jit(solution)/shard_map/ppermute | solution.py:605
  521.7 24.3 %collective-permute-start.53 = (bf16[256,1024]{1,0:T(8,128)(2,1)}, bf16[256,1024]{1,0:T(8,128)(2,1)S(1)}, u32[]{:S(2)}, u32[]{:S(2)}) collective-permute-start(bf16[256,1024]{1,0:T(8,128)(2,1)} %collective-permute-done.37.refs_6_), channel_id=1, source_target_pairs={{0,2},{2,0},{4,6},{6,4},{8,10},{10,8},{12,14},{14,12},{16,18},{18,... | collective-permute-start | bytes 1572872 | tf_op jit(solution)/shard_map/ppermute | solution.py:601
  521.7 32.6 %collective-permute-start.42 = (bf16[256,768]{1,0:T(8,128)(2,1)S(1)}, bf16[256,768]{1,0:T(8,128)(2,1)}, u32[]{:S(2)}, u32[]{:S(2)}) collective-permute-start(bf16[256,768]{1,0:T(8,128)(2,1)S(1)} %add_convert_fusion.14.refs_1_), channel_id=1, source_target_pairs={{0,2},{2,0},{4,6},{6,4},{8,10},{10,8},{12,14},{14,12},{16,18},{18,... | collective-permute-start | bytes 1179656 | tf_op jit(solution)/shard_map/ppermute | solution.py:601
  522.2 32.1 %collective-permute-start.46 = (bf16[256,768]{1,0:T(8,128)(2,1)S(1)}, bf16[256,768]{1,0:T(8,128)(2,1)S(1)}, u32[]{:S(2)}, u32[]{:S(2)}) collective-permute-start(bf16[256,768]{1,0:T(8,128)(2,1)S(1)} %add_convert_fusion.12.refs_5_), channel_id=1, source_target_pairs={{0,2},{2,0},{4,6},{6,4},{8,10},{10,8},{12,14},{14,12},{16,18},{18,... | collective-permute-start | bytes 1179656 | tf_op jit(solution)/shard_map/ppermute | solution.py:601
  522.4 31.9 %collective-permute-start.43 = (bf16[256,768]{1,0:T(8,128)(2,1)}, bf16[256,768]{1,0:T(8,128)(2,1)}, u32[]{:S(2)}, u32[]{:S(2)}) collective-permute-start(bf16[256,768]{1,0:T(8,128)(2,1)} %collective-permute-done.40.refs_2_), channel_id=1, source_target_pairs={{0,2},{2,0},{4,6},{6,4},{8,10},{10,8},{12,14},{14,12},{16,18},{18,... | collective-permute-start | bytes 1179656 | tf_op jit(solution)/shard_map/ppermute | solution.py:601
  523.7 30.6 %collective-permute-start.47 = (bf16[256,768]{1,0:T(8,128)(2,1)}, bf16[256,768]{1,0:T(8,128)(2,1)}, u32[]{:S(2)}, u32[]{:S(2)}) collective-permute-start(bf16[256,768]{1,0:T(8,128)(2,1)} %collective-permute-done.45.refs_6_), channel_id=1, source_target_pairs={{0,2},{2,0},{4,6},{6,4},{8,10},{10,8},{12,14},{14,12},{16,18},{18,... | collective-permute-start | bytes 1179656 | tf_op jit(solution)/shard_map/ppermute | solution.py:601
  (80 other events, 1439.1 us)

commit v3 on v2

--- a/solution.py
+++ b/solution.py
@@ -15,7 +15,7 @@
 TILE = 256
 GROUP = 256
 VMEM_LIMIT = 60 * 1024 * 1024
-BYTES_PER_US = 900000
+FLOPS_PER_US = 1000000000
 NN = (((1,), (0,)), ((), ()))
 NT = (((1,), (1,)), ((), ()))
 TN = (((0,), (0,)), ((), ()))
@@ -45,7 +45,7 @@
         input_output_aliases=aliases or {},
         compiler_params=pltpu.CompilerParams(vmem_limit_bytes=VMEM_LIMIT),
         cost_estimate=pl.CostEstimate(
-            flops=0, transcendentals=0, bytes_accessed=int(us * BYTES_PER_US)
+            flops=int(us * FLOPS_PER_US), transcendentals=0, bytes_accessed=1
         ),
         name=name,
     )(*prefetch, *[array for array, _ in inputs], *deps)
@@ -67,10 +67,6 @@
     return pl.BlockSpec((1, TILE, size), lambda i, place, *_: (place[0], jnp.minimum(i, 1), 0))
 
 
-def near_rows(size):
-    return pl.BlockSpec((TILE, size), lambda i, *_: (jnp.minimum(i, 1), 0))
-
-
 def far_rows(size):
     return pl.BlockSpec((TILE, size), lambda i, *_: (jnp.maximum(i - 2, 0), 0))
 
@@ -82,7 +78,7 @@
 def put_rows(near, far, rows):
     @pl.when(pl.program_id(0) < 2)
     def _():
-        near[...] = rows
+        near[0] = rows
 
     @pl.when(pl.program_id(0) >= 2)
     def _():
@@ -307,7 +303,7 @@
             (gains, whole(gains.shape)), (biases, whole(biases.shape)),
         ],
         [
-            (shape((rows // 2, width), BF16), near_rows(width)),
+            (shape((2, rows // 2, width), BF16), own_rows(width)),
             (shape((rows // 2, width), BF16), far_rows(width)),
             (shape((rows, width), F32), row_block(width)),
             (shape((rows, width), BF16), row_block(width)),
@@ -533,7 +529,7 @@
             (w_qkv, whole(w_qkv.shape)), (gains, whole(gains.shape)),
         ],
         [
-            (shape((rows // 2, width), BF16), near_rows(width)),
+            (shape((2, rows // 2, width), BF16), own_rows(width)),
             (shape((rows // 2, width), BF16), far_rows(width)),
             (shape((8, width), F32), whole((8, width))),
         ],
@@ -543,57 +539,20 @@
     )
 
 
-def in_packs_kernel(place, own, got, out):
-    @pl.when(pl.program_id(0) < 2)
-    def _():
-        out[0] = own[...]
-
-    @pl.when(pl.program_id(0) >= 2)
-    def _():
-        out[0] = got[...]
-
-
-def in_packs(place, own, got, deps):
-    rows, width = own.shape
-
-    def at(i, place):
-        mine = i < 2
-        return (jnp.where(mine, place[0], 1 - place[0]), jnp.where(mine, i, i - 2), 0)
-
-    return call(
-        in_packs_kernel,
-        (2 * rows // TILE,),
-        [place],
-        [(own, near_rows(width)), (got, far_rows(width))],
-        [(shape((2, rows, width), BF16), pl.BlockSpec((1, TILE, width), at))],
-        deps,
-        "in_packs",
-        3,
-    )[0]
-
-
-def weight_grad_kernel(addend_count, place, left, right, *refs):
-    addends = refs[:addend_count]
-    outs = refs[addend_count:]
-    step = pl.program_id(0)
-    share = pl.num_programs(0) // len(outs)
-    rights = [right[...]] if len(right.shape) == 2 else [right[p] for p in range(right.shape[0])]
+def weight_grad_kernel(source_count, place, *refs):
+    out = refs[-1]
+    addends = refs[2 * source_count : -1]
     start = 0
-    for piece in rights:
-        cols = slice(start, start + piece.shape[1])
-        start = cols.stop
-        total = dot(left[...], piece, TN)
-        for addend in addends:
-            total = total + addend[:, cols].astype(F32)
-        total = total.astype(BF16)
-        if len(outs) == 1:
-            outs[0][:, cols] = total
-            continue
-        for number, out in enumerate(outs):
-
-            @pl.when(step // share == number)
-            def _(out=out, cols=cols, total=total):
-                out[:, cols] = total
+    for number in range(source_count):
+        left, right = refs[2 * number], refs[2 * number + 1]
+        rights = [right] if len(right.shape) == 2 else [right.at[p] for p in range(3)]
+        for piece in rights:
+            cols = slice(start, start + piece.shape[1])
+            start = cols.stop
+            total = dot(left[...], piece[...], TN)
+            for addend in addends:
+                total = total + addend[:, cols].astype(F32)
+            out[:, cols] = total.astype(BF16)
 
 
 def swap_wide(rows, bit):
@@ -605,6 +564,23 @@
     return lax.ppermute(rows, "narrow", [(0, 1), (1, 0)])
 
 
+def swap_crossed(rows, first):
+    pairs = []
+    for i in range(lax.axis_size("wide")):
+        for n in range(2):
+            along_x = (i % 2 == 0) == first
+            peer = (i, 1 - n) if along_x else (i ^ 2, n)
+            pairs.append((2 * i + n, 2 * peer[0] + peer[1]))
+    return lax.ppermute(rows, ("wide", "narrow"), pairs)
+
+
+def swap_two(rows, even_bit, odd_bit):
+    size = lax.axis_size("wide")
+    return lax.ppermute(
+        rows, "wide", [(i, i ^ (even_bit if i % 2 == 0 else odd_bit)) for i in range(size)]
+    )
+
+
 def pair_sum(mine, theirs):
     return (mine.astype(F32) + theirs.astype(F32)).astype(BF16)
 
@@ -614,154 +590,176 @@
 
 
 class Reduction:
-    def __init__(self, place, left, right, count, cols, row_of, right_of, us):
-        self.place, self.left, self.right = place, left, right
-        self.count, self.cols, self.us = count, cols, us
-        self.row_of, self.right_of = row_of, right_of
-        self.state = [None] * count
-
-    def blocks(self, steps, block_of, addends, outs, deps):
-        tokens = self.left.shape[0]
-        row = lambda i, place: (0, self.row_of(*block_of(i, place)))
-        if self.right.ndim == 2:
-            right = pl.BlockSpec(
-                (tokens, self.cols), lambda i, place: (0, self.right_of(*block_of(i, place)))
-            )
-        else:
-            right = pl.BlockSpec(
-                (3, tokens, self.cols // 3),
-                lambda i, place: (0, 0, self.right_of(*block_of(i, place))),
-            )
-        share = steps // outs
-        out = shape((share * TILE, self.cols), BF16)
-        out_at = lambda number: pl.BlockSpec(
-            (TILE, self.cols), lambda i, place: (jnp.clip(i - number * share, 0, share - 1), 0)
-        )
-        add_at = lambda at: pl.BlockSpec((TILE, self.cols), lambda i, place: (at(i), 0))
+    def __init__(self, place, sources, rows, cols, halves, us):
+        self.place, self.sources = place, sources
+        self.rows, self.cols, self.halves, self.us = rows, cols, halves, us
+        self.bits = []
+        bit = 4
+        while bit < lax.axis_size("wide"):
+            self.bits.append(bit)
+            bit *= 2
+
+    def blocks(self, steps, core_of, pair_of, addends, deps):
+        tokens = self.sources[0][0].shape[0]
+
+        def at(place_of):
+            def index(i, h, place):
+                core = core_of(place)
+                first, second = pair_of(i, place)
+                x = jnp.where(core == 0, first, second)
+                b = jnp.where(core == 0, second, first)
+                return place_of(x, core, b, h)
+
+            return index
+
+        inputs = []
+        for left, left_of, right, right_of, width in self.sources:
+            inputs.append((left, pl.BlockSpec((tokens, self.rows), at(left_of))))
+            dims = (tokens, width) if right.ndim == 2 else (3, tokens, width)
+            inputs.append((right, pl.BlockSpec(dims, at(right_of))))
+        block = (self.rows, self.cols // self.halves)
+        for array, row in addends:
+            inputs.append((array, pl.BlockSpec(block, lambda i, h, place, row=row: (row(i), h))))
         return call(
-            functools.partial(weight_grad_kernel, len(addends)),
-            (steps,),
+            functools.partial(weight_grad_kernel, len(self.sources)),
+            (steps, self.halves),
             [self.place],
-            [(self.left, pl.BlockSpec((tokens, TILE), row)), (self.right, right)]
-            + [(array, add_at(at)) for array, at in addends],
-            [(out, out_at(number)) for number in range(outs)],
+            inputs,
+            [
+                (
+                    shape((steps * self.rows, self.cols), BF16),
+                    pl.BlockSpec(block, lambda i, h, place: (i, h)),
+                )
+            ],
             deps,
             "weight_grad",
-            1.5 + self.us * steps,
-        )
+            0.5 + 0.3 * self.us * steps,
+        )[0]
 
     def far(self, deps):
-        count = self.count
-
-        def block_of(i, place):
-            n, c, b = place[0], place[1], place[2]
-            return choose(i // (2 * count), n), 1 - c, choose(i % 2, b), (i // 2) % count
-
-        sent = self.blocks(4 * count, block_of, [], 1, deps)[0]
-        self.from_core = swap_wide(sent, 1)
+        pair_of = lambda i, place: (choose(i // 2, place[4]), choose(i % 2, place[3]))
+        sent = self.blocks(4, lambda place: 1 - place[1], pair_of, [], deps)
+        self.core = swap_wide(sent, 1)
         return sent
 
-    def give(self, deps):
-        def block_of(i, place):
-            n, c, b = place[0], place[1], place[2]
-            return 1 - n, c, choose(i % 2, b), i // 2
-
-        sent = self.blocks(
-            2 * self.count, block_of, [(self.from_core, lambda i: i)], self.count, deps
-        )
-        for k, part in enumerate(sent):
-            self.state[k] = swap_narrow(part)
-        return sent[0]
-
-    def keep(self, k, deps):
-        count = self.count
-
-        def block_of(i, place):
-            n, c, b = place[0], place[1], place[2]
-            return n, c, choose(i, b), k
-
-        addends = [(self.from_core, lambda i: 2 * (count + k) + i), (self.state[k], lambda i: i)]
-        sent, kept = self.blocks(2, block_of, addends, 2, deps)
-        self.state[k] = (kept, swap_wide(sent, 2), 4)
+    def first(self, deps):
+        pair_of = lambda i, place: (1 - place[3], choose(i, place[4]))
+        sent = self.blocks(2, lambda place: place[1], pair_of, [(self.core, lambda i: i)], deps)
+        self.near = swap_crossed(sent, True)
         return sent
 
-    def step(self, k, dep):
-        mine, got, bit = self.state[k]
-        total = pair_sum(mine, tie(got, dep))
-        if bit < lax.axis_size("wide"):
-            self.state[k] = (total, swap_wide(total, bit), 2 * bit)
+    def second(self, deps):
+        pair_of = lambda i, place: (place[3], 1 - place[4])
+        addends = [(self.core, lambda i: 2), (self.near, lambda i: 0)]
+        sent = self.blocks(1, lambda place: place[1], pair_of, addends, deps)
+        self.side = swap_crossed(sent, False)
+        return sent
+
+    def keep(self, deps):
+        pair_of = lambda i, place: (place[3], place[4])
+        addends = [(self.core, lambda i: 3), (self.near, lambda i: 1), (self.side, lambda i: 0)]
+        self.total = self.blocks(1, lambda place: place[1], pair_of, addends, deps)
+        self.hop = 0
+        self.send()
+        return self.total
+
+    def send(self):
+        self.got = swap_two(self.total, self.bits[self.hop], self.bits[-1 - self.hop])
+        self.hop += 1
+
+    def step(self, dep):
+        self.total = pair_sum(self.total, tie(self.got, dep))
+        if self.hop < len(self.bits):
+            self.send()
         else:
-            self.state[k] = [total, swap_wide(total, 2), swap_wide(total, 1)]
-        return total
-
-    def spread(self, k, dep):
-        whole_y = tie(self.state[k][1], dep)
-        self.state[k][1] = whole_y
-        self.state[k].append(swap_wide(whole_y, 1))
-        return whole_y
-
-    def done_steps(self, k):
-        return isinstance(self.state[k], list)
+            self.from_y = swap_wide(self.total, 2)
+            self.from_core = swap_wide(self.total, 1)
+        return self.total
+
+    def spread(self, dep):
+        self.from_y = tie(self.from_y, dep)
+        self.from_both = swap_wide(self.from_y, 1)
+        return self.from_y
+
+    def pieces(self):
+        return [self.total, self.from_y, self.from_core, self.from_both]
 
 
 def gather_kernel(place, *refs):
     out = refs[-1]
-    for number, piece in enumerate(refs[:-1]):
+    for number, piece in enumerate(refs[:4]):
 
         @pl.when(pl.program_id(0) == number)
         def _(piece=piece):
             out[...] = piece[...].astype(F32)
 
 
-def gather(place, pieces, dims, block_at, deps):
-    flat = [piece for group in pieces for piece in group]
-    rows, cols = flat[0].shape
-
-    def at(i, place):
-        c = jnp.where(i % 4 < 2, place[1], 1 - place[1])
-        b = jnp.where(i % 2 == 0, place[2], 1 - place[2])
-        return block_at(c, b, i // 4)
+def piece_owner(number, place):
+    c = jnp.where(number < 2, place[1], 1 - place[1])
+    b = jnp.where(number % 2 == 0, place[2], 1 - place[2])
+    return c, b
+
+
+def gather(place, pieces, dims, cols, first, parts, block_at, deps):
+    rows = pieces[0].shape[0]
+
+    def part_of(number):
+        def index(i, h, place):
+            turn = jnp.where(i == number, h, jnp.where(i < number, 0, parts - 1))
+            return (0, first + turn)
+
+        return pl.BlockSpec((rows, cols), index)
 
     return call(
         gather_kernel,
-        (len(flat),),
+        (4, parts),
         [place],
-        [(piece, pl.BlockSpec((rows, cols), lambda i, *_: (0, 0))) for piece in flat],
-        [(shape(dims, F32), pl.BlockSpec((rows, cols), at))],
+        [(piece, part_of(number)) for number, piece in enumerate(pieces)],
+        [
+            (
+                shape(dims, F32),
+                pl.BlockSpec(
+                    (rows, cols), lambda i, h, place: block_at(*piece_owner(i, place), h)
+                ),
+            )
+        ],
         deps,
         "gather",
-        1 + 0.7 * len(flat),
+        6,
     )[0]
 
 
 def gather_mixed_kernel(place, *refs):
     out = refs[-1]
-    quarter = refs[0].shape[1] // 3
+    quarter = refs[0].shape[1]
+    mine = pl.program_id(0) == place[1]
     for core in range(2):
 
-        @pl.when((pl.program_id(0) == place[1]) == (core == 0))
+        @pl.when(mine == (core == 0))
         def _(core=core):
-            for side in range(2):
-                for other in range(2):
-                    piece = refs[4 * side + 2 * core + other]
-                    b = place[2] if other == 0 else 1 - place[2]
-                    for part in range(3):
-                        at = pl.multiple_of((4 * part + 2 * side + b) * quarter, quarter)
-                        values = piece[:, part * quarter : (part + 1) * quarter]
-                        out[:, pl.ds(at, quarter)] = values.astype(F32)
-
-
-def gather_mixed(place, pieces, dims, deps):
-    flat = [piece for group in pieces for piece in group]
+            for other in range(2):
+                b = place[2] if other == 0 else 1 - place[2]
+                at = pl.multiple_of(b * quarter, quarter)
+                out[:, pl.ds(at, quarter)] = refs[2 * core + other][...].astype(F32)
+
+
+def gather_mixed(place, pieces, dims, half, earlier, deps):
+    piece = pl.BlockSpec((TILE, TILE), lambda i, p, place: (0, p))
     return call(
         gather_mixed_kernel,
-        (2,),
+        (2, 3),
         [place],
-        [(piece, whole(piece.shape)) for piece in flat],
-        [(shape(dims, F32), pl.BlockSpec((TILE, dims[1]), lambda i, *_: (i, 0)))],
-        deps,
+        [(array, piece) for array in pieces],
+        [
+            (
+                shape(dims, F32),
+                pl.BlockSpec((TILE, 2 * TILE), lambda i, p, place: (i, 2 * p + half)),
+            )
+        ],
+        earlier + deps,
         "gather_mixed",
-        5,
+        4,
+        aliases={5: 0} if earlier else None,
     )[0]
 
 
@@ -773,7 +771,11 @@
     ff = w_up.shape[1]
     n = lax.axis_index("narrow")
     w = lax.axis_index("wide")
-    place = jnp.stack([n, w % 2, (w // 2) % 2]).astype(jnp.int32)
+    core = w % 2
+    side = (w // 2) % 2
+    place = jnp.stack(
+        [n, core, side, jnp.where(core == 0, n, side), jnp.where(core == 0, side, n)]
+    ).astype(jnp.int32)
     pick = lambda array, index: lax.dynamic_index_in_dim(array, index, 0, keepdims=False)
 
     far_tok = swap_narrow(pick(tokens, 1 - n))
@@ -809,83 +811,117 @@
     )
     got_out = swap_narrow(far_out)
 
-    reduce = functools.partial(Reduction, place)
-    down = reduce(active, back2, 2, 1024, lambda x, c, b, k: 8 * x + 4 * c + 2 * b + k,
-                  lambda x, c, b, k: 0, 0.8)
-    up = reduce(normed2, hidden_back, 2, 1024, lambda x, c, b, k: 2 * x + c,
-                lambda x, c, b, k: 2 * b + k, 0.8)
+    half_wide = width // 2
+    down = Reduction(
+        place,
+        [(active, lambda x, c, b, h: (0, 4 * x + 2 * c + b),
+          back2, lambda x, c, b, h: (0, h), half_wide)],
+        2 * TILE, width, 2, 1.5,
+    )
+    up = Reduction(
+        place,
+        [(normed2, lambda x, c, b, h: (0, x),
+          hidden_back, lambda x, c, b, h: (0, 2 * (2 * c + b) + h), half_wide)],
+        2 * TILE, width, 2, 1.5,
+    )
     last = down.far([])
     last = up.far([last])
-    last = down.give([last])
-    last = up.give([last])
+    last = down.first([last])
+    last = up.first([last])
     middle_back, branch_back, att_back, sums12 = return_pass(
         place, tokens, far_tok, cotangent, far_cot, branch, hidden_back, w_out, w_up,
-        norm_gains, norm_biases, [last],
-    )
-    proj = reduce(att, branch_back, 1, 512, lambda x, c, b, k: 2 * x + c, lambda x, c, b, k: b, 0.5)
-    a = proj.far([])
-    b = down.keep(0, [a])
-    left_back = attend_back(info, mixed, att, att_back, stats, cos_t, sin_t, 0, [b])
-    qkv = [reduce(normed, left_back, 1, 768, lambda x, c, b, k: 2 * x + c, lambda x, c, b, k: b, 0.7)]
-    a = qkv[0].far([])
-    b = down.keep(1, [a])
-    d = proj.give([b])
-    e = down.step(0, d)
-    right_back = attend_back(info, mixed, att, att_back, stats, cos_t, sin_t, 1, [d, e])
-    qkv.append(
-        reduce(normed, right_back, 1, 768, lambda x, c, b, k: 2 * x + c, lambda x, c, b, k: b, 0.7)
-    )
-    a = qkv[1].far([])
-    b = qkv[0].give([a])
-    d = up.keep(0, [b])
-    e = down.step(1, d)
-    f = down.step(0, e)
+        norm_gains, norm_biases, [last, got_out],
+    )
+    last = down.second([middle_back])
+    left_back = attend_back(info, mixed, att, att_back, stats, cos_t, sin_t, 0, [last])
+    by_rows = lambda x, c, b, h: (0, 2 * x + c)
+    by_parts = lambda x, c, b, h: (0, 0, b)
+    left = Reduction(
+        place,
+        [(normed, by_rows, left_back, by_parts, TILE),
+         (att, by_rows, branch_back, lambda x, c, b, h: (0, b), half_wide)],
+        TILE, 5 * TILE, 1, 1.2,
+    )
+    last = left.far([])
+    last = down.keep([last])
+    last = up.second([last])
+    right_back = attend_back(info, mixed, att, att_back, stats, cos_t, sin_t, 1, [last])
+    right = Reduction(
+        place, [(normed, by_rows, right_back, by_parts, TILE)], TILE, 3 * TILE, 1, 0.8
+    )
+    last = right.far([])
+    last = left.first([last])
+    last = up.keep([last])
+    a = down.step(last)
     near_grad, far_grad, sums0 = finish(
-        place, tokens, far_tok, middle_back, left_back, right_back, w_qkv, norm_gains, [d, f]
-    )
-    a = qkv[1].give([near_grad])
-    got_grad = swap_narrow(tie(far_grad, a))
+        place, tokens, far_tok, middle_back, left_back, right_back, w_qkv, norm_gains, [last, a]
+    )
+    last = right.first([near_grad])
     norm_term = jnp.concatenate(
         [sums0[0:1], sums12[0:1], sums12[2:3], sums3[0:1],
          sums0[1:2], sums12[1:2], sums12[3:4], sums3[1:2]], axis=0
     )
-    norm_term = norm_term + swap_narrow(norm_term)
-    a = up.keep(1, [a])
-    out = in_packs(place, near_out, got_out, [a])
-    last = proj.keep(0, [a])
-    bit = 1
-    chunks = [(down, 0), (down, 1), (up, 0), (up, 1), (proj, 0)]
-    mixed_chunks = [(qkv[0], 0), (qkv[1], 0)]
-    waiting = list(mixed_chunks)
-    while chunks:
-        later = []
-        for red, k in chunks:
-            if red.done_steps(k):
-                last = red.spread(k, last)
-            else:
-                last = red.step(k, last)
-                later.append((red, k))
-        chunks = later
-        if bit < lax.axis_size("wide"):
-            norm_term = norm_term + swap_wide(norm_term, bit)
-            bit *= 2
-        if waiting:
-            red, k = waiting.pop(0)
-            last = red.keep(k, [last])
-            chunks.append((red, k))
-    while bit < lax.axis_size("wide"):
-        norm_term = norm_term + swap_wide(norm_term, bit)
-        bit *= 2
+    norm_got = swap_narrow(tie(norm_term, last))
+    hops = [2 ** bit for bit in range(lax.axis_size("wide").bit_length() - 1)]
+
+    def norm_step(last):
+        nonlocal norm_term, norm_got
+        norm_term = norm_term + tie(norm_got, last)
+        if hops:
+            norm_got = swap_wide(norm_term, hops.pop(0))
+        return norm_term
+
+    late = left.second([last])
+    out = lax.dynamic_update_slice(near_out, tie(got_out, late)[None], (1 - n, 0, 0))
+    last = down.step(late)
+    last = up.step(last)
+    last = norm_step(last)
+    last = right.second([last])
+    last = left.keep([last])
+    got_grad = swap_narrow(tie(far_grad, last))
+    last = norm_step(last)
+    last = right.keep([last])
+    extra = len(left.bits) - 2
+    for _ in range(extra):
+        last = down.step(last)
+        last = up.step(last)
+    last = down.spread(last)
+    last = norm_step(last)
+    last = left.step(last)
+    last = up.step(last)
+    last = right.step(last)
+    last = norm_step(last)
+    for _ in range(extra):
+        last = left.step(last)
+        last = right.step(last)
     grad_down = gather(
-        place, down.state, (ff // 2, width), lambda c, b, k: (4 * c + 2 * b + k, 0), []
-    )
-    grad_up = gather(place, up.state, (width // 2, ff), lambda c, b, k: (c, 2 * b + k), [])
-    grad_out_proj = gather(place, proj.state, (width // 2, width), lambda c, b, k: (c, b), [])
+        place, down.pieces(), (ff // 2, width), half_wide, 0, 2,
+        lambda c, b, h: (2 * c + b, h), [last],
+    )
+    last = left.step(grad_down)
+    last = right.step(last)
+    while hops:
+        last = norm_step(last)
+    last = up.spread(last)
+    last = norm_step(last)
+    grad_tok = lax.dynamic_update_slice(near_grad, tie(got_grad, last)[None], (1 - n, 0, 0))
+    grad_up = gather(
+        place, up.pieces(), (half_wide, ff), half_wide, 0, 2,
+        lambda c, b, h: (0, 2 * (2 * c + b) + h), [last],
+    )
+    last = left.spread(grad_up)
+    last = right.spread(last)
+    grad_out_proj = gather(
+        place, left.pieces(), (half_wide, width), TILE, 3, 2,
+        lambda c, b, h: (c, 2 * b + h), [last],
+    )
     grad_qkv = gather_mixed(
-        place, [qkv[0].state[0], qkv[1].state[0]], (width // 2, 3 * width), []
-    )
-    grad_tok = in_packs(place, near_grad, got_grad, [])
-    norm_term = lax.dynamic_slice_in_dim(norm_term, n * (width // 2), width // 2, 1)
+        place, left.pieces(), (half_wide, 3 * width), 0, [], [grad_out_proj]
+    )
+    grad_qkv = gather_mixed(
+        place, right.pieces(), (half_wide, 3 * width), 1, [grad_qkv], []
+    )
+    norm_term = lax.dynamic_slice_in_dim(norm_term, n * half_wide, half_wide, 1)
     return (
         out,
         grad_tok,

time: 570 us -> 505 us (0.89)
  starting transfers between devices: 78.7 us -> 32.4 us
  waiting for transfers between devices: 124 us -> 88.2 us
  Pallas kernels: 316 us -> 335 us
  other arithmetic: 25.4 us -> 16.5 us
  local copies, waits for them, and re-layouts: 14.4 us -> 21.7 us
    ppermute x51 -> x20, waiting for transfers between devices: 114 us -> 9.39 us  [swap_wide(): return lax.ppermute(rows, 'wide', [(i, i ^ bit) for i in range(size)])]
    ppermute x0 -> x16, waiting for transfers between devices: none -> 59.2 us  [the longest x8 48.1 us: swap_two(): lax.ppermute(rows, 'wide', [(i, i ^ (even_bit if i % 2 == 0 else odd_bit)...]
    ppermute x51 -> x20, starting transfers between devices: 65.4 us -> 9.03 us  [swap_wide(): return lax.ppermute(rows, 'wide', [(i, i ^ bit) for i in range(size)])]
    ppermute x0 -> x16, starting transfers between devices: none -> 19.9 us  [the longest x8 10.1 us: swap_crossed(): return lax.ppermute(rows, ('wide', 'narrow'), pairs)]
    pallas_call x31 -> x29, Pallas kernels: 316 us -> 335 us  [call(): pl.pallas_call(body, grid_spec=pltpu.PrefetchScalarGridSpec(num_scalar_pr...]
    convert_element_type x21 -> x8, other arithmetic: 18.9 us -> 8.7 us  [pair_sum(): return (mine.astype(F32) + theirs.astype(F32)).astype(BF16)]
    ppermute x12 -> x5, waiting for transfers between devices: 9.81 us -> 19.6 us  [swap_narrow(): return lax.ppermute(rows, 'narrow', [(0, 1), (1, 0)])]
    ppermute x12 -> x5, starting transfers between devices: 13.2 us -> 3.56 us  [swap_narrow(): return lax.ppermute(rows, 'narrow', [(0, 1), (1, 0)])]
  transfers between devices with their start and end apart: 63 -> 41, of which waited for: 22 -> 13; matrix products, arithmetic and copies ran while one was open for 5% -> 5% of each run, Pallas kernels for 44% -> 54%
where the time goes in v3:
time: 505 us; the launch traced here: 496 us
  Pallas kernels  335 us (66%)
  waiting for transfers between devices  88.2 us (17%)
  starting transfers between devices  32.4 us (6%)
  local copies, waits for them, and re-layouts  21.7 us (4%)
  other arithmetic  16.5 us (3%)
    pallas_call x29, Pallas kernels, call(): pl.pallas_call(body, grid_spec=pltpu.PrefetchScalarGridSpec(num_scalar_pr...  335 us
    ppermute x8, waiting for transfers between devices, swap_two(): lax.ppermute(rows, 'wide', [(i, i ^ (even_bit if i % 2 == 0 else odd_bit)...  48.1 us
    ppermute x5, waiting for transfers between devices, swap_narrow(): return lax.ppermute(rows, 'narrow', [(0, 1), (1, 0)])  19.6 us
    ppermute x8, waiting for transfers between devices, swap_crossed(): return lax.ppermute(rows, ('wide', 'narrow'), pairs)  11.1 us
    unnamed x59, local copies, waits for them, and re-layouts  10.9 us
  transfers between devices with their start and end apart: 41, of which 13 were waited for; matrix products, arithmetic and copies ran while one was open for 5% of the time, Pallas kernels for 54%

profile of v3, /device:TPU:0, one launch (start us, length us, event | category | flops | bytes accessed | tf_op | source)
XLA Modules:
  0.0 496.0 jit_solution(578920022241420750)
XLA Ops:
  11.8 9.3 %project.2 = (bf16[1024,1024]{1,0:T(8,128)(2,1)}, bf16[1024,3072]{1,0:T(8,128)(2,1)}) custom-call(s32[5]{0:T(128)} %stack.36.refs_0_, bf16[2,512,1024]{2,1,0:T(8,128)(2,1)} %refs_1_.7, bf16[1024,3072]{1,0:T(8,128)(2,1)} %refs_6_.3, f32[4,1024]{1,0:T(4,128)} %refs_7_.5, f32[4,1024]{1,0:T(4,128)} %refs_10_.3, f32[1024,128]{1,0:T(8,128)} %get-tuple-element.109.refs_5_, ...), custom_call_target="tpu_custom_call" | custom-call | flops 8000000000 | bytes 1 | tf_op jit(solution)/shard_map/project/pallas_call | solution.py:35
  23.6 5.4 %collective-permute-done.refs_1_.refs_2_ = bf16[512,1024]{1,0:T(8,128)(2,1)} collective-permute-done((bf16[512,1024]{1,0:T(8,128)(2,1)S(1)}, bf16[512,1024]{1,0:T(8,128)(2,1)}, u32[]{:S(2)}, u32[]{:S(2)}) %collective-permute-start) | collective-permute-done | bytes 1048608 | tf_op jit(solution)/shard_map/ppermute | solution.py:564
  29.1 9.2 %project.3 = (bf16[1024,1024]{1,0:T(8,128)(2,1)}, bf16[1024,3072]{1,0:T(8,128)(2,1)}) custom-call(s32[5]{0:T(128)} %stack.36.refs_0_, bf16[512,1024]{1,0:T(8,128)(2,1)} %collective-permute-done.refs_1_.refs_2_, bf16[1024,3072]{1,0:T(8,128)(2,1)} %refs_6_.3, f32[4,1024]{1,0:T(4,128)} %refs_7_.5, ...), custom_call_target="tpu_custom_call", output_to_operand_aliasing={{0}: (7, {}), {1}: (8, {})} | custom-call | flops 8000000000 | bytes 1 | tf_op jit(solution)/shard_map/project/pallas_call | solution.py:35
  38.3 36.1 %attend.1 = (bf16[1024,1024]{1,0:T(8,128)(2,1)}, f32[4,4,1024]{2,1,0:T(4,128)}) custom-call(s32[5]{0:T(128)} %concatenate.19.refs_0_, bf16[1024,3072]{1,0:T(8,128)(2,1)} %get-tuple-element.54.refs_1_.refs_2_.refs_3_, bf16[1024,3072]{1,0:T(8,128)(2,1)} %get-tuple-element.54.refs_1_.refs_2_.refs_3_, bf16[1024,3072]{1,0:T(8,128)(2,1)} %get-tuple-element.54.refs_1_.refs_2_.refs_3_), custom_call_target="tpu_custom_call" | custom-call | flops 35999997952 | bytes 1 | tf_op jit(solution)/shard_map/attend/pallas_call | solution.py:35
  74.3 50.7 %feed.1 = (bf16[2,512,1024]{2,1,0:T(8,128)(2,1)}, bf16[512,1024]{1,0:T(8,128)(2,1)}, f32[1024,1024]{1,0:T(8,128)}, bf16[1024,1024]{1,0:T(8,128)(2,1)}, bf16[1024...) custom-call(s32[5]{0:T(128)} %stack.36.refs_0_, ...), custom_call_target="tpu_custom_call" | custom-call | flops 49000001536 | bytes 1 | tf_op jit(solution)/shard_map/feed/pallas_call | solution.py:35
  125.1 12.4 %weight_grad.16.refs_3_ = bf16[2048,1024]{1,0:T(8,128)(2,1)} custom-call(s32[5]{0:T(128)} %stack.36.refs_0_, bf16[1024,4096]{1,0:T(8,128)(2,1)} %get-tuple-element.62.refs_1_, bf16[1024,1024]{1,0:T(8,128)(2,1)} %get-tuple-element.63.refs_2_), custom_call_target="tpu_custom_call" | custom-call | flops 2300000000 | bytes 1 | tf_op jit(solution)/shard_map/weight_grad/pallas_call | solution.py:35
  137.5 12.3 %weight_grad.17.refs_4_ = bf16[2048,1024]{1,0:T(8,128)(2,1)} custom-call(s32[5]{0:T(128)} %stack.36.refs_0_, bf16[1024,1024]{1,0:T(8,128)(2,1)} %get-tuple-element.61.refs_1_, bf16[1024,4096]{1,0:T(8,128)(2,1)} %get-tuple-element.60.refs_2_.refs_6_, bf16[2048,1024]{1,0:T(8,128)(2,1)} %weight_grad.16.refs_3_), custom_call_target="tpu_custom_call" | custom-call | flops 2300000000 | bytes 1 | tf_op jit(solution)/shard_map/weight_grad/pallas_call | solution.py:35
  151.1 7.5 %weight_grad.18.refs_4_ = bf16[1024,1024]{1,0:T(8,128)(2,1)} custom-call(s32[5]{0:T(128)} %stack.36.refs_0_, bf16[1024,4096]{1,0:T(8,128)(2,1)} %get-tuple-element.62.refs_1_, bf16[1024,1024]{1,0:T(8,128)(2,1)} %get-tuple-element.63.refs_2_, bf16[2048,1024]{1,0:T(8,128)(2,1)} %collective-permute-done.4.refs_3_, bf16[2048,1024]{1,0:T(8,128)(2,1)} %weight_grad.17.refs_4_), custom_call_target="tpu_custom_call" | custom-call | flops 1400000000 | bytes 1 | tf_op jit(solution)/shard_map/weight_grad/pallas_call | solution.py:35
  160.7 7.3 %weight_grad.19.refs_11_ = bf16[1024,1024]{1,0:T(8,128)(2,1)} custom-call(s32[5]{0:T(128)} %stack.36.refs_0_, bf16[1024,1024]{1,0:T(8,128)(2,1)} %get-tuple-element.61.refs_1_, bf16[1024,4096]{1,0:T(8,128)(2,1)} %get-tuple-element.60.refs_2_.refs_6_, bf16[2048,1024]{1,0:T(8,128)(2,1)} %collective-permute-done.3.refs_3_, bf16[1024,1024]{1,0:T(8,128)(2,1)} %weight_grad.18.refs_4_), custom_call_target="tpu_custom_call" | custom-call | flops 1400000000 | bytes 1 | tf_op jit(solution)/shard_map/weight_grad/pallas_call | solution.py:35
  168.0 7.6 %collective-permute-done.2.refs_12_ = bf16[512,1024]{1,0:T(8,128)(2,1)S(1)} collective-permute-done((bf16[512,1024]{1,0:T(8,128)(2,1)}, bf16[512,1024]{1,0:T(8,128)(2,1)S(1)}, u32[]{:S(2)}, u32[]{:S(2)}) %collective-permute-start.2) | collective-permute-done | bytes 1048608 | tf_op jit(solution)/shard_map/ppermute | solution.py:564
  176.6 25.3 %return_pass.1 = (f32[1024,1024]{1,0:T(8,128)}, bf16[1024,1024]{1,0:T(8,128)(2,1)}, bf16[1024,1024]{1,0:T(8,128)(2,1)}, f32[8,1024]{1,0:T(8,128)}) custom-call(s32[5]{0:T(128)} %stack.36.refs_0_, bf16[2,512,1024]{2,1,0:T(8,128)(2,1)} %refs_1_.7, bf16[512,1024]{1,0:T(8,128)(2,1)} %collective-permute-done.refs_1_.refs_2_, bf16[2,512,1024]{2,1,0:T(8,128)(2,1)} %refs_3_.7, ...), custom_call_target="tpu_custom_call" | custom-call | flops 24000000000 | bytes 1 | tf_op jit(solution)/shard_map/return_pass/pallas_call | solution.py:35
  210.4 24.3 %attend_back.2.refs_2_.refs_4_ = bf16[3,1024,512]{2,1,0:T(8,128)(2,1)} custom-call(s32[5]{0:T(128)} %concatenate.19.refs_0_, bf16[1024,3072]{1,0:T(8,128)(2,1)} %get-tuple-element.54.refs_1_.refs_2_.refs_3_, bf16[1024,3072]{1,0:T(8,128)(2,1)} %get-tuple-element.54.refs_1_.refs_2_.refs_3_, bf16[1024,3072]{1,0:T(8,128)(2,1)} %get-tuple-element.54.refs_1_.refs_2_.refs_3_, ...), custom_call_target="tpu_custom_call" | custom-call | flops 22000001024 | bytes 1 | tf_op jit(solution)/shard_map/attend_back/pallas_call | solution.py:35
  234.7 9.0 %weight_grad.21.refs_6_ = bf16[1024,1280]{1,0:T(8,128)(2,1)} custom-call(s32[5]{0:T(128)} %stack.36.refs_0_, bf16[1024,1024]{1,0:T(8,128)(2,1)} %get-tuple-element.58.refs_1_, bf16[3,1024,512]{2,1,0:T(8,128)(2,1)} %attend_back.2.refs_2_.refs_4_, bf16[1024,1024]{1,0:T(8,128)(2,1)} %get-tuple-element.55.refs_5_.refs_4_.refs_3_, ...), custom_call_target="tpu_custom_call" | custom-call | flops 1940000000 | bytes 1 | tf_op jit(solution)/shard_map/weight_grad/pallas_call | solution.py:35
  245.5 5.4 %weight_grad.22.refs_5_ = bf16[512,1024]{1,0:T(8,128)(2,1)} custom-call(s32[5]{0:T(128)} %stack.36.refs_0_, bf16[1024,4096]{1,0:T(8,128)(2,1)} %get-tuple-element.62.refs_1_, bf16[1024,1024]{1,0:T(8,128)(2,1)} %get-tuple-element.63.refs_2_, bf16[2048,1024]{1,0:T(8,128)(2,1)} %collective-permute-done.4.refs_3_, bf16[1024,1024]{1,0:T(8,128)(2,1)} %copy-done.2, ...), custom_call_target="tpu_custom_call" | custom-call | flops 950000000 | bytes 1 | tf_op jit(solution)/shard_map/weight_grad/pallas_call | solution.py:35
  251.8 5.4 %weight_grad.23.refs_9_ = bf16[512,1024]{1,0:T(8,128)(2,1)} custom-call(s32[5]{0:T(128)} %stack.36.refs_0_, bf16[1024,1024]{1,0:T(8,128)(2,1)} %get-tuple-element.61.refs_1_, bf16[1024,4096]{1,0:T(8,128)(2,1)} %get-tuple-element.60.refs_2_.refs_6_, bf16[2048,1024]{1,0:T(8,128)(2,1)} %collective-permute-done.3.refs_3_, ...), custom_call_target="tpu_custom_call" | custom-call | flops 950000000 | bytes 1 | tf_op jit(solution)/shard_map/weight_grad/pallas_call | solution.py:35
  257.2 24.2 %attend_back.3.refs_2_.refs_5_ = bf16[3,1024,512]{2,1,0:T(8,128)(2,1)} custom-call(s32[5]{0:T(128)} %concatenate.19.refs_0_, bf16[1024,3072]{1,0:T(8,128)(2,1)} %get-tuple-element.54.refs_1_.refs_2_.refs_3_, bf16[1024,3072]{1,0:T(8,128)(2,1)} %get-tuple-element.54.refs_1_.refs_2_.refs_3_, bf16[1024,3072]{1,0:T(8,128)(2,1)} %get-tuple-element.54.refs_1_.refs_2_.refs_3_, ...), custom_call_target="tpu_custom_call" | custom-call | flops 22000001024 | bytes 1 | tf_op jit(solution)/shard_map/attend_back/pallas_call | solution.py:35
  281.4 6.8 %weight_grad.24.refs_6_ = bf16[1024,768]{1,0:T(8,128)(2,1)} custom-call(s32[5]{0:T(128)} %stack.36.refs_0_, bf16[1024,1024]{1,0:T(8,128)(2,1)} %get-tuple-element.58.refs_1_, bf16[3,1024,512]{2,1,0:T(8,128)(2,1)} %attend_back.3.refs_2_.refs_5_), custom_call_target="tpu_custom_call" | custom-call | flops 1460000000 | bytes 1 | tf_op jit(solution)/shard_map/weight_grad/pallas_call | solution.py:35
  289.8 5.6 %weight_grad.25.refs_6_ = bf16[512,1280]{1,0:T(8,128)(2,1)} custom-call(s32[5]{0:T(128)} %stack.36.refs_0_, bf16[1024,1024]{1,0:T(8,128)(2,1)} %get-tuple-element.58.refs_1_, bf16[3,1024,512]{2,1,0:T(8,128)(2,1)} %attend_back.2.refs_2_.refs_4_, bf16[1024,1024]{1,0:T(8,128)(2,1)} %get-tuple-element.55.refs_5_.refs_4_.refs_3_, ...), custom_call_target="tpu_custom_call" | custom-call | flops 1220000000 | bytes 1 | tf_op jit(solution)/shard_map/weight_grad/pallas_call | solution.py:35
  300.0 5.5 %weight_grad.26.refs_8_ = bf16[512,1024]{1,0:T(8,128)(2,1)} custom-call(s32[5]{0:T(128)} %stack.36.refs_0_, bf16[1024,1024]{1,0:T(8,128)(2,1)} %get-tuple-element.61.refs_1_, bf16[1024,4096]{1,0:T(8,128)(2,1)} %get-tuple-element.60.refs_2_.refs_6_, bf16[2048,1024]{1,0:T(8,128)(2,1)} %collective-permute-done.3.refs_3_, ...), custom_call_target="tpu_custom_call" | custom-call | flops 950000000 | bytes 1 | tf_op jit(solution)/shard_map/weight_grad/pallas_call | solution.py:35
  308.8 15.5 %finish.1 = (bf16[2,512,1024]{2,1,0:T(8,128)(2,1)}, bf16[512,1024]{1,0:T(8,128)(2,1)}, f32[8,1024]{1,0:T(8,128)}) custom-call(s32[5]{0:T(128)} %stack.36.refs_0_, bf16[2,512,1024]{2,1,0:T(8,128)(2,1)} %refs_1_.7, bf16[512,1024]{1,0:T(8,128)(2,1)} %collective-permute-done.refs_1_.refs_2_, f32[1024,1024]{1,0:T(8,128)} %get-tuple-element.66.refs_5_.refs_3_, ...), custom_call_target="tpu_custom_call" | custom-call | flops 15000000512 | bytes 1 | tf_op jit(solution)/shard_map/finish/pallas_call | solution.py:35
  338.1 13.5 %collective-permute-done.17 = bf16[512,1024]{1,0:T(8,128)(2,1)} collective-permute-done((bf16[512,1024]{1,0:T(8,128)(2,1)S(1)}, bf16[512,1024]{1,0:T(8,128)(2,1)}, u32[]{:S(2)}, u32[]{:S(2)}) %collective-permute-start.17) | collective-permute-done | bytes 1048608 | tf_op jit(solution)/shard_map/ppermute | solution.py:579
  362.1 5.1 %weight_grad.30 = bf16[256,1280]{1,0:T(8,128)(2,1)} custom-call(s32[5]{0:T(128)} %stack.36.refs_0_, bf16[1024,1024]{1,0:T(8,128)(2,1)} %get-tuple-element.58.refs_1_, bf16[3,1024,512]{2,1,0:T(8,128)(2,1)} %attend_back.2.refs_2_.refs_4_, bf16[1024,1024]{1,0:T(8,128)(2,1)} %get-tuple-element.55.refs_5_.refs_4_.refs_3_, ...), custom_call_target="tpu_custom_call" | custom-call | flops 860000000 | bytes 1 | tf_op jit(solution)/shard_map/weight_grad/pallas_call | solution.py:35
  372.8 11.1 %collective-permute-done.22.refs_5_ = bf16[256,768]{1,0:T(8,128)(2,1)S(1)} collective-permute-done((bf16[256,768]{1,0:T(8,128)(2,1)S(1)}, bf16[256,768]{1,0:T(8,128)(2,1)S(1)}, u32[]{:S(2)}, u32[]{:S(2)}) %collective-permute-start.22) | collective-permute-done | bytes 393248 | tf_op jit(solution)/shard_map/ppermute | solution.py:574
  391.6 8.1 %collective-permute-done.26 = bf16[256,1280]{1,0:T(8,128)(2,1)S(1)} collective-permute-done((bf16[256,1280]{1,0:T(8,128)(2,1)}, bf16[256,1280]{1,0:T(8,128)(2,1)S(1)}, u32[]{:S(2)}, u32[]{:S(2)}) %collective-permute-start.26) | collective-permute-done | bytes 655392 | tf_op jit(solution)/shard_map/ppermute | solution.py:579
  399.8 16.8 %collective-permute-done.25 = bf16[512,1024]{1,0:T(8,128)(2,1)} collective-permute-done((bf16[512,1024]{1,0:T(8,128)(2,1)S(1)}, bf16[512,1024]{1,0:T(8,128)(2,1)}, u32[]{:S(2)}, u32[]{:S(2)}) %collective-permute-start.25) | collective-permute-done | bytes 1048608 | tf_op jit(solution)/shard_map/ppermute | solution.py:579
  424.2 8.7 %gather.3 = f32[2048,1024]{1,0:T(8,128)} custom-call(s32[5]{0:T(128)} %stack.36.refs_0_, bf16[512,1024]{1,0:T(8,128)(2,1)} %copy-done.12, bf16[512,1024]{1,0:T(8,128)(2,1)} %collective-permute-done.21.refs_2_, bf16[512,1024]{1,0:T(8,128)(2,1)} %collective-permute-done.31.refs_3_, bf16[512,1024]{1,0:T(8,128)(2,1)} %collective-permute-done.32.refs_4_, ...), custom_call_target="tpu_custom_call" | custom-call | flops 6000000000 | bytes 1 | tf_op jit(solution)/shard_map/gather/pallas_call | solution.py:35
  435.3 7.6 %collective-permute-done.29 = bf16[256,768]{1,0:T(8,128)(2,1)S(1)} collective-permute-done((bf16[256,768]{1,0:T(8,128)(2,1)S(1)}, bf16[256,768]{1,0:T(8,128)(2,1)S(1)}, u32[]{:S(2)}, u32[]{:S(2)}) %collective-permute-start.29) | collective-permute-done | bytes 393248 | tf_op jit(solution)/shard_map/ppermute | solution.py:579
  456.3 8.8 %gather.4 = f32[512,4096]{1,0:T(8,128)} custom-call(s32[5]{0:T(128)} %stack.36.refs_0_, bf16[512,1024]{1,0:T(8,128)(2,1)} %add_convert_fusion.refs_1_, bf16[512,1024]{1,0:T(8,128)(2,1)} %collective-permute-done.28.refs_2_, bf16[512,1024]{1,0:T(8,128)(2,1)} %collective-permute-done.35.refs_3_, bf16[512,1024]{1,0:T(8,128)(2,1)} %copy-done.26, ...), custom_call_target="tpu_custom_call" | custom-call | flops 6000000000 | bytes 1 | tf_op jit(solution)/shard_map/gather/pallas_call | solution.py:35
  467.0 6.5 %collective-permute-done.18 = bf16[512,1024]{1,0:T(8,128)(2,1)} collective-permute-done((bf16[512,1024]{1,0:T(8,128)(2,1)}, bf16[512,1024]{1,0:T(8,128)(2,1)}, u32[]{:S(2)}, u32[]{:S(2)}) %collective-permute-start.18) | collective-permute-done | bytes 1048608 | tf_op jit(solution)/shard_map/ppermute | solution.py:564
  475.7 6.3 %gather.5.refs_5_ = f32[512,1024]{1,0:T(8,128)} custom-call(s32[5]{0:T(128)} %stack.36.refs_0_, bf16[256,1280]{1,0:T(8,128)(2,1)} %copy-done.19, bf16[256,1280]{1,0:T(8,128)(2,1)} %collective-permute-done.34.refs_2_, bf16[256,1280]{1,0:T(8,128)(2,1)} %collective-permute-done.39.refs_3_, bf16[256,1280]{1,0:T(8,128)(2,1)} %collective-permute-done.40.refs_4_, ...), custom_call_target="tpu_custom_call" | custom-call | flops 6000000000 | bytes 1 | tf_op jit(solution)/shard_map/gather/pallas_call | solution.py:35
  482.0 6.0 %gather_mixed.2.refs_5_ = f32[512,3072]{1,0:T(8,128)} custom-call(s32[5]{0:T(128)} %stack.36.refs_0_, bf16[256,1280]{1,0:T(8,128)(2,1)} %copy-done.19, bf16[256,1280]{1,0:T(8,128)(2,1)} %collective-permute-done.34.refs_2_, bf16[256,1280]{1,0:T(8,128)(2,1)} %collective-permute-done.39.refs_3_, bf16[256,1280]{1,0:T(8,128)(2,1)} %collective-permute-done.40.refs_4_, ...), custom_call_target="tpu_custom_call" | custom-call | flops 4000000000 | bytes 1 | tf_op jit(solution)/shard_map/gather_mixed/pallas_call | solution.py:35
  489.6 6.0 %gather_mixed.3 = f32[512,3072]{1,0:T(8,128)} custom-call(s32[5]{0:T(128)} %stack.36.refs_0_, bf16[256,768]{1,0:T(8,128)(2,1)} %add_convert_fusion.6.refs_1_, bf16[256,768]{1,0:T(8,128)(2,1)} %collective-permute-done.33.refs_5_.refs_2_, bf16[256,768]{1,0:T(8,128)(2,1)} %copy-done.27, bf16[256,768]{1,0:T(8,128)(2,1)} %copy-done.28, ...), custom_call_target="tpu_custom_call", output_to_operand_aliasing={{}: (5, {})} | custom-call | flops 4000000000 | bytes 1 | tf_op jit(solution)/shard_map/gather_mixed/pallas_call | solution.py:35
  (169 shorter events, 104.5 us)
Async XLA Ops:
  1.9 27.1 %collective-permute-start = (bf16[512,1024]{1,0:T(8,128)(2,1)S(1)}, bf16[512,1024]{1,0:T(8,128)(2,1)}, u32[]{:S(2)}, u32[]{:S(2)}) collective-permute-start(bf16[512,1024]{1,0:T(8,128)(2,1)S(1)} %dynamic-slice_bitcast_fusion.1), channel_id=1, source_target_pairs={{0,1},{1,0},{2,3},{3,2},{4,5},{5,4},{6,7},{7,6},{8,9},{9,8},{10,11... | collective-permute-start | bytes 3145736 | tf_op jit(solution)/shard_map/ppermute | solution.py:564
  21.1 53.2 %collective-permute-start.1 = (bf16[512,1024]{1,0:T(8,128)(2,1)S(1)}, bf16[512,1024]{1,0:T(8,128)(2,1)}, u32[]{:S(2)}, u32[]{:S(2)}) collective-permute-start(bf16[512,1024]{1,0:T(8,128)(2,1)S(1)} %copy-done.17), channel_id=1, source_target_pairs={{0,1},{1,0},{2,3},{3,2},{4,5},{5,4},{6,7},{7,6},{8,9},{9,8},{10,11... | collective-permute-start | bytes 3145736 | tf_op jit(solution)/shard_map/ppermute | solution.py:564
  149.9 25.8 %collective-permute-start.2 = (bf16[512,1024]{1,0:T(8,128)(2,1)}, bf16[512,1024]{1,0:T(8,128)(2,1)S(1)}, u32[]{:S(2)}, u32[]{:S(2)}) collective-permute-start(bf16[512,1024]{1,0:T(8,128)(2,1)} %get-tuple-element.57), channel_id=1, source_target_pairs={{0,1},{1,0},{2,3},{3,2},{4,5},{5,4},{6,7},{7,6},{8,9},{9,8},{10,11... | collective-permute-start | bytes 3145736 | tf_op jit(solution)/shard_map/ppermute | solution.py:564
  158.6 43.3 %collective-permute-start.5 = (bf16[1024,1024]{1,0:T(8,128)(2,1)}, bf16[1024,1024]{1,0:T(8,128)(2,1)S(1)}, u32[]{:S(2)}, u32[]{:S(2)}) collective-permute-start(bf16[1024,1024]{1,0:T(8,128)(2,1)} %weight_grad.18.refs_4_), channel_id=1, source_target_pairs={{0,1},{1,0},{2,6},{3,7},{4,5},{5,4},{6,2},{7,3},{8,9},{9,8},{10,14... | collective-permute-start | bytes 6291464 | tf_op jit(solution)/shard_map/ppermute | solution.py:574
  167.9 83.9 %collective-permute-start.7 = (bf16[1024,1024]{1,0:T(8,128)(2,1)}, bf16[1024,1024]{1,0:T(8,128)(2,1)}, u32[]{:S(2)}, u32[]{:S(2)}) collective-permute-start(bf16[1024,1024]{1,0:T(8,128)(2,1)} %weight_grad.19.refs_11_), channel_id=1, source_target_pairs={{0,1},{1,0},{2,6},{3,7},{4,5},{5,4},{6,2},{7,3},{8,9},{9,8},{10,14... | collective-permute-start | bytes 6291464 | tf_op jit(solution)/shard_map/ppermute | solution.py:574
  208.4 36.2 %collective-permute-start.8 = (bf16[512,1024]{1,0:T(8,128)(2,1)}, bf16[512,1024]{1,0:T(8,128)(2,1)S(1)}, u32[]{:S(2)}, u32[]{:S(2)}) collective-permute-start(bf16[512,1024]{1,0:T(8,128)(2,1)} %weight_grad.20.refs_9_), channel_id=1, source_target_pairs={{0,4},{1,5},{2,3},{3,2},{4,0},{5,1},{6,7},{7,6},{8,12},{9,13},{10,... | collective-permute-start | bytes 3145736 | tf_op jit(solution)/shard_map/ppermute | solution.py:574
  243.7 44.6 %collective-permute-start.6 = (bf16[1024,1280]{1,0:T(8,128)(2,1)}, bf16[1024,1280]{1,0:T(8,128)(2,1)S(1)}, u32[]{:S(2)}, u32[]{:S(2)}) collective-permute-start(bf16[1024,1280]{1,0:T(8,128)(2,1)} %weight_grad.21.refs_6_), channel_id=1, source_target_pairs={{0,2},{2,0},{4,6},{6,4},{8,10},{10,8},{12,14},{14,12},{16,18},{18,... | collective-permute-start | bytes 7864328 | tf_op jit(solution)/shard_map/ppermute | solution.py:560
  250.9 54.5 %collective-permute-start.12 = (bf16[512,1024]{1,0:T(8,128)(2,1)}, bf16[512,1024]{1,0:T(8,128)(2,1)}, u32[]{:S(2)}, u32[]{:S(2)}) collective-permute-start(bf16[512,1024]{1,0:T(8,128)(2,1)} %weight_grad.22.refs_5_), channel_id=1, source_target_pairs={{0,8},{2,18},{4,12},{6,22},{8,0},{10,26},{12,4},{14,30},{16,24},{1... | collective-permute-start | bytes 3145736 | tf_op jit(solution)/shard_map/ppermute | solution.py:579
  257.2 41.8 %collective-permute-start.11 = (bf16[512,1024]{1,0:T(8,128)(2,1)}, bf16[512,1024]{1,0:T(8,128)(2,1)S(1)}, u32[]{:S(2)}, u32[]{:S(2)}) collective-permute-start(bf16[512,1024]{1,0:T(8,128)(2,1)} %weight_grad.23.refs_9_), channel_id=1, source_target_pairs={{0,4},{1,5},{2,3},{3,2},{4,0},{5,1},{6,7},{7,6},{8,12},{9,13},{10,... | collective-permute-start | bytes 3145736 | tf_op jit(solution)/shard_map/ppermute | solution.py:574
  288.2 36.0 %collective-permute-start.10 = (bf16[1024,768]{1,0:T(8,128)(2,1)}, bf16[1024,768]{1,0:T(8,128)(2,1)}, u32[]{:S(2)}, u32[]{:S(2)}) collective-permute-start(bf16[1024,768]{1,0:T(8,128)(2,1)} %weight_grad.24.refs_6_), channel_id=1, source_target_pairs={{0,2},{2,0},{4,6},{6,4},{8,10},{10,8},{12,14},{14,12},{16,18},{18,... | collective-permute-start | bytes 4718600 | tf_op jit(solution)/shard_map/ppermute | solution.py:560
  295.4 36.6 %collective-permute-start.9 = (bf16[512,1280]{1,0:T(8,128)(2,1)}, bf16[512,1280]{1,0:T(8,128)(2,1)S(1)}, u32[]{:S(2)}, u32[]{:S(2)}) collective-permute-start(bf16[512,1280]{1,0:T(8,128)(2,1)} %weight_grad.25.refs_6_), channel_id=1, source_target_pairs={{0,1},{1,0},{2,6},{3,7},{4,5},{5,4},{6,2},{7,3},{8,9},{9,8},{10,14... | collective-permute-start | bytes 3932168 | tf_op jit(solution)/shard_map/ppermute | solution.py:574
  305.4 49.8 %collective-permute-start.16 = (bf16[512,1024]{1,0:T(8,128)(2,1)}, bf16[512,1024]{1,0:T(8,128)(2,1)}, u32[]{:S(2)}, u32[]{:S(2)}) collective-permute-start(bf16[512,1024]{1,0:T(8,128)(2,1)} %weight_grad.26.refs_8_), channel_id=1, source_target_pairs={{0,8},{2,18},{4,12},{6,22},{8,0},{10,26},{12,4},{14,30},{16,24},{1... | collective-permute-start | bytes 3145736 | tf_op jit(solution)/shard_map/ppermute | solution.py:579
  307.1 44.6 %collective-permute-start.17 = (bf16[512,1024]{1,0:T(8,128)(2,1)S(1)}, bf16[512,1024]{1,0:T(8,128)(2,1)}, u32[]{:S(2)}, u32[]{:S(2)}) collective-permute-start(bf16[512,1024]{1,0:T(8,128)(2,1)S(1)} %add_convert_fusion.3.refs_9_), channel_id=1, source_target_pairs={{0,16},{2,10},{4,20},{6,14},{8,24},{10,2},{12,28},{14,6},{16,0},{1... | collective-permute-start | bytes 3145736 | tf_op jit(solution)/shard_map/ppermute | solution.py:579
  328.9 28.6 %collective-permute-start.14 = (bf16[512,768]{1,0:T(8,128)(2,1)}, bf16[512,768]{1,0:T(8,128)(2,1)}, u32[]{:S(2)}, u32[]{:S(2)}) collective-permute-start(bf16[512,768]{1,0:T(8,128)(2,1)} %weight_grad.27.refs_7_), channel_id=1, source_target_pairs={{0,1},{1,0},{2,6},{3,7},{4,5},{5,4},{6,2},{7,3},{8,9},{9,8},{10,14... | collective-permute-start | bytes 2359304 | tf_op jit(solution)/shard_map/ppermute | solution.py:574
  331.6 25.3 %collective-permute-start.15 = (f32[8,1024]{1,0:T(8,128)S(1)}, f32[8,1024]{1,0:T(8,128)S(1)}, u32[]{:S(2)}, u32[]{:S(2)}) collective-permute-start(f32[8,1024]{1,0:T(8,128)S(1)} %concatenate.20), channel_id=1, source_target_pairs={{0,1},{1,0},{2,3},{3,2},{4,5},{5,4},{6,7},{7,6},{8,9},{9,8},{10,11... | collective-permute-start | bytes 98312 | tf_op jit(solution)/shard_map/ppermute | solution.py:564
  337.9 23.4 %collective-permute-start.13 = (bf16[256,1280]{1,0:T(8,128)(2,1)}, bf16[256,1280]{1,0:T(8,128)(2,1)S(1)}, u32[]{:S(2)}, u32[]{:S(2)}) collective-permute-start(bf16[256,1280]{1,0:T(8,128)(2,1)} %weight_grad.28), channel_id=1, source_target_pairs={{0,4},{1,5},{2,3},{3,2},{4,0},{5,1},{6,7},{7,6},{8,12},{9,13},{10,... | collective-permute-start | bytes 1966088 | tf_op jit(solution)/shard_map/ppermute | solution.py:574
  353.3 37.2 %collective-permute-start.21 = (bf16[512,1024]{1,0:T(8,128)(2,1)S(1)}, bf16[512,1024]{1,0:T(8,128)(2,1)}, u32[]{:S(2)}, u32[]{:S(2)}) collective-permute-start(bf16[512,1024]{1,0:T(8,128)(2,1)S(1)} %add_convert_fusion.2.refs_1_), channel_id=1, source_target_pairs={{0,4},{2,6},{4,0},{6,2},{8,12},{10,14},{12,8},{14,10},{16,20},{18,... | collective-permute-start | bytes 3145736 | tf_op jit(solution)/shard_map/ppermute | solution.py:560
  367.3 32.4 %collective-permute-start.26 = (bf16[256,1280]{1,0:T(8,128)(2,1)}, bf16[256,1280]{1,0:T(8,128)(2,1)S(1)}, u32[]{:S(2)}, u32[]{:S(2)}) collective-permute-start(bf16[256,1280]{1,0:T(8,128)(2,1)} %weight_grad.30), channel_id=1, source_target_pairs={{0,8},{2,18},{4,12},{6,22},{8,0},{10,26},{12,4},{14,30},{16,24},{1... | collective-permute-start | bytes 1966088 | tf_op jit(solution)/shard_map/ppermute | solution.py:579
  368.5 48.1 %collective-permute-start.25 = (bf16[512,1024]{1,0:T(8,128)(2,1)S(1)}, bf16[512,1024]{1,0:T(8,128)(2,1)}, u32[]{:S(2)}, u32[]{:S(2)}) collective-permute-start(bf16[512,1024]{1,0:T(8,128)(2,1)S(1)} %add_convert_fusion.1), channel_id=1, source_target_pairs={{0,16},{2,10},{4,20},{6,14},{8,24},{10,2},{12,28},{14,6},{16,0},{1... | collective-permute-start | bytes 3145736 | tf_op jit(solution)/shard_map/ppermute | solution.py:579
  372.6 50.3 %collective-permute-start.31 = (bf16[512,1024]{1,0:T(8,128)(2,1)S(1)}, bf16[512,1024]{1,0:T(8,128)(2,1)}, u32[]{:S(2)}, u32[]{:S(2)}) collective-permute-start(bf16[512,1024]{1,0:T(8,128)(2,1)S(1)} %add_convert_fusion.2.refs_1_), channel_id=1, source_target_pairs={{0,2},{2,0},{4,6},{6,4},{8,10},{10,8},{12,14},{14,12},{16,18},{18,... | collective-permute-start | bytes 3145736 | tf_op jit(solution)/shard_map/ppermute | solution.py:560
  390.5 28.7 %collective-permute-start.24 = (bf16[256,768]{1,0:T(8,128)(2,1)}, bf16[256,768]{1,0:T(8,128)(2,1)S(1)}, u32[]{:S(2)}, u32[]{:S(2)}) collective-permute-start(bf16[256,768]{1,0:T(8,128)(2,1)} %weight_grad.31), channel_id=1, source_target_pairs={{0,8},{2,18},{4,12},{6,22},{8,0},{10,26},{12,4},{14,30},{16,24},{1... | collective-permute-start | bytes 1179656 | tf_op jit(solution)/shard_map/ppermute | solution.py:579
  390.8 33.4 %collective-permute-start.32 = (bf16[512,1024]{1,0:T(8,128)(2,1)}, bf16[512,1024]{1,0:T(8,128)(2,1)}, u32[]{:S(2)}, u32[]{:S(2)}) collective-permute-start(bf16[512,1024]{1,0:T(8,128)(2,1)} %collective-permute-done.21.refs_2_), channel_id=1, source_target_pairs={{0,2},{2,0},{4,6},{6,4},{8,10},{10,8},{12,14},{14,12},{16,18},{18,... | collective-permute-start | bytes 3145736 | tf_op jit(solution)/shard_map/ppermute | solution.py:560
  399.7 19.6 %collective-permute-start.23 = (f32[8,1024]{1,0:T(8,128)S(1)}, f32[8,1024]{1,0:T(8,128)S(1)}, u32[]{:S(2)}, u32[]{:S(2)}) collective-permute-start(f32[8,1024]{1,0:T(8,128)S(1)} %add.94), channel_id=1, source_target_pairs={{0,8},{2,10},{4,12},{6,14},{8,0},{10,2},{12,4},{14,6},{16,24},{18,... | collective-permute-start | bytes 98312 | tf_op jit(solution)/shard_map/ppermute | solution.py:560
  416.6 18.5 %collective-permute-start.30 = (bf16[256,1280]{1,0:T(8,128)(2,1)S(1)}, bf16[256,1280]{1,0:T(8,128)(2,1)S(1)}, u32[]{:S(2)}, u32[]{:S(2)}) collective-permute-start(bf16[256,1280]{1,0:T(8,128)(2,1)S(1)} %add_convert_fusion.5), channel_id=1, source_target_pairs={{0,16},{2,10},{4,20},{6,14},{8,24},{10,2},{12,28},{14,6},{16,0},{1... | collective-permute-start | bytes 1966088 | tf_op jit(solution)/shard_map/ppermute | solution.py:579
  419.2 36.1 %collective-permute-start.35 = (bf16[512,1024]{1,0:T(8,128)(2,1)}, bf16[512,1024]{1,0:T(8,128)(2,1)}, u32[]{:S(2)}, u32[]{:S(2)}) collective-permute-start(bf16[512,1024]{1,0:T(8,128)(2,1)} %add_convert_fusion.refs_1_), channel_id=1, source_target_pairs={{0,2},{2,0},{4,6},{6,4},{8,10},{10,8},{12,14},{14,12},{16,18},{18,... | collective-permute-start | bytes 3145736 | tf_op jit(solution)/shard_map/ppermute | solution.py:560
  419.3 23.5 %collective-permute-start.29 = (bf16[256,768]{1,0:T(8,128)(2,1)S(1)}, bf16[256,768]{1,0:T(8,128)(2,1)S(1)}, u32[]{:S(2)}, u32[]{:S(2)}) collective-permute-start(bf16[256,768]{1,0:T(8,128)(2,1)S(1)} %add_convert_fusion.7), channel_id=1, source_target_pairs={{0,16},{2,10},{4,20},{6,14},{8,24},{10,2},{12,28},{14,6},{16,0},{1... | collective-permute-start | bytes 1179656 | tf_op jit(solution)/shard_map/ppermute | solution.py:579
  422.9 24.7 %collective-permute-start.28 = (bf16[512,1024]{1,0:T(8,128)(2,1)}, bf16[512,1024]{1,0:T(8,128)(2,1)}, u32[]{:S(2)}, u32[]{:S(2)}) collective-permute-start(bf16[512,1024]{1,0:T(8,128)(2,1)} %add_convert_fusion.refs_1_), channel_id=1, source_target_pairs={{0,4},{2,6},{4,0},{6,2},{8,12},{10,14},{12,8},{14,10},{16,20},{18,... | collective-permute-start | bytes 3145736 | tf_op jit(solution)/shard_map/ppermute | solution.py:560
  447.7 25.9 %collective-permute-start.18 = (bf16[512,1024]{1,0:T(8,128)(2,1)}, bf16[512,1024]{1,0:T(8,128)(2,1)}, u32[]{:S(2)}, u32[]{:S(2)}) collective-permute-start(bf16[512,1024]{1,0:T(8,128)(2,1)} %get-tuple-element.79), channel_id=1, source_target_pairs={{0,1},{1,0},{2,3},{3,2},{4,5},{5,4},{6,7},{7,6},{8,9},{9,8},{10,11... | collective-permute-start | bytes 3145736 | tf_op jit(solution)/shard_map/ppermute | solution.py:564
  447.8 17.7 %collective-permute-start.34 = (bf16[256,1280]{1,0:T(8,128)(2,1)S(1)}, bf16[256,1280]{1,0:T(8,128)(2,1)}, u32[]{:S(2)}, u32[]{:S(2)}) collective-permute-start(bf16[256,1280]{1,0:T(8,128)(2,1)S(1)} %add_convert_fusion.4.refs_1_), channel_id=1, source_target_pairs={{0,4},{2,6},{4,0},{6,2},{8,12},{10,14},{12,8},{14,10},{16,20},{18,... | collective-permute-start | bytes 1966088 | tf_op jit(solution)/shard_map/ppermute | solution.py:560
  454.1 21.4 %collective-permute-start.33 = (bf16[256,768]{1,0:T(8,128)(2,1)}, bf16[256,768]{1,0:T(8,128)(2,1)}, u32[]{:S(2)}, u32[]{:S(2)}) collective-permute-start(bf16[256,768]{1,0:T(8,128)(2,1)} %add_convert_fusion.6.refs_1_), channel_id=1, source_target_pairs={{0,4},{2,6},{4,0},{6,2},{8,12},{10,14},{12,8},{14,10},{16,20},{18,... | collective-permute-start | bytes 1179656 | tf_op jit(solution)/shard_map/ppermute | solution.py:560
  455.3 20.3 %collective-permute-start.39 = (bf16[256,1280]{1,0:T(8,128)(2,1)S(1)}, bf16[256,1280]{1,0:T(8,128)(2,1)}, u32[]{:S(2)}, u32[]{:S(2)}) collective-permute-start(bf16[256,1280]{1,0:T(8,128)(2,1)S(1)} %add_convert_fusion.4.refs_1_), channel_id=1, source_target_pairs={{0,2},{2,0},{4,6},{6,4},{8,10},{10,8},{12,14},{14,12},{16,18},{18,... | collective-permute-start | bytes 1966088 | tf_op jit(solution)/shard_map/ppermute | solution.py:560
  466.8 21.3 %collective-permute-start.37 = (bf16[256,768]{1,0:T(8,128)(2,1)}, bf16[256,768]{1,0:T(8,128)(2,1)S(1)}, u32[]{:S(2)}, u32[]{:S(2)}) collective-permute-start(bf16[256,768]{1,0:T(8,128)(2,1)} %add_convert_fusion.6.refs_1_), channel_id=1, source_target_pairs={{0,2},{2,0},{4,6},{6,4},{8,10},{10,8},{12,14},{14,12},{16,18},{18,... | collective-permute-start | bytes 1179656 | tf_op jit(solution)/shard_map/ppermute | solution.py:560
  (38 other events, 356.0 us)

commit v4 on v3

--- a/solution.py
+++ b/solution.py
@@ -85,6 +85,32 @@
         far[...] = rows
 
 
+class Stream:
+    def __init__(self, sems, parts):
+        self.copies = [
+            pltpu.make_async_copy(source.at[:, cols], target.at[:, cols], sems.at[number])
+            for number, (source, target, cols) in enumerate(parts)
+        ]
+        self.taken = 0
+
+        @pl.when(pl.program_id(0) == 0)
+        def _():
+            for copy in self.copies:
+                copy.start()
+
+    def take(self, count):
+        parts = self.copies[self.taken : self.taken + count]
+        self.taken += count
+
+        @pl.when(pl.program_id(0) == 0)
+        def _():
+            for copy in parts:
+                copy.wait()
+
+
+ANY = pl.BlockSpec(memory_space=pl.ANY)
+
+
 def tie(array, *deps):
     return lax.optimization_barrier((array,) + deps)[0]
 
@@ -106,7 +132,8 @@
     return jnp.sum(rows, axis=0, keepdims=True)
 
 
-def project_kernel(place, tok, w, gains, biases, cosine, sine, normed_out, mixed_out):
+def project_kernel(place, tok, w_far, gains, biases, cosine, sine, normed_out, mixed_out, w, sems):
+    stream = Stream(sems, [(w_far, w, slice(at, at + 512)) for at in range(0, w.shape[1], 512)])
     rows = tok[0] if len(tok.shape) == 3 else tok[...]
     unit, _ = norm_parts(rows.astype(F32))
     normed = (unit * gains[0:1, :] + biases[0:1, :]).astype(BF16)
@@ -118,6 +145,8 @@
     cos = cosine[...]
     sin = sine[...]
     for start in range(0, 3 * width, 256):
+        if start in (0, 512, 1536):
+            stream.take({0: 1, 512: 2, 1536: 3}[start])
         part = dot(normed, w[:, start : start + 256])
         if start >= 2 * width:
             mixed_out[:, start : start + 256] = part.astype(BF16)
@@ -143,7 +172,7 @@
         [place],
         [
             (tok, own_rows(width) if own else row_block(width)),
-            (w_qkv, whole(w_qkv.shape)),
+            (w_qkv, ANY),
             (gains, whole(gains.shape)),
             (biases, whole(biases.shape)),
             (cosine, at(128)),
@@ -156,6 +185,7 @@
         list(earlier),
         "project",
         8,
+        scratch=[pltpu.VMEM(w_qkv.shape, BF16), pltpu.SemaphoreType.DMA((6,))],
         aliases={7: 0, 8: 1} if earlier else None,
     )
 
@@ -244,10 +274,17 @@
     )
 
 
-def feed_kernel(place, own_tok, far_tok, own_cot, far_cot, att, w_out, w_up, w_down, gains, biases,
-                near_out, far_out, branch_out, normed2_out, active_out, back2_out, hidden_back_out, sums,
-                slope):
+def feed_kernel(place, own_tok, far_tok, own_cot, far_cot, att, out_far, up_far, down_far,
+                gains, biases, near_out, far_out, branch_out, normed2_out, active_out, back2_out, hidden_back_out, sums,
+                slope, w_out, w_up, w_down, sems):
     chunk = 1024
+    parts = [(out_far, w_out, slice(0, w_out.shape[1]))]
+    for start in range(0, w_up.shape[1], chunk):
+        parts.append((up_far, w_up, slice(start, start + chunk)))
+        parts.append((down_far.at[start : start + chunk], w_down.at[start : start + chunk],
+                      slice(0, w_down.shape[1])))
+    stream = Stream(sems, parts)
+    stream.take(1)
     residual = pick_rows(own_tok, far_tok)
     branch = dot(att[...], w_out[...])
     branch_out[...] = branch
@@ -261,6 +298,8 @@
     branch2 = jnp.zeros_like(branch)
     for start in range(0, ff, chunk):
         cols = slice(start, start + chunk)
+        if start <= 2 * chunk:
+            stream.take(2 if start < 2 * chunk else 4)
         z = dot(normed2, w_up[:, cols])
         square = z * z
         bend = jnp.tanh(z * (root + (root * 0.044715) * square))
@@ -298,8 +337,7 @@
         [
             (tokens, own_rows(width)), (far_tok, far_rows(width)),
             (cotangent, own_rows(width)), (far_cot, far_rows(width)),
-            (att, row_block(width)),
-            (w_out, whole(w_out.shape)), (w_up, whole(w_up.shape)), (w_down, whole(w_down.shape)),
+            (att, row_block(width)), (w_out, ANY), (w_up, ANY), (w_down, ANY),
             (gains, whole(gains.shape)), (biases, whole(biases.shape)),
         ],
         [
@@ -315,16 +353,34 @@
         [],
         "feed",
         49,
-        scratch=[pltpu.VMEM((TILE, ff), F32)],
-    )
-
-
-def return_kernel(place, own_tok, far_tok, own_cot, far_cot, branch, hidden_back, w_out, w_up, gains, biases,
-                  middle_back_out, branch_back_out, att_back_out, sums):
+        scratch=[
+            pltpu.VMEM((TILE, ff), F32),
+            pltpu.VMEM(w_out.shape, BF16), pltpu.VMEM(w_up.shape, BF16), pltpu.VMEM(w_down.shape, BF16),
+            pltpu.SemaphoreType.DMA((9,)),
+        ],
+    )
+
+
+def return_kernel(place, own_tok, far_tok, own_cot, far_cot, branch, hidden_back, out_far, up_far,
+                  gains, biases, middle_back_out, branch_back_out, att_back_out, sums,
+                  w_out, w_up, sems):
+    chunk = 1024
+    starts = range(0, w_up.shape[1], chunk)
+    stream = Stream(
+        sems,
+        [(up_far, w_up, slice(start, start + chunk)) for start in starts]
+        + [(out_far, w_out, slice(0, w_out.shape[1]))],
+    )
     unit1, rstd1 = norm_parts(branch[...])
     middle = pick_rows(own_tok, far_tok) + unit1 * gains[1:2, :] + biases[1:2, :]
     unit2, rstd2 = norm_parts(middle)
-    grad2 = dot(hidden_back[...], w_up[...], NT)
+    grad2 = None
+    for start in starts:
+        if start <= 2 * chunk:
+            stream.take(1 if start < 2 * chunk else 3)
+        cols = slice(start, start + chunk)
+        term = dot(hidden_back[:, cols], w_up[:, cols], NT)
+        grad2 = term if grad2 is None else grad2 + term
     middle_back = pick_rows(own_cot, far_cot) + norm_back(unit2, rstd2, gains[2:3, :], grad2)
     middle_back_out[...] = middle_back
     branch_back = norm_back(unit1, rstd1, gains[1:2, :], middle_back).astype(BF16)
@@ -353,7 +409,7 @@
             (tokens, own_rows(width)), (far_tok, far_rows(width)),
             (cotangent, own_rows(width)), (far_cot, far_rows(width)),
             (branch, row_block(width)), (hidden_back, row_block(ff)),
-            (w_out, whole(w_out.shape)), (w_up, whole(w_up.shape)),
+            (w_out, ANY), (w_up, ANY),
             (gains, whole(gains.shape)), (biases, whole(biases.shape)),
         ],
         [
@@ -365,6 +421,9 @@
         deps,
         "return_pass",
         24,
+        scratch=[
+            pltpu.VMEM(w_out.shape, BF16), pltpu.VMEM(w_up.shape, BF16), pltpu.SemaphoreType.DMA((5,)),
+        ],
     )
 
 
@@ -456,34 +515,33 @@
         ).astype(BF16)
 
 
-def attend_back(info, mixed, att, grad, stats, cos_t, sin_t, half, deps):
+def attend_back(info, mixed, att, grad, stats, cos_t, sin_t, group, earlier, deps):
     rows, wide = mixed.shape
     width = wide // 3
     groups = width // GROUP
     heads = GROUP // HEAD_DIM
-    first = half * (groups // 2)
-    spec = lambda shift: pl.BlockSpec((rows, GROUP), lambda g, s: (0, g + first + shift * groups))
+    spec = lambda shift: pl.BlockSpec((rows, GROUP), lambda i, s: (0, group + shift * groups))
     per_head = pltpu.VMEM((heads, rows, HEAD_DIM), BF16)
     turned = pltpu.VMEM((GROUP, rows), BF16)
-    angles = pl.BlockSpec((HEAD_DIM // 2, rows), lambda g, s: (0, 0))
+    angles = pl.BlockSpec((HEAD_DIM // 2, rows), lambda i, s: (0, 0))
     return call(
         attend_back_kernel,
-        (groups // 2,),
+        (1,),
         [info],
         [
             (mixed, spec(0)), (mixed, spec(1)), (mixed, spec(2)), (att, spec(0)), (grad, spec(0)),
-            (stats, pl.BlockSpec((1, heads, rows), lambda g, s: (g + first, 0, 0))),
+            (stats, pl.BlockSpec((1, heads, rows), lambda i, s: (group, 0, 0))),
             (cos_t, angles), (sin_t, angles),
         ],
         [
             (
-                shape((3, rows, width // 2), BF16),
-                pl.BlockSpec((3, rows, GROUP), lambda g, s: (0, 0, g)),
+                shape((3, rows, 2 * GROUP), BF16),
+                pl.BlockSpec((3, rows, GROUP), lambda i, s: (0, 0, group % 2)),
             ),
         ],
-        deps,
+        earlier + deps,
         "attend_back",
-        22,
+        12,
         scratch=[
             per_head, per_head, per_head, per_head,
             turned, turned, turned,
@@ -492,17 +550,23 @@
             pltpu.VMEM((heads, rows, HEAD_DIM), F32),
             pltpu.VMEM((heads, rows, HEAD_DIM), F32),
         ],
+        aliases={9: 0} if earlier else None,
     )[0]
 
 
-def finish_kernel(place, own_tok, far_tok, middle_back, left_back, right_back, w_qkv, gains,
-                  near_out, far_out, sums):
+def finish_kernel(place, own_tok, far_tok, middle_back, left_back, right_back, w_far, gains,
+                  near_out, far_out, sums, w_qkv, sems):
     half = left_back.shape[2]
+    stream = Stream(
+        sems, [(w_far, w_qkv, slice(at, at + half)) for at in range(0, w_qkv.shape[1], half)]
+    )
     unit, rstd = norm_parts(pick_rows(own_tok, far_tok))
     grad = None
     for part in range(3):
         for side, back in enumerate((left_back, right_back)):
             start = (2 * part + side) * half
+            if start in (0, half, 3 * half):
+                stream.take({0: 1, half: 2, 3 * half: 3}[start])
             term = dot(back[part], w_qkv[:, start : start + half], NT)
             grad = term if grad is None else grad + term
     back = middle_back[...] + norm_back(unit, rstd, gains[0:1, :], grad)
@@ -526,7 +590,7 @@
         [
             (tokens, own_rows(width)), (far_tok, far_rows(width)),
             (middle_back, row_block(width)), (left_back, parts), (right_back, parts),
-            (w_qkv, whole(w_qkv.shape)), (gains, whole(gains.shape)),
+            (w_qkv, ANY), (gains, whole(gains.shape)),
         ],
         [
             (shape((2, rows // 2, width), BF16), own_rows(width)),
@@ -535,13 +599,15 @@
         ],
         deps,
         "finish",
-        15,
-    )
-
-
-def weight_grad_kernel(source_count, place, *refs):
-    out = refs[-1]
-    addends = refs[2 * source_count : -1]
+        8,
+        scratch=[pltpu.VMEM(w_qkv.shape, BF16), pltpu.SemaphoreType.DMA((6,))],
+    )
+
+
+def weight_grad_kernel(source_count, out_count, place, *refs):
+    outs = refs[-out_count:]
+    addends = refs[2 * source_count : -out_count]
+    share = pl.num_programs(0) // out_count
     start = 0
     for number in range(source_count):
         left, right = refs[2 * number], refs[2 * number + 1]
@@ -552,7 +618,15 @@
             total = dot(left[...], piece[...], TN)
             for addend in addends:
                 total = total + addend[:, cols].astype(F32)
-            out[:, cols] = total.astype(BF16)
+            total = total.astype(BF16)
+            if out_count == 1:
+                outs[0][:, cols] = total
+                continue
+            for turn, out in enumerate(outs):
+
+                @pl.when(pl.program_id(0) // share == turn)
+                def _(out=out, cols=cols, total=total):
+                    out[:, cols] = total
 
 
 def swap_wide(rows, bit):
@@ -599,7 +673,7 @@
             self.bits.append(bit)
             bit *= 2
 
-    def blocks(self, steps, core_of, pair_of, addends, deps):
+    def blocks(self, steps, core_of, pair_of, addends, deps, outs=1):
         tokens = self.sources[0][0].shape[0]
 
         def at(place_of):
@@ -618,47 +692,53 @@
             dims = (tokens, width) if right.ndim == 2 else (3, tokens, width)
             inputs.append((right, pl.BlockSpec(dims, at(right_of))))
         block = (self.rows, self.cols // self.halves)
+        share = steps // outs
         for array, row in addends:
             inputs.append((array, pl.BlockSpec(block, lambda i, h, place, row=row: (row(i), h))))
         return call(
-            functools.partial(weight_grad_kernel, len(self.sources)),
+            functools.partial(weight_grad_kernel, len(self.sources), outs),
             (steps, self.halves),
             [self.place],
             inputs,
             [
                 (
-                    shape((steps * self.rows, self.cols), BF16),
-                    pl.BlockSpec(block, lambda i, h, place: (i, h)),
+                    shape((share * self.rows, self.cols), BF16),
+                    pl.BlockSpec(
+                        block, lambda i, h, place, at=turn * share: (jnp.clip(i - at, 0, share - 1), h)
+                    ),
                 )
+                for turn in range(outs)
             ],
             deps,
             "weight_grad",
             0.5 + 0.3 * self.us * steps,
-        )[0]
+        )
 
     def far(self, deps):
         pair_of = lambda i, place: (choose(i // 2, place[4]), choose(i % 2, place[3]))
-        sent = self.blocks(4, lambda place: 1 - place[1], pair_of, [], deps)
-        self.core = swap_wide(sent, 1)
-        return sent
+        sent = self.blocks(4, lambda place: 1 - place[1], pair_of, [], deps, outs=2)
+        self.core = [swap_wide(part, 1) for part in sent]
+        return sent[0]
 
     def first(self, deps):
         pair_of = lambda i, place: (1 - place[3], choose(i, place[4]))
-        sent = self.blocks(2, lambda place: place[1], pair_of, [(self.core, lambda i: i)], deps)
+        sent = self.blocks(
+            2, lambda place: place[1], pair_of, [(self.core[0], lambda i: i)], deps + self.core[1:]
+        )[0]
         self.near = swap_crossed(sent, True)
         return sent
 
     def second(self, deps):
         pair_of = lambda i, place: (place[3], 1 - place[4])
-        addends = [(self.core, lambda i: 2), (self.near, lambda i: 0)]
-        sent = self.blocks(1, lambda place: place[1], pair_of, addends, deps)
+        addends = [(self.core[1], lambda i: 0), (self.near, lambda i: 0)]
+        sent = self.blocks(1, lambda place: place[1], pair_of, addends, deps)[0]
         self.side = swap_crossed(sent, False)
         return sent
 
     def keep(self, deps):
         pair_of = lambda i, place: (place[3], place[4])
-        addends = [(self.core, lambda i: 3), (self.near, lambda i: 1), (self.side, lambda i: 0)]
-        self.total = self.blocks(1, lambda place: place[1], pair_of, addends, deps)
+        addends = [(self.core[1], lambda i: 1), (self.near, lambda i: 1), (self.side, lambda i: 0)]
+        self.total = self.blocks(1, lambda place: place[1], pair_of, addends, deps)[0]
         self.hop = 0
         self.send()
         return self.total
@@ -672,9 +752,11 @@
         if self.hop < len(self.bits):
             self.send()
         else:
-            self.from_y = swap_wide(self.total, 2)
             self.from_core = swap_wide(self.total, 1)
         return self.total
+
+    def open(self, dep):
+        self.from_y = swap_wide(tie(self.total, dep), 2)
 
     def spread(self, dep):
         self.from_y = tie(self.from_y, dep)
@@ -809,20 +891,18 @@
         place, tokens, far_tok, cotangent, far_cot, att, w_out, w_up, w_down,
         norm_gains, norm_biases,
     )
-    got_out = swap_narrow(far_out)
-
     half_wide = width // 2
     down = Reduction(
         place,
         [(active, lambda x, c, b, h: (0, 4 * x + 2 * c + b),
-          back2, lambda x, c, b, h: (0, h), half_wide)],
-        2 * TILE, width, 2, 1.5,
+          back2, lambda x, c, b, h: (0, 0), width)],
+        2 * TILE, width, 1, 1.5,
     )
     up = Reduction(
         place,
         [(normed2, lambda x, c, b, h: (0, x),
-          hidden_back, lambda x, c, b, h: (0, 2 * (2 * c + b) + h), half_wide)],
-        2 * TILE, width, 2, 1.5,
+          hidden_back, lambda x, c, b, h: (0, 2 * c + b), width)],
+        2 * TILE, width, 1, 1.5,
     )
     last = down.far([])
     last = up.far([last])
@@ -830,10 +910,18 @@
     last = up.first([last])
     middle_back, branch_back, att_back, sums12 = return_pass(
         place, tokens, far_tok, cotangent, far_cot, branch, hidden_back, w_out, w_up,
-        norm_gains, norm_biases, [last, got_out],
-    )
+        norm_gains, norm_biases, [last],
+    )
+
+    def back(group, earlier, deps):
+        return attend_back(
+            info, mixed, att, att_back, stats, cos_t, sin_t, group, earlier, deps
+        )
+
     last = down.second([middle_back])
-    left_back = attend_back(info, mixed, att, att_back, stats, cos_t, sin_t, 0, [last])
+    left_back = back(0, [], [last])
+    last = up.second([left_back])
+    left_back = back(1, [left_back], [last])
     by_rows = lambda x, c, b, h: (0, 2 * x + c)
     by_parts = lambda x, c, b, h: (0, 0, b)
     left = Reduction(
@@ -842,26 +930,35 @@
          (att, by_rows, branch_back, lambda x, c, b, h: (0, b), half_wide)],
         TILE, 5 * TILE, 1, 1.2,
     )
-    last = left.far([])
-    last = down.keep([last])
-    last = up.second([last])
-    right_back = attend_back(info, mixed, att, att_back, stats, cos_t, sin_t, 1, [last])
+    last = down.keep([left_back])
+    last = up.keep([last])
+    got_out = swap_narrow(tie(far_out, last))
+    last = left.far([last])
+    right_back = back(2, [], [last])
+    last = down.step(right_back)
+    last = left.first([last])
+    right_back = back(3, [right_back], [last])
     right = Reduction(
         place, [(normed, by_rows, right_back, by_parts, TILE)], TILE, 3 * TILE, 1, 0.8
     )
     last = right.far([])
-    last = left.first([last])
-    last = up.keep([last])
-    a = down.step(last)
+    last = up.step(last)
+    last = left.second([last])
+    last = right.first([last, got_out])
+    extra = len(down.bits) - 2
+    for _ in range(extra):
+        last = down.step(last)
+    last = down.step(last)
     near_grad, far_grad, sums0 = finish(
-        place, tokens, far_tok, middle_back, left_back, right_back, w_qkv, norm_gains, [last, a]
-    )
-    last = right.first([near_grad])
+        place, tokens, far_tok, middle_back, left_back, right_back, w_qkv, norm_gains,
+        [last, down.from_core],
+    )
+    last = right.second([near_grad])
+    last = left.keep([last])
     norm_term = jnp.concatenate(
         [sums0[0:1], sums12[0:1], sums12[2:3], sums3[0:1],
          sums0[1:2], sums12[1:2], sums12[3:4], sums3[1:2]], axis=0
     )
-    norm_got = swap_narrow(tie(norm_term, last))
     hops = [2 ** bit for bit in range(lax.axis_size("wide").bit_length() - 1)]
 
     def norm_step(last):
@@ -871,45 +968,43 @@
             norm_got = swap_wide(norm_term, hops.pop(0))
         return norm_term
 
-    late = left.second([last])
-    out = lax.dynamic_update_slice(near_out, tie(got_out, late)[None], (1 - n, 0, 0))
-    last = down.step(late)
+    last = right.keep([last])
+    down.open(last)
+    for _ in range(extra):
+        last = up.step(last)
     last = up.step(last)
-    last = norm_step(last)
-    last = right.second([last])
-    last = left.keep([last])
-    got_grad = swap_narrow(tie(far_grad, last))
-    last = norm_step(last)
-    last = right.keep([last])
-    extra = len(left.bits) - 2
-    for _ in range(extra):
-        last = down.step(last)
-        last = up.step(last)
-    last = down.spread(last)
-    last = norm_step(last)
-    last = left.step(last)
-    last = up.step(last)
-    last = right.step(last)
-    last = norm_step(last)
+    norm_got = swap_narrow(tie(norm_term, last))
     for _ in range(extra):
         last = left.step(last)
         last = right.step(last)
+    last = left.step(last)
+    up.open(last)
+    last = norm_step(last)
+    last = down.spread(last)
+    last = right.step(last)
+    got_grad = swap_narrow(tie(far_grad, last))
     grad_down = gather(
         place, down.pieces(), (ff // 2, width), half_wide, 0, 2,
         lambda c, b, h: (2 * c + b, h), [last],
     )
-    last = left.step(grad_down)
+    last = norm_step(grad_down)
+    out = lax.dynamic_update_slice(near_out, tie(got_out, last)[None], (1 - n, 0, 0))
+    last = left.step(last)
+    last = up.spread(last)
+    left.open(last)
+    last = norm_step(last)
     last = right.step(last)
-    while hops:
-        last = norm_step(last)
-    last = up.spread(last)
-    last = norm_step(last)
-    grad_tok = lax.dynamic_update_slice(near_grad, tie(got_grad, last)[None], (1 - n, 0, 0))
+    right.open(last)
     grad_up = gather(
         place, up.pieces(), (half_wide, ff), half_wide, 0, 2,
         lambda c, b, h: (0, 2 * (2 * c + b) + h), [last],
     )
-    last = left.spread(grad_up)
+    last = grad_up
+    while hops:
+        last = norm_step(last)
+    last = norm_step(last)
+    grad_tok = lax.dynamic_update_slice(near_grad, tie(got_grad, last)[None], (1 - n, 0, 0))
+    last = left.spread(last)
     last = right.spread(last)
     grad_out_proj = gather(
         place, left.pieces(), (half_wide, width), TILE, 3, 2,

time: 505 us -> 503 us (level)
  waiting for transfers between devices: 88.2 us -> 60.5 us
  starting transfers between devices: 32.4 us -> 59.2 us
    ppermute x8, waiting for transfers between devices: 48.1 us -> 26.8 us  [swap_two(): lax.ppermute(rows, 'wide', [(i, i ^ (even_bit if i % 2 == 0 else odd_bit)...]
    ppermute x20 -> x24, waiting for transfers between devices: 9.39 us -> 29.4 us  [swap_wide(): return lax.ppermute(rows, 'wide', [(i, i ^ bit) for i in range(size)])]
    ppermute x5, waiting for transfers between devices: 19.6 us -> 4.23 us  [swap_narrow(): return lax.ppermute(rows, 'narrow', [(0, 1), (1, 0)])]
    ppermute x8, starting transfers between devices: 10.1 us -> 25.4 us  [swap_crossed(): return lax.ppermute(rows, ('wide', 'narrow'), pairs)]
    ppermute x8, waiting for transfers between devices: 11.1 us -> 0.02 us  [swap_crossed(): return lax.ppermute(rows, ('wide', 'narrow'), pairs)]
    ppermute x5, starting transfers between devices: 3.56 us -> 10.8 us  [swap_narrow(): return lax.ppermute(rows, 'narrow', [(0, 1), (1, 0)])]
    unnamed x59 -> x57, local copies, waits for them, and re-layouts: 10.9 us -> 13.6 us
    ppermute x20 -> x24, starting transfers between devices: 9.03 us -> 11.6 us  [swap_wide(): return lax.ppermute(rows, 'wide', [(i, i ^ bit) for i in range(size)])]
  transfers between devices with their start and end apart: 41 -> 45, of which waited for: 13 -> 8; matrix products, arithmetic and copies ran while one was open for 5% -> 5% of each run, Pallas kernels for 54% -> 54%
where the time goes in v4:
time: 503 us; the launch traced here: 497 us
  Pallas kernels  334 us (66%)
  waiting for transfers between devices  60.5 us (12%)
  starting transfers between devices  59.2 us (12%)
  local copies, waits for them, and re-layouts  24.6 us (5%)
  other arithmetic  17.2 us (3%)
    pallas_call x31, Pallas kernels, call(): pl.pallas_call(body, grid_spec=pltpu.PrefetchScalarGridSpec(num_scalar_pr...  334 us
    ppermute x24, waiting for transfers between devices, swap_wide(): return lax.ppermute(rows, 'wide', [(i, i ^ bit) for i in range(size)])  29.4 us
    ppermute x8, waiting for transfers between devices, swap_two(): lax.ppermute(rows, 'wide', [(i, i ^ (even_bit if i % 2 == 0 else odd_bit)...  26.8 us
    ppermute x8, starting transfers between devices, swap_crossed(): return lax.ppermute(rows, ('wide', 'narrow'), pairs)  25.4 us
    unnamed x57, local copies, waits for them, and re-layouts  13.6 us
    ppermute x24, starting transfers between devices, swap_wide(): return lax.ppermute(rows, 'wide', [(i, i ^ bit) for i in range(size)])  11.6 us
    ppermute x8, starting transfers between devices, swap_two(): lax.ppermute(rows, 'wide', [(i, i ^ (even_bit if i % 2 == 0 else odd_bit)...  11.4 us
    ppermute x5, starting transfers between devices, swap_narrow(): return lax.ppermute(rows, 'narrow', [(0, 1), (1, 0)])  10.8 us
  transfers between devices with their start and end apart: 45, of which 8 were waited for; matrix products, arithmetic and copies ran while one was open for 5% of the time, Pallas kernels for 54%

profile of v4, /device:TPU:0, one launch (start us, length us, event | category | flops | bytes accessed | tf_op | source)
XLA Modules:
  0.0 497.2 jit_solution(13932046898383196386)
XLA Ops:
  11.9 10.3 %project.2 = (bf16[1024,1024]{1,0:T(8,128)(2,1)}, bf16[1024,3072]{1,0:T(8,128)(2,1)}) custom-call(s32[5]{0:T(128)} %stack.36.refs_0_, bf16[2,512,1024]{2,1,0:T(8,128)(2,1)} %refs_1_.7, bf16[1024,3072]{1,0:T(8,128)(2,1)} %refs_6_.3, f32[4,1024]{1,0:T(4,128)} %refs_7_.5, f32[4,1024]{1,0:T(4,128)} %refs_10_.3, f32[1024,128]{1,0:T(8,128)} %get-tuple-element.135.refs_5_, ...), custom_call_target="tpu_custom_call" | custom-call | flops 8000000000 | bytes 1 | tf_op jit(solution)/shard_map/project/pallas_call | solution.py:35
  29.1 10.2 %project.3 = (bf16[1024,1024]{1,0:T(8,128)(2,1)}, bf16[1024,3072]{1,0:T(8,128)(2,1)}) custom-call(s32[5]{0:T(128)} %stack.36.refs_0_, bf16[512,1024]{1,0:T(8,128)(2,1)} %collective-permute-done.refs_1_.refs_2_, bf16[1024,3072]{1,0:T(8,128)(2,1)} %refs_6_.3, f32[4,1024]{1,0:T(4,128)} %refs_7_.5, ...), custom_call_target="tpu_custom_call", output_to_operand_aliasing={{0}: (7, {}), {1}: (8, {})} | custom-call | flops 8000000000 | bytes 1 | tf_op jit(solution)/shard_map/project/pallas_call | solution.py:35
  39.2 24.4 %attend.1 = (bf16[1024,1024]{1,0:T(8,128)(2,1)}, f32[4,4,1024]{2,1,0:T(4,128)}) custom-call(s32[5]{0:T(128)} %concatenate.19.refs_0_, bf16[1024,3072]{1,0:T(8,128)(2,1)} %get-tuple-element.67.refs_1_.refs_2_.refs_3_, bf16[1024,3072]{1,0:T(8,128)(2,1)} %get-tuple-element.67.refs_1_.refs_2_.refs_3_, bf16[1024,3072]{1,0:T(8,128)(2,1)} %get-tuple-element.67.refs_1_.refs_2_.refs_3_), custom_call_target="tpu_custom_call" | custom-call | flops 35999997952 | bytes 1 | tf_op jit(solution)/shard_map/attend/pallas_call | solution.py:35
  63.6 50.8 %feed.1 = (bf16[2,512,1024]{2,1,0:T(8,128)(2,1)}, bf16[512,1024]{1,0:T(8,128)(2,1)}, f32[1024,1024]{1,0:T(8,128)}, bf16[1024,1024]{1,0:T(8,128)(2,1)}, bf16[1024...) custom-call(s32[5]{0:T(128)} %stack.36.refs_0_, ...), custom_call_target="tpu_custom_call" | custom-call | flops 49000001536 | bytes 1 | tf_op jit(solution)/shard_map/feed/pallas_call | solution.py:35
  114.4 9.8 %weight_grad.16 = (bf16[1024,1024]{1,0:T(8,128)(2,1)}, bf16[1024,1024]{1,0:T(8,128)(2,1)}) custom-call(s32[5]{0:T(128)} %stack.36.refs_0_, bf16[1024,4096]{1,0:T(8,128)(2,1)} %get-tuple-element.73.refs_1_, bf16[1024,1024]{1,0:T(8,128)(2,1)} %get-tuple-element.74.refs_2_), custom_call_target="tpu_custom_call" | custom-call | flops 2300000000 | bytes 1 | tf_op jit(solution)/shard_map/weight_grad/pallas_call | solution.py:35
  124.8 19.4 %weight_grad.17 = (bf16[1024,1024]{1,0:T(8,128)(2,1)}, bf16[1024,1024]{1,0:T(8,128)(2,1)}) custom-call(s32[5]{0:T(128)} %stack.36.refs_0_, bf16[1024,1024]{1,0:T(8,128)(2,1)} %get-tuple-element.71.refs_1_, bf16[1024,4096]{1,0:T(8,128)(2,1)} %get-tuple-element.72.refs_2_.refs_6_, bf16[1024,1024]{1,0:T(8,128)(2,1)} %get-tuple-element.75.refs_3_), custom_call_target="tpu_custom_call" | custom-call | flops 2300000000 | bytes 1 | tf_op jit(solution)/shard_map/weight_grad/pallas_call | solution.py:35
  146.0 6.6 %weight_grad.18.refs_4_ = bf16[1024,1024]{1,0:T(8,128)(2,1)} custom-call(s32[5]{0:T(128)} %stack.36.refs_0_, bf16[1024,4096]{1,0:T(8,128)(2,1)} %get-tuple-element.73.refs_1_, bf16[1024,1024]{1,0:T(8,128)(2,1)} %get-tuple-element.74.refs_2_, bf16[1024,1024]{1,0:T(8,128)(2,1)} %collective-permute-done.4.refs_3_, ...), custom_call_target="tpu_custom_call" | custom-call | flops 1400000000 | bytes 1 | tf_op jit(solution)/shard_map/weight_grad/pallas_call | solution.py:35
  152.6 13.7 %collective-permute-start.7 = (bf16[1024,1024]{1,0:T(8,128)(2,1)}, bf16[1024,1024]{1,0:T(8,128)(2,1)}, u32[]{:S(2)}, u32[]{:S(2)}) collective-permute-start(bf16[1024,1024]{1,0:T(8,128)(2,1)} %weight_grad.18.refs_4_), channel_id=1, source_target_pairs={{0,1},{1,0},{2,6},{3,7},{4,5},{5,4},{6,2},{7,3},{8,9},{9,8},{10,14... | collective-permute-start | bytes 6291464 | tf_op jit(solution)/shard_map/ppermute | solution.py:648
  167.7 6.5 %weight_grad.19.refs_11_ = bf16[1024,1024]{1,0:T(8,128)(2,1)} custom-call(s32[5]{0:T(128)} %stack.36.refs_0_, bf16[1024,1024]{1,0:T(8,128)(2,1)} %get-tuple-element.71.refs_1_, bf16[1024,4096]{1,0:T(8,128)(2,1)} %get-tuple-element.72.refs_2_.refs_6_, bf16[1024,1024]{1,0:T(8,128)(2,1)} %collective-permute-done.3.refs_3_, ...), custom_call_target="tpu_custom_call" | custom-call | flops 1400000000 | bytes 1 | tf_op jit(solution)/shard_map/weight_grad/pallas_call | solution.py:35
  174.2 27.6 %return_pass.1 = (f32[1024,1024]{1,0:T(8,128)}, bf16[1024,1024]{1,0:T(8,128)(2,1)}, bf16[1024,1024]{1,0:T(8,128)(2,1)}, f32[8,1024]{1,0:T(8,128)}) custom-call(s32[5]{0:T(128)} %stack.36.refs_0_, bf16[2,512,1024]{2,1,0:T(8,128)(2,1)} %refs_1_.7, bf16[512,1024]{1,0:T(8,128)(2,1)} %collective-permute-done.refs_1_.refs_2_, bf16[2,512,1024]{2,1,0:T(8,128)(2,1)} %refs_3_.7, ...), custom_call_target="tpu_custom_call" | custom-call | flops 24000000000 | bytes 1 | tf_op jit(solution)/shard_map/return_pass/pallas_call | solution.py:35
  201.8 5.5 %weight_grad.20.refs_9_ = bf16[512,1024]{1,0:T(8,128)(2,1)} custom-call(s32[5]{0:T(128)} %stack.36.refs_0_, bf16[1024,4096]{1,0:T(8,128)(2,1)} %get-tuple-element.73.refs_1_, bf16[1024,1024]{1,0:T(8,128)(2,1)} %get-tuple-element.74.refs_2_, bf16[1024,1024]{1,0:T(8,128)(2,1)} %collective-permute-done.5.refs_5_.refs_3_, ...), custom_call_target="tpu_custom_call" | custom-call | flops 950000000 | bytes 1 | tf_op jit(solution)/shard_map/weight_grad/pallas_call | solution.py:35
  209.3 11.1 %attend_back.4.refs_5_.refs_9_ = bf16[3,1024,512]{2,1,0:T(8,128)(2,1)} custom-call(s32[5]{0:T(128)} %concatenate.19.refs_0_, bf16[1024,3072]{1,0:T(8,128)(2,1)} %get-tuple-element.67.refs_1_.refs_2_.refs_3_, bf16[1024,3072]{1,0:T(8,128)(2,1)} %get-tuple-element.67.refs_1_.refs_2_.refs_3_, bf16[1024,3072]{1,0:T(8,128)(2,1)} %get-tuple-element.67.refs_1_.refs_2_.refs_3_, ...), custom_call_target="tpu_custom_call" | custom-call | flops 12000000000 | bytes 1 | tf_op jit(solution)/shard_map/attend_back/pallas_call | solution.py:35
  221.8 5.6 %weight_grad.21.refs_10_ = bf16[512,1024]{1,0:T(8,128)(2,1)} custom-call(s32[5]{0:T(128)} %stack.36.refs_0_, bf16[1024,1024]{1,0:T(8,128)(2,1)} %get-tuple-element.71.refs_1_, bf16[1024,4096]{1,0:T(8,128)(2,1)} %get-tuple-element.72.refs_2_.refs_6_, bf16[1024,1024]{1,0:T(8,128)(2,1)} %copy-done, bf16[1024,1024]{1,0:T(8,128)(2,1)} %copy-done.7, ...), custom_call_target="tpu_custom_call" | custom-call | flops 950000000 | bytes 1 | tf_op jit(solution)/shard_map/weight_grad/pallas_call | solution.py:35
  230.2 11.1 %attend_back.5.refs_6_.refs_2_.refs_4_ = bf16[3,1024,512]{2,1,0:T(8,128)(2,1)} custom-call(s32[5]{0:T(128)} %concatenate.19.refs_0_, bf16[1024,3072]{1,0:T(8,128)(2,1)} %get-tuple-element.67.refs_1_.refs_2_.refs_3_, bf16[1024,3072]{1,0:T(8,128)(2,1)} %get-tuple-element.67.refs_1_.refs_2_.refs_3_, ...), custom_call_target="tpu_custom_call", output_to_operand_aliasing={{}: (9, {})} | custom-call | flops 12000000000 | bytes 1 | tf_op jit(solution)/shard_map/attend_back/pallas_call | solution.py:35
  242.3 5.9 %weight_grad.22.refs_6_ = bf16[512,1024]{1,0:T(8,128)(2,1)} custom-call(s32[5]{0:T(128)} %stack.36.refs_0_, bf16[1024,4096]{1,0:T(8,128)(2,1)} %get-tuple-element.73.refs_1_, bf16[1024,1024]{1,0:T(8,128)(2,1)} %get-tuple-element.74.refs_2_, bf16[1024,1024]{1,0:T(8,128)(2,1)} %collective-permute-done.5.refs_5_.refs_3_, ...), custom_call_target="tpu_custom_call" | custom-call | flops 950000000 | bytes 1 | tf_op jit(solution)/shard_map/weight_grad/pallas_call | solution.py:35
  250.8 5.9 %weight_grad.23.refs_5_ = bf16[512,1024]{1,0:T(8,128)(2,1)} custom-call(s32[5]{0:T(128)} %stack.36.refs_0_, bf16[1024,1024]{1,0:T(8,128)(2,1)} %get-tuple-element.71.refs_1_, bf16[1024,4096]{1,0:T(8,128)(2,1)} %get-tuple-element.72.refs_2_.refs_6_, bf16[1024,1024]{1,0:T(8,128)(2,1)} %copy-done, bf16[1024,1024]{1,0:T(8,128)(2,1)} %copy-done.7, ...), custom_call_target="tpu_custom_call" | custom-call | flops 950000000 | bytes 1 | tf_op jit(solution)/shard_map/weight_grad/pallas_call | solution.py:35
  262.0 11.4 %weight_grad.24 = (bf16[512,1280]{1,0:T(8,128)(2,1)}, bf16[512,1280]{1,0:T(8,128)(2,1)}) custom-call(s32[5]{0:T(128)} %stack.36.refs_0_, bf16[1024,1024]{1,0:T(8,128)(2,1)} %get-tuple-element.84.refs_1_, bf16[3,1024,512]{2,1,0:T(8,128)(2,1)} %attend_back.5.refs_6_.refs_2_.refs_4_, bf16[1024,1024]{1,0:T(8,128)(2,1)} %get-tuple-element.68.refs_5_.refs_4_.refs_3_, ...), custom_call_target="tpu_custom_call" | custom-call | flops 1940000000 | bytes 1 | tf_op jit(solution)/shard_map/weight_grad/pallas_call | solution.py:35
  273.9 11.2 %attend_back.6.refs_9_ = bf16[3,1024,512]{2,1,0:T(8,128)(2,1)} custom-call(s32[5]{0:T(128)} %concatenate.19.refs_0_, bf16[1024,3072]{1,0:T(8,128)(2,1)} %get-tuple-element.67.refs_1_.refs_2_.refs_3_, bf16[1024,3072]{1,0:T(8,128)(2,1)} %get-tuple-element.67.refs_1_.refs_2_.refs_3_, bf16[1024,3072]{1,0:T(8,128)(2,1)} %get-tuple-element.67.refs_1_.refs_2_.refs_3_, ...), custom_call_target="tpu_custom_call" | custom-call | flops 12000000000 | bytes 1 | tf_op jit(solution)/shard_map/attend_back/pallas_call | solution.py:35
  292.0 5.6 %weight_grad.25.refs_10_ = bf16[512,1280]{1,0:T(8,128)(2,1)} custom-call(s32[5]{0:T(128)} %stack.36.refs_0_, bf16[1024,1024]{1,0:T(8,128)(2,1)} %get-tuple-element.84.refs_1_, bf16[3,1024,512]{2,1,0:T(8,128)(2,1)} %attend_back.5.refs_6_.refs_2_.refs_4_, bf16[1024,1024]{1,0:T(8,128)(2,1)} %get-tuple-element.68.refs_5_.refs_4_.refs_3_, ...), custom_call_target="tpu_custom_call" | custom-call | flops 1220000000 | bytes 1 | tf_op jit(solution)/shard_map/weight_grad/pallas_call | solution.py:35
  297.6 10.8 %attend_back.7.refs_2_.refs_5_ = bf16[3,1024,512]{2,1,0:T(8,128)(2,1)} custom-call(s32[5]{0:T(128)} %concatenate.19.refs_0_, bf16[1024,3072]{1,0:T(8,128)(2,1)} %get-tuple-element.67.refs_1_.refs_2_.refs_3_, bf16[1024,3072]{1,0:T(8,128)(2,1)} %get-tuple-element.67.refs_1_.refs_2_.refs_3_, ...), custom_call_target="tpu_custom_call", output_to_operand_aliasing={{}: (9, {})} | custom-call | flops 12000000000 | bytes 1 | tf_op jit(solution)/shard_map/attend_back/pallas_call | solution.py:35
  308.4 9.1 %weight_grad.26 = (bf16[512,768]{1,0:T(8,128)(2,1)}, bf16[512,768]{1,0:T(8,128)(2,1)}) custom-call(s32[5]{0:T(128)} %stack.36.refs_0_, bf16[1024,1024]{1,0:T(8,128)(2,1)} %get-tuple-element.84.refs_1_, bf16[3,1024,512]{2,1,0:T(8,128)(2,1)} %attend_back.7.refs_2_.refs_5_), custom_call_target="tpu_custom_call" | custom-call | flops 1460000000 | bytes 1 | tf_op jit(solution)/shard_map/weight_grad/pallas_call | solution.py:35
  341.4 17.0 %finish.1 = (bf16[2,512,1024]{2,1,0:T(8,128)(2,1)}, bf16[512,1024]{1,0:T(8,128)(2,1)}, f32[8,1024]{1,0:T(8,128)}) custom-call(s32[5]{0:T(128)} %stack.36.refs_0_, bf16[2,512,1024]{2,1,0:T(8,128)(2,1)} %refs_1_.7, bf16[512,1024]{1,0:T(8,128)(2,1)} %collective-permute-done.refs_1_.refs_2_, f32[1024,1024]{1,0:T(8,128)} %get-tuple-element.82.refs_5_.refs_3_, ...), custom_call_target="tpu_custom_call" | custom-call | flops 8000000000 | bytes 1 | tf_op jit(solution)/shard_map/finish/pallas_call | solution.py:35
  383.5 5.6 %collective-permute-done.25 = bf16[256,1280]{1,0:T(8,128)(2,1)S(1)} collective-permute-done((bf16[256,1280]{1,0:T(8,128)(2,1)}, bf16[256,1280]{1,0:T(8,128)(2,1)S(1)}, u32[]{:S(2)}, u32[]{:S(2)}) %collective-permute-start.25) | collective-permute-done | bytes 655392 | tf_op jit(solution)/shard_map/ppermute | solution.py:653
  389.3 12.6 %collective-permute-done.27.refs_2_ = bf16[512,1024]{1,0:T(8,128)(2,1)} collective-permute-done((bf16[512,1024]{1,0:T(8,128)(2,1)S(1)}, bf16[512,1024]{1,0:T(8,128)(2,1)}, u32[]{:S(2)}, u32[]{:S(2)}) %collective-permute-start.27) | collective-permute-done | bytes 1048608 | tf_op jit(solution)/shard_map/ppermute | solution.py:634
  405.1 15.7 %collective-permute-done.29 = bf16[256,768]{1,0:T(8,128)(2,1)S(1)} collective-permute-done((bf16[256,768]{1,0:T(8,128)(2,1)S(1)}, bf16[256,768]{1,0:T(8,128)(2,1)S(1)}, u32[]{:S(2)}, u32[]{:S(2)}) %collective-permute-start.29) | collective-permute-done | bytes 393248 | tf_op jit(solution)/shard_map/ppermute | solution.py:653
  423.3 8.7 %gather.3 = f32[2048,1024]{1,0:T(8,128)} custom-call(s32[5]{0:T(128)} %stack.36.refs_0_, bf16[512,1024]{1,0:T(8,128)(2,1)} %copy-done.15, bf16[512,1024]{1,0:T(8,128)(2,1)} %collective-permute-done.27.refs_2_, bf16[512,1024]{1,0:T(8,128)(2,1)} %copy-done.24, bf16[512,1024]{1,0:T(8,128)(2,1)} %copy-done.25, bf16[256,768]{1,0:T(8,128)(2,1)} %add_convert_fusion.7.refs_5_), custom_call_target="tpu_custom_call" | custom-call | flops 6000000000 | bytes 1 | tf_op jit(solution)/shard_map/gather/pallas_call | solution.py:35
  433.0 12.9 %collective-permute-done.32.refs_2_ = bf16[512,1024]{1,0:T(8,128)(2,1)} collective-permute-done((bf16[512,1024]{1,0:T(8,128)(2,1)}, bf16[512,1024]{1,0:T(8,128)(2,1)}, u32[]{:S(2)}, u32[]{:S(2)}) %collective-permute-start.32) | collective-permute-done | bytes 1048608 | tf_op jit(solution)/shard_map/ppermute | solution.py:634
  451.2 5.5 %collective-permute-done.37 = bf16[256,768]{1,0:T(8,128)(2,1)S(1)} collective-permute-done((bf16[256,768]{1,0:T(8,128)(2,1)S(1)}, bf16[256,768]{1,0:T(8,128)(2,1)S(1)}, u32[]{:S(2)}, u32[]{:S(2)}) %collective-permute-start.37) | collective-permute-done | bytes 393248 | tf_op jit(solution)/shard_map/ppermute | solution.py:653
  458.2 8.7 %gather.4 = f32[512,4096]{1,0:T(8,128)} custom-call(s32[5]{0:T(128)} %stack.36.refs_0_, bf16[512,1024]{1,0:T(8,128)(2,1)} %add_convert_fusion.refs_1_, bf16[512,1024]{1,0:T(8,128)(2,1)} %collective-permute-done.32.refs_2_, bf16[512,1024]{1,0:T(8,128)(2,1)} %collective-permute-done.35.refs_3_, bf16[512,1024]{1,0:T(8,128)(2,1)} %collective-permute-done.36.refs_4_, ...), custom_call_target="tpu_custom_call" | custom-call | flops 6000000000 | bytes 1 | tf_op jit(solution)/shard_map/gather/pallas_call | solution.py:35
  477.2 6.3 %gather.5.refs_5_ = f32[512,1024]{1,0:T(8,128)} custom-call(s32[5]{0:T(128)} %stack.36.refs_0_, bf16[256,1280]{1,0:T(8,128)(2,1)} %add_convert_fusion.4.refs_1_, bf16[256,1280]{1,0:T(8,128)(2,1)} %collective-permute-done.40.refs_2_, bf16[256,1280]{1,0:T(8,128)(2,1)} %collective-permute-done.43.refs_3_, bf16[256,1280]{1,0:T(8,128)(2,1)} %collective-permute-done.44.refs_4_, ...), custom_call_target="tpu_custom_call" | custom-call | flops 6000000000 | bytes 1 | tf_op jit(solution)/shard_map/gather/pallas_call | solution.py:35
  483.5 6.0 %gather_mixed.2.refs_5_ = f32[512,3072]{1,0:T(8,128)} custom-call(s32[5]{0:T(128)} %stack.36.refs_0_, bf16[256,1280]{1,0:T(8,128)(2,1)} %add_convert_fusion.4.refs_1_, bf16[256,1280]{1,0:T(8,128)(2,1)} %collective-permute-done.40.refs_2_, bf16[256,1280]{1,0:T(8,128)(2,1)} %collective-permute-done.43.refs_3_, ...), custom_call_target="tpu_custom_call" | custom-call | flops 4000000000 | bytes 1 | tf_op jit(solution)/shard_map/gather_mixed/pallas_call | solution.py:35
  491.0 6.0 %gather_mixed.3 = f32[512,3072]{1,0:T(8,128)} custom-call(s32[5]{0:T(128)} %stack.36.refs_0_, bf16[256,768]{1,0:T(8,128)(2,1)} %copy-done.22, bf16[256,768]{1,0:T(8,128)(2,1)} %collective-permute-done.39.refs_5_.refs_2_, bf16[256,768]{1,0:T(8,128)(2,1)} %copy-done.26, bf16[256,768]{1,0:T(8,128)(2,1)} %copy-done.27, ...), custom_call_target="tpu_custom_call", output_to_operand_aliasing={{}: (5, {})} | custom-call | flops 4000000000 | bytes 1 | tf_op jit(solution)/shard_map/gather_mixed/pallas_call | solution.py:35
  (177 shorter events, 117.7 us)
Async XLA Ops:
  1.9 27.1 %collective-permute-start = (bf16[512,1024]{1,0:T(8,128)(2,1)S(1)}, bf16[512,1024]{1,0:T(8,128)(2,1)}, u32[]{:S(2)}, u32[]{:S(2)}) collective-permute-start(bf16[512,1024]{1,0:T(8,128)(2,1)S(1)} %dynamic-slice_bitcast_fusion.1), channel_id=1, source_target_pairs={{0,1},{1,0},{2,3},{3,2},{4,5},{5,4},{6,7},{7,6},{8,9},{9,8},{10,11... | collective-permute-start | bytes 3145736 | tf_op jit(solution)/shard_map/ppermute | solution.py:638
  22.2 41.5 %collective-permute-start.1 = (bf16[512,1024]{1,0:T(8,128)(2,1)S(1)}, bf16[512,1024]{1,0:T(8,128)(2,1)}, u32[]{:S(2)}, u32[]{:S(2)}) collective-permute-start(bf16[512,1024]{1,0:T(8,128)(2,1)S(1)} %copy-done.19), channel_id=1, source_target_pairs={{0,1},{1,0},{2,3},{3,2},{4,5},{5,4},{6,7},{7,6},{8,9},{9,8},{10,11... | collective-permute-start | bytes 3145736 | tf_op jit(solution)/shard_map/ppermute | solution.py:638
  124.3 21.7 %collective-permute-start.5 = (bf16[1024,1024]{1,0:T(8,128)(2,1)}, bf16[1024,1024]{1,0:T(8,128)(2,1)}, u32[]{:S(2)}, u32[]{:S(2)}) collective-permute-start(bf16[1024,1024]{1,0:T(8,128)(2,1)} %get-tuple-element.78), channel_id=1, source_target_pairs={{0,2},{2,0},{4,6},{6,4},{8,10},{10,8},{12,14},{14,12},{16,18},{18,... | collective-permute-start | bytes 6291464 | tf_op jit(solution)/shard_map/ppermute | solution.py:634
  124.3 21.7 %collective-permute-start.4 = (bf16[1024,1024]{1,0:T(8,128)(2,1)}, bf16[1024,1024]{1,0:T(8,128)(2,1)}, u32[]{:S(2)}, u32[]{:S(2)}) collective-permute-start(bf16[1024,1024]{1,0:T(8,128)(2,1)} %get-tuple-element.75.refs_3_), channel_id=1, source_target_pairs={{0,2},{2,0},{4,6},{6,4},{8,10},{10,8},{12,14},{14,12},{16,18},{18,... | collective-permute-start | bytes 6291464 | tf_op jit(solution)/shard_map/ppermute | solution.py:634
  144.2 22.1 %collective-permute-start.2 = (bf16[1024,1024]{1,0:T(8,128)(2,1)}, bf16[1024,1024]{1,0:T(8,128)(2,1)S(1)}, u32[]{:S(2)}, u32[]{:S(2)}) collective-permute-start(bf16[1024,1024]{1,0:T(8,128)(2,1)} %get-tuple-element.76), channel_id=1, source_target_pairs={{0,2},{2,0},{4,6},{6,4},{8,10},{10,8},{12,14},{14,12},{16,18},{18,... | collective-permute-start | bytes 6291464 | tf_op jit(solution)/shard_map/ppermute | solution.py:634
  144.3 22.1 %collective-permute-start.3 = (bf16[1024,1024]{1,0:T(8,128)(2,1)}, bf16[1024,1024]{1,0:T(8,128)(2,1)}, u32[]{:S(2)}, u32[]{:S(2)}) collective-permute-start(bf16[1024,1024]{1,0:T(8,128)(2,1)} %get-tuple-element.77.refs_4_), channel_id=1, source_target_pairs={{0,2},{2,0},{4,6},{6,4},{8,10},{10,8},{12,14},{14,12},{16,18},{18,... | collective-permute-start | bytes 6291464 | tf_op jit(solution)/shard_map/ppermute | solution.py:634
  152.6 49.1 %collective-permute-start.7 = (bf16[1024,1024]{1,0:T(8,128)(2,1)}, bf16[1024,1024]{1,0:T(8,128)(2,1)}, u32[]{:S(2)}, u32[]{:S(2)}) collective-permute-start(bf16[1024,1024]{1,0:T(8,128)(2,1)} %weight_grad.18.refs_4_), channel_id=1, source_target_pairs={{0,1},{1,0},{2,6},{3,7},{4,5},{5,4},{6,2},{7,3},{8,9},{9,8},{10,14... | collective-permute-start | bytes 6291464 | tf_op jit(solution)/shard_map/ppermute | solution.py:648
  174.2 46.2 %collective-permute-start.6 = (bf16[1024,1024]{1,0:T(8,128)(2,1)}, bf16[1024,1024]{1,0:T(8,128)(2,1)S(1)}, u32[]{:S(2)}, u32[]{:S(2)}) collective-permute-start(bf16[1024,1024]{1,0:T(8,128)(2,1)} %weight_grad.19.refs_11_), channel_id=1, source_target_pairs={{0,1},{1,0},{2,6},{3,7},{4,5},{5,4},{6,2},{7,3},{8,9},{9,8},{10,14... | collective-permute-start | bytes 6291464 | tf_op jit(solution)/shard_map/ppermute | solution.py:648
  207.3 34.1 %collective-permute-start.9 = (bf16[512,1024]{1,0:T(8,128)(2,1)}, bf16[512,1024]{1,0:T(8,128)(2,1)S(1)}, u32[]{:S(2)}, u32[]{:S(2)}) collective-permute-start(bf16[512,1024]{1,0:T(8,128)(2,1)} %weight_grad.20.refs_9_), channel_id=1, source_target_pairs={{0,4},{1,5},{2,3},{3,2},{4,0},{5,1},{6,7},{7,6},{8,12},{9,13},{10,... | collective-permute-start | bytes 3145736 | tf_op jit(solution)/shard_map/ppermute | solution.py:648
  227.4 22.4 %collective-permute-start.8 = (bf16[512,1024]{1,0:T(8,128)(2,1)}, bf16[512,1024]{1,0:T(8,128)(2,1)S(1)}, u32[]{:S(2)}, u32[]{:S(2)}) collective-permute-start(bf16[512,1024]{1,0:T(8,128)(2,1)} %weight_grad.21.refs_10_), channel_id=1, source_target_pairs={{0,4},{1,5},{2,3},{3,2},{4,0},{5,1},{6,7},{7,6},{8,12},{9,13},{10,... | collective-permute-start | bytes 3145736 | tf_op jit(solution)/shard_map/ppermute | solution.py:648
  248.3 36.9 %collective-permute-start.12 = (bf16[512,1024]{1,0:T(8,128)(2,1)}, bf16[512,1024]{1,0:T(8,128)(2,1)}, u32[]{:S(2)}, u32[]{:S(2)}) collective-permute-start(bf16[512,1024]{1,0:T(8,128)(2,1)} %weight_grad.22.refs_6_), channel_id=1, source_target_pairs={{0,8},{2,18},{4,12},{6,22},{8,0},{10,26},{12,4},{14,30},{16,24},{1... | collective-permute-start | bytes 3145736 | tf_op jit(solution)/shard_map/ppermute | solution.py:653
  256.7 60.7 %collective-permute-start.17 = (bf16[512,1024]{1,0:T(8,128)(2,1)}, bf16[512,1024]{1,0:T(8,128)(2,1)}, u32[]{:S(2)}, u32[]{:S(2)}) collective-permute-start(bf16[512,1024]{1,0:T(8,128)(2,1)} %weight_grad.23.refs_5_), channel_id=1, source_target_pairs={{0,8},{2,18},{4,12},{6,22},{8,0},{10,26},{12,4},{14,30},{16,24},{1... | collective-permute-start | bytes 3145736 | tf_op jit(solution)/shard_map/ppermute | solution.py:653
  257.2 69.3 %collective-permute-start.10 = (bf16[512,1024]{1,0:T(8,128)(2,1)}, bf16[512,1024]{1,0:T(8,128)(2,1)}, u32[]{:S(2)}, u32[]{:S(2)}) collective-permute-start(bf16[512,1024]{1,0:T(8,128)(2,1)} %get-tuple-element.83), channel_id=1, source_target_pairs={{0,1},{1,0},{2,3},{3,2},{4,5},{5,4},{6,7},{7,6},{8,9},{9,8},{10,11... | collective-permute-start | bytes 3145736 | tf_op jit(solution)/shard_map/ppermute | solution.py:638
  273.4 17.4 %collective-permute-start.13 = (bf16[512,1280]{1,0:T(8,128)(2,1)}, bf16[512,1280]{1,0:T(8,128)(2,1)S(1)}, u32[]{:S(2)}, u32[]{:S(2)}) collective-permute-start(bf16[512,1280]{1,0:T(8,128)(2,1)} %get-tuple-element.88), channel_id=1, source_target_pairs={{0,2},{2,0},{4,6},{6,4},{8,10},{10,8},{12,14},{14,12},{16,18},{18,... | collective-permute-start | bytes 3932168 | tf_op jit(solution)/shard_map/ppermute | solution.py:634
  273.4 17.4 %collective-permute-start.11 = (bf16[512,1280]{1,0:T(8,128)(2,1)}, bf16[512,1280]{1,0:T(8,128)(2,1)}, u32[]{:S(2)}, u32[]{:S(2)}) collective-permute-start(bf16[512,1280]{1,0:T(8,128)(2,1)} %get-tuple-element.86.refs_9_), channel_id=1, source_target_pairs={{0,2},{2,0},{4,6},{6,4},{8,10},{10,8},{12,14},{14,12},{16,18},{18,... | collective-permute-start | bytes 3932168 | tf_op jit(solution)/shard_map/ppermute | solution.py:634
  286.8 44.2 %collective-permute-start.14 = (bf16[512,1024]{1,0:T(8,128)(2,1)S(1)}, bf16[512,1024]{1,0:T(8,128)(2,1)}, u32[]{:S(2)}, u32[]{:S(2)}) collective-permute-start(bf16[512,1024]{1,0:T(8,128)(2,1)S(1)} %add_convert_fusion.3.refs_6_), channel_id=1, source_target_pairs={{0,16},{2,10},{4,20},{6,14},{8,24},{10,2},{12,28},{14,6},{16,0},{1... | collective-permute-start | bytes 3145736 | tf_op jit(solution)/shard_map/ppermute | solution.py:653
  297.6 23.0 %collective-permute-start.16 = (bf16[512,1280]{1,0:T(8,128)(2,1)}, bf16[512,1280]{1,0:T(8,128)(2,1)S(1)}, u32[]{:S(2)}, u32[]{:S(2)}) collective-permute-start(bf16[512,1280]{1,0:T(8,128)(2,1)} %weight_grad.25.refs_10_), channel_id=1, source_target_pairs={{0,1},{1,0},{2,6},{3,7},{4,5},{5,4},{6,2},{7,3},{8,9},{9,8},{10,14... | collective-permute-start | bytes 3932168 | tf_op jit(solution)/shard_map/ppermute | solution.py:648
  333.7 24.8 %collective-permute-start.21 = (bf16[512,768]{1,0:T(8,128)(2,1)}, bf16[512,768]{1,0:T(8,128)(2,1)S(1)}, u32[]{:S(2)}, u32[]{:S(2)}) collective-permute-start(bf16[512,768]{1,0:T(8,128)(2,1)} %weight_grad.28), channel_id=1, source_target_pairs={{0,1},{1,0},{2,6},{3,7},{4,5},{5,4},{6,2},{7,3},{8,9},{9,8},{10,14... | collective-permute-start | bytes 2359304 | tf_op jit(solution)/shard_map/ppermute | solution.py:648
  338.5 42.3 %collective-permute-start.20 = (bf16[512,1024]{1,0:T(8,128)(2,1)S(1)}, bf16[512,1024]{1,0:T(8,128)(2,1)}, u32[]{:S(2)}, u32[]{:S(2)}) collective-permute-start(bf16[512,1024]{1,0:T(8,128)(2,1)S(1)} %copy-done.5), channel_id=1, source_target_pairs={{0,16},{2,10},{4,20},{6,14},{8,24},{10,2},{12,28},{14,6},{16,0},{1... | collective-permute-start | bytes 3145736 | tf_op jit(solution)/shard_map/ppermute | solution.py:653
  339.8 25.6 %collective-permute-start.23 = (bf16[256,1280]{1,0:T(8,128)(2,1)}, bf16[256,1280]{1,0:T(8,128)(2,1)S(1)}, u32[]{:S(2)}, u32[]{:S(2)}) collective-permute-start(bf16[256,1280]{1,0:T(8,128)(2,1)} %weight_grad.27.refs_4_), channel_id=1, source_target_pairs={{0,4},{1,5},{2,3},{3,2},{4,0},{5,1},{6,7},{7,6},{8,12},{9,13},{10,... | collective-permute-start | bytes 1966088 | tf_op jit(solution)/shard_map/ppermute | solution.py:648
  371.4 17.7 %collective-permute-start.25 = (bf16[256,1280]{1,0:T(8,128)(2,1)}, bf16[256,1280]{1,0:T(8,128)(2,1)S(1)}, u32[]{:S(2)}, u32[]{:S(2)}) collective-permute-start(bf16[256,1280]{1,0:T(8,128)(2,1)} %weight_grad.30.refs_6_), channel_id=1, source_target_pairs={{0,8},{2,18},{4,12},{6,22},{8,0},{10,26},{12,4},{14,30},{16,24},{1... | collective-permute-start | bytes 1966088 | tf_op jit(solution)/shard_map/ppermute | solution.py:653
  377.9 24.0 %collective-permute-start.27 = (bf16[512,1024]{1,0:T(8,128)(2,1)S(1)}, bf16[512,1024]{1,0:T(8,128)(2,1)}, u32[]{:S(2)}, u32[]{:S(2)}) collective-permute-start(bf16[512,1024]{1,0:T(8,128)(2,1)S(1)} %copy-done.16), channel_id=1, source_target_pairs={{0,4},{2,6},{4,0},{6,2},{8,12},{10,14},{12,8},{14,10},{16,20},{18,... | collective-permute-start | bytes 3145736 | tf_op jit(solution)/shard_map/ppermute | solution.py:634
  401.9 20.5 %collective-permute-start.28 = (bf16[512,1024]{1,0:T(8,128)(2,1)}, bf16[512,1024]{1,0:T(8,128)(2,1)S(1)}, u32[]{:S(2)}, u32[]{:S(2)}) collective-permute-start(bf16[512,1024]{1,0:T(8,128)(2,1)} %collective-permute-done.27.refs_2_), channel_id=1, source_target_pairs={{0,2},{2,0},{4,6},{6,4},{8,10},{10,8},{12,14},{14,12},{16,18},{18,... | collective-permute-start | bytes 3145736 | tf_op jit(solution)/shard_map/ppermute | solution.py:634
  401.9 18.8 %collective-permute-start.29 = (bf16[256,768]{1,0:T(8,128)(2,1)S(1)}, bf16[256,768]{1,0:T(8,128)(2,1)S(1)}, u32[]{:S(2)}, u32[]{:S(2)}) collective-permute-start(bf16[256,768]{1,0:T(8,128)(2,1)S(1)} %copy-done.13), channel_id=1, source_target_pairs={{0,8},{2,18},{4,12},{6,22},{8,0},{10,26},{12,4},{14,30},{16,24},{1... | collective-permute-start | bytes 1179656 | tf_op jit(solution)/shard_map/ppermute | solution.py:653
  402.6 54.2 %collective-permute-start.35 = (bf16[512,1024]{1,0:T(8,128)(2,1)}, bf16[512,1024]{1,0:T(8,128)(2,1)}, u32[]{:S(2)}, u32[]{:S(2)}) collective-permute-start(bf16[512,1024]{1,0:T(8,128)(2,1)} %add_convert_fusion.refs_1_), channel_id=1, source_target_pairs={{0,2},{2,0},{4,6},{6,4},{8,10},{10,8},{12,14},{14,12},{16,18},{18,... | collective-permute-start | bytes 3145736 | tf_op jit(solution)/shard_map/ppermute | solution.py:634
  403.4 28.6 %collective-permute-start.26 = (f32[8,1024]{1,0:T(8,128)S(1)}, f32[8,1024]{1,0:T(8,128)S(1)}, u32[]{:S(2)}, u32[]{:S(2)}) collective-permute-start(f32[8,1024]{1,0:T(8,128)S(1)} %add.94), channel_id=1, source_target_pairs={{0,2},{2,0},{4,6},{6,4},{8,10},{10,8},{12,14},{14,12},{16,18},{18,... | collective-permute-start | bytes 98312 | tf_op jit(solution)/shard_map/ppermute | solution.py:634
  403.4 28.6 %collective-permute-start.33 = (bf16[256,1280]{1,0:T(8,128)(2,1)S(1)}, bf16[256,1280]{1,0:T(8,128)(2,1)S(1)}, u32[]{:S(2)}, u32[]{:S(2)}) collective-permute-start(bf16[256,1280]{1,0:T(8,128)(2,1)S(1)} %add_convert_fusion.5), channel_id=1, source_target_pairs={{0,16},{2,10},{4,20},{6,14},{8,24},{10,2},{12,28},{14,6},{16,0},{1... | collective-permute-start | bytes 1966088 | tf_op jit(solution)/shard_map/ppermute | solution.py:653
  420.7 25.2 %collective-permute-start.32 = (bf16[512,1024]{1,0:T(8,128)(2,1)}, bf16[512,1024]{1,0:T(8,128)(2,1)}, u32[]{:S(2)}, u32[]{:S(2)}) collective-permute-start(bf16[512,1024]{1,0:T(8,128)(2,1)} %add_convert_fusion.refs_1_), channel_id=1, source_target_pairs={{0,4},{2,6},{4,0},{6,2},{8,12},{10,14},{12,8},{14,10},{16,20},{18,... | collective-permute-start | bytes 3145736 | tf_op jit(solution)/shard_map/ppermute | solution.py:634
  446.3 29.9 %collective-permute-start.30 = (bf16[512,1024]{1,0:T(8,128)(2,1)}, bf16[512,1024]{1,0:T(8,128)(2,1)S(1)}, u32[]{:S(2)}, u32[]{:S(2)}) collective-permute-start(bf16[512,1024]{1,0:T(8,128)(2,1)} %get-tuple-element.107), channel_id=1, source_target_pairs={{0,1},{1,0},{2,3},{3,2},{4,5},{5,4},{6,7},{7,6},{8,9},{9,8},{10,11... | collective-permute-start | bytes 3145736 | tf_op jit(solution)/shard_map/ppermute | solution.py:638
  450.0 23.5 %collective-permute-start.40 = (bf16[256,1280]{1,0:T(8,128)(2,1)}, bf16[256,1280]{1,0:T(8,128)(2,1)}, u32[]{:S(2)}, u32[]{:S(2)}) collective-permute-start(bf16[256,1280]{1,0:T(8,128)(2,1)} %add_convert_fusion.4.refs_1_), channel_id=1, source_target_pairs={{0,4},{2,6},{4,0},{6,2},{8,12},{10,14},{12,8},{14,10},{16,20},{18,... | collective-permute-start | bytes 1966088 | tf_op jit(solution)/shard_map/ppermute | solution.py:634
  456.8 19.5 %collective-permute-start.39 = (bf16[256,768]{1,0:T(8,128)(2,1)S(1)}, bf16[256,768]{1,0:T(8,128)(2,1)}, u32[]{:S(2)}, u32[]{:S(2)}) collective-permute-start(bf16[256,768]{1,0:T(8,128)(2,1)S(1)} %add_convert_fusion.6.refs_5_.refs_1_), channel_id=1, source_target_pairs={{0,4},{2,6},{4,0},{6,2},{8,12},{10,14},{12,8},{14,10},{16,20},{18,... | collective-permute-start | bytes 1179656 | tf_op jit(solution)/shard_map/ppermute | solution.py:634
  475.8 13.7 %collective-permute-start.41 = (bf16[256,768]{1,0:T(8,128)(2,1)}, bf16[256,768]{1,0:T(8,128)(2,1)S(1)}, u32[]{:S(2)}, u32[]{:S(2)}) collective-permute-start(bf16[256,768]{1,0:T(8,128)(2,1)} %copy-done.22), channel_id=1, source_target_pairs={{0,2},{2,0},{4,6},{6,4},{8,10},{10,8},{12,14},{14,12},{16,18},{18,... | collective-permute-start | bytes 1179656 | tf_op jit(solution)/shard_map/ppermute | solution.py:634
  (41 other events, 256.4 us)

commit v5 on v4

--- a/solution.py
+++ b/solution.py
@@ -14,7 +14,6 @@
 BF16 = jnp.bfloat16
 TILE = 256
 GROUP = 256
-VMEM_LIMIT = 60 * 1024 * 1024
 FLOPS_PER_US = 1000000000
 NN = (((1,), (0,)), ((), ()))
 NT = (((1,), (1,)), ((), ()))
@@ -25,7 +24,7 @@
     return lax.dot_general(left, right, dims, preferred_element_type=F32)
 
 
-def call(kernel, grid, prefetch, inputs, outputs, deps, name, us, scratch=(), aliases=None):
+def call(kernel, grid, prefetch, inputs, outputs, deps, name, vmem, us, scratch=(), aliases=None):
     given = len(prefetch) + len(inputs)
 
     def body(*refs):
@@ -43,7 +42,7 @@
         ),
         out_shape=tuple(shape for shape, _ in outputs),
         input_output_aliases=aliases or {},
-        compiler_params=pltpu.CompilerParams(vmem_limit_bytes=VMEM_LIMIT),
+        compiler_params=pltpu.CompilerParams(vmem_limit_bytes=vmem * 1024 * 1024),
         cost_estimate=pl.CostEstimate(
             flops=int(us * FLOPS_PER_US), transcendentals=0, bytes_accessed=1
         ),
@@ -55,6 +54,10 @@
     return jax.ShapeDtypeStruct(dims, dtype)
 
 
+def far_away(array):
+    return pltpu.with_memory_space_constraint(array, pltpu.HBM)
+
+
 def whole(dims):
     return pl.BlockSpec(dims, lambda *_: (0,) * len(dims), pipeline_mode=pl.Buffered(1))
 
@@ -83,32 +86,6 @@
     @pl.when(pl.program_id(0) >= 2)
     def _():
         far[...] = rows
-
-
-class Stream:
-    def __init__(self, sems, parts):
-        self.copies = [
-            pltpu.make_async_copy(source.at[:, cols], target.at[:, cols], sems.at[number])
-            for number, (source, target, cols) in enumerate(parts)
-        ]
-        self.taken = 0
-
-        @pl.when(pl.program_id(0) == 0)
-        def _():
-            for copy in self.copies:
-                copy.start()
-
-    def take(self, count):
-        parts = self.copies[self.taken : self.taken + count]
-        self.taken += count
-
-        @pl.when(pl.program_id(0) == 0)
-        def _():
-            for copy in parts:
-                copy.wait()
-
-
-ANY = pl.BlockSpec(memory_space=pl.ANY)
 
 
 def tie(array, *deps):
@@ -132,8 +109,7 @@
     return jnp.sum(rows, axis=0, keepdims=True)
 
 
-def project_kernel(place, tok, w_far, gains, biases, cosine, sine, normed_out, mixed_out, w, sems):
-    stream = Stream(sems, [(w_far, w, slice(at, at + 512)) for at in range(0, w.shape[1], 512)])
+def project_kernel(place, tok, w, gains, biases, cosine, sine, normed_out, mixed_out):
     rows = tok[0] if len(tok.shape) == 3 else tok[...]
     unit, _ = norm_parts(rows.astype(F32))
     normed = (unit * gains[0:1, :] + biases[0:1, :]).astype(BF16)
@@ -145,8 +121,6 @@
     cos = cosine[...]
     sin = sine[...]
     for start in range(0, 3 * width, 256):
-        if start in (0, 512, 1536):
-            stream.take({0: 1, 512: 2, 1536: 3}[start])
         part = dot(normed, w[:, start : start + 256])
         if start >= 2 * width:
             mixed_out[:, start : start + 256] = part.astype(BF16)
@@ -172,20 +146,20 @@
         [place],
         [
             (tok, own_rows(width) if own else row_block(width)),
-            (w_qkv, ANY),
+            (far_away(w_qkv), whole(w_qkv.shape)),
             (gains, whole(gains.shape)),
             (biases, whole(biases.shape)),
             (cosine, at(128)),
             (sine, at(128)),
         ],
         [
-            (shape((pack_len, width), BF16), at(width)),
-            (shape((pack_len, wide), BF16), at(wide)),
-        ],
-        list(earlier),
+            (pltpu.HBM((pack_len, width), BF16), at(width)),
+            (pltpu.HBM((pack_len, wide), BF16), at(wide)),
+        ],
+        [far_away(array) for array in earlier],
         "project",
+        24,
         8,
-        scratch=[pltpu.VMEM(w_qkv.shape, BF16), pltpu.SemaphoreType.DMA((6,))],
         aliases={7: 0, 8: 1} if earlier else None,
     )
 
@@ -254,9 +228,9 @@
         attend_kernel,
         (groups,),
         [info],
-        [(mixed, part(0)), (mixed, part(1)), (mixed, part(2))],
-        [
-            (shape((rows, width), BF16), part(0)),
+        [(far_away(mixed), part(0)), (far_away(mixed), part(1)), (far_away(mixed), part(2))],
+        [
+            (pltpu.HBM((rows, width), BF16), part(0)),
             (
                 shape((groups, heads, rows), F32),
                 pl.BlockSpec((1, heads, rows), lambda g, s: (g, 0, 0)),
@@ -264,6 +238,7 @@
         ],
         [],
         "attend",
+        24,
         36,
         scratch=[
             pltpu.VMEM((heads, rows, HEAD_DIM), BF16),
@@ -274,17 +249,10 @@
     )
 
 
-def feed_kernel(place, own_tok, far_tok, own_cot, far_cot, att, out_far, up_far, down_far,
-                gains, biases, near_out, far_out, branch_out, normed2_out, active_out, back2_out, hidden_back_out, sums,
-                slope, w_out, w_up, w_down, sems):
+def feed_kernel(place, own_tok, far_tok, own_cot, far_cot, att, w_out, w_up, w_down, gains, biases,
+                near_out, far_out, branch_out, normed2_out, active_out, back2_out, hidden_back_out, sums,
+                slope):
     chunk = 1024
-    parts = [(out_far, w_out, slice(0, w_out.shape[1]))]
-    for start in range(0, w_up.shape[1], chunk):
-        parts.append((up_far, w_up, slice(start, start + chunk)))
-        parts.append((down_far.at[start : start + chunk], w_down.at[start : start + chunk],
-                      slice(0, w_down.shape[1])))
-    stream = Stream(sems, parts)
-    stream.take(1)
     residual = pick_rows(own_tok, far_tok)
     branch = dot(att[...], w_out[...])
     branch_out[...] = branch
@@ -298,8 +266,6 @@
     branch2 = jnp.zeros_like(branch)
     for start in range(0, ff, chunk):
         cols = slice(start, start + chunk)
-        if start <= 2 * chunk:
-            stream.take(2 if start < 2 * chunk else 4)
         z = dot(normed2, w_up[:, cols])
         square = z * z
         bend = jnp.tanh(z * (root + (root * 0.044715) * square))
@@ -335,52 +301,36 @@
         (rows // TILE,),
         [place],
         [
-            (tokens, own_rows(width)), (far_tok, far_rows(width)),
-            (cotangent, own_rows(width)), (far_cot, far_rows(width)),
-            (att, row_block(width)), (w_out, ANY), (w_up, ANY), (w_down, ANY),
+            (far_away(tokens), own_rows(width)), (far_tok, far_rows(width)),
+            (far_away(cotangent), own_rows(width)), (far_cot, far_rows(width)),
+            (far_away(att), row_block(width)),
+            (w_out, whole(w_out.shape)), (w_up, whole(w_up.shape)), (w_down, whole(w_down.shape)),
             (gains, whole(gains.shape)), (biases, whole(biases.shape)),
         ],
         [
-            (shape((2, rows // 2, width), BF16), own_rows(width)),
+            (pltpu.HBM((2, rows // 2, width), BF16), own_rows(width)),
             (shape((rows // 2, width), BF16), far_rows(width)),
-            (shape((rows, width), F32), row_block(width)),
+            (pltpu.HBM((rows, width), F32), row_block(width)),
             (shape((rows, width), BF16), row_block(width)),
-            (shape((rows, ff), BF16), row_block(ff)),
+            (pltpu.HBM((rows, ff), BF16), row_block(ff)),
             (shape((rows, width), BF16), row_block(width)),
-            (shape((rows, ff), BF16), row_block(ff)),
+            (pltpu.HBM((rows, ff), BF16), row_block(ff)),
             (shape((8, width), F32), whole((8, width))),
         ],
         [],
         "feed",
+        52,
         49,
-        scratch=[
-            pltpu.VMEM((TILE, ff), F32),
-            pltpu.VMEM(w_out.shape, BF16), pltpu.VMEM(w_up.shape, BF16), pltpu.VMEM(w_down.shape, BF16),
-            pltpu.SemaphoreType.DMA((9,)),
-        ],
-    )
-
-
-def return_kernel(place, own_tok, far_tok, own_cot, far_cot, branch, hidden_back, out_far, up_far,
-                  gains, biases, middle_back_out, branch_back_out, att_back_out, sums,
-                  w_out, w_up, sems):
-    chunk = 1024
-    starts = range(0, w_up.shape[1], chunk)
-    stream = Stream(
-        sems,
-        [(up_far, w_up, slice(start, start + chunk)) for start in starts]
-        + [(out_far, w_out, slice(0, w_out.shape[1]))],
-    )
+        scratch=[pltpu.VMEM((TILE, ff), F32)],
+    )
+
+
+def return_kernel(place, own_tok, far_tok, own_cot, far_cot, branch, hidden_back, w_out, w_up, gains, biases,
+                  middle_back_out, branch_back_out, att_back_out, sums):
     unit1, rstd1 = norm_parts(branch[...])
     middle = pick_rows(own_tok, far_tok) + unit1 * gains[1:2, :] + biases[1:2, :]
     unit2, rstd2 = norm_parts(middle)
-    grad2 = None
-    for start in starts:
-        if start <= 2 * chunk:
-            stream.take(1 if start < 2 * chunk else 3)
-        cols = slice(start, start + chunk)
-        term = dot(hidden_back[:, cols], w_up[:, cols], NT)
-        grad2 = term if grad2 is None else grad2 + term
+    grad2 = dot(hidden_back[...], w_up[...], NT)
     middle_back = pick_rows(own_cot, far_cot) + norm_back(unit2, rstd2, gains[2:3, :], grad2)
     middle_back_out[...] = middle_back
     branch_back = norm_back(unit1, rstd1, gains[1:2, :], middle_back).astype(BF16)
@@ -406,24 +356,22 @@
         (rows // TILE,),
         [place],
         [
-            (tokens, own_rows(width)), (far_tok, far_rows(width)),
-            (cotangent, own_rows(width)), (far_cot, far_rows(width)),
-            (branch, row_block(width)), (hidden_back, row_block(ff)),
-            (w_out, ANY), (w_up, ANY),
+            (far_away(tokens), own_rows(width)), (far_tok, far_rows(width)),
+            (far_away(cotangent), own_rows(width)), (far_cot, far_rows(width)),
+            (far_away(branch), row_block(width)), (far_away(hidden_back), row_block(ff)),
+            (far_away(w_out), whole(w_out.shape)), (far_away(w_up), whole(w_up.shape)),
             (gains, whole(gains.shape)), (biases, whole(biases.shape)),
         ],
         [
-            (shape((rows, width), F32), row_block(width)),
+            (pltpu.HBM((rows, width), F32), row_block(width)),
             (shape((rows, width), BF16), row_block(width)),
             (shape((rows, width), BF16), row_block(width)),
             (shape((8, width), F32), whole((8, width))),
         ],
         deps,
         "return_pass",
+        32,
         24,
-        scratch=[
-            pltpu.VMEM(w_out.shape, BF16), pltpu.VMEM(w_up.shape, BF16), pltpu.SemaphoreType.DMA((5,)),
-        ],
     )
 
 
@@ -515,33 +463,36 @@
         ).astype(BF16)
 
 
-def attend_back(info, mixed, att, grad, stats, cos_t, sin_t, group, earlier, deps):
+def attend_back(info, mixed, att, grad, stats, cos_t, sin_t, half, deps):
     rows, wide = mixed.shape
     width = wide // 3
     groups = width // GROUP
     heads = GROUP // HEAD_DIM
-    spec = lambda shift: pl.BlockSpec((rows, GROUP), lambda i, s: (0, group + shift * groups))
+    first = half * (groups // 2)
+    spec = lambda shift: pl.BlockSpec((rows, GROUP), lambda i, s: (0, i + first + shift * groups))
     per_head = pltpu.VMEM((heads, rows, HEAD_DIM), BF16)
     turned = pltpu.VMEM((GROUP, rows), BF16)
     angles = pl.BlockSpec((HEAD_DIM // 2, rows), lambda i, s: (0, 0))
     return call(
         attend_back_kernel,
-        (1,),
+        (groups // 2,),
         [info],
         [
-            (mixed, spec(0)), (mixed, spec(1)), (mixed, spec(2)), (att, spec(0)), (grad, spec(0)),
-            (stats, pl.BlockSpec((1, heads, rows), lambda i, s: (group, 0, 0))),
+            (far_away(mixed), spec(0)), (far_away(mixed), spec(1)), (far_away(mixed), spec(2)),
+            (far_away(att), spec(0)), (far_away(grad), spec(0)),
+            (stats, pl.BlockSpec((1, heads, rows), lambda i, s: (i + first, 0, 0))),
             (cos_t, angles), (sin_t, angles),
         ],
         [
             (
-                shape((3, rows, 2 * GROUP), BF16),
-                pl.BlockSpec((3, rows, GROUP), lambda i, s: (0, 0, group % 2)),
+                pltpu.HBM((3, rows, 2 * GROUP), BF16),
+                pl.BlockSpec((3, rows, GROUP), lambda i, s: (0, 0, i)),
             ),
         ],
-        earlier + deps,
+        deps,
         "attend_back",
-        12,
+        32,
+        24,
         scratch=[
             per_head, per_head, per_head, per_head,
             turned, turned, turned,
@@ -550,23 +501,17 @@
             pltpu.VMEM((heads, rows, HEAD_DIM), F32),
             pltpu.VMEM((heads, rows, HEAD_DIM), F32),
         ],
-        aliases={9: 0} if earlier else None,
     )[0]
 
 
-def finish_kernel(place, own_tok, far_tok, middle_back, left_back, right_back, w_far, gains,
-                  near_out, far_out, sums, w_qkv, sems):
+def finish_kernel(place, own_tok, far_tok, middle_back, left_back, right_back, w_qkv, gains,
+                  near_out, far_out, sums):
     half = left_back.shape[2]
-    stream = Stream(
-        sems, [(w_far, w_qkv, slice(at, at + half)) for at in range(0, w_qkv.shape[1], half)]
-    )
     unit, rstd = norm_parts(pick_rows(own_tok, far_tok))
     grad = None
     for part in range(3):
         for side, back in enumerate((left_back, right_back)):
             start = (2 * part + side) * half
-            if start in (0, half, 3 * half):
-                stream.take({0: 1, half: 2, 3 * half: 3}[start])
             term = dot(back[part], w_qkv[:, start : start + half], NT)
             grad = term if grad is None else grad + term
     back = middle_back[...] + norm_back(unit, rstd, gains[0:1, :], grad)
@@ -588,19 +533,19 @@
         (rows // TILE,),
         [place],
         [
-            (tokens, own_rows(width)), (far_tok, far_rows(width)),
-            (middle_back, row_block(width)), (left_back, parts), (right_back, parts),
-            (w_qkv, ANY), (gains, whole(gains.shape)),
-        ],
-        [
-            (shape((2, rows // 2, width), BF16), own_rows(width)),
+            (far_away(tokens), own_rows(width)), (far_tok, far_rows(width)),
+            (far_away(middle_back), row_block(width)), (far_away(left_back), parts), (far_away(right_back), parts),
+            (far_away(w_qkv), whole(w_qkv.shape)), (gains, whole(gains.shape)),
+        ],
+        [
+            (pltpu.HBM((2, rows // 2, width), BF16), own_rows(width)),
             (shape((rows // 2, width), BF16), far_rows(width)),
             (shape((8, width), F32), whole((8, width))),
         ],
         deps,
         "finish",
-        8,
-        scratch=[pltpu.VMEM(w_qkv.shape, BF16), pltpu.SemaphoreType.DMA((6,))],
+        24,
+        15,
     )
 
 
@@ -612,10 +557,11 @@
     for number in range(source_count):
         left, right = refs[2 * number], refs[2 * number + 1]
         rights = [right] if len(right.shape) == 2 else [right.at[p] for p in range(3)]
+        turned = left[...].T
         for piece in rights:
             cols = slice(start, start + piece.shape[1])
             start = cols.stop
-            total = dot(left[...], piece[...], TN)
+            total = dot(turned, piece[...])
             for addend in addends:
                 total = total + addend[:, cols].astype(F32)
             total = total.astype(BF16)
@@ -711,6 +657,7 @@
             ],
             deps,
             "weight_grad",
+            24,
             0.5 + 0.3 * self.us * steps,
         )
 
@@ -807,6 +754,7 @@
         ],
         deps,
         "gather",
+        20,
         6,
     )[0]
 
@@ -840,6 +788,7 @@
         ],
         earlier + deps,
         "gather_mixed",
+        16,
         4,
         aliases={5: 0} if earlier else None,
     )[0]
@@ -894,14 +843,14 @@
     half_wide = width // 2
     down = Reduction(
         place,
-        [(active, lambda x, c, b, h: (0, 4 * x + 2 * c + b),
+        [(far_away(active), lambda x, c, b, h: (0, 4 * x + 2 * c + b),
           back2, lambda x, c, b, h: (0, 0), width)],
         2 * TILE, width, 1, 1.5,
     )
     up = Reduction(
         place,
         [(normed2, lambda x, c, b, h: (0, x),
-          hidden_back, lambda x, c, b, h: (0, 2 * c + b), width)],
+          far_away(hidden_back), lambda x, c, b, h: (0, 2 * c + b), width)],
         2 * TILE, width, 1, 1.5,
     )
     last = down.far([])
@@ -913,35 +862,31 @@
         norm_gains, norm_biases, [last],
     )
 
-    def back(group, earlier, deps):
-        return attend_back(
-            info, mixed, att, att_back, stats, cos_t, sin_t, group, earlier, deps
-        )
-
-    last = down.second([middle_back])
-    left_back = back(0, [], [last])
-    last = up.second([left_back])
-    left_back = back(1, [left_back], [last])
+    def back(half, deps):
+        return attend_back(info, mixed, att, att_back, stats, cos_t, sin_t, half, deps)
+
+    last = down.second([sums12])
+    left_back = back(0, [last])
     by_rows = lambda x, c, b, h: (0, 2 * x + c)
     by_parts = lambda x, c, b, h: (0, 0, b)
     left = Reduction(
         place,
-        [(normed, by_rows, left_back, by_parts, TILE),
-         (att, by_rows, branch_back, lambda x, c, b, h: (0, b), half_wide)],
+        [(normed, by_rows, far_away(left_back), by_parts, TILE),
+         (far_away(att), by_rows, branch_back, lambda x, c, b, h: (0, b), half_wide)],
         TILE, 5 * TILE, 1, 1.2,
     )
-    last = down.keep([left_back])
+    last = up.second([far_away(left_back)])
+    last = down.keep([last])
+    last = left.far([last])
     last = up.keep([last])
     got_out = swap_narrow(tie(far_out, last))
-    last = left.far([last])
-    right_back = back(2, [], [last])
-    last = down.step(right_back)
-    last = left.first([last])
-    right_back = back(3, [right_back], [last])
+    right_back = back(1, [last])
+    last = left.first([far_away(right_back)])
+    last = down.step(last)
     right = Reduction(
-        place, [(normed, by_rows, right_back, by_parts, TILE)], TILE, 3 * TILE, 1, 0.8
-    )
-    last = right.far([])
+        place, [(normed, by_rows, far_away(right_back), by_parts, TILE)], TILE, 3 * TILE, 1, 0.8
+    )
+    last = right.far([last])
     last = up.step(last)
     last = left.second([last])
     last = right.first([last, got_out])
@@ -949,11 +894,12 @@
     for _ in range(extra):
         last = down.step(last)
     last = down.step(last)
+    down.open(last)
     near_grad, far_grad, sums0 = finish(
         place, tokens, far_tok, middle_back, left_back, right_back, w_qkv, norm_gains,
         [last, down.from_core],
     )
-    last = right.second([near_grad])
+    last = right.second([sums0])
     last = left.keep([last])
     norm_term = jnp.concatenate(
         [sums0[0:1], sums12[0:1], sums12[2:3], sums3[0:1],
@@ -969,20 +915,20 @@
         return norm_term
 
     last = right.keep([last])
-    down.open(last)
     for _ in range(extra):
         last = up.step(last)
     last = up.step(last)
+    up.open(last)
     norm_got = swap_narrow(tie(norm_term, last))
     for _ in range(extra):
         last = left.step(last)
         last = right.step(last)
     last = left.step(last)
-    up.open(last)
     last = norm_step(last)
+    last = right.step(last)
     last = down.spread(last)
-    last = right.step(last)
     got_grad = swap_narrow(tie(far_grad, last))
+    last = norm_step(last)
     grad_down = gather(
         place, down.pieces(), (ff // 2, width), half_wide, 0, 2,
         lambda c, b, h: (2 * c + b, h), [last],
@@ -990,11 +936,11 @@
     last = norm_step(grad_down)
     out = lax.dynamic_update_slice(near_out, tie(got_out, last)[None], (1 - n, 0, 0))
     last = left.step(last)
-    last = up.spread(last)
     left.open(last)
-    last = norm_step(last)
     last = right.step(last)
     right.open(last)
+    last = norm_step(last)
+    last = up.spread(last)
     grad_up = gather(
         place, up.pieces(), (half_wide, ff), half_wide, 0, 2,
         lambda c, b, h: (0, 2 * (2 * c + b) + h), [last],
@@ -1011,7 +957,7 @@
         lambda c, b, h: (c, 2 * b + h), [last],
     )
     grad_qkv = gather_mixed(
-        place, left.pieces(), (half_wide, 3 * width), 0, [], [grad_out_proj]
+        place, left.pieces(), (half_wide, 3 * width), 0, [], [last]
     )
     grad_qkv = gather_mixed(
         place, right.pieces(), (half_wide, 3 * width), 1, [grad_qkv], []

time: 503 us -> 448 us (0.89)
  Pallas kernels: 334 us -> 275 us
  waiting for transfers between devices: 60.5 us -> 68.3 us
  local copies, waits for them, and re-layouts: 24.6 us -> 17.2 us
  starting transfers between devices: 59.2 us -> 64.6 us
    pallas_call x31 -> x29, Pallas kernels: 334 us -> 275 us  [call(): pl.pallas_call(body, grid_spec=pltpu.PrefetchScalarGridSpec(num_scalar_pr...]
    ppermute x8, waiting for transfers between devices: 26.8 us -> 9.73 us  [swap_two(): lax.ppermute(rows, 'wide', [(i, i ^ (even_bit if i % 2 == 0 else odd_bit)...]
    ppermute x8, starting transfers between devices: 25.4 us -> 13.2 us  [swap_crossed(): return lax.ppermute(rows, ('wide', 'narrow'), pairs)]
    ppermute x5, waiting for transfers between devices: 4.23 us -> 15.1 us  [swap_narrow(): return lax.ppermute(rows, 'narrow', [(0, 1), (1, 0)])]
    ppermute x8, starting transfers between devices: 11.4 us -> 22.2 us  [swap_two(): lax.ppermute(rows, 'wide', [(i, i ^ (even_bit if i % 2 == 0 else odd_bit)...]
    ppermute x24, starting transfers between devices: 11.6 us -> 21.4 us  [swap_wide(): return lax.ppermute(rows, 'wide', [(i, i ^ bit) for i in range(size)])]
    ppermute x8, waiting for transfers between devices: 0.02 us -> 8.41 us  [swap_crossed(): return lax.ppermute(rows, ('wide', 'narrow'), pairs)]
    unnamed x57 -> x53, local copies, waits for them, and re-layouts: 13.6 us -> 6.34 us
  transfers between devices with their start and end apart: 45 -> 45, of which waited for: 8 -> 13; matrix products, arithmetic and copies ran while one was open for 5% -> 5% of each run, Pallas kernels for 54% -> 48%
where the time goes in v5:
time: 448 us; the launch traced here: 441 us
  Pallas kernels  275 us (61%)
  waiting for transfers between devices  68.3 us (15%)
  starting transfers between devices  64.6 us (14%)
  local copies, waits for them, and re-layouts  17.2 us (4%)
  other arithmetic  13.6 us (3%)
    pallas_call x29, Pallas kernels, call(): pl.pallas_call(body, grid_spec=pltpu.PrefetchScalarGridSpec(num_scalar_pr...  275 us
    ppermute x24, waiting for transfers between devices, swap_wide(): return lax.ppermute(rows, 'wide', [(i, i ^ bit) for i in range(size)])  35 us
    ppermute x8, starting transfers between devices, swap_two(): lax.ppermute(rows, 'wide', [(i, i ^ (even_bit if i % 2 == 0 else odd_bit)...  22.2 us
    ppermute x24, starting transfers between devices, swap_wide(): return lax.ppermute(rows, 'wide', [(i, i ^ bit) for i in range(size)])  21.4 us
    ppermute x5, waiting for transfers between devices, swap_narrow(): return lax.ppermute(rows, 'narrow', [(0, 1), (1, 0)])  15.1 us
    ppermute x8, starting transfers between devices, swap_crossed(): return lax.ppermute(rows, ('wide', 'narrow'), pairs)  13.2 us
    ppermute x8, waiting for transfers between devices, swap_two(): lax.ppermute(rows, 'wide', [(i, i ^ (even_bit if i % 2 == 0 else odd_bit)...  9.73 us
  transfers between devices with their start and end apart: 45, of which 13 were waited for; matrix products, arithmetic and copies ran while one was open for 5% of the time, Pallas kernels for 48%

profile of v5, /device:TPU:0, one launch (start us, length us, event | category | flops | bytes accessed | tf_op | source)
XLA Modules:
  0.0 440.6 jit_solution(199892040875187335)
XLA Ops:
  15.2 8.7 %project.2 = (bf16[1024,1024]{1,0:T(8,128)(2,1)}, bf16[1024,3072]{1,0:T(8,128)(2,1)}) custom-call(s32[5]{0:T(128)S(1)} %stack.36.refs_0_, bf16[2,512,1024]{2,1,0:T(8,128)(2,1)S(1)} %copy-done.10, bf16[1024,3072]{1,0:T(8,128)(2,1)} %refs_6_.3, f32[4,1024]{1,0:T(4,128)S(1)} %copy-done.18, f32[4,1024]{1,0:T(4,128)S(1)} %copy-done.17, ...), custom_call_target="tpu_custom_call" | custom-call | flops 8000000000 | bytes 1 | tf_op jit(solution)/shard_map/project/pallas_call | solution.py:34
  25.9 4.3 collective-permute-done.refs_1_.refs_2_
  30.2 8.9 %project.3 = (bf16[1024,1024]{1,0:T(8,128)(2,1)}, bf16[1024,3072]{1,0:T(8,128)(2,1)}) custom-call(s32[5]{0:T(128)S(1)} %stack.36.refs_0_, bf16[512,1024]{1,0:T(8,128)(2,1)} %collective-permute-done.refs_1_.refs_2_, bf16[1024,3072]{1,0:T(8,128)(2,1)} %refs_6_.3, f32[4,1024]{1,0:T(4,128)S(1)} %copy-done.18, ...), custom_call_target="tpu_custom_call", output_to_operand_aliasing={{0}: (7, {}), {1}: (8, {})} | custom-call | flops 8000000000 | bytes 1 | tf_op jit(solution)/shard_map/project/pallas_call | solution.py:34
  39.1 24.3 %attend.1 = (bf16[1024,1024]{1,0:T(8,128)(2,1)}, f32[4,4,1024]{2,1,0:T(4,128)S(1)}) custom-call(s32[5]{0:T(128)S(1)} %concatenate.19.refs_0_, bf16[1024,3072]{1,0:T(8,128)(2,1)} %get-tuple-element.67.refs_1_.refs_2_.refs_3_, bf16[1024,3072]{1,0:T(8,128)(2,1)} %get-tuple-element.67.refs_1_.refs_2_.refs_3_, ...), custom_call_target="tpu_custom_call" | custom-call | flops 35999997952 | bytes 1 | tf_op jit(solution)/shard_map/attend/pallas_call | solution.py:34
  64.3 50.8 %feed.1 = (bf16[2,512,1024]{2,1,0:T(8,128)(2,1)}, bf16[512,1024]{1,0:T(8,128)(2,1)S(1)}, f32[1024,1024]{1,0:T(8,128)}, bf16[1024,1024]{1,0:T(8,128)(2,1)}, bf16[...) custom-call(s32[5]{0:T(128)S(1)} %stack.36.refs_0_, ...), custom_call_target="tpu_custom_call" | custom-call | flops 49000001536 | bytes 1 | tf_op jit(solution)/shard_map/feed/pallas_call | solution.py:34
  116.7 7.6 %weight_grad.16 = (bf16[1024,1024]{1,0:T(8,128)(2,1)S(1)}, bf16[1024,1024]{1,0:T(8,128)(2,1)S(1)}) custom-call(s32[5]{0:T(128)S(1)} %stack.36.refs_0_, bf16[1024,4096]{1,0:T(8,128)(2,1)} %get-tuple-element.73.refs_1_, bf16[1024,1024]{1,0:T(8,128)(2,1)S(1)} %copy-done.1), custom_call_target="tpu_custom_call" | custom-call | flops 2300000000 | bytes 1 | tf_op jit(solution)/shard_map/weight_grad/pallas_call | solution.py:34
  124.4 10.2 %collective-permute-start.4 = (bf16[1024,1024]{1,0:T(8,128)(2,1)S(1)}, bf16[1024,1024]{1,0:T(8,128)(2,1)S(1)}, u32[]{:S(2)}, u32[]{:S(2)}) collective-permute-start(bf16[1024,1024]{1,0:T(8,128)(2,1)S(1)} %get-tuple-element.75.refs_3_), channel_id=1, source_target_pairs={{0,2},{2,0},{4,6},{6,4},{8,10},{10,8},{12,14},{14,12},{16,18},{18,... | collective-permute-start | bytes 6291464 | tf_op jit(solution)/shard_map/ppermute | solution.py:580
  134.6 8.5 %weight_grad.17 = (bf16[1024,1024]{1,0:T(8,128)(2,1)S(1)}, bf16[1024,1024]{1,0:T(8,128)(2,1)S(1)}) custom-call(s32[5]{0:T(128)S(1)} %stack.36.refs_0_, bf16[1024,1024]{1,0:T(8,128)(2,1)S(1)} %copy-done.3, bf16[1024,4096]{1,0:T(8,128)(2,1)} %get-tuple-element.72.refs_2_.refs_6_, bf16[1024,1024]{1,0:T(8,128)(2,1)S(1)} %get-tuple-element.75.refs_3_), custom_call_target="tpu_custom_call" | custom-call | flops 2300000000 | bytes 1 | tf_op jit(solution)/shard_map/weight_grad/pallas_call | solution.py:34
  144.3 4.4 %weight_grad.18.refs_4_ = bf16[1024,1024]{1,0:T(8,128)(2,1)S(1)} custom-call(s32[5]{0:T(128)S(1)} %stack.36.refs_0_, bf16[1024,4096]{1,0:T(8,128)(2,1)} %get-tuple-element.73.refs_1_, bf16[1024,1024]{1,0:T(8,128)(2,1)S(1)} %copy-done.2, bf16[1024,1024]{1,0:T(8,128)(2,1)S(1)} %collective-permute-done.4.refs_3_, ...), custom_call_target="tpu_custom_call" | custom-call | flops 1400000000 | bytes 1 | tf_op jit(solution)/shard_map/weight_grad/pallas_call | solution.py:34
  150.5 4.8 %weight_grad.19.refs_11_ = bf16[1024,1024]{1,0:T(8,128)(2,1)S(1)} custom-call(s32[5]{0:T(128)S(1)} %stack.36.refs_0_, bf16[1024,1024]{1,0:T(8,128)(2,1)S(1)} %copy-done.3, bf16[1024,4096]{1,0:T(8,128)(2,1)} %get-tuple-element.72.refs_2_.refs_6_, bf16[1024,1024]{1,0:T(8,128)(2,1)S(1)} %collective-permute-done.3.refs_3_, ...), custom_call_target="tpu_custom_call" | custom-call | flops 1400000000 | bytes 1 | tf_op jit(solution)/shard_map/weight_grad/pallas_call | solution.py:34
  155.8 25.0 %return_pass.1 = (f32[1024,1024]{1,0:T(8,128)}, bf16[1024,1024]{1,0:T(8,128)(2,1)S(1)}, bf16[1024,1024]{1,0:T(8,128)(2,1)S(1)}, f32[8,1024]{1,0:T(8,128)S(1)}) custom-call(s32[5]{0:T(128)S(1)} %stack.36.refs_0_, bf16[2,512,1024]{2,1,0:T(8,128)(2,1)} %refs_1_.7, bf16[512,1024]{1,0:T(8,128)(2,1)} %collective-permute-done.refs_1_.refs_2_, ...), custom_call_target="tpu_custom_call" | custom-call | flops 24000000000 | bytes 1 | tf_op jit(solution)/shard_map/return_pass/pallas_call | solution.py:34
  185.4 5.1 %collective-permute-start.9 = (bf16[512,1024]{1,0:T(8,128)(2,1)S(1)}, bf16[512,1024]{1,0:T(8,128)(2,1)S(1)}, u32[]{:S(2)}, u32[]{:S(2)}) collective-permute-start(bf16[512,1024]{1,0:T(8,128)(2,1)S(1)} %weight_grad.20.refs_9_), channel_id=1, source_target_pairs={{0,4},{1,5},{2,3},{3,2},{4,0},{5,1},{6,7},{7,6},{8,12},{9,13},{10,... | collective-permute-start | bytes 3145736 | tf_op jit(solution)/shard_map/ppermute | solution.py:594
  190.5 18.1 %attend_back.2.refs_5_.refs_2_.refs_4_ = bf16[3,1024,512]{2,1,0:T(8,128)(2,1)} custom-call(s32[5]{0:T(128)S(1)} %concatenate.19.refs_0_, bf16[1024,3072]{1,0:T(8,128)(2,1)} %get-tuple-element.67.refs_1_.refs_2_.refs_3_, bf16[1024,3072]{1,0:T(8,128)(2,1)} %get-tuple-element.67.refs_1_.refs_2_.refs_3_, ...), custom_call_target="tpu_custom_call" | custom-call | flops 24000000000 | bytes 1 | tf_op jit(solution)/shard_map/attend_back/pallas_call | solution.py:34
  212.2 5.7 %collective-permute-start.8 = (bf16[512,1024]{1,0:T(8,128)(2,1)S(1)}, bf16[512,1024]{1,0:T(8,128)(2,1)S(1)}, u32[]{:S(2)}, u32[]{:S(2)}) collective-permute-start(bf16[512,1024]{1,0:T(8,128)(2,1)S(1)} %weight_grad.21.refs_6_), channel_id=1, source_target_pairs={{0,4},{1,5},{2,3},{3,2},{4,0},{5,1},{6,7},{7,6},{8,12},{9,13},{10,... | collective-permute-start | bytes 3145736 | tf_op jit(solution)/shard_map/ppermute | solution.py:594
  221.4 9.4 %weight_grad.23 = (bf16[512,1280]{1,0:T(8,128)(2,1)S(1)}, bf16[512,1280]{1,0:T(8,128)(2,1)S(1)}) custom-call(s32[5]{0:T(128)S(1)} %stack.36.refs_0_, bf16[1024,1024]{1,0:T(8,128)(2,1)S(1)} %copy-done, bf16[3,1024,512]{2,1,0:T(8,128)(2,1)} %attend_back.2.refs_5_.refs_2_.refs_4_, bf16[1024,1024]{1,0:T(8,128)(2,1)} %get-tuple-element.68.refs_5_.refs_4_.refs_3_, ...), custom_call_target="tpu_custom_call" | custom-call | flops 1940000000 | bytes 1 | tf_op jit(solution)/shard_map/weight_grad/pallas_call | solution.py:34
  238.3 18.1 %attend_back.3.refs_6_.refs_2_.refs_5_ = bf16[3,1024,512]{2,1,0:T(8,128)(2,1)} custom-call(s32[5]{0:T(128)S(1)} %concatenate.19.refs_0_, bf16[1024,3072]{1,0:T(8,128)(2,1)} %get-tuple-element.67.refs_1_.refs_2_.refs_3_, bf16[1024,3072]{1,0:T(8,128)(2,1)} %get-tuple-element.67.refs_1_.refs_2_.refs_3_, ...), custom_call_target="tpu_custom_call" | custom-call | flops 24000000000 | bytes 1 | tf_op jit(solution)/shard_map/attend_back/pallas_call | solution.py:34
  256.4 4.0 weight_grad.25
  263.0 8.0 %collective-permute-start.14 = (bf16[512,1024]{1,0:T(8,128)(2,1)S(1)}, bf16[512,1024]{1,0:T(8,128)(2,1)S(1)}, u32[]{:S(2)}, u32[]{:S(2)}) collective-permute-start(bf16[512,1024]{1,0:T(8,128)(2,1)S(1)} %add_convert_fusion.3.refs_3_), channel_id=1, source_target_pairs={{0,16},{2,10},{4,20},{6,14},{8,24},{10,2},{12,28},{14,6},{16,0},{1... | collective-permute-start | bytes 3145736 | tf_op jit(solution)/shard_map/ppermute | solution.py:599
  271.0 7.3 %weight_grad.26 = (bf16[512,768]{1,0:T(8,128)(2,1)S(1)}, bf16[512,768]{1,0:T(8,128)(2,1)S(1)}) custom-call(s32[5]{0:T(128)S(1)} %stack.36.refs_0_, bf16[1024,1024]{1,0:T(8,128)(2,1)S(1)} %copy-done, bf16[3,1024,512]{2,1,0:T(8,128)(2,1)} %attend_back.3.refs_6_.refs_2_.refs_5_, bf16[512,1024]{1,0:T(8,128)(2,1)S(1)} %add_convert_fusion.3.refs_3_), custom_call_target="tpu_custom_call" | custom-call | flops 1460000000 | bytes 1 | tf_op jit(solution)/shard_map/weight_grad/pallas_call | solution.py:34
  279.3 7.4 %collective-permute-done.16.refs_6_ = bf16[512,1280]{1,0:T(8,128)(2,1)S(1)} collective-permute-done((bf16[512,1280]{1,0:T(8,128)(2,1)S(1)}, bf16[512,1280]{1,0:T(8,128)(2,1)S(1)}, u32[]{:S(2)}, u32[]{:S(2)}) %collective-permute-start.16) | collective-permute-done | bytes 1310752 | tf_op jit(solution)/shard_map/ppermute | solution.py:594
  289.8 10.8 %collective-permute-done.10.refs_5_ = bf16[512,1024]{1,0:T(8,128)(2,1)S(1)} collective-permute-done((bf16[512,1024]{1,0:T(8,128)(2,1)S(1)}, bf16[512,1024]{1,0:T(8,128)(2,1)S(1)}, u32[]{:S(2)}, u32[]{:S(2)}) %collective-permute-start.10) | collective-permute-done | bytes 1048608 | tf_op jit(solution)/shard_map/ppermute | solution.py:584
  305.4 7.5 %collective-permute-start.20 = (bf16[512,1024]{1,0:T(8,128)(2,1)S(1)}, bf16[512,1024]{1,0:T(8,128)(2,1)}, u32[]{:S(2)}, u32[]{:S(2)}) collective-permute-start(bf16[512,1024]{1,0:T(8,128)(2,1)S(1)} %add_convert_fusion.2.refs_7_), channel_id=1, source_target_pairs={{0,16},{2,10},{4,20},{6,14},{8,24},{10,2},{12,28},{14,6},{16,0},{1... | collective-permute-start | bytes 3145736 | tf_op jit(solution)/shard_map/ppermute | solution.py:599
  313.5 15.4 %finish.1 = (bf16[2,512,1024]{2,1,0:T(8,128)(2,1)}, bf16[512,1024]{1,0:T(8,128)(2,1)S(1)}, f32[8,1024]{1,0:T(8,128)S(1)}) custom-call(s32[5]{0:T(128)S(1)} %stack.36.refs_0_, bf16[2,512,1024]{2,1,0:T(8,128)(2,1)} %refs_1_.7, bf16[512,1024]{1,0:T(8,128)(2,1)} %collective-permute-done.refs_1_.refs_2_, f32[1024,1024]{1,0:T(8,128)} %get-tuple-element.87.refs_3_, ...), custom_call_target="tpu_custom_call" | custom-call | flops 15000000512 | bytes 1 | tf_op jit(solution)/shard_map/finish/pallas_call | solution.py:34
  333.3 4.0 weight_grad.30.refs_6_
  355.5 7.1 %collective-permute-done.28 = bf16[256,768]{1,0:T(8,128)(2,1)S(1)} collective-permute-done((bf16[256,768]{1,0:T(8,128)(2,1)S(1)}, bf16[256,768]{1,0:T(8,128)(2,1)S(1)}, u32[]{:S(2)}, u32[]{:S(2)}) %collective-permute-start.28) | collective-permute-done | bytes 393248 | tf_op jit(solution)/shard_map/ppermute | solution.py:599
  369.9 7.2 %gather.3 = f32[2048,1024]{1,0:T(8,128)} custom-call(s32[5]{0:T(128)S(1)} %stack.36.refs_0_, bf16[512,1024]{1,0:T(8,128)(2,1)} %add_convert_fusion.1.refs_8_.refs_1_, bf16[512,1024]{1,0:T(8,128)(2,1)} %collective-permute-done.27.refs_2_, bf16[512,1024]{1,0:T(8,128)(2,1)S(1)} %copy-done.14, bf16[512,1024]{1,0:T(8,128)(2,1)S(1)} %collective-permute-done.30.refs_4_, ...), custom_call_target="tpu_custom_call" | custom-call | flops 6000000000 | bytes 1 | tf_op jit(solution)/shard_map/gather/pallas_call | solution.py:34
  377.1 15.2 %collective-permute-done.29 = f32[8,1024]{1,0:T(8,128)S(1)} collective-permute-done((f32[8,1024]{1,0:T(8,128)S(1)}, f32[8,1024]{1,0:T(8,128)S(1)}, u32[]{:S(2)}, u32[]{:S(2)}) %collective-permute-start.29) | collective-permute-done | bytes 32800 | tf_op jit(solution)/shard_map/ppermute | solution.py:580
  402.0 8.5 %gather.4 = f32[512,4096]{1,0:T(8,128)} custom-call(s32[5]{0:T(128)S(1)} %stack.36.refs_0_, bf16[512,1024]{1,0:T(8,128)(2,1)S(1)} %add_convert_fusion.refs_1_, bf16[512,1024]{1,0:T(8,128)(2,1)} %collective-permute-done.36.refs_2_.refs_5_, bf16[512,1024]{1,0:T(8,128)(2,1)} %collective-permute-done.37.refs_3_, ...), custom_call_target="tpu_custom_call" | custom-call | flops 6000000000 | bytes 1 | tf_op jit(solution)/shard_map/gather/pallas_call | solution.py:34
  410.6 5.8 %collective-permute-done.40.refs_2_ = bf16[256,1280]{1,0:T(8,128)(2,1)} collective-permute-done((bf16[256,1280]{1,0:T(8,128)(2,1)S(1)}, bf16[256,1280]{1,0:T(8,128)(2,1)}, u32[]{:S(2)}, u32[]{:S(2)}) %collective-permute-start.40) | collective-permute-done | bytes 655392 | tf_op jit(solution)/shard_map/ppermute | solution.py:580
  416.5 7.4 %collective-permute-done.39.refs_5_.refs_2_ = bf16[256,768]{1,0:T(8,128)(2,1)S(1)} collective-permute-done((bf16[256,768]{1,0:T(8,128)(2,1)S(1)}, bf16[256,768]{1,0:T(8,128)(2,1)S(1)}, u32[]{:S(2)}, u32[]{:S(2)}) %collective-permute-start.39) | collective-permute-done | bytes 393248 | tf_op jit(solution)/shard_map/ppermute | solution.py:580
  426.0 5.5 %gather.5 = f32[512,1024]{1,0:T(8,128)} custom-call(s32[5]{0:T(128)S(1)} %stack.36.refs_0_, bf16[256,1280]{1,0:T(8,128)(2,1)S(1)} %add_convert_fusion.4.refs_1_, bf16[256,1280]{1,0:T(8,128)(2,1)} %collective-permute-done.40.refs_2_, bf16[256,1280]{1,0:T(8,128)(2,1)S(1)} %collective-permute-done.43.refs_3_, ...), custom_call_target="tpu_custom_call" | custom-call | flops 6000000000 | bytes 1 | tf_op jit(solution)/shard_map/gather/pallas_call | solution.py:34
  431.4 5.2 %gather_mixed.2.refs_5_ = f32[512,3072]{1,0:T(8,128)} custom-call(s32[5]{0:T(128)S(1)} %stack.36.refs_0_, bf16[256,1280]{1,0:T(8,128)(2,1)S(1)} %add_convert_fusion.4.refs_1_, bf16[256,1280]{1,0:T(8,128)(2,1)} %collective-permute-done.40.refs_2_, bf16[256,1280]{1,0:T(8,128)(2,1)S(1)} %collective-permute-done.43.refs_3_, ...), custom_call_target="tpu_custom_call" | custom-call | flops 4000000000 | bytes 1 | tf_op jit(solution)/shard_map/gather_mixed/pallas_call | solution.py:34
  (171 shorter events, 98.2 us)
Async XLA Ops:
  2.9 27.3 %collective-permute-start = (bf16[512,1024]{1,0:T(8,128)(2,1)}, bf16[512,1024]{1,0:T(8,128)(2,1)}, u32[]{:S(2)}, u32[]{:S(2)}) collective-permute-start(bf16[512,1024]{1,0:T(8,128)(2,1)} %dynamic-slice_bitcast_fusion.1), channel_id=1, source_target_pairs={{0,1},{1,0},{2,3},{3,2},{4,5},{5,4},{6,7},{7,6},{8,9},{9,8},{10,11... | collective-permute-start | bytes 3145736 | tf_op jit(solution)/shard_map/ppermute | solution.py:584
  23.9 39.4 %collective-permute-start.1 = (bf16[512,1024]{1,0:T(8,128)(2,1)}, bf16[512,1024]{1,0:T(8,128)(2,1)S(1)}, u32[]{:S(2)}, u32[]{:S(2)}) collective-permute-start(bf16[512,1024]{1,0:T(8,128)(2,1)} %dynamic-slice_bitcast_fusion), channel_id=1, source_target_pairs={{0,1},{1,0},{2,3},{3,2},{4,5},{5,4},{6,7},{7,6},{8,9},{9,8},{10,11... | collective-permute-start | bytes 3145736 | tf_op jit(solution)/shard_map/ppermute | solution.py:584
  124.4 20.0 %collective-permute-start.4 = (bf16[1024,1024]{1,0:T(8,128)(2,1)S(1)}, bf16[1024,1024]{1,0:T(8,128)(2,1)S(1)}, u32[]{:S(2)}, u32[]{:S(2)}) collective-permute-start(bf16[1024,1024]{1,0:T(8,128)(2,1)S(1)} %get-tuple-element.75.refs_3_), channel_id=1, source_target_pairs={{0,2},{2,0},{4,6},{6,4},{8,10},{10,8},{12,14},{14,12},{16,18},{18,... | collective-permute-start | bytes 6291464 | tf_op jit(solution)/shard_map/ppermute | solution.py:580
  148.8 33.4 %collective-permute-start.7 = (bf16[1024,1024]{1,0:T(8,128)(2,1)S(1)}, bf16[1024,1024]{1,0:T(8,128)(2,1)S(1)}, u32[]{:S(2)}, u32[]{:S(2)}) collective-permute-start(bf16[1024,1024]{1,0:T(8,128)(2,1)S(1)} %weight_grad.18.refs_4_), channel_id=1, source_target_pairs={{0,1},{1,0},{2,6},{3,7},{4,5},{5,4},{6,2},{7,3},{8,9},{9,8},{10,14... | collective-permute-start | bytes 6291464 | tf_op jit(solution)/shard_map/ppermute | solution.py:594
  155.3 53.3 %collective-permute-start.6 = (bf16[1024,1024]{1,0:T(8,128)(2,1)S(1)}, bf16[1024,1024]{1,0:T(8,128)(2,1)S(1)}, u32[]{:S(2)}, u32[]{:S(2)}) collective-permute-start(bf16[1024,1024]{1,0:T(8,128)(2,1)S(1)} %weight_grad.19.refs_11_), channel_id=1, source_target_pairs={{0,1},{1,0},{2,6},{3,7},{4,5},{5,4},{6,2},{7,3},{8,9},{9,8},{10,14... | collective-permute-start | bytes 6291464 | tf_op jit(solution)/shard_map/ppermute | solution.py:594
  185.4 32.5 %collective-permute-start.9 = (bf16[512,1024]{1,0:T(8,128)(2,1)S(1)}, bf16[512,1024]{1,0:T(8,128)(2,1)S(1)}, u32[]{:S(2)}, u32[]{:S(2)}) collective-permute-start(bf16[512,1024]{1,0:T(8,128)(2,1)S(1)} %weight_grad.20.refs_9_), channel_id=1, source_target_pairs={{0,4},{1,5},{2,3},{3,2},{4,0},{5,1},{6,7},{7,6},{8,12},{9,13},{10,... | collective-permute-start | bytes 3145736 | tf_op jit(solution)/shard_map/ppermute | solution.py:594
  212.2 19.4 %collective-permute-start.8 = (bf16[512,1024]{1,0:T(8,128)(2,1)S(1)}, bf16[512,1024]{1,0:T(8,128)(2,1)S(1)}, u32[]{:S(2)}, u32[]{:S(2)}) collective-permute-start(bf16[512,1024]{1,0:T(8,128)(2,1)S(1)} %weight_grad.21.refs_6_), channel_id=1, source_target_pairs={{0,4},{1,5},{2,3},{3,2},{4,0},{5,1},{6,7},{7,6},{8,12},{9,13},{10,... | collective-permute-start | bytes 3145736 | tf_op jit(solution)/shard_map/ppermute | solution.py:594
  221.2 41.3 %collective-permute-start.11 = (bf16[512,1024]{1,0:T(8,128)(2,1)S(1)}, bf16[512,1024]{1,0:T(8,128)(2,1)S(1)}, u32[]{:S(2)}, u32[]{:S(2)}) collective-permute-start(bf16[512,1024]{1,0:T(8,128)(2,1)S(1)} %weight_grad.22.refs_5_), channel_id=1, source_target_pairs={{0,8},{2,18},{4,12},{6,22},{8,0},{10,26},{12,4},{14,30},{16,24},{1... | collective-permute-start | bytes 3145736 | tf_op jit(solution)/shard_map/ppermute | solution.py:599
  230.8 25.6 %collective-permute-start.12 = (bf16[512,1280]{1,0:T(8,128)(2,1)S(1)}, bf16[512,1280]{1,0:T(8,128)(2,1)S(1)}, u32[]{:S(2)}, u32[]{:S(2)}) collective-permute-start(bf16[512,1280]{1,0:T(8,128)(2,1)S(1)} %get-tuple-element.85.refs_6_), channel_id=1, source_target_pairs={{0,2},{2,0},{4,6},{6,4},{8,10},{10,8},{12,14},{14,12},{16,18},{18,... | collective-permute-start | bytes 3932168 | tf_op jit(solution)/shard_map/ppermute | solution.py:580
  231.5 24.9 %collective-permute-start.13 = (bf16[512,1280]{1,0:T(8,128)(2,1)S(1)}, bf16[512,1280]{1,0:T(8,128)(2,1)S(1)}, u32[]{:S(2)}, u32[]{:S(2)}) collective-permute-start(bf16[512,1280]{1,0:T(8,128)(2,1)S(1)} %get-tuple-element.88), channel_id=1, source_target_pairs={{0,2},{2,0},{4,6},{6,4},{8,10},{10,8},{12,14},{14,12},{16,18},{18,... | collective-permute-start | bytes 3932168 | tf_op jit(solution)/shard_map/ppermute | solution.py:580
  235.3 43.1 %collective-permute-start.17 = (bf16[512,1024]{1,0:T(8,128)(2,1)S(1)}, bf16[512,1024]{1,0:T(8,128)(2,1)S(1)}, u32[]{:S(2)}, u32[]{:S(2)}) collective-permute-start(bf16[512,1024]{1,0:T(8,128)(2,1)S(1)} %weight_grad.24.refs_9_), channel_id=1, source_target_pairs={{0,8},{2,18},{4,12},{6,22},{8,0},{10,26},{12,4},{14,30},{16,24},{1... | collective-permute-start | bytes 3145736 | tf_op jit(solution)/shard_map/ppermute | solution.py:599
  260.5 26.2 %collective-permute-start.16 = (bf16[512,1280]{1,0:T(8,128)(2,1)S(1)}, bf16[512,1280]{1,0:T(8,128)(2,1)S(1)}, u32[]{:S(2)}, u32[]{:S(2)}) collective-permute-start(bf16[512,1280]{1,0:T(8,128)(2,1)S(1)} %weight_grad.25), channel_id=1, source_target_pairs={{0,1},{1,0},{2,6},{3,7},{4,5},{5,4},{6,2},{7,3},{8,9},{9,8},{10,14... | collective-permute-start | bytes 3932168 | tf_op jit(solution)/shard_map/ppermute | solution.py:594
  260.8 39.7 %collective-permute-start.10 = (bf16[512,1024]{1,0:T(8,128)(2,1)S(1)}, bf16[512,1024]{1,0:T(8,128)(2,1)S(1)}, u32[]{:S(2)}, u32[]{:S(2)}) collective-permute-start(bf16[512,1024]{1,0:T(8,128)(2,1)S(1)} %get-tuple-element.86), channel_id=1, source_target_pairs={{0,1},{1,0},{2,3},{3,2},{4,5},{5,4},{6,7},{7,6},{8,9},{9,8},{10,11... | collective-permute-start | bytes 3145736 | tf_op jit(solution)/shard_map/ppermute | solution.py:584
  263.0 41.0 %collective-permute-start.14 = (bf16[512,1024]{1,0:T(8,128)(2,1)S(1)}, bf16[512,1024]{1,0:T(8,128)(2,1)S(1)}, u32[]{:S(2)}, u32[]{:S(2)}) collective-permute-start(bf16[512,1024]{1,0:T(8,128)(2,1)S(1)} %add_convert_fusion.3.refs_3_), channel_id=1, source_target_pairs={{0,16},{2,10},{4,20},{6,14},{8,24},{10,2},{12,28},{14,6},{16,0},{1... | collective-permute-start | bytes 3145736 | tf_op jit(solution)/shard_map/ppermute | solution.py:599
  278.3 22.3 %collective-permute-start.15 = (bf16[512,768]{1,0:T(8,128)(2,1)S(1)}, bf16[512,768]{1,0:T(8,128)(2,1)S(1)}, u32[]{:S(2)}, u32[]{:S(2)}) collective-permute-start(bf16[512,768]{1,0:T(8,128)(2,1)S(1)} %get-tuple-element.90), channel_id=1, source_target_pairs={{0,2},{2,0},{4,6},{6,4},{8,10},{10,8},{12,14},{14,12},{16,18},{18,... | collective-permute-start | bytes 2359304 | tf_op jit(solution)/shard_map/ppermute | solution.py:580
  278.4 22.2 %collective-permute-start.18 = (bf16[512,768]{1,0:T(8,128)(2,1)S(1)}, bf16[512,768]{1,0:T(8,128)(2,1)S(1)}, u32[]{:S(2)}, u32[]{:S(2)}) collective-permute-start(bf16[512,768]{1,0:T(8,128)(2,1)S(1)} %get-tuple-element.92), channel_id=1, source_target_pairs={{0,2},{2,0},{4,6},{6,4},{8,10},{10,8},{12,14},{14,12},{16,18},{18,... | collective-permute-start | bytes 2359304 | tf_op jit(solution)/shard_map/ppermute | solution.py:580
  305.4 43.1 %collective-permute-start.20 = (bf16[512,1024]{1,0:T(8,128)(2,1)S(1)}, bf16[512,1024]{1,0:T(8,128)(2,1)}, u32[]{:S(2)}, u32[]{:S(2)}) collective-permute-start(bf16[512,1024]{1,0:T(8,128)(2,1)S(1)} %add_convert_fusion.2.refs_7_), channel_id=1, source_target_pairs={{0,16},{2,10},{4,20},{6,14},{8,24},{10,2},{12,28},{14,6},{16,0},{1... | collective-permute-start | bytes 3145736 | tf_op jit(solution)/shard_map/ppermute | solution.py:599
  312.9 17.0 %collective-permute-start.21 = (bf16[512,768]{1,0:T(8,128)(2,1)S(1)}, bf16[512,768]{1,0:T(8,128)(2,1)S(1)}, u32[]{:S(2)}, u32[]{:S(2)}) collective-permute-start(bf16[512,768]{1,0:T(8,128)(2,1)S(1)} %weight_grad.28), channel_id=1, source_target_pairs={{0,1},{1,0},{2,6},{3,7},{4,5},{5,4},{6,2},{7,3},{8,9},{9,8},{10,14... | collective-permute-start | bytes 2359304 | tf_op jit(solution)/shard_map/ppermute | solution.py:594
  313.2 20.2 %collective-permute-start.23 = (bf16[256,1280]{1,0:T(8,128)(2,1)S(1)}, bf16[256,1280]{1,0:T(8,128)(2,1)S(1)}, u32[]{:S(2)}, u32[]{:S(2)}) collective-permute-start(bf16[256,1280]{1,0:T(8,128)(2,1)S(1)} %weight_grad.27.refs_4_), channel_id=1, source_target_pairs={{0,4},{1,5},{2,3},{3,2},{4,0},{5,1},{6,7},{7,6},{8,12},{9,13},{10,... | collective-permute-start | bytes 1966088 | tf_op jit(solution)/shard_map/ppermute | solution.py:594
  337.3 16.7 %collective-permute-start.25 = (bf16[256,1280]{1,0:T(8,128)(2,1)}, bf16[256,1280]{1,0:T(8,128)(2,1)}, u32[]{:S(2)}, u32[]{:S(2)}) collective-permute-start(bf16[256,1280]{1,0:T(8,128)(2,1)} %weight_grad.30.refs_6_), channel_id=1, source_target_pairs={{0,8},{2,18},{4,12},{6,22},{8,0},{10,26},{12,4},{14,30},{16,24},{1... | collective-permute-start | bytes 1966088 | tf_op jit(solution)/shard_map/ppermute | solution.py:599
  339.2 25.1 %collective-permute-start.27 = (bf16[512,1024]{1,0:T(8,128)(2,1)}, bf16[512,1024]{1,0:T(8,128)(2,1)}, u32[]{:S(2)}, u32[]{:S(2)}) collective-permute-start(bf16[512,1024]{1,0:T(8,128)(2,1)} %add_convert_fusion.1.refs_8_.refs_1_), channel_id=1, source_target_pairs={{0,4},{2,6},{4,0},{6,2},{8,12},{10,14},{12,8},{14,10},{16,20},{18,... | collective-permute-start | bytes 3145736 | tf_op jit(solution)/shard_map/ppermute | solution.py:580
  348.0 14.6 %collective-permute-start.28 = (bf16[256,768]{1,0:T(8,128)(2,1)S(1)}, bf16[256,768]{1,0:T(8,128)(2,1)S(1)}, u32[]{:S(2)}, u32[]{:S(2)}) collective-permute-start(bf16[256,768]{1,0:T(8,128)(2,1)S(1)} %weight_grad.31), channel_id=1, source_target_pairs={{0,8},{2,18},{4,12},{6,22},{8,0},{10,26},{12,4},{14,30},{16,24},{1... | collective-permute-start | bytes 1179656 | tf_op jit(solution)/shard_map/ppermute | solution.py:599
  364.4 28.5 %collective-permute-start.34 = (bf16[256,1280]{1,0:T(8,128)(2,1)S(1)}, bf16[256,1280]{1,0:T(8,128)(2,1)S(1)}, u32[]{:S(2)}, u32[]{:S(2)}) collective-permute-start(bf16[256,1280]{1,0:T(8,128)(2,1)S(1)} %add_convert_fusion.5), channel_id=1, source_target_pairs={{0,16},{2,10},{4,20},{6,14},{8,24},{10,2},{12,28},{14,6},{16,0},{1... | collective-permute-start | bytes 1966088 | tf_op jit(solution)/shard_map/ppermute | solution.py:599
  366.1 33.0 %collective-permute-start.37 = (bf16[512,1024]{1,0:T(8,128)(2,1)S(1)}, bf16[512,1024]{1,0:T(8,128)(2,1)}, u32[]{:S(2)}, u32[]{:S(2)}) collective-permute-start(bf16[512,1024]{1,0:T(8,128)(2,1)S(1)} %add_convert_fusion.refs_1_), channel_id=1, source_target_pairs={{0,2},{2,0},{4,6},{6,4},{8,10},{10,8},{12,14},{14,12},{16,18},{18,... | collective-permute-start | bytes 3145736 | tf_op jit(solution)/shard_map/ppermute | solution.py:580
  366.1 30.8 %collective-permute-start.36 = (bf16[512,1024]{1,0:T(8,128)(2,1)S(1)}, bf16[512,1024]{1,0:T(8,128)(2,1)}, u32[]{:S(2)}, u32[]{:S(2)}) collective-permute-start(bf16[512,1024]{1,0:T(8,128)(2,1)S(1)} %add_convert_fusion.refs_1_), channel_id=1, source_target_pairs={{0,4},{2,6},{4,0},{6,2},{8,12},{10,14},{12,8},{14,10},{16,20},{18,... | collective-permute-start | bytes 3145736 | tf_op jit(solution)/shard_map/ppermute | solution.py:580
  367.3 25.8 %collective-permute-start.33 = (bf16[256,768]{1,0:T(8,128)(2,1)S(1)}, bf16[256,768]{1,0:T(8,128)(2,1)S(1)}, u32[]{:S(2)}, u32[]{:S(2)}) collective-permute-start(bf16[256,768]{1,0:T(8,128)(2,1)S(1)} %add_convert_fusion.7), channel_id=1, source_target_pairs={{0,16},{2,10},{4,20},{6,14},{8,24},{10,2},{12,28},{14,6},{16,0},{1... | collective-permute-start | bytes 1179656 | tf_op jit(solution)/shard_map/ppermute | solution.py:599
  368.7 23.7 %collective-permute-start.29 = (f32[8,1024]{1,0:T(8,128)S(1)}, f32[8,1024]{1,0:T(8,128)S(1)}, u32[]{:S(2)}, u32[]{:S(2)}) collective-permute-start(f32[8,1024]{1,0:T(8,128)S(1)} %add.96.refs_5_), channel_id=1, source_target_pairs={{0,4},{2,6},{4,0},{6,2},{8,12},{10,14},{12,8},{14,10},{16,20},{18,... | collective-permute-start | bytes 98312 | tf_op jit(solution)/shard_map/ppermute | solution.py:580
  396.9 27.0 %collective-permute-start.31 = (bf16[512,1024]{1,0:T(8,128)(2,1)S(1)}, bf16[512,1024]{1,0:T(8,128)(2,1)}, u32[]{:S(2)}, u32[]{:S(2)}) collective-permute-start(bf16[512,1024]{1,0:T(8,128)(2,1)S(1)} %copy-done.12), channel_id=1, source_target_pairs={{0,1},{1,0},{2,3},{3,2},{4,5},{5,4},{6,7},{7,6},{8,9},{9,8},{10,11... | collective-permute-start | bytes 3145736 | tf_op jit(solution)/shard_map/ppermute | solution.py:584
  398.7 17.7 %collective-permute-start.40 = (bf16[256,1280]{1,0:T(8,128)(2,1)S(1)}, bf16[256,1280]{1,0:T(8,128)(2,1)}, u32[]{:S(2)}, u32[]{:S(2)}) collective-permute-start(bf16[256,1280]{1,0:T(8,128)(2,1)S(1)} %add_convert_fusion.4.refs_1_), channel_id=1, source_target_pairs={{0,4},{2,6},{4,0},{6,2},{8,12},{10,14},{12,8},{14,10},{16,20},{18,... | collective-permute-start | bytes 1966088 | tf_op jit(solution)/shard_map/ppermute | solution.py:580
  399.0 26.9 %collective-permute-start.43 = (bf16[256,1280]{1,0:T(8,128)(2,1)S(1)}, bf16[256,1280]{1,0:T(8,128)(2,1)S(1)}, u32[]{:S(2)}, u32[]{:S(2)}) collective-permute-start(bf16[256,1280]{1,0:T(8,128)(2,1)S(1)} %add_convert_fusion.4.refs_1_), channel_id=1, source_target_pairs={{0,2},{2,0},{4,6},{6,4},{8,10},{10,8},{12,14},{14,12},{16,18},{18,... | collective-permute-start | bytes 1966088 | tf_op jit(solution)/shard_map/ppermute | solution.py:580
  399.1 24.8 %collective-permute-start.39 = (bf16[256,768]{1,0:T(8,128)(2,1)S(1)}, bf16[256,768]{1,0:T(8,128)(2,1)S(1)}, u32[]{:S(2)}, u32[]{:S(2)}) collective-permute-start(bf16[256,768]{1,0:T(8,128)(2,1)S(1)} %add_convert_fusion.6.refs_1_), channel_id=1, source_target_pairs={{0,4},{2,6},{4,0},{6,2},{8,12},{10,14},{12,8},{14,10},{16,20},{18,... | collective-permute-start | bytes 1179656 | tf_op jit(solution)/shard_map/ppermute | solution.py:580
  410.5 26.2 %collective-permute-start.41 = (bf16[256,768]{1,0:T(8,128)(2,1)S(1)}, bf16[256,768]{1,0:T(8,128)(2,1)S(1)}, u32[]{:S(2)}, u32[]{:S(2)}) collective-permute-start(bf16[256,768]{1,0:T(8,128)(2,1)S(1)} %add_convert_fusion.6.refs_1_), channel_id=1, source_target_pairs={{0,2},{2,0},{4,6},{6,4},{8,10},{10,8},{12,14},{14,12},{16,18},{18,... | collective-permute-start | bytes 1179656 | tf_op jit(solution)/shard_map/ppermute | solution.py:580
  (39 other events, 337.7 us)

commit v6 on v5

--- a/solution.py
+++ b/solution.py
@@ -252,7 +252,7 @@
 def feed_kernel(place, own_tok, far_tok, own_cot, far_cot, att, w_out, w_up, w_down, gains, biases,
                 near_out, far_out, branch_out, normed2_out, active_out, back2_out, hidden_back_out, sums,
                 slope):
-    chunk = 1024
+    chunk = 512
     residual = pick_rows(own_tok, far_tok)
     branch = dot(att[...], w_out[...])
     branch_out[...] = branch
@@ -264,9 +264,12 @@
     ff = w_up.shape[1]
     root = math.sqrt(2.0 / math.pi)
     branch2 = jnp.zeros_like(branch)
+    ahead = dot(normed2, w_up[:, :chunk])
     for start in range(0, ff, chunk):
         cols = slice(start, start + chunk)
-        z = dot(normed2, w_up[:, cols])
+        z = ahead
+        if start + chunk < ff:
+            ahead = dot(normed2, w_up[:, start + chunk : start + 2 * chunk])
         square = z * z
         bend = jnp.tanh(z * (root + (root * 0.044715) * square))
         half = 0.5 + 0.5 * bend
@@ -545,7 +548,7 @@
         deps,
         "finish",
         24,
-        15,
+        8,
     )
 
 
@@ -658,7 +661,7 @@
             deps,
             "weight_grad",
             24,
-            0.5 + 0.3 * self.us * steps,
+            0.15 + 0.1 * self.us * steps,
         )
 
     def far(self, deps):
@@ -773,8 +776,8 @@
                 out[:, pl.ds(at, quarter)] = refs[2 * core + other][...].astype(F32)
 
 
-def gather_mixed(place, pieces, dims, half, earlier, deps):
-    piece = pl.BlockSpec((TILE, TILE), lambda i, p, place: (0, p))
+def gather_mixed(place, pieces, dims, first, half, earlier, deps):
+    piece = pl.BlockSpec((TILE, TILE), lambda i, p, place: (0, first + p))
     return call(
         gather_mixed_kernel,
         (2, 3),
@@ -871,8 +874,8 @@
     by_parts = lambda x, c, b, h: (0, 0, b)
     left = Reduction(
         place,
-        [(normed, by_rows, far_away(left_back), by_parts, TILE),
-         (far_away(att), by_rows, branch_back, lambda x, c, b, h: (0, b), half_wide)],
+        [(far_away(att), by_rows, branch_back, lambda x, c, b, h: (0, b), half_wide),
+         (normed, by_rows, far_away(left_back), by_parts, TILE)],
         TILE, 5 * TILE, 1, 1.2,
     )
     last = up.second([far_away(left_back)])
@@ -881,26 +884,25 @@
     last = up.keep([last])
     got_out = swap_narrow(tie(far_out, last))
     right_back = back(1, [last])
-    last = left.first([far_away(right_back)])
+    last = left.first([far_away(right_back), got_out])
     last = down.step(last)
     right = Reduction(
         place, [(normed, by_rows, far_away(right_back), by_parts, TILE)], TILE, 3 * TILE, 1, 0.8
     )
     last = right.far([last])
     last = up.step(last)
-    last = left.second([last])
-    last = right.first([last, got_out])
+    near_grad, far_grad, sums0 = finish(
+        place, tokens, far_tok, middle_back, left_back, right_back, w_qkv, norm_gains, [last]
+    )
+    last = left.second([sums0])
+    last = right.first([last])
     extra = len(down.bits) - 2
     for _ in range(extra):
         last = down.step(last)
     last = down.step(last)
     down.open(last)
-    near_grad, far_grad, sums0 = finish(
-        place, tokens, far_tok, middle_back, left_back, right_back, w_qkv, norm_gains,
-        [last, down.from_core],
-    )
-    last = right.second([sums0])
-    last = left.keep([last])
+    last = left.keep([last, down.from_core])
+    last = right.second([last])
     norm_term = jnp.concatenate(
         [sums0[0:1], sums12[0:1], sums12[2:3], sums3[0:1],
          sums0[1:2], sums12[1:2], sums12[3:4], sums3[1:2]], axis=0
@@ -914,21 +916,21 @@
             norm_got = swap_wide(norm_term, hops.pop(0))
         return norm_term
 
-    last = right.keep([last])
+    norm_got = swap_narrow(tie(norm_term, last))
     for _ in range(extra):
         last = up.step(last)
     last = up.step(last)
+    last = norm_step(last)
+    last = right.keep([last])
     up.open(last)
-    norm_got = swap_narrow(tie(norm_term, last))
+    last = norm_step(last)
     for _ in range(extra):
         last = left.step(last)
         last = right.step(last)
     last = left.step(last)
-    last = norm_step(last)
     last = right.step(last)
+    got_grad = swap_narrow(tie(far_grad, last))
     last = down.spread(last)
-    got_grad = swap_narrow(tie(far_grad, last))
-    last = norm_step(last)
     grad_down = gather(
         place, down.pieces(), (ff // 2, width), half_wide, 0, 2,
         lambda c, b, h: (2 * c + b, h), [last],
@@ -951,16 +953,16 @@
     last = norm_step(last)
     grad_tok = lax.dynamic_update_slice(near_grad, tie(got_grad, last)[None], (1 - n, 0, 0))
     last = left.spread(last)
-    last = right.spread(last)
     grad_out_proj = gather(
-        place, left.pieces(), (half_wide, width), TILE, 3, 2,
-        lambda c, b, h: (c, 2 * b + h), [last],
+        place, left.pieces(), (half_wide, width), half_wide, 0, 1,
+        lambda c, b, h: (c, b), [last],
     )
     grad_qkv = gather_mixed(
-        place, left.pieces(), (half_wide, 3 * width), 0, [], [last]
-    )
+        place, left.pieces(), (half_wide, 3 * width), 2, 0, [], [last]
+    )
+    right.spread(grad_qkv)
     grad_qkv = gather_mixed(
-        place, right.pieces(), (half_wide, 3 * width), 1, [grad_qkv], []
+        place, right.pieces(), (half_wide, 3 * width), 0, 1, [grad_qkv], []
     )
     norm_term = lax.dynamic_slice_in_dim(norm_term, n * half_wide, half_wide, 1)
     return (

time: 448 us -> 435 us (0.971)
  starting transfers between devices: 64.6 us -> 37 us
  Pallas kernels: 275 us -> 294 us
    ppermute x24, waiting for transfers between devices: 35 us -> 5.65 us  [swap_wide(): return lax.ppermute(rows, 'wide', [(i, i ^ bit) for i in range(size)])]
    ppermute x8, waiting for transfers between devices: 9.73 us -> 32.1 us  [swap_two(): lax.ppermute(rows, 'wide', [(i, i ^ (even_bit if i % 2 == 0 else odd_bit)...]
    pallas_call x29, Pallas kernels: 275 us -> 294 us  [call(): pl.pallas_call(body, grid_spec=pltpu.PrefetchScalarGridSpec(num_scalar_pr...]
    ppermute x8, starting transfers between devices: 22.2 us -> 12.4 us  [swap_two(): lax.ppermute(rows, 'wide', [(i, i ^ (even_bit if i % 2 == 0 else odd_bit)...]
    ppermute x24, starting transfers between devices: 21.4 us -> 12.6 us  [swap_wide(): return lax.ppermute(rows, 'wide', [(i, i ^ bit) for i in range(size)])]
    ppermute x8, starting transfers between devices: 13.2 us -> 6.79 us  [swap_crossed(): return lax.ppermute(rows, ('wide', 'narrow'), pairs)]
    ppermute x8, waiting for transfers between devices: 8.41 us -> 13.4 us  [swap_crossed(): return lax.ppermute(rows, ('wide', 'narrow'), pairs)]
  transfers between devices with their start and end apart: 45 -> 45, of which waited for: 13 -> 13; matrix products, arithmetic and copies ran while one was open for 5% -> 5% of each run, Pallas kernels for 48% -> 54%
where the time goes in v6:
time: 435 us; the launch traced here: 428 us
  Pallas kernels  294 us (68%)
  waiting for transfers between devices  64 us (15%)
  starting transfers between devices  37 us (9%)
  local copies, waits for them, and re-layouts  16 us (4%)
  other arithmetic  14.7 us (3%)
    pallas_call x29, Pallas kernels, call(): pl.pallas_call(body, grid_spec=pltpu.PrefetchScalarGridSpec(num_scalar_pr...  294 us
    ppermute x8, waiting for transfers between devices, swap_two(): lax.ppermute(rows, 'wide', [(i, i ^ (even_bit if i % 2 == 0 else odd_bit)...  32.1 us
    ppermute x8, waiting for transfers between devices, swap_crossed(): return lax.ppermute(rows, ('wide', 'narrow'), pairs)  13.4 us
    ppermute x5, waiting for transfers between devices, swap_narrow(): return lax.ppermute(rows, 'narrow', [(0, 1), (1, 0)])  12.9 us
    ppermute x24, starting transfers between devices, swap_wide(): return lax.ppermute(rows, 'wide', [(i, i ^ bit) for i in range(size)])  12.6 us
    ppermute x8, starting transfers between devices, swap_two(): lax.ppermute(rows, 'wide', [(i, i ^ (even_bit if i % 2 == 0 else odd_bit)...  12.4 us
  transfers between devices with their start and end apart: 45, of which 13 were waited for; matrix products, arithmetic and copies ran while one was open for 5% of the time, Pallas kernels for 54%

profile of v6, /device:TPU:0, one launch (start us, length us, event | category | flops | bytes accessed | tf_op | source)
XLA Modules:
  0.0 428.0 jit_solution(14201917268620754378)
XLA Ops:
  11.7 3.5 pad_maximum_fusion
  15.2 8.7 %project.2 = (bf16[1024,1024]{1,0:T(8,128)(2,1)}, bf16[1024,3072]{1,0:T(8,128)(2,1)}) custom-call(s32[5]{0:T(128)S(1)} %stack.36.refs_0_, bf16[2,512,1024]{2,1,0:T(8,128)(2,1)S(1)} %copy-done.12, bf16[1024,3072]{1,0:T(8,128)(2,1)} %refs_6_.3, f32[4,1024]{1,0:T(4,128)S(1)} %copy-done.18, f32[4,1024]{1,0:T(4,128)S(1)} %copy-done.17, ...), custom_call_target="tpu_custom_call" | custom-call | flops 8000000000 | bytes 1 | tf_op jit(solution)/shard_map/project/pallas_call | solution.py:34
  25.9 4.3 collective-permute-done.refs_1_.refs_2_
  30.2 8.9 %project.3 = (bf16[1024,1024]{1,0:T(8,128)(2,1)}, bf16[1024,3072]{1,0:T(8,128)(2,1)}) custom-call(s32[5]{0:T(128)S(1)} %stack.36.refs_0_, bf16[512,1024]{1,0:T(8,128)(2,1)} %collective-permute-done.refs_1_.refs_2_, bf16[1024,3072]{1,0:T(8,128)(2,1)} %refs_6_.3, f32[4,1024]{1,0:T(4,128)S(1)} %copy-done.18, ...), custom_call_target="tpu_custom_call", output_to_operand_aliasing={{0}: (7, {}), {1}: (8, {})} | custom-call | flops 8000000000 | bytes 1 | tf_op jit(solution)/shard_map/project/pallas_call | solution.py:34
  39.1 35.9 %attend.1 = (bf16[1024,1024]{1,0:T(8,128)(2,1)}, f32[4,4,1024]{2,1,0:T(4,128)S(1)}) custom-call(s32[5]{0:T(128)S(1)} %concatenate.19.refs_0_, bf16[1024,3072]{1,0:T(8,128)(2,1)} %get-tuple-element.67.refs_1_.refs_2_.refs_3_, bf16[1024,3072]{1,0:T(8,128)(2,1)} %get-tuple-element.67.refs_1_.refs_2_.refs_3_, ...), custom_call_target="tpu_custom_call" | custom-call | flops 35999997952 | bytes 1 | tf_op jit(solution)/shard_map/attend/pallas_call | solution.py:34
  76.0 50.9 %feed.1 = (bf16[2,512,1024]{2,1,0:T(8,128)(2,1)}, bf16[512,1024]{1,0:T(8,128)(2,1)S(1)}, f32[1024,1024]{1,0:T(8,128)}, bf16[1024,1024]{1,0:T(8,128)(2,1)}, bf16[...) custom-call(s32[5]{0:T(128)S(1)} %stack.36.refs_0_, ...), custom_call_target="tpu_custom_call" | custom-call | flops 49000001536 | bytes 1 | tf_op jit(solution)/shard_map/feed/pallas_call | solution.py:34
  128.4 7.5 %weight_grad.16 = (bf16[1024,1024]{1,0:T(8,128)(2,1)S(1)}, bf16[1024,1024]{1,0:T(8,128)(2,1)S(1)}) custom-call(s32[5]{0:T(128)S(1)} %stack.36.refs_0_, bf16[1024,4096]{1,0:T(8,128)(2,1)} %get-tuple-element.73.refs_1_, bf16[1024,1024]{1,0:T(8,128)(2,1)S(1)} %copy-done.1), custom_call_target="tpu_custom_call" | custom-call | flops 750000000 | bytes 1 | tf_op jit(solution)/shard_map/weight_grad/pallas_call | solution.py:34
  136.5 8.1 %weight_grad.17 = (bf16[1024,1024]{1,0:T(8,128)(2,1)S(1)}, bf16[1024,1024]{1,0:T(8,128)(2,1)S(1)}) custom-call(s32[5]{0:T(128)S(1)} %stack.36.refs_0_, bf16[1024,1024]{1,0:T(8,128)(2,1)S(1)} %copy-done.3, bf16[1024,4096]{1,0:T(8,128)(2,1)} %get-tuple-element.72.refs_2_.refs_6_, bf16[1024,1024]{1,0:T(8,128)(2,1)S(1)} %get-tuple-element.75.refs_3_), custom_call_target="tpu_custom_call" | custom-call | flops 750000000 | bytes 1 | tf_op jit(solution)/shard_map/weight_grad/pallas_call | solution.py:34
  145.8 4.8 %weight_grad.18.refs_4_ = bf16[1024,1024]{1,0:T(8,128)(2,1)S(1)} custom-call(s32[5]{0:T(128)S(1)} %stack.36.refs_0_, bf16[1024,4096]{1,0:T(8,128)(2,1)} %get-tuple-element.73.refs_1_, bf16[1024,1024]{1,0:T(8,128)(2,1)S(1)} %copy-done.2, bf16[1024,1024]{1,0:T(8,128)(2,1)S(1)} %collective-permute-done.4.refs_3_, ...), custom_call_target="tpu_custom_call" | custom-call | flops 450000000 | bytes 1 | tf_op jit(solution)/shard_map/weight_grad/pallas_call | solution.py:34
  152.7 4.8 %weight_grad.19.refs_11_ = bf16[1024,1024]{1,0:T(8,128)(2,1)S(1)} custom-call(s32[5]{0:T(128)S(1)} %stack.36.refs_0_, bf16[1024,1024]{1,0:T(8,128)(2,1)S(1)} %copy-done.3, bf16[1024,4096]{1,0:T(8,128)(2,1)} %get-tuple-element.72.refs_2_.refs_6_, bf16[1024,1024]{1,0:T(8,128)(2,1)S(1)} %collective-permute-done.3.refs_3_, ...), custom_call_target="tpu_custom_call" | custom-call | flops 450000000 | bytes 1 | tf_op jit(solution)/shard_map/weight_grad/pallas_call | solution.py:34
  158.8 24.9 %return_pass.1 = (f32[1024,1024]{1,0:T(8,128)}, bf16[1024,1024]{1,0:T(8,128)(2,1)S(1)}, bf16[1024,1024]{1,0:T(8,128)(2,1)S(1)}, f32[8,1024]{1,0:T(8,128)S(1)}) custom-call(s32[5]{0:T(128)S(1)} %stack.36.refs_0_, bf16[2,512,1024]{2,1,0:T(8,128)(2,1)} %refs_1_.7, bf16[512,1024]{1,0:T(8,128)(2,1)} %collective-permute-done.refs_1_.refs_2_, ...), custom_call_target="tpu_custom_call" | custom-call | flops 24000000000 | bytes 1 | tf_op jit(solution)/shard_map/return_pass/pallas_call | solution.py:34
  188.3 23.7 %attend_back.2.refs_5_.refs_4_ = bf16[3,1024,512]{2,1,0:T(8,128)(2,1)} custom-call(s32[5]{0:T(128)S(1)} %concatenate.19.refs_0_, bf16[1024,3072]{1,0:T(8,128)(2,1)} %get-tuple-element.67.refs_1_.refs_2_.refs_3_, bf16[1024,3072]{1,0:T(8,128)(2,1)} %get-tuple-element.67.refs_1_.refs_2_.refs_3_, bf16[1024,3072]{1,0:T(8,128)(2,1)} %get-tuple-element.67.refs_1_.refs_2_.refs_3_, ...), custom_call_target="tpu_custom_call" | custom-call | flops 24000000000 | bytes 1 | tf_op jit(solution)/shard_map/attend_back/pallas_call | solution.py:34
  212.1 3.5 weight_grad.21.refs_6_
  221.9 10.3 %weight_grad.23 = (bf16[512,1280]{1,0:T(8,128)(2,1)S(1)}, bf16[512,1280]{1,0:T(8,128)(2,1)S(1)}) custom-call(s32[5]{0:T(128)S(1)} %stack.36.refs_0_, bf16[1024,1024]{1,0:T(8,128)(2,1)} %get-tuple-element.68.refs_5_.refs_4_.refs_1_, bf16[1024,1024]{1,0:T(8,128)(2,1)S(1)} %get-tuple-element.83.refs_2_, bf16[1024,1024]{1,0:T(8,128)(2,1)S(1)} %copy-done, ...), custom_call_target="tpu_custom_call" | custom-call | flops 630000000 | bytes 1 | tf_op jit(solution)/shard_map/weight_grad/pallas_call | solution.py:34
  232.8 3.7 weight_grad.24.refs_9_
  240.1 23.7 %attend_back.3.refs_6_.refs_2_.refs_5_ = bf16[3,1024,512]{2,1,0:T(8,128)(2,1)} custom-call(s32[5]{0:T(128)S(1)} %concatenate.19.refs_0_, bf16[1024,3072]{1,0:T(8,128)(2,1)} %get-tuple-element.67.refs_1_.refs_2_.refs_3_, bf16[1024,3072]{1,0:T(8,128)(2,1)} %get-tuple-element.67.refs_1_.refs_2_.refs_3_, ...), custom_call_target="tpu_custom_call" | custom-call | flops 24000000000 | bytes 1 | tf_op jit(solution)/shard_map/attend_back/pallas_call | solution.py:34
  264.2 4.0 weight_grad.25
  270.6 7.3 %weight_grad.26 = (bf16[512,768]{1,0:T(8,128)(2,1)S(1)}, bf16[512,768]{1,0:T(8,128)(2,1)S(1)}) custom-call(s32[5]{0:T(128)S(1)} %stack.36.refs_0_, bf16[1024,1024]{1,0:T(8,128)(2,1)S(1)} %copy-done, bf16[3,1024,512]{2,1,0:T(8,128)(2,1)} %attend_back.3.refs_6_.refs_2_.refs_5_, bf16[512,1024]{1,0:T(8,128)(2,1)S(1)} %add_convert_fusion.3.refs_3_), custom_call_target="tpu_custom_call" | custom-call | flops 470000000 | bytes 1 | tf_op jit(solution)/shard_map/weight_grad/pallas_call | solution.py:34
  279.8 15.1 %finish.1 = (bf16[2,512,1024]{2,1,0:T(8,128)(2,1)}, bf16[512,1024]{1,0:T(8,128)(2,1)S(1)}, f32[8,1024]{1,0:T(8,128)S(1)}) custom-call(s32[5]{0:T(128)S(1)} %stack.36.refs_0_, bf16[2,512,1024]{2,1,0:T(8,128)(2,1)} %refs_1_.7, bf16[512,1024]{1,0:T(8,128)(2,1)} %collective-permute-done.refs_1_.refs_2_, f32[1024,1024]{1,0:T(8,128)} %get-tuple-element.87.refs_3_, ...), custom_call_target="tpu_custom_call" | custom-call | flops 8000000000 | bytes 1 | tf_op jit(solution)/shard_map/finish/pallas_call | solution.py:34
  299.0 3.6 weight_grad.28
  306.4 13.4 %collective-permute-done.19.refs_7_ = bf16[256,1280]{1,0:T(8,128)(2,1)S(1)} collective-permute-done((bf16[256,1280]{1,0:T(8,128)(2,1)S(1)}, bf16[256,1280]{1,0:T(8,128)(2,1)S(1)}, u32[]{:S(2)}, u32[]{:S(2)}) %collective-permute-start.19) | collective-permute-done | bytes 655392 | tf_op jit(solution)/shard_map/ppermute | solution.py:597
  325.9 3.4 weight_grad.30
  333.3 6.3 %collective-permute-done.23 = bf16[512,1024]{1,0:T(8,128)(2,1)} collective-permute-done((bf16[512,1024]{1,0:T(8,128)(2,1)}, bf16[512,1024]{1,0:T(8,128)(2,1)}, u32[]{:S(2)}, u32[]{:S(2)}) %collective-permute-start.23) | collective-permute-done | bytes 1048608 | tf_op jit(solution)/shard_map/ppermute | solution.py:602
  348.2 10.3 %collective-permute-done.28 = bf16[256,768]{1,0:T(8,128)(2,1)S(1)} collective-permute-done((bf16[256,768]{1,0:T(8,128)(2,1)S(1)}, bf16[256,768]{1,0:T(8,128)(2,1)S(1)}, u32[]{:S(2)}, u32[]{:S(2)}) %collective-permute-start.28) | collective-permute-done | bytes 393248 | tf_op jit(solution)/shard_map/ppermute | solution.py:602
  364.7 5.6 %gather.3 = f32[2048,1024]{1,0:T(8,128)} custom-call(s32[5]{0:T(128)S(1)} %stack.36.refs_0_, bf16[512,1024]{1,0:T(8,128)(2,1)S(1)} %copy-done.5, bf16[512,1024]{1,0:T(8,128)(2,1)S(1)} %collective-permute-done.27.refs_2_.refs_5_, bf16[512,1024]{1,0:T(8,128)(2,1)S(1)} %copy-done.11, bf16[512,1024]{1,0:T(8,128)(2,1)S(1)} %collective-permute-done.30.refs_4_, ...), custom_call_target="tpu_custom_call" | custom-call | flops 6000000000 | bytes 1 | tf_op jit(solution)/shard_map/gather/pallas_call | solution.py:34
  370.8 7.4 %collective-permute-done.34 = bf16[256,1280]{1,0:T(8,128)(2,1)S(1)} collective-permute-done((bf16[256,1280]{1,0:T(8,128)(2,1)S(1)}, bf16[256,1280]{1,0:T(8,128)(2,1)S(1)}, u32[]{:S(2)}, u32[]{:S(2)}) %collective-permute-start.34) | collective-permute-done | bytes 655392 | tf_op jit(solution)/shard_map/ppermute | solution.py:602
  378.3 8.1 %collective-permute-done.33 = bf16[256,768]{1,0:T(8,128)(2,1)S(1)} collective-permute-done((bf16[256,768]{1,0:T(8,128)(2,1)S(1)}, bf16[256,768]{1,0:T(8,128)(2,1)S(1)}, u32[]{:S(2)}, u32[]{:S(2)}) %collective-permute-start.33) | collective-permute-done | bytes 393248 | tf_op jit(solution)/shard_map/ppermute | solution.py:602
  393.2 8.1 %gather.4 = f32[512,4096]{1,0:T(8,128)} custom-call(s32[5]{0:T(128)S(1)} %stack.36.refs_0_, bf16[512,1024]{1,0:T(8,128)(2,1)} %add_convert_fusion.refs_1_, bf16[512,1024]{1,0:T(8,128)(2,1)} %collective-permute-done.36.refs_2_.refs_5_, bf16[512,1024]{1,0:T(8,128)(2,1)S(1)} %collective-permute-done.37.refs_3_, ...), custom_call_target="tpu_custom_call" | custom-call | flops 6000000000 | bytes 1 | tf_op jit(solution)/shard_map/gather/pallas_call | solution.py:34
  402.2 3.9 collective-permute-done.40.refs_2_.refs_5_
  406.2 7.0 %collective-permute-done.31 = bf16[512,1024]{1,0:T(8,128)(2,1)} collective-permute-done((bf16[512,1024]{1,0:T(8,128)(2,1)S(1)}, bf16[512,1024]{1,0:T(8,128)(2,1)}, u32[]{:S(2)}, u32[]{:S(2)}) %collective-permute-start.31) | collective-permute-done | bytes 1048608 | tf_op jit(solution)/shard_map/ppermute | solution.py:587
  415.4 5.2 %gather_mixed.2.refs_5_ = f32[512,3072]{1,0:T(8,128)} custom-call(s32[5]{0:T(128)S(1)} %stack.36.refs_0_, bf16[256,1280]{1,0:T(8,128)(2,1)S(1)} %add_convert_fusion.4.refs_1_, bf16[256,1280]{1,0:T(8,128)(2,1)} %collective-permute-done.40.refs_2_.refs_5_, bf16[256,1280]{1,0:T(8,128)(2,1)S(1)} %collective-permute-done.41.refs_3_, ...), custom_call_target="tpu_custom_call" | custom-call | flops 4000000000 | bytes 1 | tf_op jit(solution)/shard_map/gather_mixed/pallas_call | solution.py:34
  424.1 3.5 gather_mixed.3
  (171 shorter events, 86.4 us)
Async XLA Ops:
  2.9 27.3 %collective-permute-start = (bf16[512,1024]{1,0:T(8,128)(2,1)}, bf16[512,1024]{1,0:T(8,128)(2,1)}, u32[]{:S(2)}, u32[]{:S(2)}) collective-permute-start(bf16[512,1024]{1,0:T(8,128)(2,1)} %dynamic-slice_bitcast_fusion.1), channel_id=1, source_target_pairs={{0,1},{1,0},{2,3},{3,2},{4,5},{5,4},{6,7},{7,6},{8,9},{9,8},{10,11... | collective-permute-start | bytes 3145736 | tf_op jit(solution)/shard_map/ppermute | solution.py:587
  23.9 51.1 %collective-permute-start.1 = (bf16[512,1024]{1,0:T(8,128)(2,1)}, bf16[512,1024]{1,0:T(8,128)(2,1)S(1)}, u32[]{:S(2)}, u32[]{:S(2)}) collective-permute-start(bf16[512,1024]{1,0:T(8,128)(2,1)} %dynamic-slice_bitcast_fusion), channel_id=1, source_target_pairs={{0,1},{1,0},{2,3},{3,2},{4,5},{5,4},{6,7},{7,6},{8,9},{9,8},{10,11... | collective-permute-start | bytes 3145736 | tf_op jit(solution)/shard_map/ppermute | solution.py:587
  150.6 34.5 %collective-permute-start.7 = (bf16[1024,1024]{1,0:T(8,128)(2,1)S(1)}, bf16[1024,1024]{1,0:T(8,128)(2,1)S(1)}, u32[]{:S(2)}, u32[]{:S(2)}) collective-permute-start(bf16[1024,1024]{1,0:T(8,128)(2,1)S(1)} %weight_grad.18.refs_4_), channel_id=1, source_target_pairs={{0,1},{1,0},{2,6},{3,7},{4,5},{5,4},{6,2},{7,3},{8,9},{9,8},{10,14... | collective-permute-start | bytes 6291464 | tf_op jit(solution)/shard_map/ppermute | solution.py:597
  157.5 54.5 %collective-permute-start.6 = (bf16[1024,1024]{1,0:T(8,128)(2,1)S(1)}, bf16[1024,1024]{1,0:T(8,128)(2,1)S(1)}, u32[]{:S(2)}, u32[]{:S(2)}) collective-permute-start(bf16[1024,1024]{1,0:T(8,128)(2,1)S(1)} %weight_grad.19.refs_11_), channel_id=1, source_target_pairs={{0,1},{1,0},{2,6},{3,7},{4,5},{5,4},{6,2},{7,3},{8,9},{9,8},{10,14... | collective-permute-start | bytes 6291464 | tf_op jit(solution)/shard_map/ppermute | solution.py:597
  188.3 27.4 %collective-permute-start.9 = (bf16[512,1024]{1,0:T(8,128)(2,1)S(1)}, bf16[512,1024]{1,0:T(8,128)(2,1)S(1)}, u32[]{:S(2)}, u32[]{:S(2)}) collective-permute-start(bf16[512,1024]{1,0:T(8,128)(2,1)S(1)} %weight_grad.20.refs_9_), channel_id=1, source_target_pairs={{0,4},{1,5},{2,3},{3,2},{4,0},{5,1},{6,7},{7,6},{8,12},{9,13},{10,... | collective-permute-start | bytes 3145736 | tf_op jit(solution)/shard_map/ppermute | solution.py:597
  215.6 17.2 %collective-permute-start.8 = (bf16[512,1024]{1,0:T(8,128)(2,1)S(1)}, bf16[512,1024]{1,0:T(8,128)(2,1)S(1)}, u32[]{:S(2)}, u32[]{:S(2)}) collective-permute-start(bf16[512,1024]{1,0:T(8,128)(2,1)S(1)} %weight_grad.21.refs_6_), channel_id=1, source_target_pairs={{0,4},{1,5},{2,3},{3,2},{4,0},{5,1},{6,7},{7,6},{8,12},{9,13},{10,... | collective-permute-start | bytes 3145736 | tf_op jit(solution)/shard_map/ppermute | solution.py:597
  219.0 50.6 %collective-permute-start.12 = (bf16[512,1024]{1,0:T(8,128)(2,1)S(1)}, bf16[512,1024]{1,0:T(8,128)(2,1)S(1)}, u32[]{:S(2)}, u32[]{:S(2)}) collective-permute-start(bf16[512,1024]{1,0:T(8,128)(2,1)S(1)} %weight_grad.22.refs_5_), channel_id=1, source_target_pairs={{0,8},{2,18},{4,12},{6,22},{8,0},{10,26},{12,4},{14,30},{16,24},{1... | collective-permute-start | bytes 3145736 | tf_op jit(solution)/shard_map/ppermute | solution.py:602
  232.2 32.0 %collective-permute-start.13 = (bf16[512,1280]{1,0:T(8,128)(2,1)S(1)}, bf16[512,1280]{1,0:T(8,128)(2,1)S(1)}, u32[]{:S(2)}, u32[]{:S(2)}) collective-permute-start(bf16[512,1280]{1,0:T(8,128)(2,1)S(1)} %get-tuple-element.85.refs_6_), channel_id=1, source_target_pairs={{0,2},{2,0},{4,6},{6,4},{8,10},{10,8},{12,14},{14,12},{16,18},{18,... | collective-permute-start | bytes 3932168 | tf_op jit(solution)/shard_map/ppermute | solution.py:583
  236.5 41.5 %collective-permute-start.11 = (bf16[512,1024]{1,0:T(8,128)(2,1)S(1)}, bf16[512,1024]{1,0:T(8,128)(2,1)S(1)}, u32[]{:S(2)}, u32[]{:S(2)}) collective-permute-start(bf16[512,1024]{1,0:T(8,128)(2,1)S(1)} %weight_grad.24.refs_9_), channel_id=1, source_target_pairs={{0,8},{2,18},{4,12},{6,22},{8,0},{10,26},{12,4},{14,30},{16,24},{1... | collective-permute-start | bytes 3145736 | tf_op jit(solution)/shard_map/ppermute | solution.py:602
  238.3 25.8 %collective-permute-start.10 = (bf16[512,1024]{1,0:T(8,128)(2,1)S(1)}, bf16[512,1024]{1,0:T(8,128)(2,1)S(1)}, u32[]{:S(2)}, u32[]{:S(2)}) collective-permute-start(bf16[512,1024]{1,0:T(8,128)(2,1)S(1)} %get-tuple-element.86), channel_id=1, source_target_pairs={{0,1},{1,0},{2,3},{3,2},{4,5},{5,4},{6,7},{7,6},{8,9},{9,8},{10,11... | collective-permute-start | bytes 3145736 | tf_op jit(solution)/shard_map/ppermute | solution.py:587
  239.8 24.4 %collective-permute-start.14 = (bf16[512,1280]{1,0:T(8,128)(2,1)S(1)}, bf16[512,1280]{1,0:T(8,128)(2,1)S(1)}, u32[]{:S(2)}, u32[]{:S(2)}) collective-permute-start(bf16[512,1280]{1,0:T(8,128)(2,1)S(1)} %get-tuple-element.88), channel_id=1, source_target_pairs={{0,2},{2,0},{4,6},{6,4},{8,10},{10,8},{12,14},{14,12},{16,18},{18,... | collective-permute-start | bytes 3932168 | tf_op jit(solution)/shard_map/ppermute | solution.py:583
  268.2 27.7 %collective-permute-start.17 = (bf16[512,1280]{1,0:T(8,128)(2,1)S(1)}, bf16[512,1280]{1,0:T(8,128)(2,1)S(1)}, u32[]{:S(2)}, u32[]{:S(2)}) collective-permute-start(bf16[512,1280]{1,0:T(8,128)(2,1)S(1)} %weight_grad.25), channel_id=1, source_target_pairs={{0,1},{1,0},{2,6},{3,7},{4,5},{5,4},{6,2},{7,3},{8,9},{9,8},{10,14... | collective-permute-start | bytes 3932168 | tf_op jit(solution)/shard_map/ppermute | solution.py:597
  270.0 32.6 %collective-permute-start.20 = (bf16[512,1024]{1,0:T(8,128)(2,1)S(1)}, bf16[512,1024]{1,0:T(8,128)(2,1)S(1)}, u32[]{:S(2)}, u32[]{:S(2)}) collective-permute-start(bf16[512,1024]{1,0:T(8,128)(2,1)S(1)} %add_convert_fusion.3.refs_3_), channel_id=1, source_target_pairs={{0,16},{2,10},{4,20},{6,14},{8,24},{10,2},{12,28},{14,6},{16,0},{1... | collective-permute-start | bytes 3145736 | tf_op jit(solution)/shard_map/ppermute | solution.py:602
  277.9 21.1 %collective-permute-start.16 = (bf16[512,768]{1,0:T(8,128)(2,1)S(1)}, bf16[512,768]{1,0:T(8,128)(2,1)S(1)}, u32[]{:S(2)}, u32[]{:S(2)}) collective-permute-start(bf16[512,768]{1,0:T(8,128)(2,1)S(1)} %get-tuple-element.90), channel_id=1, source_target_pairs={{0,2},{2,0},{4,6},{6,4},{8,10},{10,8},{12,14},{14,12},{16,18},{18,... | collective-permute-start | bytes 2359304 | tf_op jit(solution)/shard_map/ppermute | solution.py:583
  278.0 21.0 %collective-permute-start.15 = (bf16[512,768]{1,0:T(8,128)(2,1)S(1)}, bf16[512,768]{1,0:T(8,128)(2,1)S(1)}, u32[]{:S(2)}, u32[]{:S(2)}) collective-permute-start(bf16[512,768]{1,0:T(8,128)(2,1)S(1)} %get-tuple-element.94), channel_id=1, source_target_pairs={{0,2},{2,0},{4,6},{6,4},{8,10},{10,8},{12,14},{14,12},{16,18},{18,... | collective-permute-start | bytes 2359304 | tf_op jit(solution)/shard_map/ppermute | solution.py:583
  303.0 16.7 %collective-permute-start.21 = (bf16[512,1024]{1,0:T(8,128)(2,1)S(1)}, bf16[512,1024]{1,0:T(8,128)(2,1)S(1)}, u32[]{:S(2)}, u32[]{:S(2)}) collective-permute-start(bf16[512,1024]{1,0:T(8,128)(2,1)S(1)} %add_convert_fusion.1.refs_8_.refs_1_), channel_id=1, source_target_pairs={{0,2},{2,0},{4,6},{6,4},{8,10},{10,8},{12,14},{14,12},{16,18},{18,... | collective-permute-start | bytes 3145736 | tf_op jit(solution)/shard_map/ppermute | solution.py:583
  303.2 16.6 %collective-permute-start.19 = (bf16[256,1280]{1,0:T(8,128)(2,1)S(1)}, bf16[256,1280]{1,0:T(8,128)(2,1)S(1)}, u32[]{:S(2)}, u32[]{:S(2)}) collective-permute-start(bf16[256,1280]{1,0:T(8,128)(2,1)S(1)} %weight_grad.27.refs_4_), channel_id=1, source_target_pairs={{0,4},{1,5},{2,3},{3,2},{4,0},{5,1},{6,7},{7,6},{8,12},{9,13},{10,... | collective-permute-start | bytes 1966088 | tf_op jit(solution)/shard_map/ppermute | solution.py:597
  304.5 35.2 %collective-permute-start.23 = (bf16[512,1024]{1,0:T(8,128)(2,1)}, bf16[512,1024]{1,0:T(8,128)(2,1)}, u32[]{:S(2)}, u32[]{:S(2)}) collective-permute-start(bf16[512,1024]{1,0:T(8,128)(2,1)} %add_convert_fusion.2.refs_8_), channel_id=1, source_target_pairs={{0,16},{2,10},{4,20},{6,14},{8,24},{10,2},{12,28},{14,6},{16,0},{1... | collective-permute-start | bytes 3145736 | tf_op jit(solution)/shard_map/ppermute | solution.py:602
  306.0 19.9 %collective-permute-start.18 = (bf16[512,768]{1,0:T(8,128)(2,1)S(1)}, bf16[512,768]{1,0:T(8,128)(2,1)S(1)}, u32[]{:S(2)}, u32[]{:S(2)}) collective-permute-start(bf16[512,768]{1,0:T(8,128)(2,1)S(1)} %weight_grad.28), channel_id=1, source_target_pairs={{0,1},{1,0},{2,6},{3,7},{4,5},{5,4},{6,2},{7,3},{8,9},{9,8},{10,14... | collective-permute-start | bytes 2359304 | tf_op jit(solution)/shard_map/ppermute | solution.py:597
  323.0 23.8 %collective-permute-start.29 = (bf16[256,1280]{1,0:T(8,128)(2,1)S(1)}, bf16[256,1280]{1,0:T(8,128)(2,1)}, u32[]{:S(2)}, u32[]{:S(2)}) collective-permute-start(bf16[256,1280]{1,0:T(8,128)(2,1)S(1)} %weight_grad.29.refs_5_), channel_id=1, source_target_pairs={{0,8},{2,18},{4,12},{6,22},{8,0},{10,26},{12,4},{14,30},{16,24},{1... | collective-permute-start | bytes 1966088 | tf_op jit(solution)/shard_map/ppermute | solution.py:602
  329.3 14.6 %collective-permute-start.25 = (bf16[256,768]{1,0:T(8,128)(2,1)}, bf16[256,768]{1,0:T(8,128)(2,1)}, u32[]{:S(2)}, u32[]{:S(2)}) collective-permute-start(bf16[256,768]{1,0:T(8,128)(2,1)} %weight_grad.30), channel_id=1, source_target_pairs={{0,4},{1,5},{2,3},{3,2},{4,0},{5,1},{6,7},{7,6},{8,12},{9,13},{10,... | collective-permute-start | bytes 1179656 | tf_op jit(solution)/shard_map/ppermute | solution.py:597
  331.5 28.1 %collective-permute-start.27 = (bf16[512,1024]{1,0:T(8,128)(2,1)}, bf16[512,1024]{1,0:T(8,128)(2,1)S(1)}, u32[]{:S(2)}, u32[]{:S(2)}) collective-permute-start(bf16[512,1024]{1,0:T(8,128)(2,1)} %copy-done.4), channel_id=1, source_target_pairs={{0,4},{2,6},{4,0},{6,2},{8,12},{10,14},{12,8},{14,10},{16,20},{18,... | collective-permute-start | bytes 3145736 | tf_op jit(solution)/shard_map/ppermute | solution.py:583
  359.7 18.5 %collective-permute-start.34 = (bf16[256,1280]{1,0:T(8,128)(2,1)S(1)}, bf16[256,1280]{1,0:T(8,128)(2,1)S(1)}, u32[]{:S(2)}, u32[]{:S(2)}) collective-permute-start(bf16[256,1280]{1,0:T(8,128)(2,1)S(1)} %add_convert_fusion.5), channel_id=1, source_target_pairs={{0,16},{2,10},{4,20},{6,14},{8,24},{10,2},{12,28},{14,6},{16,0},{1... | collective-permute-start | bytes 1966088 | tf_op jit(solution)/shard_map/ppermute | solution.py:602
  360.3 29.6 %collective-permute-start.37 = (bf16[512,1024]{1,0:T(8,128)(2,1)}, bf16[512,1024]{1,0:T(8,128)(2,1)S(1)}, u32[]{:S(2)}, u32[]{:S(2)}) collective-permute-start(bf16[512,1024]{1,0:T(8,128)(2,1)} %add_convert_fusion.refs_1_), channel_id=1, source_target_pairs={{0,2},{2,0},{4,6},{6,4},{8,10},{10,8},{12,14},{14,12},{16,18},{18,... | collective-permute-start | bytes 3145736 | tf_op jit(solution)/shard_map/ppermute | solution.py:583
  362.1 25.4 %collective-permute-start.36 = (bf16[512,1024]{1,0:T(8,128)(2,1)}, bf16[512,1024]{1,0:T(8,128)(2,1)}, u32[]{:S(2)}, u32[]{:S(2)}) collective-permute-start(bf16[512,1024]{1,0:T(8,128)(2,1)} %add_convert_fusion.refs_1_), channel_id=1, source_target_pairs={{0,4},{2,6},{4,0},{6,2},{8,12},{10,14},{12,8},{14,10},{16,20},{18,... | collective-permute-start | bytes 3145736 | tf_op jit(solution)/shard_map/ppermute | solution.py:583
  362.3 24.1 %collective-permute-start.33 = (bf16[256,768]{1,0:T(8,128)(2,1)S(1)}, bf16[256,768]{1,0:T(8,128)(2,1)S(1)}, u32[]{:S(2)}, u32[]{:S(2)}) collective-permute-start(bf16[256,768]{1,0:T(8,128)(2,1)S(1)} %add_convert_fusion.7), channel_id=1, source_target_pairs={{0,16},{2,10},{4,20},{6,14},{8,24},{10,2},{12,28},{14,6},{16,0},{1... | collective-permute-start | bytes 1179656 | tf_op jit(solution)/shard_map/ppermute | solution.py:602
  370.3 16.2 %collective-permute-start.32 = (f32[8,1024]{1,0:T(8,128)S(1)}, f32[8,1024]{1,0:T(8,128)S(1)}, u32[]{:S(2)}, u32[]{:S(2)}) collective-permute-start(f32[8,1024]{1,0:T(8,128)S(1)} %add.97), channel_id=1, source_target_pairs={{0,8},{2,10},{4,12},{6,14},{8,0},{10,2},{12,4},{14,6},{16,24},{18,... | collective-permute-start | bytes 98312 | tf_op jit(solution)/shard_map/ppermute | solution.py:583
  387.5 25.7 %collective-permute-start.31 = (bf16[512,1024]{1,0:T(8,128)(2,1)S(1)}, bf16[512,1024]{1,0:T(8,128)(2,1)}, u32[]{:S(2)}, u32[]{:S(2)}) collective-permute-start(bf16[512,1024]{1,0:T(8,128)(2,1)S(1)} %copy-done.14), channel_id=1, source_target_pairs={{0,1},{1,0},{2,3},{3,2},{4,5},{5,4},{6,7},{7,6},{8,9},{9,8},{10,11... | collective-permute-start | bytes 3145736 | tf_op jit(solution)/shard_map/ppermute | solution.py:587
  388.4 17.7 %collective-permute-start.40 = (bf16[256,1280]{1,0:T(8,128)(2,1)S(1)}, bf16[256,1280]{1,0:T(8,128)(2,1)}, u32[]{:S(2)}, u32[]{:S(2)}) collective-permute-start(bf16[256,1280]{1,0:T(8,128)(2,1)S(1)} %add_convert_fusion.4.refs_1_), channel_id=1, source_target_pairs={{0,4},{2,6},{4,0},{6,2},{8,12},{10,14},{12,8},{14,10},{16,20},{18,... | collective-permute-start | bytes 1966088 | tf_op jit(solution)/shard_map/ppermute | solution.py:583
  389.9 25.5 %collective-permute-start.41 = (bf16[256,1280]{1,0:T(8,128)(2,1)S(1)}, bf16[256,1280]{1,0:T(8,128)(2,1)S(1)}, u32[]{:S(2)}, u32[]{:S(2)}) collective-permute-start(bf16[256,1280]{1,0:T(8,128)(2,1)S(1)} %add_convert_fusion.4.refs_1_), channel_id=1, source_target_pairs={{0,2},{2,0},{4,6},{6,4},{8,10},{10,8},{12,14},{14,12},{16,18},{18,... | collective-permute-start | bytes 1966088 | tf_op jit(solution)/shard_map/ppermute | solution.py:583
  389.9 34.2 %collective-permute-start.43 = (bf16[256,768]{1,0:T(8,128)(2,1)S(1)}, bf16[256,768]{1,0:T(8,128)(2,1)S(1)}, u32[]{:S(2)}, u32[]{:S(2)}) collective-permute-start(bf16[256,768]{1,0:T(8,128)(2,1)S(1)} %add_convert_fusion.6.refs_1_), channel_id=1, source_target_pairs={{0,2},{2,0},{4,6},{6,4},{8,10},{10,8},{12,14},{14,12},{16,18},{18,... | collective-permute-start | bytes 1179656 | tf_op jit(solution)/shard_map/ppermute | solution.py:583
  401.3 19.3 %collective-permute-start.39 = (bf16[256,768]{1,0:T(8,128)(2,1)S(1)}, bf16[256,768]{1,0:T(8,128)(2,1)S(1)}, u32[]{:S(2)}, u32[]{:S(2)}) collective-permute-start(bf16[256,768]{1,0:T(8,128)(2,1)S(1)} %add_convert_fusion.6.refs_1_), channel_id=1, source_target_pairs={{0,4},{2,6},{4,0},{6,2},{8,12},{10,14},{12,8},{14,10},{16,20},{18,... | collective-permute-start | bytes 1179656 | tf_op jit(solution)/shard_map/ppermute | solution.py:583
  (39 other events, 333.9 us)
